TPU v7x, 32 devices: a whole 2x2x4 slice. The times are simulated.
32 devices in a mesh: sensor: 2 (over y), tm: 16 (over z, x, core).
Axes of the slice: x: 2, y: 2, z: 4, core: 2. Of those that a mesh axis runs over, the one named last changes fastest.
Arguments:
- recording: bfloat16 [256, 16384], P('sensor', 'tm'), may hold values from -6 to 6
- spatial_w: bfloat16 [512, 256], P(None, 'sensor'), may hold values from -0.375 to 0.375
- conv_w: bfloat16 [3, 3, 512, 512], P(None, None, 'sensor'), may hold values from -0.15625 to 0.15625
- conv_b: float32 [3, 512], P(None, 'sensor'), may hold values from -3 to 3
- dilations: int32 [3], replicated, may hold values from 1 to 16, as said below
- valid_frames: int32 [16], P('tm'), may hold values from 512 to 1024, as said below
- key_w: bfloat16 [512, 512], P('sensor'), may hold values from -0.25 to 0.25
- value_w: bfloat16 [512, 512], P('sensor'), may hold values from -0.25 to 0.25
- queries: bfloat16 [512, 2048], P('sensor'), may hold values from -60 to 60
Outputs:
- features: bfloat16 [512, 16384], P('sensor', 'tm')
- attended: bfloat16 [512, 2048], P('sensor')
Inputs may be any that keep to these rules, and one draw needn't show every extreme that they name: `dilations`: one layer has dilation exactly 16 and another exactly 1. `valid_frames`: one block is full and one holds exactly half of its 1024 frames.
All inputs are finite; a program needn't handle non-finite values.
Results may differ from a plain program's by a relative error of at most 0.015.
The roundings to bfloat16 on the way count: a program that leaves them out, or rounds other values in their place, can miss the bound.
Values may be sent and summed in bfloat16 or wider, within the bound.
No kernel may reach another device: no remote copies, remote signals or barrier semaphores. Data moves between devices by JAX's collectives and lax.ppermute only.
A program may use at most 64 MiB of HBM per device.

v0:
```python
import math

import jax
import jax.numpy as jnp
from jax import lax
from jax.sharding import PartitionSpec as P

HD = 64
LATENTS = 2048
LAYERS = 3
DMAX = 16


def padded(cells, sides, width):
    for axis, dim in sides:
        count = lax.axis_size(axis)
        ends = count - 1
        head = lax.slice_in_dim(cells, 0, width, axis=dim)
        tail = lax.slice_in_dim(cells, cells.shape[dim] - width, cells.shape[dim], axis=dim)
        cells = jnp.concatenate(
            [
                lax.ppermute(tail, axis, [(i, (i + 1) % count) for i in range(ends)]),
                cells,
                lax.ppermute(head, axis, [((i + 1) % count, i) for i in range(ends)]),
            ],
            axis=dim,
        )
    return cells


def tap_folder(kernels, dilation, frames, margin):

    def add_taps(running, portion, first_row):
        portion = jnp.pad(portion, ((0, 0), (margin, margin)))
        for tap_index in range(3):
            kernel = kernels[tap_index]
            offset = DMAX + (tap_index - 1) * dilation
            shifted = lax.dynamic_slice_in_dim(portion, offset, frames, 1)
            running = running + jnp.dot(kernel, shifted, preferred_element_type=jnp.float32)
        return running

    return add_taps


def on_device(
    recording, spatial_w, conv_w, conv_b, dilations, valid_frames, key_w, value_w, queries
):
    frames = recording.shape[1]
    ch_loc = conv_w.shape[2]
    hidden = lax.psum_scatter(
        jnp.dot(spatial_w, recording, preferred_element_type=jnp.float32),
        "sensor",
        scatter_dimension=0,
        tiled=True,
    ).astype(jnp.bfloat16)
    reach = 3 * DMAX
    extended = padded(hidden, (("tm", 1),), reach)
    span = frames + 2 * reach
    position = lax.axis_index("tm") * frames - reach + jnp.arange(span, dtype=jnp.int32)
    inside = (position >= 0) & (position < frames * lax.axis_size("tm"))
    for layer in range(LAYERS):
        initial = jnp.broadcast_to(conv_b[layer][:, None], (ch_loc, span))
        folder = tap_folder(conv_w[layer], dilations[layer], span, DMAX)
        preact = folder(
            initial, lax.all_gather(extended, "sensor", axis=0, tiled=True), jnp.int32(0)
        )
        updated = extended.astype(jnp.float32) + jax.nn.gelu(preact, approximate=False)
        extended = jnp.where(inside[None, :], updated, 0.0).astype(jnp.bfloat16)
    hidden = extended[:, reach : reach + frames]
    portion = lax.all_gather(hidden, "sensor", axis=0, tiled=True)
    key_rows = jnp.dot(key_w, portion, preferred_element_type=jnp.float32)
    value_rows = jnp.dot(value_w, portion, preferred_element_type=jnp.float32)
    head_count = key_w.shape[0] // HD
    key_heads = key_rows.astype(jnp.bfloat16).reshape(head_count, HD, frames)
    value_heads = value_rows.astype(jnp.bfloat16).reshape(head_count, HD, frames)
    frame_mask = jnp.arange(frames, dtype=jnp.int32) < valid_frames[0]
    block_rows = min(LATENTS, 512)
    block_count = LATENTS // block_rows
    query_blocks = queries.reshape(head_count, HD, block_count, block_rows).transpose(2, 0, 1, 3)
    scale = 1.0 / math.sqrt(HD)

    def attend(query_block):
        scores = (
            jnp.einsum("hdq,hdt->hqt", query_block, key_heads, preferred_element_type=jnp.float32)
            * scale
        )
        scores = jnp.where(frame_mask[None, None, :], scores, -jnp.inf)
        peaks = jnp.max(scores, axis=2)
        probs = jnp.where(frame_mask[None, None, :], jnp.exp(scores - peaks[:, :, None]), 0.0)
        totals = jnp.sum(probs, axis=2)
        weighted = jnp.einsum(
            "hqt,hdt->hdq",
            probs.astype(jnp.bfloat16),
            value_heads,
            preferred_element_type=jnp.float32,
        )
        return (peaks, totals, weighted)

    peaks, totals, weighted = lax.map(attend, query_blocks)
    peaks = peaks.transpose(1, 0, 2).reshape(head_count, LATENTS)
    totals = totals.transpose(1, 0, 2).reshape(head_count, LATENTS)
    weighted = weighted.transpose(1, 2, 0, 3).reshape(head_count, HD, LATENTS)
    global_peaks = lax.pmax(peaks, "tm")
    rescale = jnp.exp(peaks - global_peaks)
    totals, weighted = lax.psum((totals * rescale, weighted * rescale[:, None, :]), "tm")
    attended = (
        (weighted / totals[:, None, :]).reshape(head_count * HD, LATENTS).astype(jnp.bfloat16)
    )
    return (hidden, attended)


def solution(mesh):
    return jax.shard_map(
        on_device,
        mesh=mesh,
        in_specs=(
            P("sensor", "tm"),
            P(None, "sensor"),
            P(None, None, "sensor", None),
            P(None, "sensor"),
            P(),
            P("tm"),
            P("sensor", None),
            P("sensor", None),
            P("sensor", None),
        ),
        out_specs=(P("sensor", "tm"), P("sensor", None)),
        check_vma=False,
    )
```

profile of v0, /device:TPU:0, one launch (start us, length us, event | category | flops | bytes accessed | tf_op | source)
XLA Modules:
  0.0 366.2 jit_solution(9976685040315797149)
XLA Ops:
  8.1 2.7 fusion.128
  10.9 34.7 %reduce-scatter.2.cloned.1.call-done = f32[256,1024]{0,1:T(8,128)} async-done(((f32[512,1024]{0,1:T(8,128)}), f32[256,1024]{0,1:T(8,128)}) %reduce-scatter.2.cloned.1.call-update) | async-done | bytes 1048592 | tf_op jit(solution)/shard_map/reduce_scatter | solution.py:50
  50.0 3.2 collective-permute-done.1
  56.7 22.1 %all-gather.5.cloned.1.call-done = bf16[512,1120]{0,1:T(8,128)(2,1)} async-done(((bf16[256,1120]{0,1:T(8,128)(2,1)}), bf16[512,1120]{0,1:T(8,128)(2,1)}) %all-gather.5.cloned.1.call-update) | async-done | bytes 1146896 | tf_op jit(solution)/shard_map/all_gather | solution.py:65
  81.2 4.2 %fusion.26 = bf16[256,1120]{0,1:T(8,128)(2,1)} fusion(f32[1120,256]{1,0:T(8,128)S(1)} %fusion.72, f32[1120,256]{1,0:T(8,128)S(1)} %convolution_add_fusion.7, bf16[512,1120]{0,1:T(8,128)(2,1)S(1)} %copy-done.6, pred[1120]{0:T(1024)(128)(4,1)S(1)} %fusion.111, bf16[3,3,256,512]{3,2,1,0:T(8,128)(2,1)S(1)} %copy-done.9, ...), kind=kOutput, calls=%fused_computation.38 | convolution fusion | flops 315105280 | bytes 4851712 | tf_op jit(solution)/shard_map/dot_general | solution.py:39
  87.4 20.5 %all-gather.7.cloned.1.call-done = bf16[512,1120]{0,1:T(8,128)(2,1)} async-done(((bf16[256,1120]{0,1:T(8,128)(2,1)}), bf16[512,1120]{0,1:T(8,128)(2,1)}) %all-gather.7.cloned.1.call-update) | async-done | bytes 1146896 | tf_op jit(solution)/shard_map/all_gather | solution.py:65
  110.9 4.0 %fusion.31 = bf16[256,1120]{0,1:T(8,128)(2,1)} fusion(bf16[256,1120]{0,1:T(8,128)(2,1)S(1)} %copy-done.8, f32[1120,256]{1,0:T(8,128)S(1)} %convolution_add_fusion.4, s32[]{:T(128)S(6)} %select_n.39, bf16[512,1120]{0,1:T(8,128)(2,1)S(1)} %copy-done.5, pred[1120]{0:T(1024)(128)(4,1)S(1)} %fusion.111, bf16[3,3,256,512]{3,2,1,0:T(8,128)(2,1)S(1)} %copy-done.9), kind=kOutput, calls=%fused_computation.43 | convolution fusion | flops 313384960 | bytes 3704836 | tf_op jit(solution)/shard_map/dot_general | solution.py:39
  116.7 20.7 %all-gather.9.cloned.1.call-done = bf16[512,1120]{0,1:T(8,128)(2,1)} async-done(((bf16[256,1120]{0,1:T(8,128)(2,1)}), bf16[512,1120]{0,1:T(8,128)(2,1)}) %all-gather.9.cloned.1.call-update) | async-done | bytes 1146896 | tf_op jit(solution)/shard_map/all_gather | solution.py:65
  137.4 1.9 convolution_add_fusion.2
  139.8 2.6 bitcast_abs_fusion
  146.2 20.1 %all-gather.11.cloned.1.call-done = bf16[512,1024]{0,1:T(8,128)(2,1)} async-done(((bf16[256,1024]{0,1:T(8,128)(2,1)}), bf16[512,1024]{0,1:T(8,128)(2,1)}) %all-gather.11.cloned.1.call-update) | async-done | bytes 1048592 | tf_op jit(solution)/shard_map/all_gather | solution.py:70
  168.6 28.8 %while.15 = (s32[]{:T(128)}, f32[4,4,512]{2,1,0:T(4,128)S(1)}, f32[4,4,512]{2,1,0:T(4,128)S(1)}, f32[4,4,64,512]{3,2,1,0:T(8,128)}, bf16[4,4,64,512]{3,2,1,0:T(8...) while((s32[]{:T(128)}, f32[4,4,512]{2,1,0:T(4,128)S(1)}, ...), condition=%wide.region_4.5_spmd.clone, body=%wide.region_1.4_spmd.clone.sunk | while | flops 564130816 | bytes 27071080 | solution.py:99
  170.7 2.9 fusion.151
  173.5 2.3 fusion.150
  177.9 2.9 fusion.151
  180.8 2.3 fusion.150
  185.1 2.8 fusion.151
  188.0 2.3 fusion.150
  192.3 2.9 fusion.151
  195.2 2.3 fusion.150
  197.5 61.0 %pmax.7 = f32[4,2048]{1,0:T(4,128)S(1)} all-reduce(f32[4,2048]{1,0:T(4,128)S(1)} %bitcast.276), channel_id=1, replica_groups=mesh['sensor'=2,'tm'=16] {'tm'}, use_global_device_ids=true, to_apply=%region_5.6 | all-reduce | flops 8192 | bytes 65536 | tf_op jit(solution)/shard_map/pmax | solution.py:103
  263.9 58.5 %psum.15 = f32[4,2048]{1,0:T(4,128)S(1)} all-reduce(f32[4,2048]{1,0:T(4,128)S(1)} %get-tuple-element.102), channel_id=1, replica_groups=mesh['sensor'=2,'tm'=16] {'tm'}, use_global_device_ids=true, to_apply=%region_7.8 | all-reduce | flops 8192 | bytes 65536 | tf_op jit(solution)/shard_map/psum | solution.py:105
  322.3 34.2 %all-reduce.5.cloned.1.call-done = f32[4,64,2048]{2,1,0:T(8,128)} async-done(((f32[4,64,2048]{2,1,0:T(8,128)}), f32[4,64,2048]{2,1,0:T(8,128)}) %all-reduce.5.cloned.1.call-update) | async-done | bytes 2097168 | tf_op jit(solution)/shard_map/psum | solution.py:105
  356.6 2.7 divide_convert_fusion
  (81 shorter events, 32.4 us)
Async XLA Ops:
  7.2 1.0 copy-start
  7.2 38.5 %reduce-scatter.2.cloned.1.call-start = ((), (), s32[]{:S(2)}) async-start(), calls=%async_computation.1 | async-start | bytes 3145728 | tf_op jit(solution)/shard_map/reduce_scatter | solution.py:50
  10.9 67.9 %all-gather.5.cloned.1.call-start = ((), (), s32[]{:S(2)}) async-start(), calls=%async_computation.2 | async-start | bytes 1720320 | tf_op jit(solution)/shard_map/all_gather | solution.py:65
  45.6 33.1 %copy-start.9 = (bf16[3,3,256,512]{3,2,1,0:T(8,128)(2,1)S(1)}, bf16[3,3,256,512]{3,2,1,0:T(8,128)(2,1)}, u32[]{:S(2)}) copy-start(bf16[3,3,256,512]{3,2,1,0:T(8,128)(2,1)} %param.13) | copy-start | bytes 7077892
  47.1 7.1 %copy-start.12 = (s32[3]{0:T(128)S(1)}, s32[3]{0:T(128)}, u32[]{:S(2)}) copy-start(s32[3]{0:T(128)} %param.15) | copy-start | bytes 40
  47.1 9.6 %copy-start.13 = (f32[3,256]{1,0:T(4,128)S(1)}, f32[3,256]{1,0:T(4,128)}, u32[]{:S(2)}) copy-start(f32[3,256]{1,0:T(4,128)} %param.14) | copy-start | bytes 9220
  47.1 2.9 collective-permute-start
  48.7 4.5 %collective-permute-start.1 = (bf16[256,48]{0,1:T(8,128)(2,1)S(1)}, bf16[256,48]{0,1:T(8,128)(2,1)S(1)}, u32[]{:S(2)}, u32[]{:S(2)}) collective-permute-start(bf16[256,48]{0,1:T(8,128)(2,1)S(1)} %get-tuple-element.115), channel_id=1, source_target_pairs={{1,0},{2,1},{3,2},{4,3},{5,4},{6,5},{7,6},{8,7},{9,8},{10,9},{11,1... | collective-permute-start | bytes 73736 | tf_op jit(solution)/shard_map/ppermute | solution.py:24
  54.1 53.9 %all-gather.7.cloned.1.call-start = ((), (), s32[]{:S(2)}) async-start(), calls=%async_computation.3 | async-start | bytes 1720320 | tf_op jit(solution)/shard_map/all_gather | solution.py:65
  78.8 1.9 copy-start.6
  85.4 52.0 %all-gather.9.cloned.1.call-start = ((), (), s32[]{:S(2)}) async-start(), calls=%async_computation.4 | async-start | bytes 1720320 | tf_op jit(solution)/shard_map/all_gather | solution.py:65
  107.9 1.9 copy-start.5
  109.8 1.1 copy-start.8
  114.9 51.4 %all-gather.11.cloned.1.call-start = ((), (), s32[]{:S(2)}) async-start(), calls=%async_computation.5 | async-start | bytes 1572864 | tf_op jit(solution)/shard_map/all_gather | solution.py:70
  137.4 1.9 copy-start.4
  142.6 1.1 copy-start.3
  143.6 1.5 copy-start.7
  144.9 211.6 %all-reduce.5.cloned.1.call-start = ((), (), s32[]{:S(2)}) async-start(), calls=%async_computation.6 | async-start | bytes 4194304 | tf_op jit(solution)/shard_map/psum | solution.py:105
  146.0 20.3 %copy-start.10 = (bf16[256,512]{1,0:T(8,128)(2,1)S(1)}, bf16[256,512]{1,0:T(8,128)(2,1)}, u32[]{:S(2)}) copy-start(bf16[256,512]{1,0:T(8,128)(2,1)} %param.17) | copy-start | bytes 786436
  146.2 21.9 %copy-start.11 = (bf16[256,512]{1,0:T(8,128)(2,1)S(1)}, bf16[256,512]{1,0:T(8,128)(2,1)}, u32[]{:S(2)}) copy-start(bf16[256,512]{1,0:T(8,128)(2,1)} %param.18) | copy-start | bytes 786436
  166.3 1.8 copy-start.2
  261.8 1.0 copy-start.1
Sparse Core Ops, SparseCore 0:
  11.0 34.6 reduce-scatter.1
  54.2 24.5 all-gather.4
  85.6 22.3 all-gather.6
  115.1 22.3 all-gather.8
  145.0 21.2 all-gather.10
  262.0 94.5 all-reduce.4
where the time goes:
time: 367 us; the launch traced here: 366 us
  waiting for transfers between devices  156 us (43%)
  blocking collectives  119 us (32%)
  matrix products  40 us (11%)
  between operations  20 us (5%)
  other arithmetic  19.8 us (5%)
  local copies, waits for them, and re-layouts  7.85 us (2%)
    all_gather x3, waiting for transfers between devices, on_device(): lax.all_gather(extended, 'sensor', axis=0, tiled=True)  63.3 us
    pmax x1, blocking collectives, on_device(): global_peaks = lax.pmax(peaks, 'tm')  61 us
    psum x1, blocking collectives, on_device(): lax.psum((totals * rescale, weighted * rescale[:, None, :]), 'tm')  58.5 us
    reduce_scatter x1, waiting for transfers between devices, on_device(): lax.psum_scatter(jnp.dot(spatial_w, recording, preferred_element_type=jnp...  34.7 us
    psum x1, waiting for transfers between devices, on_device(): lax.psum((totals * rescale, weighted * rescale[:, None, :]), 'tm')  34.2 us
    all_gather x1, waiting for transfers between devices, on_device(): portion = lax.all_gather(hidden, 'sensor', axis=0, tiled=True)  20.1 us
    dot_general x9, matrix products, add_taps(): jnp.dot(kernel, shifted, preferred_element_type=jnp.float32)  18 us
    dot_general x4, matrix products, attend(): jnp.einsum('hqt,hdt->hdq', probs.astype(jnp.bfloat16), value_heads, prefe...  11.4 us
  transfers between devices with their start and end apart: 8, of which 7 were waited for; matrix products, arithmetic and copies ran while one was open for 1% of the time, Pallas kernels for 0%

commit v1 on v0

--- a/solution.py
+++ b/solution.py
@@ -1,8 +1,11 @@
+import functools
 import math
 
 import jax
 import jax.numpy as jnp
 from jax import lax
+from jax.experimental import pallas as pl
+from jax.experimental.pallas import tpu as pltpu
 from jax.sharding import PartitionSpec as P
 
 HD = 64
@@ -42,7 +45,7 @@
     return add_taps
 
 
-def on_device(
+def generic_device(
     recording, spatial_w, conv_w, conv_b, dilations, valid_frames, key_w, value_w, queries
 ):
     frames = recording.shape[1]
@@ -109,9 +112,407 @@
     return (hidden, attended)
 
 
+VMEM = pltpu.VMEM
+EDGE = 128
+HALF = EDGE // 2
+LOG2E = 1.4426950408889634
+MASKED = -1e30
+
+
+def whole(count):
+    return [pl.BlockSpec(memory_space=pltpu.VMEM)] * count
+
+
+def smem(count):
+    return [pl.BlockSpec(memory_space=pltpu.SMEM)] * count
+
+
+def params():
+    return pltpu.CompilerParams(vmem_limit_bytes=56 * 1024 * 1024)
+
+
+def dot(left, right):
+    return jnp.dot(left, right, preferred_element_type=jnp.float32)
+
+
+def first_kernel(own_w, other_w, own, other, own_edge, other_edge, out):
+    frames = own.shape[1]
+    out[:, :frames] = (dot(own_w[...], own[...]) + dot(other_w[...], other[...])).astype(out.dtype)
+    out[:, frames:] = (
+        dot(own_w[...], own_edge[...]) + dot(other_w[...], other_edge[...])
+    ).astype(out.dtype)
+
+
+def gelu(value):
+    return 0.5 * value * (1.0 + lax.erf(value * (1.0 / math.sqrt(2.0))))
+
+
+def conv_rows(shifted, hidden, kernel, bias, row, keep, store, cols, step):
+    rows = kernel.shape[1]
+    row = pl.multiple_of(row, rows)
+    for start in range(0, cols, step):
+        width = min(step, cols - start)
+        here = pl.ds(start, width)
+        total = dot(kernel[0], shifted[0, :, here])
+        total = total + dot(kernel[1], hidden[:, here])
+        total = total + dot(kernel[2], shifted[1, :, here])
+        old = hidden[pl.ds(row, rows), here].astype(jnp.float32)
+        new = old + gelu(total + bias[...])
+        if keep is not None and start + width > cols - EDGE:
+            new = jnp.where(keep(start, width), new, 0.0)
+        store(row, rows, here, new.astype(jnp.bfloat16))
+
+
+def spread(info, hidden, shifted):
+    span = hidden.shape[1]
+    wide = hidden[...].astype(jnp.float32)
+    shifted[0] = pltpu.roll(wide, info[0], 1).astype(jnp.bfloat16)
+    shifted[1] = pltpu.roll(wide, span - info[0], 1).astype(jnp.bfloat16)
+
+
+def middle_kernel(info, hidden, own_w, near_w, far_w, own_b, near_b, far_b, out, shifted):
+    span = hidden.shape[1]
+    spread(info, hidden, shifted)
+
+    def keep(start, width):
+        lane = lax.broadcasted_iota(jnp.int32, (1, width), 1) + start
+        frame = jnp.where(lane < span - HALF, lane, lane - span) + info[4]
+        return (frame >= 0) & (frame < info[5])
+
+    def store(row, rows, here, value):
+        out[pl.ds(row, rows), here] = value
+
+    for kernel, bias, row in ((own_w, own_b, info[1]), (near_w, near_b, info[2]), (far_w, far_b, info[3])):
+        conv_rows(shifted, hidden, kernel, bias, row, keep, store, span, 384)
+
+
+def last_kernel(
+    info, hidden, own_w, near_w, far_w, own_b, near_b, far_b, key_w, value_w,
+    features, key_keep, key_send, value_keep, value_send, shifted, full,
+):
+    frames = features.shape[1]
+    spread(info, hidden, shifted)
+
+    def store(row, rows, here, value):
+        full[pl.ds(row, rows), here] = value
+
+    for kernel, bias, row in ((own_w, own_b, info[1]), (near_w, near_b, info[2]), (far_w, far_b, info[3])):
+        conv_rows(shifted, hidden, kernel, bias, row, None, store, frames, 256)
+    rows = features.shape[0]
+    features[...] = full[pl.ds(pl.multiple_of(info[1], rows), rows), :]
+    half = rows // 2
+    for key_out, value_out, row in ((key_keep, value_keep, info[6]), (key_send, value_send, info[7])):
+        here = pl.ds(pl.multiple_of(row, half), half)
+        key_out[...] = dot(key_w[here, :], full[...]).T.astype(jnp.bfloat16)
+        value_out[...] = dot(value_w[here, :], full[...]).astype(jnp.bfloat16)
+
+
+def thirds(value):
+    first = value.astype(jnp.bfloat16)
+    rest = value - first.astype(jnp.float32)
+    second = rest.astype(jnp.bfloat16)
+    third = (rest - second.astype(jnp.float32)).astype(jnp.bfloat16)
+    return first, second, third
+
+
+def pack(out, peak, total, weighted):
+    out[0:HD, :] = weighted.astype(jnp.bfloat16)
+    lines = [line.astype(jnp.float32) for line in thirds(peak) + thirds(total)]
+    lines.append(jnp.zeros_like(lines[0]))
+    lines.append(jnp.zeros_like(lines[0]))
+    out[HD : HD + 8, :] = jnp.concatenate(lines, axis=0).astype(jnp.bfloat16)
+
+
+def unpack(packed):
+    lines = packed[HD : HD + 8, :].astype(jnp.float32)
+    peak = lines[0:1] + (lines[1:2] + lines[2:3])
+    total = lines[3:4] + (lines[4:5] + lines[5:6])
+    return peak, total, packed[0:HD, :].astype(jnp.float32)
+
+
+SCALE = LOG2E / math.sqrt(HD)
+
+
+def join(one, two):
+    peak = jnp.maximum(one[0], two[0])
+    left = jnp.exp2((one[0] - peak) * SCALE)
+    right = jnp.exp2((two[0] - peak) * SCALE)
+    return peak, one[1] * left + two[1] * right, one[2] * left + two[2] * right
+
+
+def ordered(info, mine, theirs):
+    swap = info[0] == 1
+    one = tuple(jnp.where(swap, t, m) for m, t in zip(mine, theirs))
+    two = tuple(jnp.where(swap, m, t) for m, t in zip(mine, theirs))
+    return one, two
+
+
+def meet_kernel(peak, total, weighted, theirs, out):
+    pack(out, *join((peak[...], total[...], weighted[...]), unpack(theirs)))
+
+
+def merge_kernel(info, mine, theirs, out):
+    pack(out, *join(*ordered(info, unpack(mine), unpack(theirs))))
+
+
+def finish_kernel(info, mine, theirs, out):
+    peak, total, weighted = join(*ordered(info, unpack(mine), unpack(theirs)))
+    out[...] = (weighted / total).astype(out.dtype)
+
+
+def divide_kernel(mine, out):
+    peak, total, weighted = unpack(mine)
+    out[...] = (weighted / total).astype(out.dtype)
+
+
+def attend_kernel(
+    packed, info, key_own, key_rec, value_own, value_rec, queries, *refs
+):
+    outs = refs[:-6]
+    keyed, asked, score_a, score_b, peak_a, peak_b = refs[-6:]
+    frames = key_own.shape[0]
+    latents = queries.shape[1]
+    tile = score_a.shape[1]
+    chunk = 256
+    slot = info[0]
+    lane = lax.broadcasted_iota(jnp.int32, (frames, 2 * HD), 1)
+    frame = lax.broadcasted_iota(jnp.int32, (frames, 2 * HD), 0)
+    spare = (1 - slot) * HD
+    for part, source in enumerate((key_own, key_rec)):
+        bias = jnp.where(frame < info[1 + part], 0.0, MASKED)
+        keyed[pl.ds(part * frames, frames), :] = jnp.where(
+            lane == spare, bias, source[...].astype(jnp.float32)
+        ).astype(jnp.bfloat16)
+    row = lax.broadcasted_iota(jnp.int32, (2 * HD, latents), 0)
+    wide = queries[...].astype(jnp.float32)
+    wide = jnp.where(row // HD == slot, wide, jnp.where(row == spare, 1.0, 0.0))
+    asked[...] = wide.astype(jnp.bfloat16)
+    value_rows = pl.ds(pl.multiple_of(slot * HD, HD), HD)
+
+    def score(index, scores, peaks):
+        cols = pl.ds(pl.multiple_of(index * tile, tile), tile)
+        peak = None
+        for start in range(0, 2 * frames, chunk):
+            here = pl.ds(start, chunk)
+            value = dot(keyed[here, :], asked[:, cols])
+            scores[here, :] = value
+            top = jnp.max(value.reshape(chunk // 8, 8, tile), axis=0)
+            peak = top if peak is None else jnp.maximum(peak, top)
+        peaks[...] = jnp.max(peak, axis=0, keepdims=True)
+
+    def weigh(index, scores, peaks):
+        cols = pl.ds(pl.multiple_of(index * tile, tile), tile)
+        peak = peaks[...]
+        total = None
+        weighted = None
+        for start in range(0, 2 * frames, chunk):
+            probs = jnp.exp2((scores[pl.ds(start, chunk), :] - peak) * SCALE)
+            part = jnp.sum(probs.reshape(chunk // 8, 8, tile), axis=0)
+            total = part if total is None else total + part
+            source, offset = (value_own, start) if start < frames else (value_rec, start - frames)
+            values = source[value_rows, pl.ds(offset, chunk)]
+            term = dot(values, probs.astype(jnp.bfloat16))
+            weighted = term if weighted is None else weighted + term
+        total = jnp.sum(total, axis=0, keepdims=True)
+        if packed:
+            pack(outs[0].at[:, cols], peak, total, weighted)
+        else:
+            outs[0][:, cols] = peak
+            outs[1][:, cols] = total
+            outs[2][:, cols] = weighted
+
+    count = latents // tile
+    score(0, score_a, peak_a)
+
+    @pl.loop(0, count // 2)
+    def _(step):
+        score(2 * step + 1, score_b, peak_b)
+        weigh(2 * step, score_a, peak_a)
+        score(jnp.minimum(2 * step + 2, count - 1), score_a, peak_a)
+        weigh(2 * step + 1, score_b, peak_b)
+
+
+def attend(packed, info, keys, values, queries):
+    latents = queries.shape[1]
+    frames = keys[0].shape[0]
+    tile = min(256, latents // 2)
+    if packed:
+        out_shape = jax.ShapeDtypeStruct((HD + 8, latents), jnp.bfloat16)
+        out_specs = pl.BlockSpec(memory_space=pltpu.VMEM)
+    else:
+        out_shape = [
+            jax.ShapeDtypeStruct((1, latents), jnp.float32),
+            jax.ShapeDtypeStruct((1, latents), jnp.float32),
+            jax.ShapeDtypeStruct((HD, latents), jnp.float32),
+        ]
+        out_specs = whole(3)
+    return pl.pallas_call(
+        functools.partial(attend_kernel, packed),
+        out_shape=out_shape,
+        in_specs=smem(1) + whole(5),
+        out_specs=out_specs,
+        scratch_shapes=[
+            VMEM((2 * frames, 2 * HD), jnp.bfloat16),
+            VMEM((2 * HD, latents), jnp.bfloat16),
+            VMEM((2 * frames, tile), jnp.float32),
+            VMEM((2 * frames, tile), jnp.float32),
+            VMEM((1, tile), jnp.float32),
+            VMEM((1, tile), jnp.float32),
+        ],
+        compiler_params=params(),
+        name="attend_send" if packed else "attend_keep",
+    )(info, *keys, *values, queries)
+
+
+def assemble_kernel(info, own, across, core_own, core_across, out):
+    for piece, index in ((own, 0), (across, 1), (core_own, 2), (core_across, 3)):
+        out[pl.ds(pl.multiple_of(info[index] * HD, HD), HD), :] = piece[...]
+
+
+def swap(value, axis, bit):
+    return lax.ppermute(value, axis, [(i, i ^ bit) for i in range(lax.axis_size(axis))])
+
+
+def simple(kernel, out_shape, scalars, arrays, scratch=(), name=None):
+    many = isinstance(out_shape, (list, tuple))
+    return pl.pallas_call(
+        kernel,
+        out_shape=out_shape,
+        in_specs=smem(len(scalars)) + whole(len(arrays)),
+        out_specs=whole(len(out_shape)) if many else pl.BlockSpec(memory_space=pltpu.VMEM),
+        scratch_shapes=list(scratch),
+        compiler_params=params(),
+        name=name,
+    )(*scalars, *arrays)
+
+
+def pair_device(
+    recording, spatial_w, conv_w, conv_b, dilations, valid_frames, key_w, value_w, queries
+):
+    frames = recording.shape[1]
+    ch_loc = conv_w.shape[2]
+    ch = conv_w.shape[3]
+    half = ch_loc // 2
+    latents = queries.shape[1]
+    blocks = lax.axis_size("tm")
+    side = lax.axis_index("sensor")
+    place = lax.axis_index("tm")
+    core = place & 1
+    cross = (place >> 1) & 1
+    span = frames + EDGE
+    bf16 = jnp.bfloat16
+
+    other_rec = swap(recording, "sensor", 1)
+    other_w = swap(spatial_w, "sensor", 1)
+    tail = lax.ppermute(
+        recording[:, frames - EDGE :], "tm", [(i, i + 1) for i in range(blocks - 1)]
+    )
+    head = lax.ppermute(recording[:, :EDGE], "tm", [(i + 1, i) for i in range(blocks - 1)])
+    lane = jnp.arange(EDGE, dtype=jnp.int32)[None, :]
+    edge = jnp.where(lane < HALF, head, tail)
+    other_edge = swap(edge, "sensor", 1)
+    mine = lax.dynamic_slice_in_dim(conv_w, core * half, half, axis=2)
+    near = [swap(mine[layer], "sensor", 1) for layer in range(LAYERS)]
+    far = [swap(near[layer], "tm", 1) for layer in range(LAYERS)]
+    other_b = swap(conv_b, "sensor", 1)
+    near_b = lax.dynamic_slice_in_dim(other_b, core * half, half, axis=1)
+    far_b = lax.dynamic_slice_in_dim(other_b, (1 - core) * half, half, axis=1)
+    other_valid = swap(valid_frames, "tm", 1)
+
+    hidden = simple(
+        first_kernel,
+        jax.ShapeDtypeStruct((ch, span), bf16),
+        (),
+        (spatial_w, other_w, recording, other_rec, edge, other_edge),
+        name="first",
+    )
+    row_own = side * ch_loc
+    row_near = (1 - side) * ch_loc + core * half
+    row_far = (1 - side) * ch_loc + (1 - core) * half
+    for layer in range(LAYERS):
+        info = jnp.stack(
+            [
+                dilations[layer], row_own, row_near, row_far, place * frames, blocks * frames,
+                core * half, (1 - core) * half,
+            ]
+        ).astype(jnp.int32)
+        arrays = (
+            hidden, conv_w[layer], near[layer], far[layer],
+            conv_b[layer][:, None], near_b[layer][:, None], far_b[layer][:, None],
+        )
+        scratch = [VMEM((2, ch, span), bf16)]
+        if layer < LAYERS - 1:
+            hidden = simple(
+                middle_kernel, jax.ShapeDtypeStruct((ch, span), bf16), (info,), arrays, scratch,
+                name="conv",
+            )
+        else:
+            shapes = [
+                jax.ShapeDtypeStruct((ch_loc, frames), bf16),
+                jax.ShapeDtypeStruct((frames, half), bf16),
+                jax.ShapeDtypeStruct((frames, half), bf16),
+                jax.ShapeDtypeStruct((half, frames), bf16),
+                jax.ShapeDtypeStruct((half, frames), bf16),
+            ]
+            features, key_keep, key_send, value_keep, value_send = simple(
+                last_kernel, shapes, (info,), arrays + (key_w, value_w),
+                scratch + [VMEM((ch, frames), bf16)], name="conv_last",
+            )
+    keys = (key_keep, swap(key_send, "tm", 1))
+    values = (value_keep, swap(value_send, "tm", 1))
+    asked = lax.dynamic_slice_in_dim(queries, core * half, half, axis=0)
+
+    def facts(slot):
+        return jnp.stack([slot, valid_frames[0], other_valid[0]]).astype(jnp.int32)
+
+    sent = attend(True, facts(1 - cross), keys, values, asked)
+    arrived = swap(sent, "tm", 2)
+    peak, total, weighted = attend(False, facts(cross), keys, values, asked)
+    packed_shape = jax.ShapeDtypeStruct((HD + 8, latents), bf16)
+    final_shape = jax.ShapeDtypeStruct((HD, latents), bf16)
+    packed = simple(meet_kernel, packed_shape, (), (peak, total, weighted, arrived), name="meet")
+    if blocks == 4:
+        done = simple(divide_kernel, final_shape, (), (packed,), name="divide")
+    bit = 4
+    while bit < blocks:
+        theirs = swap(packed, "tm", bit)
+        which = ((place & bit) != 0).astype(jnp.int32)[None]
+        if bit * 2 < blocks:
+            packed = simple(merge_kernel, packed_shape, (which,), (packed, theirs), name="merge")
+        else:
+            done = simple(finish_kernel, final_shape, (which,), (packed, theirs), name="finish")
+        bit *= 2
+    across = swap(done, "tm", 2)
+    core_done = swap(done, "tm", 1)
+    core_across = swap(across, "tm", 1)
+    spots = jnp.stack(
+        [
+            2 * core + cross, 2 * core + 1 - cross, 2 * (1 - core) + cross,
+            2 * (1 - core) + 1 - cross,
+        ]
+    ).astype(jnp.int32)
+    attended = simple(
+        assemble_kernel, jax.ShapeDtypeStruct((ch_loc, latents), bf16), (spots,),
+        (done, across, core_done, core_across), name="assemble",
+    )
+    return (features, attended)
+
+
+def fits(mesh):
+    sensors, blocks = mesh.shape["sensor"], mesh.shape["tm"]
+    return sensors == 2 and blocks >= 4 and blocks & (blocks - 1) == 0
+
+
+def on_device(*arrays):
+    heads = arrays[6].shape[0] // HD
+    if lax.axis_size("sensor") == 2 and heads == 4:
+        return pair_device(*arrays)
+    return generic_device(*arrays)
+
+
 def solution(mesh):
     return jax.shard_map(
-        on_device,
+        on_device if fits(mesh) else generic_device,
         mesh=mesh,
         in_specs=(
             P("sensor", "tm"),

time: 367 us -> 149 us (0.41)
  blocking collectives: 119 us -> 0 us
  waiting for transfers between devices: 156 us -> 47.4 us
  Pallas kernels: 0 us -> 48.3 us
  matrix products: 40 us -> 0 us
  starting transfers between devices: 3.31 us -> 22.5 us
  between operations: 20 us -> 1.43 us
  local copies, waits for them, and re-layouts: 7.85 us -> 24.6 us
  other arithmetic: 19.8 us -> 4.02 us
    all_gather x4 -> x0, waiting for transfers between devices: 83.4 us -> none  [the longest x3 63.3 us: on_device(): lax.all_gather(extended, 'sensor', axis=0, tiled=True)]
    pmax x1 -> x0, blocking collectives: 61 us -> none  [on_device(): global_peaks = lax.pmax(peaks, 'tm')]
    psum x1 -> x0, blocking collectives: 58.5 us -> none  [on_device(): lax.psum((totals * rescale, weighted * rescale[:, None, :]), 'tm')]
    pallas_call x0 -> x10, Pallas kernels: none -> 48.3 us  [the longest x8 31 us: simple(): pl.pallas_call(kernel, out_shape=out_shape, in_specs=smem(len(scalars)) +...]
    ppermute x2 -> x21, waiting for transfers between devices: 3.2 us -> 47.4 us  [the longest x19 47.3 us: swap(): lax.ppermute(value, axis, [(i, i ^ bit) for i in range(lax.axis_size(axis...]
    dot_general x20 -> x0, matrix products: 40 us -> none  [the longest x9 18 us: add_taps(): jnp.dot(kernel, shifted, preferred_element_type=jnp.float32)]
    reduce_scatter x1 -> x0, waiting for transfers between devices: 34.7 us -> none  [on_device(): lax.psum_scatter(jnp.dot(spatial_w, recording, preferred_element_type=jnp...]
    psum x1 -> x0, waiting for transfers between devices: 34.2 us -> none  [on_device(): lax.psum((totals * rescale, weighted * rescale[:, None, :]), 'tm')]
  transfers between devices with their start and end apart: 8 -> 21, of which waited for: 7 -> 8; matrix products, arithmetic and copies ran while one was open for 1% -> 13% of each run, Pallas kernels for 0% -> 21%
where the time goes in v1:
time: 149 us; the launch traced here: 148 us
  Pallas kernels  48.3 us (32%)
  waiting for transfers between devices  47.4 us (32%)
  local copies, waits for them, and re-layouts  24.6 us (17%)
  starting transfers between devices  22.5 us (15%)
  other arithmetic  4.02 us (3%)
    ppermute x19, waiting for transfers between devices, swap(): lax.ppermute(value, axis, [(i, i ^ bit) for i in range(lax.axis_size(axis...  47.3 us
    pallas_call x8, Pallas kernels, simple(): pl.pallas_call(kernel, out_shape=out_shape, in_specs=smem(len(scalars)) +...  31 us
    ppermute x19, starting transfers between devices, swap(): lax.ppermute(value, axis, [(i, i ^ bit) for i in range(lax.axis_size(axis...  17.6 us
    pallas_call x2, Pallas kernels, attend(): pl.pallas_call(functools.partial(attend_kernel, packed), out_shape=out_sh...  17.3 us
    unnamed x40, local copies, waits for them, and re-layouts  7.24 us
    another operation x3, local copies, waits for them, and re-layouts, pair_device(): jnp.stack([dilations[layer], row_own, row_near, row_far, place * frames,...  3.83 us
    ppermute x1, starting transfers between devices, pair_device(): lax.ppermute(recording[:, frames - EDGE:], 'tm', [(i, i + 1) for i in ran...  3.63 us
  transfers between devices with their start and end apart: 21, of which 8 were waited for; matrix products, arithmetic and copies ran while one was open for 13% of the time, Pallas kernels for 21%

profile of v1, /device:TPU:0, one launch (start us, length us, event | category | flops | bytes accessed | tf_op | source)
XLA Modules:
  0.0 148.3 jit_solution(11873994211106498515)
XLA Ops:
  3.5 3.6 %collective-permute-start.3 = (bf16[128,128]{1,0:T(8,128)(2,1)}, bf16[128,128]{1,0:T(8,128)(2,1)}, u32[]{:S(2)}, u32[]{:S(2)}) collective-permute-start(bf16[128,128]{1,0:T(8,128)(2,1)} %get-tuple-element.24), channel_id=1, source_target_pairs={{0,1},{1,2},{2,3},{3,4},{4,5},{5,6},{6,7},{7,8},{8,9},{9,10},{10,1... | collective-permute-start | bytes 98312 | tf_op jit(solution)/shard_map/ppermute | solution.py:407
  7.2 2.3 %dynamic-slice_bitcast_fusion = (bf16[3,128,512]{2,1,0:T(8,128)(2,1)}, bf16[3,128,512]{2,1,0:T(8,128)(2,1)}, bf16[3,128,512]{2,1,0:T(8,128)(2,1)}) fusion(bf16[3,3,256,512]{3,2,1,0:T(8,128)(2,1)} %param.11, s32[]{:T(128)S(6)} %add.42, s32[]{:T(128)S(6)} %select_n.13, s32[]{:T(128)S(6)} %add.41), kind=kLoop, calls=%fused_computation.3 | loop fusion | bytes 2359308 | tf_op jit(solution)/shard_map/squeeze | solution.py:415
  9.4 3.0 %collective-permute-start.5 = (bf16[3,128,512]{2,1,0:T(8,128)(2,1)}, bf16[3,128,512]{2,1,0:T(8,128)(2,1)}, u32[]{:S(2)}, u32[]{:S(2)}) collective-permute-start(bf16[3,128,512]{2,1,0:T(8,128)(2,1)} %get-tuple-element.20), channel_id=1, source_target_pairs={{0,16},{16,0},{1,17},{17,1},{2,18},{18,2},{3,19},{19,3},{4,20},{20... | collective-permute-start | bytes 1179656 | tf_op jit(solution)/shard_map/ppermute | solution.py:373
  12.5 2.0 %collective-permute-start.10 = (bf16[3,128,512]{2,1,0:T(8,128)(2,1)}, bf16[3,128,512]{2,1,0:T(8,128)(2,1)}, u32[]{:S(2)}, u32[]{:S(2)}) collective-permute-start(bf16[3,128,512]{2,1,0:T(8,128)(2,1)} %get-tuple-element.18), channel_id=1, source_target_pairs={{0,16},{16,0},{1,17},{17,1},{2,18},{18,2},{3,19},{19,3},{4,20},{20... | collective-permute-start | bytes 1179656 | tf_op jit(solution)/shard_map/ppermute | solution.py:373
  23.6 2.0 %collective-permute-start.7 = (f32[3,256]{1,0:T(4,128)S(1)}, f32[3,256]{1,0:T(4,128)S(1)}, u32[]{:S(2)}, u32[]{:S(2)}) collective-permute-start(f32[3,256]{1,0:T(4,128)S(1)} %copy-done.19), channel_id=1, source_target_pairs={{0,16},{16,0},{1,17},{17,1},{2,18},{18,2},{3,19},{19,3},{4,20},{20... | collective-permute-start | bytes 9224 | tf_op jit(solution)/shard_map/ppermute | solution.py:373
  25.6 5.5 %collective-permute-done.8.near_w = bf16[3,128,512]{2,1,0:T(8,128)(2,1)} collective-permute-done((bf16[3,128,512]{2,1,0:T(8,128)(2,1)}, bf16[3,128,512]{2,1,0:T(8,128)(2,1)}, u32[]{:S(2)}, u32[]{:S(2)}) %collective-permute-start.8) | collective-permute-done | bytes 393248 | tf_op jit(solution)/shard_map/ppermute | solution.py:373
  31.3 8.2 %collective-permute-done.10.near_w = bf16[3,128,512]{2,1,0:T(8,128)(2,1)} collective-permute-done((bf16[3,128,512]{2,1,0:T(8,128)(2,1)}, bf16[3,128,512]{2,1,0:T(8,128)(2,1)}, u32[]{:S(2)}, u32[]{:S(2)}) %collective-permute-start.10) | collective-permute-done | bytes 393248 | tf_op jit(solution)/shard_map/ppermute | solution.py:373
  40.4 4.7 %collective-permute-done.7 = f32[3,256]{1,0:T(4,128)S(1)} collective-permute-done((f32[3,256]{1,0:T(4,128)S(1)}, f32[3,256]{1,0:T(4,128)S(1)}, u32[]{:S(2)}, u32[]{:S(2)}) %collective-permute-start.7) | collective-permute-done | bytes 3104 | tf_op jit(solution)/shard_map/ppermute | solution.py:373
  46.8 2.2 %collective-permute-done.4.other_edge = bf16[128,128]{1,0:T(8,128)(2,1)S(1)} collective-permute-done((bf16[128,128]{1,0:T(8,128)(2,1)S(1)}, bf16[128,128]{1,0:T(8,128)(2,1)S(1)}, u32[]{:S(2)}, u32[]{:S(2)}) %collective-permute-start.4) | collective-permute-done | bytes 32800 | tf_op jit(solution)/shard_map/ppermute | solution.py:373
  49.0 1.7 %collective-permute-start = (bf16[512,128]{1,0:T(8,128)(2,1)S(1)}, bf16[512,128]{1,0:T(8,128)(2,1)S(1)}, u32[]{:S(2)}, u32[]{:S(2)}) collective-permute-start(bf16[512,128]{1,0:T(8,128)(2,1)S(1)} %copy-done.15), channel_id=1, source_target_pairs={{0,16},{16,0},{1,17},{17,1},{2,18},{18,2},{3,19},{19,3},{4,20},{20... | collective-permute-start | bytes 393224 | tf_op jit(solution)/shard_map/ppermute | solution.py:373
  56.4 3.0 %first.1.hidden = bf16[512,1152]{1,0:T(8,128)(2,1)} custom-call(bf16[512,128]{1,0:T(8,128)(2,1)} %own_w.1, bf16[512,128]{1,0:T(8,128)(2,1)} %copy-done.16, bf16[128,1024]{1,0:T(8,128)(2,1)} %own.1, bf16[128,1024]{1,0:T(8,128)(2,1)} %copy-done.13, bf16[128,128]{1,0:T(8,128)(2,1)} %copy-done.14, bf16[128,128]{1,0:T(8,128)(2,1)} %copy-done.17), custom_call_target="tpu_custom_call" | custom-call | tf_op jit(solution)/shard_map/first/pallas_call | solution.py:378
  60.2 6.6 %conv.2.hidden = bf16[512,1152]{1,0:T(8,128)(2,1)} custom-call(s32[8]{0:T(128)} %stack.74.info, bf16[512,1152]{1,0:T(8,128)(2,1)} %first.1.hidden, bf16[3,256,512]{2,1,0:T(8,128)(2,1)} %get-tuple-element.22.own_w, bf16[3,128,512]{2,1,0:T(8,128)(2,1)} %collective-permute-done.5.near_w, bf16[3,128,512]{2,1,0:T(8,128)(2,1)} %copy-done.5, f32[256,1]{1,0:T(8,128)} %copy.17.own_b, ...), custom_call_target="tpu_custom_call" | custom-call | tf_op jit(solution)/shard_map/conv/pallas_call | solution.py:378
  67.5 6.6 %conv.3.hidden = bf16[512,1152]{1,0:T(8,128)(2,1)} custom-call(s32[8]{0:T(128)} %stack.73.info, bf16[512,1152]{1,0:T(8,128)(2,1)} %conv.2.hidden, bf16[3,256,512]{2,1,0:T(8,128)(2,1)} %get-tuple-element.23.own_w, bf16[3,128,512]{2,1,0:T(8,128)(2,1)} %collective-permute-done.8.near_w, bf16[3,128,512]{2,1,0:T(8,128)(2,1)} %copy-done.4, f32[256,1]{1,0:T(8,128)} %copy.20.own_b, ...), custom_call_target="tpu_custom_call" | custom-call | tf_op jit(solution)/shard_map/conv/pallas_call | solution.py:378
  74.9 6.5 %conv_last.1 = (bf16[256,1024]{1,0:T(8,128)(2,1)}, bf16[1024,128]{1,0:T(8,128)(2,1)}, bf16[1024,128]{1,0:T(8,128)(2,1)}, bf16[128,1024]{1,0:T(8,128)(2,1)}, bf16[128,1024]{1,0:T(8,128)(2,1)}) custom-call(s32[8]{0:T(128)} %stack.72.info, bf16[512,1152]{1,0:T(8,128)(2,1)} %conv.3.hidden, bf16[3,256,512]{2,1,0:T(8,128)(2,1)} %get-tuple-element.21.own_w, ...), custom_call_target="tpu_custom_call" | custom-call | tf_op jit(solution)/shard_map/conv_last/pallas_call | solution.py:378
  84.8 8.6 %attend_send.1 = bf16[72,2048]{1,0:T(8,128)(2,1)} custom-call(s32[3]{0:T(128)} %add_add_fusion.1.info, bf16[1024,128]{1,0:T(8,128)(2,1)} %get-tuple-element.11.key_own, bf16[1024,128]{1,0:T(8,128)(2,1)} %copy-done.2, bf16[128,1024]{1,0:T(8,128)(2,1)} %get-tuple-element.13.value_own, bf16[128,1024]{1,0:T(8,128)(2,1)} %copy-done.3, ...), custom_call_target="tpu_custom_call" | custom-call | tf_op jit(solution)/shard_map/attend_send/pallas_call | solution.py:349
  95.3 8.7 %attend_keep.1 = (f32[1,2048]{1,0:T(1,128)}, f32[1,2048]{1,0:T(1,128)}, f32[64,2048]{1,0:T(8,128)}) custom-call(s32[3]{0:T(128)} %add_add_fusion.info, bf16[1024,128]{1,0:T(8,128)(2,1)} %get-tuple-element.11.key_own, bf16[1024,128]{1,0:T(8,128)(2,1)} %copy-done.2, bf16[128,1024]{1,0:T(8,128)(2,1)} %get-tuple-element.13.value_own, ...), custom_call_target="tpu_custom_call" | custom-call | tf_op jit(solution)/shard_map/attend_keep/pallas_call | solution.py:349
  104.7 2.1 %meet.1.mine = bf16[72,2048]{1,0:T(8,128)(2,1)} custom-call(f32[1,2048]{1,0:T(1,128)} %get-tuple-element.15.peak, f32[1,2048]{1,0:T(1,128)} %get-tuple-element.16.total, f32[64,2048]{1,0:T(8,128)} %get-tuple-element.17.weighted, bf16[72,2048]{1,0:T(8,128)(2,1)} %copy-done.8), custom_call_target="tpu_custom_call" | custom-call | tf_op jit(solution)/shard_map/meet/pallas_call | solution.py:378
  108.4 7.3 %collective-permute-done.16.theirs = bf16[72,2048]{1,0:T(8,128)(2,1)S(1)} collective-permute-done((bf16[72,2048]{1,0:T(8,128)(2,1)}, bf16[72,2048]{1,0:T(8,128)(2,1)S(1)}, u32[]{:S(2)}, u32[]{:S(2)}) %collective-permute-start.16) | collective-permute-done | bytes 294944 | tf_op jit(solution)/shard_map/ppermute | solution.py:373
  116.4 2.0 %merge.1.mine = bf16[72,2048]{1,0:T(8,128)(2,1)} custom-call(s32[1]{0:T(128)} %bitcast.26.info, bf16[72,2048]{1,0:T(8,128)(2,1)} %meet.1.mine, bf16[72,2048]{1,0:T(8,128)(2,1)} %copy-done.7), custom_call_target="tpu_custom_call" | custom-call | tf_op jit(solution)/shard_map/merge/pallas_call | solution.py:378
  118.4 2.6 %collective-permute-start.17 = (bf16[72,2048]{1,0:T(8,128)(2,1)}, bf16[72,2048]{1,0:T(8,128)(2,1)S(1)}, u32[]{:S(2)}, u32[]{:S(2)}) collective-permute-start(bf16[72,2048]{1,0:T(8,128)(2,1)} %merge.1.mine), channel_id=1, source_target_pairs={{0,8},{1,9},{2,10},{3,11},{4,12},{5,13},{6,14},{7,15},{8,0},{9,1},... | collective-permute-start | bytes 884744 | tf_op jit(solution)/shard_map/ppermute | solution.py:373
  121.0 12.7 %collective-permute-done.17.theirs = bf16[72,2048]{1,0:T(8,128)(2,1)S(1)} collective-permute-done((bf16[72,2048]{1,0:T(8,128)(2,1)}, bf16[72,2048]{1,0:T(8,128)(2,1)S(1)}, u32[]{:S(2)}, u32[]{:S(2)}) %collective-permute-start.17) | collective-permute-done | bytes 294944 | tf_op jit(solution)/shard_map/ppermute | solution.py:373
  134.4 2.0 %finish.1.own = bf16[64,2048]{1,0:T(8,128)(2,1)} custom-call(s32[1]{0:T(128)} %bitcast.25.info, bf16[72,2048]{1,0:T(8,128)(2,1)} %merge.1.mine, bf16[72,2048]{1,0:T(8,128)(2,1)} %copy-done.9), custom_call_target="tpu_custom_call" | custom-call | tf_op jit(solution)/shard_map/finish/pallas_call | solution.py:378
  137.8 5.9 %collective-permute-done.18.across = bf16[64,2048]{1,0:T(8,128)(2,1)S(1)} collective-permute-done((bf16[64,2048]{1,0:T(8,128)(2,1)}, bf16[64,2048]{1,0:T(8,128)(2,1)S(1)}, u32[]{:S(2)}, u32[]{:S(2)}) %collective-permute-start.18) | collective-permute-done | bytes 262176 | tf_op jit(solution)/shard_map/ppermute | solution.py:373
  146.0 2.2 %assemble.1 = bf16[256,2048]{1,0:T(8,128)(2,1)} custom-call(s32[4]{0:T(128)} %pad_add_fusion.info, bf16[64,2048]{1,0:T(8,128)(2,1)} %finish.1.own, bf16[64,2048]{1,0:T(8,128)(2,1)} %copy-done.10, bf16[64,2048]{1,0:T(8,128)(2,1)} %copy-done.11, bf16[64,2048]{1,0:T(8,128)(2,1)} %copy-done.12), custom_call_target="tpu_custom_call" | custom-call | tf_op jit(solution)/shard_map/assemble/pallas_call | solution.py:378
  (93 shorter events, 34.9 us)
Async XLA Ops:
  0.6 81.3 %copy-start = (bf16[256,2048]{1,0:T(8,128)(2,1)S(1)}, bf16[256,2048]{1,0:T(8,128)(2,1)}, u32[]{:S(2)}) copy-start(bf16[256,2048]{1,0:T(8,128)(2,1)} %param.17) | copy-start | bytes 3145732
  2.2 21.2 %collective-permute-start.2 = (bf16[128,128]{1,0:T(8,128)(2,1)}, bf16[128,128]{1,0:T(8,128)(2,1)}, u32[]{:S(2)}, u32[]{:S(2)}) collective-permute-start(bf16[128,128]{1,0:T(8,128)(2,1)} %get-tuple-element.25), channel_id=1, source_target_pairs={{1,0},{2,1},{3,2},{4,3},{5,4},{6,5},{7,6},{8,7},{9,8},{10,9},{11,1... | collective-permute-start | bytes 98312 | tf_op jit(solution)/shard_map/ppermute | solution.py:410
  3.5 20.0 %collective-permute-start.3 = (bf16[128,128]{1,0:T(8,128)(2,1)}, bf16[128,128]{1,0:T(8,128)(2,1)}, u32[]{:S(2)}, u32[]{:S(2)}) collective-permute-start(bf16[128,128]{1,0:T(8,128)(2,1)} %get-tuple-element.24), channel_id=1, source_target_pairs={{0,1},{1,2},{2,3},{3,4},{4,5},{5,6},{6,7},{7,8},{8,9},{9,10},{10,1... | collective-permute-start | bytes 98312 | tf_op jit(solution)/shard_map/ppermute | solution.py:407
  9.4 16.1 %collective-permute-start.5 = (bf16[3,128,512]{2,1,0:T(8,128)(2,1)}, bf16[3,128,512]{2,1,0:T(8,128)(2,1)}, u32[]{:S(2)}, u32[]{:S(2)}) collective-permute-start(bf16[3,128,512]{2,1,0:T(8,128)(2,1)} %get-tuple-element.20), channel_id=1, source_target_pairs={{0,16},{16,0},{1,17},{17,1},{2,18},{18,2},{3,19},{19,3},{4,20},{20... | collective-permute-start | bytes 1179656 | tf_op jit(solution)/shard_map/ppermute | solution.py:373
  12.4 18.6 %collective-permute-start.8 = (bf16[3,128,512]{2,1,0:T(8,128)(2,1)}, bf16[3,128,512]{2,1,0:T(8,128)(2,1)}, u32[]{:S(2)}, u32[]{:S(2)}) collective-permute-start(bf16[3,128,512]{2,1,0:T(8,128)(2,1)} %get-tuple-element.19), channel_id=1, source_target_pairs={{0,16},{16,0},{1,17},{17,1},{2,18},{18,2},{3,19},{19,3},{4,20},{20... | collective-permute-start | bytes 1179656 | tf_op jit(solution)/shard_map/ppermute | solution.py:373
  12.5 27.0 %collective-permute-start.10 = (bf16[3,128,512]{2,1,0:T(8,128)(2,1)}, bf16[3,128,512]{2,1,0:T(8,128)(2,1)}, u32[]{:S(2)}, u32[]{:S(2)}) collective-permute-start(bf16[3,128,512]{2,1,0:T(8,128)(2,1)} %get-tuple-element.18), channel_id=1, source_target_pairs={{0,16},{16,0},{1,17},{17,1},{2,18},{18,2},{3,19},{19,3},{4,20},{20... | collective-permute-start | bytes 1179656 | tf_op jit(solution)/shard_map/ppermute | solution.py:373
  15.1 33.9 %copy-start.15 = (bf16[512,128]{1,0:T(8,128)(2,1)S(1)}, bf16[512,128]{1,0:T(8,128)(2,1)}, u32[]{:S(2)}) copy-start(bf16[512,128]{1,0:T(8,128)(2,1)} %own_w.1) | copy-start | bytes 393220
  23.5 31.6 %collective-permute-start.1 = (bf16[128,1024]{1,0:T(8,128)(2,1)}, bf16[128,1024]{1,0:T(8,128)(2,1)S(1)}, u32[]{:S(2)}, u32[]{:S(2)}) collective-permute-start(bf16[128,1024]{1,0:T(8,128)(2,1)} %own.1), channel_id=1, source_target_pairs={{0,16},{16,0},{1,17},{17,1},{2,18},{18,2},{3,19},{19,3},{4,20},{20... | collective-permute-start | bytes 786440 | tf_op jit(solution)/shard_map/ppermute | solution.py:373
  23.6 21.5 %collective-permute-start.7 = (f32[3,256]{1,0:T(4,128)S(1)}, f32[3,256]{1,0:T(4,128)S(1)}, u32[]{:S(2)}, u32[]{:S(2)}) collective-permute-start(f32[3,256]{1,0:T(4,128)S(1)} %copy-done.19), channel_id=1, source_target_pairs={{0,16},{16,0},{1,17},{17,1},{2,18},{18,2},{3,19},{19,3},{4,20},{20... | collective-permute-start | bytes 9224 | tf_op jit(solution)/shard_map/ppermute | solution.py:373
  25.6 33.8 %collective-permute-start.6 = (bf16[3,128,512]{2,1,0:T(8,128)(2,1)}, bf16[3,128,512]{2,1,0:T(8,128)(2,1)S(1)}, u32[]{:S(2)}, u32[]{:S(2)}) collective-permute-start(bf16[3,128,512]{2,1,0:T(8,128)(2,1)} %collective-permute-done.5.near_w), channel_id=1, source_target_pairs={{0,1},{1,0},{2,3},{3,2},{4,5},{5,4},{6,7},{7,6},{8,9},{9,8},{10,11... | collective-permute-start | bytes 1179656 | tf_op jit(solution)/shard_map/ppermute | solution.py:373
  31.1 35.7 %collective-permute-start.9 = (bf16[3,128,512]{2,1,0:T(8,128)(2,1)}, bf16[3,128,512]{2,1,0:T(8,128)(2,1)S(1)}, u32[]{:S(2)}, u32[]{:S(2)}) collective-permute-start(bf16[3,128,512]{2,1,0:T(8,128)(2,1)} %collective-permute-done.8.near_w), channel_id=1, source_target_pairs={{0,1},{1,0},{2,3},{3,2},{4,5},{5,4},{6,7},{7,6},{8,9},{9,8},{10,11... | collective-permute-start | bytes 1179656 | tf_op jit(solution)/shard_map/ppermute | solution.py:373
  39.5 34.6 %collective-permute-start.11 = (bf16[3,128,512]{2,1,0:T(8,128)(2,1)}, bf16[3,128,512]{2,1,0:T(8,128)(2,1)S(1)}, u32[]{:S(2)}, u32[]{:S(2)}) collective-permute-start(bf16[3,128,512]{2,1,0:T(8,128)(2,1)} %collective-permute-done.10.near_w), channel_id=1, source_target_pairs={{0,1},{1,0},{2,3},{3,2},{4,5},{5,4},{6,7},{7,6},{8,9},{9,8},{10,11... | collective-permute-start | bytes 1179656 | tf_op jit(solution)/shard_map/ppermute | solution.py:373
  40.4 14.7 %copy-start.14 = (bf16[128,128]{1,0:T(8,128)(2,1)}, bf16[128,128]{1,0:T(8,128)(2,1)S(1)}, u32[]{:S(2)}) copy-start(bf16[128,128]{1,0:T(8,128)(2,1)S(1)} %broadcast_select_fusion.own_edge) | copy-start | bytes 98308
  45.1 3.9 %collective-permute-start.4 = (bf16[128,128]{1,0:T(8,128)(2,1)S(1)}, bf16[128,128]{1,0:T(8,128)(2,1)S(1)}, u32[]{:S(2)}, u32[]{:S(2)}) collective-permute-start(bf16[128,128]{1,0:T(8,128)(2,1)S(1)} %broadcast_select_fusion.own_edge), channel_id=1, source_target_pairs={{0,16},{16,0},{1,17},{17,1},{2,18},{18,2},{3,19},{19,3},{4,20},{20... | collective-permute-start | bytes 98312 | tf_op jit(solution)/shard_map/ppermute | solution.py:373
  49.0 6.1 %collective-permute-start = (bf16[512,128]{1,0:T(8,128)(2,1)S(1)}, bf16[512,128]{1,0:T(8,128)(2,1)S(1)}, u32[]{:S(2)}, u32[]{:S(2)}) collective-permute-start(bf16[512,128]{1,0:T(8,128)(2,1)S(1)} %copy-done.15), channel_id=1, source_target_pairs={{0,16},{16,0},{1,17},{17,1},{2,18},{18,2},{3,19},{19,3},{4,20},{20... | collective-permute-start | bytes 393224 | tf_op jit(solution)/shard_map/ppermute | solution.py:373
  55.1 27.7 %collective-permute-start.12 = (s32[1]{0:T(128)}, s32[1]{0:T(128)}, u32[]{:S(2)}, u32[]{:S(2)}) collective-permute-start(s32[1]{0:T(128)} %param.14), channel_id=1, source_target_pairs={{0,1},{1,0},{2,3},{3,2},{4,5},{5,4},{6,7},{7,6},{8,9},{9,8},{10,11... | collective-permute-start | bytes 20 | tf_op jit(solution)/shard_map/ppermute | solution.py:373
  81.4 2.7 %collective-permute-start.13 = (bf16[1024,128]{1,0:T(8,128)(2,1)}, bf16[1024,128]{1,0:T(8,128)(2,1)S(1)}, u32[]{:S(2)}, u32[]{:S(2)}) collective-permute-start(bf16[1024,128]{1,0:T(8,128)(2,1)} %get-tuple-element.12), channel_id=1, source_target_pairs={{0,1},{1,0},{2,3},{3,2},{4,5},{5,4},{6,7},{7,6},{8,9},{9,8},{10,11... | collective-permute-start | bytes 786440 | tf_op jit(solution)/shard_map/ppermute | solution.py:373
  81.4 2.7 %collective-permute-start.14 = (bf16[128,1024]{1,0:T(8,128)(2,1)}, bf16[128,1024]{1,0:T(8,128)(2,1)S(1)}, u32[]{:S(2)}, u32[]{:S(2)}) collective-permute-start(bf16[128,1024]{1,0:T(8,128)(2,1)} %get-tuple-element.14), channel_id=1, source_target_pairs={{0,1},{1,0},{2,3},{3,2},{4,5},{5,4},{6,7},{7,6},{8,9},{9,8},{10,11... | collective-permute-start | bytes 786440 | tf_op jit(solution)/shard_map/ppermute | solution.py:373
  93.5 10.5 %collective-permute-start.15 = (bf16[72,2048]{1,0:T(8,128)(2,1)}, bf16[72,2048]{1,0:T(8,128)(2,1)S(1)}, u32[]{:S(2)}, u32[]{:S(2)}) collective-permute-start(bf16[72,2048]{1,0:T(8,128)(2,1)} %attend_send.1), channel_id=1, source_target_pairs={{0,2},{1,3},{2,0},{3,1},{4,6},{5,7},{6,4},{7,5},{8,10},{9,11},{10,... | collective-permute-start | bytes 884744 | tf_op jit(solution)/shard_map/ppermute | solution.py:373
  106.8 8.9 %collective-permute-start.16 = (bf16[72,2048]{1,0:T(8,128)(2,1)}, bf16[72,2048]{1,0:T(8,128)(2,1)S(1)}, u32[]{:S(2)}, u32[]{:S(2)}) collective-permute-start(bf16[72,2048]{1,0:T(8,128)(2,1)} %meet.1.mine), channel_id=1, source_target_pairs={{0,4},{1,5},{2,6},{3,7},{4,0},{5,1},{6,2},{7,3},{8,12},{9,13},{10,... | collective-permute-start | bytes 884744 | tf_op jit(solution)/shard_map/ppermute | solution.py:373
  118.4 15.3 %collective-permute-start.17 = (bf16[72,2048]{1,0:T(8,128)(2,1)}, bf16[72,2048]{1,0:T(8,128)(2,1)S(1)}, u32[]{:S(2)}, u32[]{:S(2)}) collective-permute-start(bf16[72,2048]{1,0:T(8,128)(2,1)} %merge.1.mine), channel_id=1, source_target_pairs={{0,8},{1,9},{2,10},{3,11},{4,12},{5,13},{6,14},{7,15},{8,0},{9,1},... | collective-permute-start | bytes 884744 | tf_op jit(solution)/shard_map/ppermute | solution.py:373
  136.4 7.4 %collective-permute-start.18 = (bf16[64,2048]{1,0:T(8,128)(2,1)}, bf16[64,2048]{1,0:T(8,128)(2,1)S(1)}, u32[]{:S(2)}, u32[]{:S(2)}) collective-permute-start(bf16[64,2048]{1,0:T(8,128)(2,1)} %finish.1.own), channel_id=1, source_target_pairs={{0,2},{1,3},{2,0},{3,1},{4,6},{5,7},{6,4},{7,5},{8,10},{9,11},{10,... | collective-permute-start | bytes 786440 | tf_op jit(solution)/shard_map/ppermute | solution.py:373
  137.8 6.6 %collective-permute-start.19 = (bf16[64,2048]{1,0:T(8,128)(2,1)}, bf16[64,2048]{1,0:T(8,128)(2,1)S(1)}, u32[]{:S(2)}, u32[]{:S(2)}) collective-permute-start(bf16[64,2048]{1,0:T(8,128)(2,1)} %finish.1.own), channel_id=1, source_target_pairs={{0,1},{1,0},{2,3},{3,2},{4,5},{5,4},{6,7},{7,6},{8,9},{9,8},{10,11... | collective-permute-start | bytes 786440 | tf_op jit(solution)/shard_map/ppermute | solution.py:373
  143.8 1.5 %collective-permute-start.20 = (bf16[64,2048]{1,0:T(8,128)(2,1)S(1)}, bf16[64,2048]{1,0:T(8,128)(2,1)S(1)}, u32[]{:S(2)}, u32[]{:S(2)}) collective-permute-start(bf16[64,2048]{1,0:T(8,128)(2,1)S(1)} %collective-permute-done.18.across), channel_id=1, source_target_pairs={{0,1},{1,0},{2,3},{3,2},{4,5},{5,4},{6,7},{7,6},{8,9},{9,8},{10,11... | collective-permute-start | bytes 786440 | tf_op jit(solution)/shard_map/ppermute | solution.py:373
  (17 other events, 59.2 us)

commit v2 on v1

--- a/solution.py
+++ b/solution.py
@@ -7,6 +7,7 @@
 from jax.experimental import pallas as pl
 from jax.experimental.pallas import tpu as pltpu
 from jax.sharding import PartitionSpec as P
+
 
 HD = 64
 LATENTS = 2048
@@ -127,8 +128,8 @@
     return [pl.BlockSpec(memory_space=pltpu.SMEM)] * count
 
 
-def params():
-    return pltpu.CompilerParams(vmem_limit_bytes=56 * 1024 * 1024)
+def params(mib):
+    return pltpu.CompilerParams(vmem_limit_bytes=mib * 1024 * 1024)
 
 
 def dot(left, right):
@@ -163,46 +164,75 @@
         store(row, rows, here, new.astype(jnp.bfloat16))
 
 
-def spread(info, hidden, shifted):
+def spread(shift, hidden, shifted):
     span = hidden.shape[1]
     wide = hidden[...].astype(jnp.float32)
-    shifted[0] = pltpu.roll(wide, info[0], 1).astype(jnp.bfloat16)
-    shifted[1] = pltpu.roll(wide, span - info[0], 1).astype(jnp.bfloat16)
-
-
-def middle_kernel(info, hidden, own_w, near_w, far_w, own_b, near_b, far_b, out, shifted):
+    shifted[0] = pltpu.roll(wide, shift, 1).astype(jnp.bfloat16)
+    shifted[1] = pltpu.roll(wide, span - shift, 1).astype(jnp.bfloat16)
+
+
+def column(row, out):
+    out[...] = jnp.broadcast_to(row, (EDGE, row.shape[1])).T
+
+
+def pieces(layer, side, core, own_w, near_w, far_w, own_b, other_b, own_col, other_col):
+    rows = own_w.shape[1]
+    half = rows // 2
+    column(own_b[layer : layer + 1, :], own_col)
+    column(other_b[layer : layer + 1, :], other_col)
+    near = pl.multiple_of(core[0] * half, half)
+    far = pl.multiple_of((1 - core[0]) * half, half)
+    base = (1 - side[0]) * rows
+    return (
+        (own_w, own_col[:, 0:1], side[0] * rows),
+        (near_w, other_col[pl.ds(near, half), 0:1], base + near),
+        (far_w, other_col[pl.ds(far, half), 0:1], base + far),
+    )
+
+
+def middle_kernel(
+    layer, blocks, dilations, side, core, place, hidden, own_w, near_w, far_w, own_b, other_b,
+    out, shifted, own_col, other_col,
+):
     span = hidden.shape[1]
-    spread(info, hidden, shifted)
+    frames = span - EDGE
+    spread(dilations[layer], hidden, shifted)
 
     def keep(start, width):
         lane = lax.broadcasted_iota(jnp.int32, (1, width), 1) + start
-        frame = jnp.where(lane < span - HALF, lane, lane - span) + info[4]
-        return (frame >= 0) & (frame < info[5])
+        frame = jnp.where(lane < span - HALF, lane, lane - span) + place[0] * frames
+        return (frame >= 0) & (frame < blocks * frames)
 
     def store(row, rows, here, value):
         out[pl.ds(row, rows), here] = value
 
-    for kernel, bias, row in ((own_w, own_b, info[1]), (near_w, near_b, info[2]), (far_w, far_b, info[3])):
+    for kernel, bias, row in pieces(
+        layer, side, core, own_w, near_w, far_w, own_b, other_b, own_col, other_col
+    ):
         conv_rows(shifted, hidden, kernel, bias, row, keep, store, span, 384)
 
 
 def last_kernel(
-    info, hidden, own_w, near_w, far_w, own_b, near_b, far_b, key_w, value_w,
-    features, key_keep, key_send, value_keep, value_send, shifted, full,
+    layer, dilations, side, core, hidden, own_w, near_w, far_w, own_b, other_b, key_w, value_w,
+    features, key_keep, key_send, value_keep, value_send, shifted, own_col, other_col, full,
 ):
     frames = features.shape[1]
-    spread(info, hidden, shifted)
+    spread(dilations[layer], hidden, shifted)
 
     def store(row, rows, here, value):
         full[pl.ds(row, rows), here] = value
 
-    for kernel, bias, row in ((own_w, own_b, info[1]), (near_w, near_b, info[2]), (far_w, far_b, info[3])):
+    for kernel, bias, row in pieces(
+        layer, side, core, own_w, near_w, far_w, own_b, other_b, own_col, other_col
+    ):
         conv_rows(shifted, hidden, kernel, bias, row, None, store, frames, 256)
     rows = features.shape[0]
-    features[...] = full[pl.ds(pl.multiple_of(info[1], rows), rows), :]
+    features[...] = full[pl.ds(pl.multiple_of(side[0] * rows, rows), rows), :]
     half = rows // 2
-    for key_out, value_out, row in ((key_keep, value_keep, info[6]), (key_send, value_send, info[7])):
-        here = pl.ds(pl.multiple_of(row, half), half)
+    for key_out, value_out, part in (
+        (key_send, value_send, 1 - core[0]), (key_keep, value_keep, core[0])
+    ):
+        here = pl.ds(pl.multiple_of(part * half, half), half)
         key_out[...] = dot(key_w[here, :], full[...]).T.astype(jnp.bfloat16)
         value_out[...] = dot(value_w[here, :], full[...]).astype(jnp.bfloat16)
 
@@ -256,17 +286,18 @@
 
 
 def finish_kernel(info, mine, theirs, out):
-    peak, total, weighted = join(*ordered(info, unpack(mine), unpack(theirs)))
+    _, total, weighted = join(*ordered(info, unpack(mine), unpack(theirs)))
     out[...] = (weighted / total).astype(out.dtype)
 
 
 def divide_kernel(mine, out):
-    peak, total, weighted = unpack(mine)
+    _, total, weighted = unpack(mine)
     out[...] = (weighted / total).astype(out.dtype)
 
 
 def attend_kernel(
-    packed, info, key_own, key_rec, value_own, value_rec, queries, *refs
+    packed, core, which, valid_own, valid_rec, key_own, key_rec, value_own, value_rec, queries,
+    *refs
 ):
     outs = refs[:-6]
     keyed, asked, score_a, score_b, peak_a, peak_b = refs[-6:]
@@ -274,17 +305,17 @@
     latents = queries.shape[1]
     tile = score_a.shape[1]
     chunk = 256
-    slot = info[0]
+    slot = which[0]
     lane = lax.broadcasted_iota(jnp.int32, (frames, 2 * HD), 1)
     frame = lax.broadcasted_iota(jnp.int32, (frames, 2 * HD), 0)
     spare = (1 - slot) * HD
-    for part, source in enumerate((key_own, key_rec)):
-        bias = jnp.where(frame < info[1 + part], 0.0, MASKED)
+    for part, (source, valid) in enumerate(((key_own, valid_own), (key_rec, valid_rec))):
+        bias = jnp.where(frame < valid[0], 0.0, MASKED)
         keyed[pl.ds(part * frames, frames), :] = jnp.where(
             lane == spare, bias, source[...].astype(jnp.float32)
         ).astype(jnp.bfloat16)
     row = lax.broadcasted_iota(jnp.int32, (2 * HD, latents), 0)
-    wide = queries[...].astype(jnp.float32)
+    wide = queries[pl.ds(pl.multiple_of(core[0] * 2 * HD, 2 * HD), 2 * HD), :].astype(jnp.float32)
     wide = jnp.where(row // HD == slot, wide, jnp.where(row == spare, 1.0, 0.0))
     asked[...] = wide.astype(jnp.bfloat16)
     value_rows = pl.ds(pl.multiple_of(slot * HD, HD), HD)
@@ -332,7 +363,7 @@
         weigh(2 * step + 1, score_b, peak_b)
 
 
-def attend(packed, info, keys, values, queries):
+def attend(packed, scalars, keys, values, queries):
     latents = queries.shape[1]
     frames = keys[0].shape[0]
     tile = min(256, latents // 2)
@@ -349,7 +380,7 @@
     return pl.pallas_call(
         functools.partial(attend_kernel, packed),
         out_shape=out_shape,
-        in_specs=smem(1) + whole(5),
+        in_specs=smem(4) + whole(5),
         out_specs=out_specs,
         scratch_shapes=[
             VMEM((2 * frames, 2 * HD), jnp.bfloat16),
@@ -359,30 +390,34 @@
             VMEM((1, tile), jnp.float32),
             VMEM((1, tile), jnp.float32),
         ],
-        compiler_params=params(),
+        compiler_params=params(20),
         name="attend_send" if packed else "attend_keep",
-    )(info, *keys, *values, queries)
-
-
-def assemble_kernel(info, own, across, core_own, core_across, out):
-    for piece, index in ((own, 0), (across, 1), (core_own, 2), (core_across, 3)):
-        out[pl.ds(pl.multiple_of(info[index] * HD, HD), HD), :] = piece[...]
+    )(*scalars, *keys, *values, queries)
+
+
+def assemble_kernel(core, cross, own, across, core_own, core_across, out):
+    mine, theirs = 2 * core[0], 2 - 2 * core[0]
+    for piece, head in (
+        (own, mine + cross[0]), (across, mine + 1 - cross[0]),
+        (core_own, theirs + cross[0]), (core_across, theirs + 1 - cross[0]),
+    ):
+        out[pl.ds(pl.multiple_of(head * HD, HD), HD), :] = piece[...]
 
 
 def swap(value, axis, bit):
     return lax.ppermute(value, axis, [(i, i ^ bit) for i in range(lax.axis_size(axis))])
 
 
-def simple(kernel, out_shape, scalars, arrays, scratch=(), name=None):
+def simple(kernel, out_shape, scalars, arrays, scratch=(), mib=16, specs=None):
     many = isinstance(out_shape, (list, tuple))
     return pl.pallas_call(
         kernel,
+        grid=(1,),
         out_shape=out_shape,
-        in_specs=smem(len(scalars)) + whole(len(arrays)),
+        in_specs=smem(len(scalars)) + (specs or whole(len(arrays))),
         out_specs=whole(len(out_shape)) if many else pl.BlockSpec(memory_space=pltpu.VMEM),
         scratch_shapes=list(scratch),
-        compiler_params=params(),
-        name=name,
+        compiler_params=params(mib),
     )(*scalars, *arrays)
 
 
@@ -395,56 +430,51 @@
     half = ch_loc // 2
     latents = queries.shape[1]
     blocks = lax.axis_size("tm")
-    side = lax.axis_index("sensor")
-    place = lax.axis_index("tm")
+    side = lax.axis_index("sensor").astype(jnp.int32).reshape(1)
+    place = lax.axis_index("tm").astype(jnp.int32).reshape(1)
     core = place & 1
     cross = (place >> 1) & 1
     span = frames + EDGE
     bf16 = jnp.bfloat16
-
-    other_rec = swap(recording, "sensor", 1)
-    other_w = swap(spatial_w, "sensor", 1)
+    across = [(0, 1), (1, 0)]
+    twins = [(i, i ^ 1) for i in range(blocks)]
+
+    other_rec = lax.ppermute(recording, "sensor", across)
     tail = lax.ppermute(
         recording[:, frames - EDGE :], "tm", [(i, i + 1) for i in range(blocks - 1)]
     )
     head = lax.ppermute(recording[:, :EDGE], "tm", [(i + 1, i) for i in range(blocks - 1)])
+    other_w = lax.ppermute(spatial_w, "sensor", across)
     lane = jnp.arange(EDGE, dtype=jnp.int32)[None, :]
     edge = jnp.where(lane < HALF, head, tail)
-    other_edge = swap(edge, "sensor", 1)
-    mine = lax.dynamic_slice_in_dim(conv_w, core * half, half, axis=2)
-    near = [swap(mine[layer], "sensor", 1) for layer in range(LAYERS)]
-    far = [swap(near[layer], "tm", 1) for layer in range(LAYERS)]
-    other_b = swap(conv_b, "sensor", 1)
-    near_b = lax.dynamic_slice_in_dim(other_b, core * half, half, axis=1)
-    far_b = lax.dynamic_slice_in_dim(other_b, (1 - core) * half, half, axis=1)
-    other_valid = swap(valid_frames, "tm", 1)
+    other_edge = lax.ppermute(edge, "sensor", across)
+    other_b = lax.ppermute(conv_b, "sensor", across)
+    mine = [
+        lax.dynamic_slice(conv_w, (layer, 0, core[0] * half, 0), (1, 3, half, ch))[0]
+        for layer in range(LAYERS)
+    ]
+    near = [lax.ppermute(mine[n], "sensor", across) for n in range(LAYERS)]
+    far = [lax.ppermute(near[n], "tm", twins) for n in range(LAYERS)]
+    other_valid = lax.ppermute(valid_frames, "tm", twins)
 
     hidden = simple(
         first_kernel,
         jax.ShapeDtypeStruct((ch, span), bf16),
         (),
         (spatial_w, other_w, recording, other_rec, edge, other_edge),
-        name="first",
     )
-    row_own = side * ch_loc
-    row_near = (1 - side) * ch_loc + core * half
-    row_far = (1 - side) * ch_loc + (1 - core) * half
+    columns = [VMEM((ch_loc, EDGE), jnp.float32)] * 2
     for layer in range(LAYERS):
-        info = jnp.stack(
-            [
-                dilations[layer], row_own, row_near, row_far, place * frames, blocks * frames,
-                core * half, (1 - core) * half,
-            ]
-        ).astype(jnp.int32)
-        arrays = (
-            hidden, conv_w[layer], near[layer], far[layer],
-            conv_b[layer][:, None], near_b[layer][:, None], far_b[layer][:, None],
-        )
-        scratch = [VMEM((2, ch, span), bf16)]
+        arrays = (hidden, conv_w, near[layer], far[layer], conv_b, other_b)
+        specs = whole(len(arrays))
+        specs[1] = pl.BlockSpec((None, 3, ch_loc, ch), lambda _, layer=layer: (layer, 0, 0, 0))
+        scratch = [VMEM((2, ch, span), bf16)] + columns
         if layer < LAYERS - 1:
             hidden = simple(
-                middle_kernel, jax.ShapeDtypeStruct((ch, span), bf16), (info,), arrays, scratch,
-                name="conv",
+                functools.partial(middle_kernel, layer, blocks),
+                jax.ShapeDtypeStruct((ch, span), bf16),
+                (dilations, side, core, place), arrays, scratch,
+                mib=28, specs=specs,
             )
         else:
             shapes = [
@@ -455,45 +485,37 @@
                 jax.ShapeDtypeStruct((half, frames), bf16),
             ]
             features, key_keep, key_send, value_keep, value_send = simple(
-                last_kernel, shapes, (info,), arrays + (key_w, value_w),
-                scratch + [VMEM((ch, frames), bf16)], name="conv_last",
+                functools.partial(last_kernel, layer), shapes, (dilations, side, core),
+                arrays + (key_w, value_w),
+                scratch + [VMEM((ch, frames), bf16)],
+                mib=28, specs=specs + whole(2),
             )
-    keys = (key_keep, swap(key_send, "tm", 1))
-    values = (value_keep, swap(value_send, "tm", 1))
-    asked = lax.dynamic_slice_in_dim(queries, core * half, half, axis=0)
-
-    def facts(slot):
-        return jnp.stack([slot, valid_frames[0], other_valid[0]]).astype(jnp.int32)
-
-    sent = attend(True, facts(1 - cross), keys, values, asked)
+    keys = (key_keep, lax.ppermute(key_send, "tm", twins))
+    values = (value_keep, lax.ppermute(value_send, "tm", twins))
+    facts = (valid_frames, other_valid)
+    sent = attend(True, (core, 1 - cross) + facts, keys, values, queries)
     arrived = swap(sent, "tm", 2)
-    peak, total, weighted = attend(False, facts(cross), keys, values, asked)
+    peak, total, weighted = attend(False, (core, cross) + facts, keys, values, queries)
     packed_shape = jax.ShapeDtypeStruct((HD + 8, latents), bf16)
     final_shape = jax.ShapeDtypeStruct((HD, latents), bf16)
-    packed = simple(meet_kernel, packed_shape, (), (peak, total, weighted, arrived), name="meet")
+    packed = simple(meet_kernel, packed_shape, (), (peak, total, weighted, arrived))
     if blocks == 4:
-        done = simple(divide_kernel, final_shape, (), (packed,), name="divide")
+        done = simple(divide_kernel, final_shape, (), (packed,))
     bit = 4
     while bit < blocks:
         theirs = swap(packed, "tm", bit)
-        which = ((place & bit) != 0).astype(jnp.int32)[None]
+        which = ((place & bit) != 0).astype(jnp.int32)
         if bit * 2 < blocks:
-            packed = simple(merge_kernel, packed_shape, (which,), (packed, theirs), name="merge")
+            packed = simple(merge_kernel, packed_shape, (which,), (packed, theirs))
         else:
-            done = simple(finish_kernel, final_shape, (which,), (packed, theirs), name="finish")
+            done = simple(finish_kernel, final_shape, (which,), (packed, theirs))
         bit *= 2
-    across = swap(done, "tm", 2)
+    crossed = swap(done, "tm", 2)
     core_done = swap(done, "tm", 1)
-    core_across = swap(across, "tm", 1)
-    spots = jnp.stack(
-        [
-            2 * core + cross, 2 * core + 1 - cross, 2 * (1 - core) + cross,
-            2 * (1 - core) + 1 - cross,
-        ]
-    ).astype(jnp.int32)
+    core_crossed = swap(crossed, "tm", 1)
     attended = simple(
-        assemble_kernel, jax.ShapeDtypeStruct((ch_loc, latents), bf16), (spots,),
-        (done, across, core_done, core_across), name="assemble",
+        assemble_kernel, jax.ShapeDtypeStruct((ch_loc, latents), bf16), (core, cross),
+        (done, crossed, core_done, core_crossed),
     )
     return (features, attended)
 
@@ -504,15 +526,15 @@
 
 
 def on_device(*arrays):
-    heads = arrays[6].shape[0] // HD
-    if lax.axis_size("sensor") == 2 and heads == 4:
-        return pair_device(*arrays)
-    return generic_device(*arrays)
+    if arrays[6].shape[0] // HD != 4:
+        return generic_device(*arrays)
+    return pair_device(*arrays)
 
 
 def solution(mesh):
+    quick = fits(mesh)
     return jax.shard_map(
-        on_device if fits(mesh) else generic_device,
+        on_device if quick else generic_device,
         mesh=mesh,
         in_specs=(
             P("sensor", "tm"),

time: 149 us -> 119 us (0.80)
  local copies, waits for them, and re-layouts: 24.6 us -> 8.46 us
  Pallas kernels: 48.3 us -> 32.7 us
  waiting for transfers between devices: 47.4 us -> 53.5 us
  other arithmetic: 4.02 us -> 0.01 us
    ppermute x0 -> x13, waiting for transfers between devices: none -> 26.4 us  [the longest x3 19.5 us: pair_device(): near = [lax.ppermute(mine[n], 'sensor', across) for n in range(LAYERS)]]
    ppermute x19 -> x6, waiting for transfers between devices: 47.3 us -> 27.1 us  [swap(): lax.ppermute(value, axis, [(i, i ^ bit) for i in range(lax.axis_size(axis...]
    pallas_call x8, Pallas kernels: 31 us -> 18.3 us  [simple(): pl.pallas_call(kernel, grid=(1,), out_shape=out_shape, in_specs=smem(len(...]
    ppermute x0 -> x13, starting transfers between devices: none -> 11.3 us  [the longest x3 5.09 us: pair_device(): near = [lax.ppermute(mine[n], 'sensor', across) for n in range(LAYERS)]]
    ppermute x19 -> x6, starting transfers between devices: 17.6 us -> 6.93 us  [swap(): lax.ppermute(value, axis, [(i, i ^ bit) for i in range(lax.axis_size(axis...]
    another operation x14 -> x0, local copies, waits for them, and re-layouts: 10.6 us -> none  [the longest x3 3.83 us: pair_device(): jnp.stack([dilations[layer], row_own, row_near, row_far, place * frames,...]
    another operation x3 -> x0, other arithmetic: 3.23 us -> none  [the longest x2 2.58 us: facts(): return jnp.stack([slot, valid_frames[0], other_valid[0]]).astype(jnp.int32)]
    pallas_call x2, Pallas kernels: 17.3 us -> 14.4 us  [attend(): pl.pallas_call(functools.partial(attend_kernel, packed), out_shape=out_sh...]
  transfers between devices with their start and end apart: 21 -> 21, of which waited for: 8 -> 11; matrix products, arithmetic and copies ran while one was open for 13% -> 1% of each run, Pallas kernels for 21% -> 16%
where the time goes in v2:
time: 119 us
  waiting for transfers between devices  53.5 us (45%)
  Pallas kernels  32.7 us (27%)
  starting transfers between devices  22.6 us (19%)
  local copies, waits for them, and re-layouts  8.46 us (7%)
  between operations  1.52 us (1%)
    ppermute x6, waiting for transfers between devices, swap(): lax.ppermute(value, axis, [(i, i ^ bit) for i in range(lax.axis_size(axis...  27.1 us
    ppermute x3, waiting for transfers between devices, pair_device(): near = [lax.ppermute(mine[n], 'sensor', across) for n in range(LAYERS)]  19.5 us
    pallas_call x8, Pallas kernels, simple(): pl.pallas_call(kernel, grid=(1,), out_shape=out_shape, in_specs=smem(len(...  18.3 us
    pallas_call x2, Pallas kernels, attend(): pl.pallas_call(functools.partial(attend_kernel, packed), out_shape=out_sh...  14.4 us
    ppermute x6, starting transfers between devices, swap(): lax.ppermute(value, axis, [(i, i ^ bit) for i in range(lax.axis_size(axis...  6.93 us
    unnamed x30, local copies, waits for them, and re-layouts  6.18 us
    ppermute x3, starting transfers between devices, pair_device(): near = [lax.ppermute(mine[n], 'sensor', across) for n in range(LAYERS)]  5.09 us
    ppermute x1, waiting for transfers between devices, pair_device(): other_w = lax.ppermute(spatial_w, 'sensor', across)  3.23 us
  transfers between devices with their start and end apart: 21, of which 11 were waited for; matrix products, arithmetic and copies ran while one was open for 1% of the time, Pallas kernels for 16%

profile of v2, /device:TPU:0, one launch (start us, length us, event | category | flops | bytes accessed | tf_op | source)
XLA Modules:
  0.0 118.8 jit_solution(1841789556182933165)
XLA Ops:
  2.2 3.1 %collective-permute-start.5 = (bf16[3,128,512]{2,1,0:T(8,128)(2,1)S(1)}, bf16[3,128,512]{2,1,0:T(8,128)(2,1)S(1)}, u32[]{:S(2)}, u32[]{:S(2)}) collective-permute-start(bf16[3,128,512]{2,1,0:T(8,128)(2,1)S(1)} %get-tuple-element.20), channel_id=1, source_target_pairs={{0,16},{16,0},{1,17},{17,1},{2,18},{18,2},{3,19},{19,3},{4,20},{20... | collective-permute-start | bytes 1179656 | tf_op jit(solution)/shard_map/ppermute | solution.py:456
  5.3 1.9 %collective-permute-start.10 = (bf16[3,128,512]{2,1,0:T(8,128)(2,1)S(1)}, bf16[3,128,512]{2,1,0:T(8,128)(2,1)S(1)}, u32[]{:S(2)}, u32[]{:S(2)}) collective-permute-start(bf16[3,128,512]{2,1,0:T(8,128)(2,1)S(1)} %get-tuple-element.18), channel_id=1, source_target_pairs={{0,16},{16,0},{1,17},{17,1},{2,18},{18,2},{3,19},{19,3},{4,20},{20... | collective-permute-start | bytes 1179656 | tf_op jit(solution)/shard_map/ppermute | solution.py:456
  9.3 3.0 %collective-permute-start.3 = (bf16[128,128]{1,0:T(8,128)(2,1)S(1)}, bf16[128,128]{1,0:T(8,128)(2,1)S(1)}, u32[]{:S(2)}, u32[]{:S(2)}) collective-permute-start(bf16[128,128]{1,0:T(8,128)(2,1)S(1)} %get-tuple-element.21), channel_id=1, source_target_pairs={{0,1},{1,2},{2,3},{3,4},{4,5},{5,6},{6,7},{7,8},{8,9},{9,10},{10,1... | collective-permute-start | bytes 98312 | tf_op jit(solution)/shard_map/ppermute | solution.py:443
  12.6 2.7 %collective-permute-done.5.near_w = bf16[3,128,512]{2,1,0:T(8,128)(2,1)S(1)} collective-permute-done((bf16[3,128,512]{2,1,0:T(8,128)(2,1)S(1)}, bf16[3,128,512]{2,1,0:T(8,128)(2,1)S(1)}, u32[]{:S(2)}, u32[]{:S(2)}) %collective-permute-start.5) | collective-permute-done | bytes 393248 | tf_op jit(solution)/shard_map/ppermute | solution.py:456
  15.2 8.4 %collective-permute-done.8.near_w = bf16[3,128,512]{2,1,0:T(8,128)(2,1)S(1)} collective-permute-done((bf16[3,128,512]{2,1,0:T(8,128)(2,1)S(1)}, bf16[3,128,512]{2,1,0:T(8,128)(2,1)S(1)}, u32[]{:S(2)}, u32[]{:S(2)}) %collective-permute-start.8) | collective-permute-done | bytes 393248 | tf_op jit(solution)/shard_map/ppermute | solution.py:456
  23.6 8.4 %collective-permute-done.10.near_w = bf16[3,128,512]{2,1,0:T(8,128)(2,1)S(1)} collective-permute-done((bf16[3,128,512]{2,1,0:T(8,128)(2,1)S(1)}, bf16[3,128,512]{2,1,0:T(8,128)(2,1)S(1)}, u32[]{:S(2)}, u32[]{:S(2)}) %collective-permute-start.10) | collective-permute-done | bytes 393248 | tf_op jit(solution)/shard_map/ppermute | solution.py:456
  32.1 2.1 %collective-permute-start.4 = (bf16[128,128]{1,0:T(8,128)(2,1)S(1)}, bf16[128,128]{1,0:T(8,128)(2,1)S(1)}, u32[]{:S(2)}, u32[]{:S(2)}) collective-permute-start(bf16[128,128]{1,0:T(8,128)(2,1)S(1)} %broadcast_select_fusion.own_edge), channel_id=1, source_target_pairs={{0,16},{16,0},{1,17},{17,1},{2,18},{18,2},{3,19},{19,3},{4,20},{20... | collective-permute-start | bytes 98312 | tf_op jit(solution)/shard_map/ppermute | solution.py:450
  34.8 2.8 %collective-permute-done.4.other_edge = bf16[128,128]{1,0:T(8,128)(2,1)S(1)} collective-permute-done((bf16[128,128]{1,0:T(8,128)(2,1)S(1)}, bf16[128,128]{1,0:T(8,128)(2,1)S(1)}, u32[]{:S(2)}, u32[]{:S(2)}) %collective-permute-start.4) | collective-permute-done | bytes 32800 | tf_op jit(solution)/shard_map/ppermute | solution.py:450
  38.1 1.7 %collective-permute-start = (bf16[512,128]{1,0:T(8,128)(2,1)S(1)}, bf16[512,128]{1,0:T(8,128)(2,1)S(1)}, u32[]{:S(2)}, u32[]{:S(2)}) collective-permute-start(bf16[512,128]{1,0:T(8,128)(2,1)S(1)} %copy-done.7), channel_id=1, source_target_pairs={{0,16},{16,0},{1,17},{17,1},{2,18},{18,2},{3,19},{19,3},{4,20},{20... | collective-permute-start | bytes 393224 | tf_op jit(solution)/shard_map/ppermute | solution.py:447
  39.9 3.2 %collective-permute-done.other_w = bf16[512,128]{1,0:T(8,128)(2,1)S(1)} collective-permute-done((bf16[512,128]{1,0:T(8,128)(2,1)S(1)}, bf16[512,128]{1,0:T(8,128)(2,1)S(1)}, u32[]{:S(2)}, u32[]{:S(2)}) %collective-permute-start) | collective-permute-done | bytes 131104 | tf_op jit(solution)/shard_map/ppermute | solution.py:447
  43.8 1.7 %collective-permute-start.7 = (f32[3,256]{1,0:T(4,128)S(1)}, f32[3,256]{1,0:T(4,128)S(1)}, u32[]{:S(2)}, u32[]{:S(2)}) collective-permute-start(f32[3,256]{1,0:T(4,128)S(1)} %copy-done.11), channel_id=1, source_target_pairs={{0,16},{16,0},{1,17},{17,1},{2,18},{18,2},{3,19},{19,3},{4,20},{20... | collective-permute-start | bytes 9224 | tf_op jit(solution)/shard_map/ppermute | solution.py:451
  49.8 1.7 %shard_map.104.hidden = bf16[512,1152]{1,0:T(8,128)(2,1)S(1)} custom-call(bf16[512,128]{1,0:T(8,128)(2,1)S(1)} %copy-done.8, bf16[512,128]{1,0:T(8,128)(2,1)S(1)} %copy-done.10, bf16[128,1024]{1,0:T(8,128)(2,1)S(1)} %copy-done.2, bf16[128,1024]{1,0:T(8,128)(2,1)} %collective-permute-done.1.other, bf16[128,128]{1,0:T(8,128)(2,1)S(1)} %copy-done.6, ...), custom_call_target="tpu_custom_call" | custom-call | tf_op jit(solution)/shard_map/pallas_call | solution.py:413
  51.5 4.8 %shard_map.105.hidden = bf16[512,1152]{1,0:T(8,128)(2,1)S(1)} custom-call(s32[3]{0:T(128)S(1)} %copy-done.14, s32[1]{0:T(128)} %bitcast.side, s32[1]{0:T(128)S(6)} %and.14.core, s32[1]{0:T(128)} %bitcast.1.place, bf16[512,1152]{1,0:T(8,128)(2,1)S(1)} %shard_map.104.hidden, bf16[3,3,256,512]{3,2,1,0:T(8,128)(2,1)S(1)} %copy-done, ...), custom_call_target="tpu_custom_call" | custom-call | tf_op jit(solution)/shard_map/pallas_call | solution.py:413
  56.4 4.9 %shard_map.106.hidden = bf16[512,1152]{1,0:T(8,128)(2,1)S(1)} custom-call(s32[3]{0:T(128)S(1)} %copy-done.14, s32[1]{0:T(128)} %bitcast.side, s32[1]{0:T(128)S(6)} %and.14.core, s32[1]{0:T(128)} %bitcast.1.place, bf16[512,1152]{1,0:T(8,128)(2,1)S(1)} %shard_map.105.hidden, bf16[3,3,256,512]{3,2,1,0:T(8,128)(2,1)S(1)} %copy-done, ...), custom_call_target="tpu_custom_call" | custom-call | tf_op jit(solution)/shard_map/pallas_call | solution.py:413
  61.3 5.3 %shard_map.107 = (bf16[256,1024]{1,0:T(8,128)(2,1)}, bf16[1024,128]{1,0:T(8,128)(2,1)S(1)}, bf16[1024,128]{1,0:T(8,128)(2,1)S(1)}, bf16[128,1024]{1,0:T(8,128)(2,1)S(1)}, bf16[128,1024]{1,0:T(8,128)(2,1)S(1)}) custom-call(s32[3]{0:T(128)S(1)} %copy-done.14, s32[1]{0:T(128)} %bitcast.side, s32[1]{0:T(128)S(6)} %and.14.core, ...), custom_call_target="tpu_custom_call" | custom-call | tf_op jit(solution)/shard_map/pallas_call | solution.py:413
  68.6 7.1 %attend_send.1 = bf16[72,2048]{1,0:T(8,128)(2,1)S(1)} custom-call(s32[1]{0:T(128)S(6)} %and.14.core, s32[1]{0:T(128)S(6)} %sub.3.which, s32[1]{0:T(128)S(6)} %copy.11.valid_own, s32[1]{0:T(128)} %collective-permute-done.12.valid_rec, bf16[1024,128]{1,0:T(8,128)(2,1)S(1)} %get-tuple-element.11.key_own, bf16[1024,128]{1,0:T(8,128)(2,1)S(1)} %collective-permute-done.13.key_rec, ...), custom_call_target="tpu_custom_call" | custom-call | tf_op jit(solution)/shard_map/attend_send/pallas_call | solution.py:380
  75.8 1.6 %collective-permute-start.15 = (bf16[72,2048]{1,0:T(8,128)(2,1)S(1)}, bf16[72,2048]{1,0:T(8,128)(2,1)S(1)}, u32[]{:S(2)}, u32[]{:S(2)}) collective-permute-start(bf16[72,2048]{1,0:T(8,128)(2,1)S(1)} %attend_send.1), channel_id=1, source_target_pairs={{0,2},{1,3},{2,0},{3,1},{4,6},{5,7},{6,4},{7,5},{8,10},{9,11},{10,... | collective-permute-start | bytes 884744 | tf_op jit(solution)/shard_map/ppermute | solution.py:408
  77.3 7.2 %attend_keep.1 = (f32[1,2048]{1,0:T(1,128)S(1)}, f32[1,2048]{1,0:T(1,128)S(1)}, f32[64,2048]{1,0:T(8,128)S(1)}) custom-call(s32[1]{0:T(128)S(6)} %and.14.core, s32[1]{0:T(128)S(6)} %and.15.which.cross, s32[1]{0:T(128)S(6)} %copy.11.valid_own, s32[1]{0:T(128)} %collective-permute-done.12.valid_rec, bf16[1024,128]{1,0:T(8,128)(2,1)S(1)} %get-tuple-element.11.key_own, ...), custom_call_target="tpu_custom_call" | custom-call | tf_op jit(solution)/shard_map/attend_keep/pallas_call | solution.py:380
  85.1 1.6 %collective-permute-start.16 = (bf16[72,2048]{1,0:T(8,128)(2,1)S(1)}, bf16[72,2048]{1,0:T(8,128)(2,1)S(1)}, u32[]{:S(2)}, u32[]{:S(2)}) collective-permute-start(bf16[72,2048]{1,0:T(8,128)(2,1)S(1)} %shard_map.108.mine), channel_id=1, source_target_pairs={{0,4},{1,5},{2,6},{3,7},{4,0},{5,1},{6,2},{7,3},{8,12},{9,13},{10,... | collective-permute-start | bytes 884744 | tf_op jit(solution)/shard_map/ppermute | solution.py:408
  86.8 6.9 %collective-permute-done.16.theirs = bf16[72,2048]{1,0:T(8,128)(2,1)S(1)} collective-permute-done((bf16[72,2048]{1,0:T(8,128)(2,1)S(1)}, bf16[72,2048]{1,0:T(8,128)(2,1)S(1)}, u32[]{:S(2)}, u32[]{:S(2)}) %collective-permute-start.16) | collective-permute-done | bytes 294944 | tf_op jit(solution)/shard_map/ppermute | solution.py:408
  93.9 2.7 %collective-permute-start.17 = (bf16[72,2048]{1,0:T(8,128)(2,1)S(1)}, bf16[72,2048]{1,0:T(8,128)(2,1)S(1)}, u32[]{:S(2)}, u32[]{:S(2)}) collective-permute-start(bf16[72,2048]{1,0:T(8,128)(2,1)S(1)} %shard_map.109.mine), channel_id=1, source_target_pairs={{0,8},{1,9},{2,10},{3,11},{4,12},{5,13},{6,14},{7,15},{8,0},{9,1},... | collective-permute-start | bytes 884744 | tf_op jit(solution)/shard_map/ppermute | solution.py:408
  96.5 12.2 %collective-permute-done.17.theirs = bf16[72,2048]{1,0:T(8,128)(2,1)S(1)} collective-permute-done((bf16[72,2048]{1,0:T(8,128)(2,1)S(1)}, bf16[72,2048]{1,0:T(8,128)(2,1)S(1)}, u32[]{:S(2)}, u32[]{:S(2)}) %collective-permute-start.17) | collective-permute-done | bytes 294944 | tf_op jit(solution)/shard_map/ppermute | solution.py:408
  110.0 6.2 %collective-permute-done.18.across = bf16[64,2048]{1,0:T(8,128)(2,1)S(1)} collective-permute-done((bf16[64,2048]{1,0:T(8,128)(2,1)S(1)}, bf16[64,2048]{1,0:T(8,128)(2,1)S(1)}, u32[]{:S(2)}, u32[]{:S(2)}) %collective-permute-start.18) | collective-permute-done | bytes 262176 | tf_op jit(solution)/shard_map/ppermute | solution.py:408
  116.2 1.5 %collective-permute-done.20.core_across = bf16[64,2048]{1,0:T(8,128)(2,1)S(1)} collective-permute-done((bf16[64,2048]{1,0:T(8,128)(2,1)S(1)}, bf16[64,2048]{1,0:T(8,128)(2,1)S(1)}, u32[]{:S(2)}, u32[]{:S(2)}) %collective-permute-start.20) | collective-permute-done | bytes 262176 | tf_op jit(solution)/shard_map/ppermute | solution.py:408
  (62 shorter events, 14.5 us)
Async XLA Ops:
  0.6 43.1 %copy-start.11 = (f32[3,256]{1,0:T(4,128)S(1)}, f32[3,256]{1,0:T(4,128)}, u32[]{:S(2)}) copy-start(f32[3,256]{1,0:T(4,128)} %own_b.5) | copy-start | bytes 9220
  0.7 50.9 %copy-start = (bf16[3,3,256,512]{3,2,1,0:T(8,128)(2,1)S(1)}, bf16[3,3,256,512]{3,2,1,0:T(8,128)(2,1)}, u32[]{:S(2)}) copy-start(bf16[3,3,256,512]{3,2,1,0:T(8,128)(2,1)} %own_w.7) | copy-start | bytes 7077892
  2.2 49.4 %copy-start.14 = (s32[3]{0:T(128)S(1)}, s32[3]{0:T(128)}, u32[]{:S(2)}) copy-start(s32[3]{0:T(128)} %dilations.5) | copy-start | bytes 40
  2.2 13.0 %collective-permute-start.5 = (bf16[3,128,512]{2,1,0:T(8,128)(2,1)S(1)}, bf16[3,128,512]{2,1,0:T(8,128)(2,1)S(1)}, u32[]{:S(2)}, u32[]{:S(2)}) collective-permute-start(bf16[3,128,512]{2,1,0:T(8,128)(2,1)S(1)} %get-tuple-element.20), channel_id=1, source_target_pairs={{0,16},{16,0},{1,17},{17,1},{2,18},{18,2},{3,19},{19,3},{4,20},{20... | collective-permute-start | bytes 1179656 | tf_op jit(solution)/shard_map/ppermute | solution.py:456
  5.3 18.4 %collective-permute-start.8 = (bf16[3,128,512]{2,1,0:T(8,128)(2,1)S(1)}, bf16[3,128,512]{2,1,0:T(8,128)(2,1)S(1)}, u32[]{:S(2)}, u32[]{:S(2)}) collective-permute-start(bf16[3,128,512]{2,1,0:T(8,128)(2,1)S(1)} %get-tuple-element.19), channel_id=1, source_target_pairs={{0,16},{16,0},{1,17},{17,1},{2,18},{18,2},{3,19},{19,3},{4,20},{20... | collective-permute-start | bytes 1179656 | tf_op jit(solution)/shard_map/ppermute | solution.py:456
  5.3 26.7 %collective-permute-start.10 = (bf16[3,128,512]{2,1,0:T(8,128)(2,1)S(1)}, bf16[3,128,512]{2,1,0:T(8,128)(2,1)S(1)}, u32[]{:S(2)}, u32[]{:S(2)}) collective-permute-start(bf16[3,128,512]{2,1,0:T(8,128)(2,1)S(1)} %get-tuple-element.18), channel_id=1, source_target_pairs={{0,16},{16,0},{1,17},{17,1},{2,18},{18,2},{3,19},{19,3},{4,20},{20... | collective-permute-start | bytes 1179656 | tf_op jit(solution)/shard_map/ppermute | solution.py:456
  8.1 4.3 %collective-permute-start.2 = (bf16[128,128]{1,0:T(8,128)(2,1)S(1)}, bf16[128,128]{1,0:T(8,128)(2,1)S(1)}, u32[]{:S(2)}, u32[]{:S(2)}) collective-permute-start(bf16[128,128]{1,0:T(8,128)(2,1)S(1)} %get-tuple-element.22), channel_id=1, source_target_pairs={{1,0},{2,1},{3,2},{4,3},{5,4},{6,5},{7,6},{8,7},{9,8},{10,9},{11,1... | collective-permute-start | bytes 98312 | tf_op jit(solution)/shard_map/ppermute | solution.py:446
  9.3 22.7 %collective-permute-start.3 = (bf16[128,128]{1,0:T(8,128)(2,1)S(1)}, bf16[128,128]{1,0:T(8,128)(2,1)S(1)}, u32[]{:S(2)}, u32[]{:S(2)}) collective-permute-start(bf16[128,128]{1,0:T(8,128)(2,1)S(1)} %get-tuple-element.21), channel_id=1, source_target_pairs={{0,1},{1,2},{2,3},{3,4},{4,5},{5,6},{6,7},{7,8},{8,9},{9,10},{10,1... | collective-permute-start | bytes 98312 | tf_op jit(solution)/shard_map/ppermute | solution.py:443
  12.4 33.1 %collective-permute-start.1 = (bf16[128,1024]{1,0:T(8,128)(2,1)}, bf16[128,1024]{1,0:T(8,128)(2,1)}, u32[]{:S(2)}, u32[]{:S(2)}) collective-permute-start(bf16[128,1024]{1,0:T(8,128)(2,1)} %own.1), channel_id=1, source_target_pairs={{0,16},{16,0},{1,17},{17,1},{2,18},{18,2},{3,19},{19,3},{4,20},{20... | collective-permute-start | bytes 786440 | tf_op jit(solution)/shard_map/ppermute | solution.py:442
  15.2 36.3 %collective-permute-start.6 = (bf16[3,128,512]{2,1,0:T(8,128)(2,1)S(1)}, bf16[3,128,512]{2,1,0:T(8,128)(2,1)}, u32[]{:S(2)}, u32[]{:S(2)}) collective-permute-start(bf16[3,128,512]{2,1,0:T(8,128)(2,1)S(1)} %collective-permute-done.5.near_w), channel_id=1, source_target_pairs={{0,1},{1,0},{2,3},{3,2},{4,5},{5,4},{6,7},{7,6},{8,9},{9,8},{10,11... | collective-permute-start | bytes 1179656 | tf_op jit(solution)/shard_map/ppermute | solution.py:457
  23.6 32.8 %collective-permute-start.9 = (bf16[3,128,512]{2,1,0:T(8,128)(2,1)S(1)}, bf16[3,128,512]{2,1,0:T(8,128)(2,1)}, u32[]{:S(2)}, u32[]{:S(2)}) collective-permute-start(bf16[3,128,512]{2,1,0:T(8,128)(2,1)S(1)} %collective-permute-done.8.near_w), channel_id=1, source_target_pairs={{0,1},{1,0},{2,3},{3,2},{4,5},{5,4},{6,7},{7,6},{8,9},{9,8},{10,11... | collective-permute-start | bytes 1179656 | tf_op jit(solution)/shard_map/ppermute | solution.py:457
  32.1 29.2 %collective-permute-start.11 = (bf16[3,128,512]{2,1,0:T(8,128)(2,1)S(1)}, bf16[3,128,512]{2,1,0:T(8,128)(2,1)}, u32[]{:S(2)}, u32[]{:S(2)}) collective-permute-start(bf16[3,128,512]{2,1,0:T(8,128)(2,1)S(1)} %collective-permute-done.10.near_w), channel_id=1, source_target_pairs={{0,1},{1,0},{2,3},{3,2},{4,5},{5,4},{6,7},{7,6},{8,9},{9,8},{10,11... | collective-permute-start | bytes 1179656 | tf_op jit(solution)/shard_map/ppermute | solution.py:457
  32.1 5.5 %collective-permute-start.4 = (bf16[128,128]{1,0:T(8,128)(2,1)S(1)}, bf16[128,128]{1,0:T(8,128)(2,1)S(1)}, u32[]{:S(2)}, u32[]{:S(2)}) collective-permute-start(bf16[128,128]{1,0:T(8,128)(2,1)S(1)} %broadcast_select_fusion.own_edge), channel_id=1, source_target_pairs={{0,16},{16,0},{1,17},{17,1},{2,18},{18,2},{3,19},{19,3},{4,20},{20... | collective-permute-start | bytes 98312 | tf_op jit(solution)/shard_map/ppermute | solution.py:450
  38.1 5.0 %collective-permute-start = (bf16[512,128]{1,0:T(8,128)(2,1)S(1)}, bf16[512,128]{1,0:T(8,128)(2,1)S(1)}, u32[]{:S(2)}, u32[]{:S(2)}) collective-permute-start(bf16[512,128]{1,0:T(8,128)(2,1)S(1)} %copy-done.7), channel_id=1, source_target_pairs={{0,16},{16,0},{1,17},{17,1},{2,18},{18,2},{3,19},{19,3},{4,20},{20... | collective-permute-start | bytes 393224 | tf_op jit(solution)/shard_map/ppermute | solution.py:447
  43.8 7.7 %collective-permute-start.7 = (f32[3,256]{1,0:T(4,128)S(1)}, f32[3,256]{1,0:T(4,128)S(1)}, u32[]{:S(2)}, u32[]{:S(2)}) collective-permute-start(f32[3,256]{1,0:T(4,128)S(1)} %copy-done.11), channel_id=1, source_target_pairs={{0,16},{16,0},{1,17},{17,1},{2,18},{18,2},{3,19},{19,3},{4,20},{20... | collective-permute-start | bytes 9224 | tf_op jit(solution)/shard_map/ppermute | solution.py:451
  66.6 2.0 %collective-permute-start.13 = (bf16[1024,128]{1,0:T(8,128)(2,1)S(1)}, bf16[1024,128]{1,0:T(8,128)(2,1)S(1)}, u32[]{:S(2)}, u32[]{:S(2)}) collective-permute-start(bf16[1024,128]{1,0:T(8,128)(2,1)S(1)} %get-tuple-element.12), channel_id=1, source_target_pairs={{0,1},{1,0},{2,3},{3,2},{4,5},{5,4},{6,7},{7,6},{8,9},{9,8},{10,11... | collective-permute-start | bytes 786440 | tf_op jit(solution)/shard_map/ppermute | solution.py:493
  66.6 2.0 %collective-permute-start.14 = (bf16[128,1024]{1,0:T(8,128)(2,1)S(1)}, bf16[128,1024]{1,0:T(8,128)(2,1)S(1)}, u32[]{:S(2)}, u32[]{:S(2)}) collective-permute-start(bf16[128,1024]{1,0:T(8,128)(2,1)S(1)} %get-tuple-element.14), channel_id=1, source_target_pairs={{0,1},{1,0},{2,3},{3,2},{4,5},{5,4},{6,7},{7,6},{8,9},{9,8},{10,11... | collective-permute-start | bytes 786440 | tf_op jit(solution)/shard_map/ppermute | solution.py:494
  67.1 1.5 %collective-permute-start.12 = (s32[1]{0:T(128)}, s32[1]{0:T(128)}, u32[]{:S(2)}, u32[]{:S(2)}) collective-permute-start(s32[1]{0:T(128)} %param.14), channel_id=1, source_target_pairs={{0,1},{1,0},{2,3},{3,2},{4,5},{5,4},{6,7},{7,6},{8,9},{9,8},{10,11... | collective-permute-start | bytes 20 | tf_op jit(solution)/shard_map/ppermute | solution.py:458
  75.8 9.1 %collective-permute-start.15 = (bf16[72,2048]{1,0:T(8,128)(2,1)S(1)}, bf16[72,2048]{1,0:T(8,128)(2,1)S(1)}, u32[]{:S(2)}, u32[]{:S(2)}) collective-permute-start(bf16[72,2048]{1,0:T(8,128)(2,1)S(1)} %attend_send.1), channel_id=1, source_target_pairs={{0,2},{1,3},{2,0},{3,1},{4,6},{5,7},{6,4},{7,5},{8,10},{9,11},{10,... | collective-permute-start | bytes 884744 | tf_op jit(solution)/shard_map/ppermute | solution.py:408
  85.1 8.5 %collective-permute-start.16 = (bf16[72,2048]{1,0:T(8,128)(2,1)S(1)}, bf16[72,2048]{1,0:T(8,128)(2,1)S(1)}, u32[]{:S(2)}, u32[]{:S(2)}) collective-permute-start(bf16[72,2048]{1,0:T(8,128)(2,1)S(1)} %shard_map.108.mine), channel_id=1, source_target_pairs={{0,4},{1,5},{2,6},{3,7},{4,0},{5,1},{6,2},{7,3},{8,12},{9,13},{10,... | collective-permute-start | bytes 884744 | tf_op jit(solution)/shard_map/ppermute | solution.py:408
  93.9 14.9 %collective-permute-start.17 = (bf16[72,2048]{1,0:T(8,128)(2,1)S(1)}, bf16[72,2048]{1,0:T(8,128)(2,1)S(1)}, u32[]{:S(2)}, u32[]{:S(2)}) collective-permute-start(bf16[72,2048]{1,0:T(8,128)(2,1)S(1)} %shard_map.109.mine), channel_id=1, source_target_pairs={{0,8},{1,9},{2,10},{3,11},{4,12},{5,13},{6,14},{7,15},{8,0},{9,1},... | collective-permute-start | bytes 884744 | tf_op jit(solution)/shard_map/ppermute | solution.py:408
  109.0 7.3 %collective-permute-start.18 = (bf16[64,2048]{1,0:T(8,128)(2,1)S(1)}, bf16[64,2048]{1,0:T(8,128)(2,1)S(1)}, u32[]{:S(2)}, u32[]{:S(2)}) collective-permute-start(bf16[64,2048]{1,0:T(8,128)(2,1)S(1)} %shard_map.110.own), channel_id=1, source_target_pairs={{0,2},{1,3},{2,0},{3,1},{4,6},{5,7},{6,4},{7,5},{8,10},{9,11},{10,... | collective-permute-start | bytes 786440 | tf_op jit(solution)/shard_map/ppermute | solution.py:408
  110.0 6.2 %collective-permute-start.19 = (bf16[64,2048]{1,0:T(8,128)(2,1)S(1)}, bf16[64,2048]{1,0:T(8,128)(2,1)S(1)}, u32[]{:S(2)}, u32[]{:S(2)}) collective-permute-start(bf16[64,2048]{1,0:T(8,128)(2,1)S(1)} %shard_map.110.own), channel_id=1, source_target_pairs={{0,1},{1,0},{2,3},{3,2},{4,5},{5,4},{6,7},{7,6},{8,9},{9,8},{10,11... | collective-permute-start | bytes 786440 | tf_op jit(solution)/shard_map/ppermute | solution.py:408
  116.2 1.5 %collective-permute-start.20 = (bf16[64,2048]{1,0:T(8,128)(2,1)S(1)}, bf16[64,2048]{1,0:T(8,128)(2,1)S(1)}, u32[]{:S(2)}, u32[]{:S(2)}) collective-permute-start(bf16[64,2048]{1,0:T(8,128)(2,1)S(1)} %collective-permute-done.18.across), channel_id=1, source_target_pairs={{0,1},{1,0},{2,3},{3,2},{4,5},{5,4},{6,7},{7,6},{8,9},{9,8},{10,11... | collective-permute-start | bytes 786440 | tf_op jit(solution)/shard_map/ppermute | solution.py:408
  (12 other events, 60.9 us)

commit v3 on v2

--- a/solution.py
+++ b/solution.py
@@ -136,99 +136,116 @@
     return jnp.dot(left, right, preferred_element_type=jnp.float32)
 
 
-def first_kernel(own_w, other_w, own, other, own_edge, other_edge, out):
+def first_kernel(
+    side, core, own_w, near_w, far_w, own, other, own_edge, other_edge, mine, theirs, weights
+):
     frames = own.shape[1]
-    out[:, :frames] = (dot(own_w[...], own[...]) + dot(other_w[...], other[...])).astype(out.dtype)
-    out[:, frames:] = (
-        dot(own_w[...], own_edge[...]) + dot(other_w[...], other_edge[...])
-    ).astype(out.dtype)
+    rows = mine.shape[0]
+    weights[core[0]] = near_w[...]
+    weights[1 - core[0]] = far_w[...]
+    for out, part in ((mine, side[0]), (theirs, 1 - side[0])):
+        left = own_w[pl.ds(pl.multiple_of(part * rows, rows), rows), :]
+        right = weights[part]
+        out[:, :frames] = (dot(left, own[...]) + dot(right, other[...])).astype(out.dtype)
+        out[:, frames:] = (dot(left, own_edge[...]) + dot(right, other_edge[...])).astype(out.dtype)
 
 
 def gelu(value):
     return 0.5 * value * (1.0 + lax.erf(value * (1.0 / math.sqrt(2.0))))
 
 
-def conv_rows(shifted, hidden, kernel, bias, row, keep, store, cols, step):
-    rows = kernel.shape[1]
-    row = pl.multiple_of(row, rows)
+def conv_rows(taps, old, kernel, bias, keep, store, cols, step):
     for start in range(0, cols, step):
         width = min(step, cols - start)
         here = pl.ds(start, width)
-        total = dot(kernel[0], shifted[0, :, here])
-        total = total + dot(kernel[1], hidden[:, here])
-        total = total + dot(kernel[2], shifted[1, :, here])
-        old = hidden[pl.ds(row, rows), here].astype(jnp.float32)
-        new = old + gelu(total + bias[...])
+        total = dot(kernel[0], taps[0, :, here])
+        total = total + dot(kernel[1], taps[1, :, here])
+        total = total + dot(kernel[2], taps[2, :, here])
+        new = old(here).astype(jnp.float32) + gelu(total + bias)
         if keep is not None and start + width > cols - EDGE:
             new = jnp.where(keep(start, width), new, 0.0)
-        store(row, rows, here, new.astype(jnp.bfloat16))
-
-
-def spread(shift, hidden, shifted):
-    span = hidden.shape[1]
-    wide = hidden[...].astype(jnp.float32)
-    shifted[0] = pltpu.roll(wide, shift, 1).astype(jnp.bfloat16)
-    shifted[1] = pltpu.roll(wide, span - shift, 1).astype(jnp.bfloat16)
+        store(here, new.astype(jnp.bfloat16))
 
 
 def column(row, out):
     out[...] = jnp.broadcast_to(row, (EDGE, row.shape[1])).T
 
 
-def pieces(layer, side, core, own_w, near_w, far_w, own_b, other_b, own_col, other_col):
-    rows = own_w.shape[1]
-    half = rows // 2
-    column(own_b[layer : layer + 1, :], own_col)
-    column(other_b[layer : layer + 1, :], other_col)
-    near = pl.multiple_of(core[0] * half, half)
-    far = pl.multiple_of((1 - core[0]) * half, half)
-    base = (1 - side[0]) * rows
-    return (
-        (own_w, own_col[:, 0:1], side[0] * rows),
-        (near_w, other_col[pl.ds(near, half), 0:1], base + near),
-        (far_w, other_col[pl.ds(far, half), 0:1], base + far),
-    )
-
-
-def middle_kernel(
-    layer, blocks, dilations, side, core, place, hidden, own_w, near_w, far_w, own_b, other_b,
-    out, shifted, own_col, other_col,
-):
-    span = hidden.shape[1]
+def keeper(place, blocks, span):
     frames = span - EDGE
-    spread(dilations[layer], hidden, shifted)
 
     def keep(start, width):
         lane = lax.broadcasted_iota(jnp.int32, (1, width), 1) + start
         frame = jnp.where(lane < span - HALF, lane, lane - span) + place[0] * frames
         return (frame >= 0) & (frame < blocks * frames)
 
-    def store(row, rows, here, value):
-        out[pl.ds(row, rows), here] = value
-
-    for kernel, bias, row in pieces(
-        layer, side, core, own_w, near_w, far_w, own_b, other_b, own_col, other_col
-    ):
-        conv_rows(shifted, hidden, kernel, bias, row, keep, store, span, 384)
+    return keep
+
+
+def own_kernel(
+    layer, blocks, last, dilations, side, place, mine, theirs, weights, biases, out, taps, col
+):
+    rows, span = mine.shape
+    shift = dilations[layer]
+    for part, source in ((side[0], mine), (1 - side[0], theirs)):
+        here = pl.ds(pl.multiple_of(part * rows, rows), rows)
+        wide = source[...].astype(jnp.float32)
+        taps[1, here, :] = source[...]
+        taps[0, here, :] = pltpu.roll(wide, shift, 1).astype(jnp.bfloat16)
+        taps[2, here, :] = pltpu.roll(wide, span - shift, 1).astype(jnp.bfloat16)
+    column(biases[layer : layer + 1, :], col)
+
+    def store(here, value):
+        out[:, here] = value
+
+    conv_rows(
+        taps, lambda here: mine[:, here], weights, col[:, 0:1],
+        None if last else keeper(place, blocks, span), store, out.shape[1], 256 if last else 384,
+    )
+
+
+def other_rows(layer, core, theirs, taps, near_w, far_w, biases, col, keep, target, cols, step):
+    half = near_w.shape[1]
+    column(biases[layer : layer + 1, :], col)
+    for weights, part in ((near_w, core[0]), (far_w, 1 - core[0])):
+        rows = pl.ds(pl.multiple_of(part * half, half), half)
+
+        def store(here, value, rows=rows):
+            target(rows, here, value)
+
+        conv_rows(
+            taps, lambda here, rows=rows: theirs[rows, here], weights, col[rows, 0:1], keep,
+            store, cols, step,
+        )
+
+
+def other_kernel(layer, blocks, core, place, theirs, taps, near_w, far_w, biases, out, col):
+    span = theirs.shape[1]
+
+    def target(rows, here, value):
+        out[rows, here] = value
+
+    other_rows(
+        layer, core, theirs, taps, near_w, far_w, biases, col, keeper(place, blocks, span), target,
+        span, 384,
+    )
 
 
 def last_kernel(
-    layer, dilations, side, core, hidden, own_w, near_w, far_w, own_b, other_b, key_w, value_w,
-    features, key_keep, key_send, value_keep, value_send, shifted, own_col, other_col, full,
+    layer, side, core, features, theirs, taps, near_w, far_w, biases, key_w, value_w,
+    key_keep, key_send, value_keep, value_send, col, full,
 ):
-    frames = features.shape[1]
-    spread(dilations[layer], hidden, shifted)
-
-    def store(row, rows, here, value):
-        full[pl.ds(row, rows), here] = value
-
-    for kernel, bias, row in pieces(
-        layer, side, core, own_w, near_w, far_w, own_b, other_b, own_col, other_col
-    ):
-        conv_rows(shifted, hidden, kernel, bias, row, None, store, frames, 256)
-    rows = features.shape[0]
-    features[...] = full[pl.ds(pl.multiple_of(side[0] * rows, rows), rows), :]
+    rows, frames = features.shape
+    base = (1 - side[0]) * rows
+    full[pl.ds(pl.multiple_of(side[0] * rows, rows), rows), :] = features[...]
     half = rows // 2
+
+    def target(part, here, value):
+        full[pl.ds(pl.multiple_of(base + part.start, half), half), here] = value
+
+    other_rows(
+        layer, core, theirs, taps, near_w, far_w, biases, col, None, target, frames, 256
+    )
     for key_out, value_out, part in (
         (key_send, value_send, 1 - core[0]), (key_keep, value_keep, core[0])
     ):
@@ -277,8 +294,11 @@
     return one, two
 
 
-def meet_kernel(peak, total, weighted, theirs, out):
-    pack(out, *join((peak[...], total[...], weighted[...]), unpack(theirs)))
+def meet_kernel(peak, total, weighted, *refs):
+    state = (peak[...], total[...], weighted[...])
+    for theirs in refs[:-1]:
+        state = join(state, unpack(theirs))
+    pack(refs[-1], *state)
 
 
 def merge_kernel(info, mine, theirs, out):
@@ -290,83 +310,72 @@
     out[...] = (weighted / total).astype(out.dtype)
 
 
-def divide_kernel(mine, out):
-    _, total, weighted = unpack(mine)
-    out[...] = (weighted / total).astype(out.dtype)
-
-
 def attend_kernel(
-    packed, core, which, valid_own, valid_rec, key_own, key_rec, value_own, value_rec, queries,
-    *refs
+    packed, core, which, half, valid_own, valid_rec, key_own, key_rec, value_own, value_rec,
+    queries, *refs
 ):
-    outs = refs[:-6]
-    keyed, asked, score_a, score_b, peak_a, peak_b = refs[-6:]
+    outs = refs[:-5]
+    keyed, asked, valued, score_a, score_b = refs[-5:]
     frames = key_own.shape[0]
-    latents = queries.shape[1]
+    latents = asked.shape[1]
     tile = score_a.shape[1]
     chunk = 256
     slot = which[0]
     lane = lax.broadcasted_iota(jnp.int32, (frames, 2 * HD), 1)
     frame = lax.broadcasted_iota(jnp.int32, (frames, 2 * HD), 0)
     spare = (1 - slot) * HD
+    value_rows = pl.ds(pl.multiple_of(slot * HD, HD), HD)
     for part, (source, valid) in enumerate(((key_own, valid_own), (key_rec, valid_rec))):
         bias = jnp.where(frame < valid[0], 0.0, MASKED)
         keyed[pl.ds(part * frames, frames), :] = jnp.where(
             lane == spare, bias, source[...].astype(jnp.float32)
         ).astype(jnp.bfloat16)
+    valued[0:HD, 0:frames] = value_own[value_rows, :]
+    valued[0:HD, frames:] = value_rec[value_rows, :]
+    valued[HD:, :] = jnp.ones((valued.shape[0] - HD, 2 * frames), jnp.bfloat16)
     row = lax.broadcasted_iota(jnp.int32, (2 * HD, latents), 0)
-    wide = queries[pl.ds(pl.multiple_of(core[0] * 2 * HD, 2 * HD), 2 * HD), :].astype(jnp.float32)
+    wide = queries[
+        pl.ds(pl.multiple_of(core[0] * 2 * HD, 2 * HD), 2 * HD),
+        pl.ds(pl.multiple_of(half[0] * latents, latents), latents),
+    ].astype(jnp.float32)
     wide = jnp.where(row // HD == slot, wide, jnp.where(row == spare, 1.0, 0.0))
     asked[...] = wide.astype(jnp.bfloat16)
-    value_rows = pl.ds(pl.multiple_of(slot * HD, HD), HD)
-
-    def score(index, scores, peaks):
-        cols = pl.ds(pl.multiple_of(index * tile, tile), tile)
-        peak = None
+
+    buffers = (score_a, score_b)
+    count = latents // tile
+    peak = None
+    for step in range(count + 1):
+        cols = slice(step * tile, (step + 1) * tile)
+        done = slice((step - 1) * tile, step * tile)
+        top = None
+        weighted = None
         for start in range(0, 2 * frames, chunk):
             here = pl.ds(start, chunk)
-            value = dot(keyed[here, :], asked[:, cols])
-            scores[here, :] = value
-            top = jnp.max(value.reshape(chunk // 8, 8, tile), axis=0)
-            peak = top if peak is None else jnp.maximum(peak, top)
-        peaks[...] = jnp.max(peak, axis=0, keepdims=True)
-
-    def weigh(index, scores, peaks):
-        cols = pl.ds(pl.multiple_of(index * tile, tile), tile)
-        peak = peaks[...]
-        total = None
-        weighted = None
-        for start in range(0, 2 * frames, chunk):
-            probs = jnp.exp2((scores[pl.ds(start, chunk), :] - peak) * SCALE)
-            part = jnp.sum(probs.reshape(chunk // 8, 8, tile), axis=0)
-            total = part if total is None else total + part
-            source, offset = (value_own, start) if start < frames else (value_rec, start - frames)
-            values = source[value_rows, pl.ds(offset, chunk)]
-            term = dot(values, probs.astype(jnp.bfloat16))
-            weighted = term if weighted is None else weighted + term
-        total = jnp.sum(total, axis=0, keepdims=True)
-        if packed:
-            pack(outs[0].at[:, cols], peak, total, weighted)
-        else:
-            outs[0][:, cols] = peak
-            outs[1][:, cols] = total
-            outs[2][:, cols] = weighted
-
-    count = latents // tile
-    score(0, score_a, peak_a)
-
-    @pl.loop(0, count // 2)
-    def _(step):
-        score(2 * step + 1, score_b, peak_b)
-        weigh(2 * step, score_a, peak_a)
-        score(jnp.minimum(2 * step + 2, count - 1), score_a, peak_a)
-        weigh(2 * step + 1, score_b, peak_b)
+            if step < count:
+                value = dot(keyed[here, :], asked[:, cols])
+                buffers[step % 2][here, :] = value
+                high = jnp.max(value.reshape(chunk // 8, 8, tile), axis=0)
+                top = high if top is None else jnp.maximum(top, high)
+            if step > 0:
+                probs = jnp.exp2((buffers[(step - 1) % 2][here, :] - peak) * SCALE)
+                term = dot(valued[:, here], probs.astype(jnp.bfloat16))
+                weighted = term if weighted is None else weighted + term
+        if step > 0:
+            total = weighted[HD : HD + 1, :]
+            if packed:
+                pack(outs[0].at[:, done], peak, total, weighted[0:HD, :])
+            else:
+                outs[0][:, done] = peak
+                outs[1][:, done] = total
+                outs[2][:, done] = weighted[0:HD, :]
+        if step < count:
+            peak = jnp.max(top, axis=0, keepdims=True)
 
 
 def attend(packed, scalars, keys, values, queries):
-    latents = queries.shape[1]
+    latents = queries.shape[1] // 2
     frames = keys[0].shape[0]
-    tile = min(256, latents // 2)
+    tile = min(256, latents)
     if packed:
         out_shape = jax.ShapeDtypeStruct((HD + 8, latents), jnp.bfloat16)
         out_specs = pl.BlockSpec(memory_space=pltpu.VMEM)
@@ -380,32 +389,31 @@
     return pl.pallas_call(
         functools.partial(attend_kernel, packed),
         out_shape=out_shape,
-        in_specs=smem(4) + whole(5),
+        in_specs=smem(5) + whole(5),
         out_specs=out_specs,
         scratch_shapes=[
             VMEM((2 * frames, 2 * HD), jnp.bfloat16),
             VMEM((2 * HD, latents), jnp.bfloat16),
+            VMEM((HD + 16, 2 * frames), jnp.bfloat16),
             VMEM((2 * frames, tile), jnp.float32),
             VMEM((2 * frames, tile), jnp.float32),
-            VMEM((1, tile), jnp.float32),
-            VMEM((1, tile), jnp.float32),
         ],
         compiler_params=params(20),
         name="attend_send" if packed else "attend_keep",
     )(*scalars, *keys, *values, queries)
 
 
-def assemble_kernel(core, cross, own, across, core_own, core_across, out):
+def assemble_kernel(core, cross, lower, *refs):
+    out = refs[-1]
+    latents = refs[0].shape[1]
     mine, theirs = 2 * core[0], 2 - 2 * core[0]
-    for piece, head in (
-        (own, mine + cross[0]), (across, mine + 1 - cross[0]),
-        (core_own, theirs + cross[0]), (core_across, theirs + 1 - cross[0]),
-    ):
-        out[pl.ds(pl.multiple_of(head * HD, HD), HD), :] = piece[...]
-
-
-def swap(value, axis, bit):
-    return lax.ppermute(value, axis, [(i, i ^ bit) for i in range(lax.axis_size(axis))])
+    heads = (mine + cross[0], mine + 1 - cross[0], theirs + cross[0], theirs + 1 - cross[0])
+    for index, piece in enumerate(refs[:-1]):
+        part = lower[0] if index % 2 == 0 else 1 - lower[0]
+        out[
+            pl.ds(pl.multiple_of(heads[index // 2] * HD, HD), HD),
+            pl.ds(pl.multiple_of(part * latents, latents), latents),
+        ] = piece[...]
 
 
 def simple(kernel, out_shape, scalars, arrays, scratch=(), mib=16, specs=None):
@@ -440,11 +448,16 @@
     twins = [(i, i ^ 1) for i in range(blocks)]
 
     other_rec = lax.ppermute(recording, "sensor", across)
+    slab = ch // 2
+    near_sp = lax.ppermute(
+        lax.dynamic_slice_in_dim(spatial_w, core[0] * slab, slab, axis=0),
+        "sensor", across,
+    )
+    far_sp = lax.ppermute(near_sp, "tm", twins)
     tail = lax.ppermute(
         recording[:, frames - EDGE :], "tm", [(i, i + 1) for i in range(blocks - 1)]
     )
     head = lax.ppermute(recording[:, :EDGE], "tm", [(i + 1, i) for i in range(blocks - 1)])
-    other_w = lax.ppermute(spatial_w, "sensor", across)
     lane = jnp.arange(EDGE, dtype=jnp.int32)[None, :]
     edge = jnp.where(lane < HALF, head, tail)
     other_edge = lax.ppermute(edge, "sensor", across)
@@ -457,72 +470,92 @@
     far = [lax.ppermute(near[n], "tm", twins) for n in range(LAYERS)]
     other_valid = lax.ppermute(valid_frames, "tm", twins)
 
-    hidden = simple(
+    half_shape = jax.ShapeDtypeStruct((ch_loc, span), bf16)
+    own_h, other_h = simple(
         first_kernel,
-        jax.ShapeDtypeStruct((ch, span), bf16),
-        (),
-        (spatial_w, other_w, recording, other_rec, edge, other_edge),
-    )
-    columns = [VMEM((ch_loc, EDGE), jnp.float32)] * 2
+        [half_shape, half_shape],
+        (side, core),
+        (spatial_w, near_sp, far_sp, recording, other_rec, edge, other_edge),
+        [VMEM((2, slab, recording.shape[0]), bf16)],
+        mib=48,
+    )
+    taps_shape = jax.ShapeDtypeStruct((3, ch, span), bf16)
+    col = [VMEM((ch_loc, EDGE), jnp.float32)]
     for layer in range(LAYERS):
-        arrays = (hidden, conv_w, near[layer], far[layer], conv_b, other_b)
-        specs = whole(len(arrays))
-        specs[1] = pl.BlockSpec((None, 3, ch_loc, ch), lambda _, layer=layer: (layer, 0, 0, 0))
-        scratch = [VMEM((2, ch, span), bf16)] + columns
-        if layer < LAYERS - 1:
-            hidden = simple(
-                functools.partial(middle_kernel, layer, blocks),
-                jax.ShapeDtypeStruct((ch, span), bf16),
-                (dilations, side, core, place), arrays, scratch,
-                mib=28, specs=specs,
-            )
-        else:
+        last = layer == LAYERS - 1
+        specs = whole(4)
+        specs[2] = pl.BlockSpec((None, 3, ch_loc, ch), lambda _, layer=layer: (layer, 0, 0, 0))
+        own_next, taps = simple(
+            functools.partial(own_kernel, layer, blocks, last),
+            [jax.ShapeDtypeStruct((ch_loc, frames), bf16) if last else half_shape, taps_shape],
+            (dilations, side, place), (own_h, other_h, conv_w, conv_b), col,
+            mib=24, specs=specs,
+        )
+        arrays = (other_h, taps, near[layer], far[layer], other_b)
+        if last:
+            features = own_next
             shapes = [
-                jax.ShapeDtypeStruct((ch_loc, frames), bf16),
                 jax.ShapeDtypeStruct((frames, half), bf16),
                 jax.ShapeDtypeStruct((frames, half), bf16),
                 jax.ShapeDtypeStruct((half, frames), bf16),
                 jax.ShapeDtypeStruct((half, frames), bf16),
             ]
-            features, key_keep, key_send, value_keep, value_send = simple(
-                functools.partial(last_kernel, layer), shapes, (dilations, side, core),
-                arrays + (key_w, value_w),
-                scratch + [VMEM((ch, frames), bf16)],
-                mib=28, specs=specs + whole(2),
+            key_keep, key_send, value_keep, value_send = simple(
+                functools.partial(last_kernel, layer), shapes, (side, core),
+                (features,) + arrays + (key_w, value_w), col + [VMEM((ch, frames), bf16)],
+                mib=24,
             )
+        else:
+            other_h = simple(
+                functools.partial(other_kernel, layer, blocks), half_shape, (core, place), arrays,
+                col, mib=24,
+            )
+            own_h = own_next
     keys = (key_keep, lax.ppermute(key_send, "tm", twins))
     values = (value_keep, lax.ppermute(value_send, "tm", twins))
-    facts = (valid_frames, other_valid)
-    sent = attend(True, (core, 1 - cross) + facts, keys, values, queries)
-    arrived = swap(sent, "tm", 2)
-    peak, total, weighted = attend(False, (core, cross) + facts, keys, values, queries)
-    packed_shape = jax.ShapeDtypeStruct((HD + 8, latents), bf16)
-    final_shape = jax.ShapeDtypeStruct((HD, latents), bf16)
-    packed = simple(meet_kernel, packed_shape, (), (peak, total, weighted, arrived))
-    if blocks == 4:
-        done = simple(divide_kernel, final_shape, (), (packed,))
-    bit = 4
+
+    def flip(value, bit):
+        return lax.ppermute(value, "tm", [(i, i ^ bit) for i in range(blocks)])
+
+    lower = (place >> 2) & 1
+
+    def run(packed, slot, part):
+        scalars = (core, slot, part, valid_frames, other_valid)
+        return attend(packed, scalars, keys, values, queries)
+
+    sent = flip(run(True, 1 - cross, 1 - lower), 2)
+    kept = flip(run(True, 1 - cross, lower), 2)
+    packed_shape = jax.ShapeDtypeStruct((HD + 8, latents // 2), bf16)
+    final_shape = jax.ShapeDtypeStruct((HD, latents // 2), bf16)
+    given = run(False, cross, 1 - lower)
+    given = simple(meet_kernel, packed_shape, (), (*given, sent))
+    given = flip(given, 4)
+    held = run(False, cross, lower)
+    packed = simple(meet_kernel, packed_shape, (), (*held, kept, given))
+    bit = 8
     while bit < blocks:
-        theirs = swap(packed, "tm", bit)
+        theirs = flip(packed, bit)
         which = ((place & bit) != 0).astype(jnp.int32)
         if bit * 2 < blocks:
             packed = simple(merge_kernel, packed_shape, (which,), (packed, theirs))
         else:
             done = simple(finish_kernel, final_shape, (which,), (packed, theirs))
         bit *= 2
-    crossed = swap(done, "tm", 2)
-    core_done = swap(done, "tm", 1)
-    core_crossed = swap(crossed, "tm", 1)
+    above = flip(done, 4)
+    beside = flip(done, 2)
+    corner = flip(above, 2)
+    pieces = [done, above, beside, corner]
+    pieces += [flip(piece, 1) for piece in pieces]
     attended = simple(
-        assemble_kernel, jax.ShapeDtypeStruct((ch_loc, latents), bf16), (core, cross),
-        (done, crossed, core_done, core_crossed),
+        assemble_kernel, jax.ShapeDtypeStruct((ch_loc, latents), bf16), (core, cross, lower),
+        pieces,
     )
     return (features, attended)
 
 
 def fits(mesh):
     sensors, blocks = mesh.shape["sensor"], mesh.shape["tm"]
-    return sensors == 2 and blocks >= 4 and blocks & (blocks - 1) == 0
+    return sensors == 2 and blocks >= 16 and blocks & (blocks - 1) == 0
 
 
 def on_device(*arrays):

time: 119 us -> 123 us (1.034)
  waiting for transfers between devices: 53.5 us -> 41.8 us
  Pallas kernels: 32.7 us -> 38.3 us
  local copies, waits for them, and re-layouts: 8.46 us -> 13.3 us
  starting transfers between devices: 22.6 us -> 26.3 us
    ppermute x7 -> x13, waiting for transfers between devices: 30.4 us -> 22.6 us  [the longest x11 14.5 us: flip(): return lax.ppermute(value, 'tm', [(i, i ^ bit) for i in range(blocks)])]
    pallas_call x8 -> x11, Pallas kernels: 18.3 us -> 21.9 us  [simple(): pl.pallas_call(kernel, grid=(1,), out_shape=out_shape, in_specs=smem(len(...]
    ppermute x3, waiting for transfers between devices: 19.5 us -> 16.9 us  [pair_device(): near = [lax.ppermute(mine[n], 'sensor', across) for n in range(LAYERS)]]
    unnamed x30 -> x34, local copies, waits for them, and re-layouts: 6.18 us -> 8.68 us
    pallas_call x2 -> x4, Pallas kernels: 14.4 us -> 16.3 us  [attend(): pl.pallas_call(functools.partial(attend_kernel, packed), out_shape=out_sh...]
    ppermute x7 -> x13, starting transfers between devices: 8.67 us -> 10.4 us  [the longest x11 10.1 us: flip(): return lax.ppermute(value, 'tm', [(i, i ^ bit) for i in range(blocks)])]
    ppermute x1, starting transfers between devices: 0.14 us -> 1.81 us  [pair_device(): other_rec = lax.ppermute(recording, 'sensor', across)]
  transfers between devices with their start and end apart: 21 -> 27, of which waited for: 11 -> 11; matrix products, arithmetic and copies ran while one was open for 1% -> 3% of each run, Pallas kernels for 16% -> 25%
where the time goes in v3:
time: 123 us; the launch traced here: 122 us
  waiting for transfers between devices  41.8 us (34%)
  Pallas kernels  38.3 us (31%)
  starting transfers between devices  26.3 us (21%)
  local copies, waits for them, and re-layouts  13.3 us (11%)
  between operations  1.58 us (1%)
    pallas_call x11, Pallas kernels, simple(): pl.pallas_call(kernel, grid=(1,), out_shape=out_shape, in_specs=smem(len(...  21.9 us
    ppermute x3, waiting for transfers between devices, pair_device(): near = [lax.ppermute(mine[n], 'sensor', across) for n in range(LAYERS)]  16.9 us
    pallas_call x4, Pallas kernels, attend(): pl.pallas_call(functools.partial(attend_kernel, packed), out_shape=out_sh...  16.3 us
    ppermute x11, waiting for transfers between devices, flip(): return lax.ppermute(value, 'tm', [(i, i ^ bit) for i in range(blocks)])  14.5 us
    ppermute x11, starting transfers between devices, flip(): return lax.ppermute(value, 'tm', [(i, i ^ bit) for i in range(blocks)])  10.1 us
    unnamed x34, local copies, waits for them, and re-layouts  8.68 us
    ppermute x1, waiting for transfers between devices, pair_device(): lax.ppermute(lax.dynamic_slice_in_dim(spatial_w, core[0] * slab, slab, ax...  7.46 us
    ppermute x3, starting transfers between devices, pair_device(): near = [lax.ppermute(mine[n], 'sensor', across) for n in range(LAYERS)]  5.02 us
  transfers between devices with their start and end apart: 27, of which 11 were waited for; matrix products, arithmetic and copies ran while one was open for 3% of the time, Pallas kernels for 25%

profile of v3, /device:TPU:0, one launch (start us, length us, event | category | flops | bytes accessed | tf_op | source)
XLA Modules:
  0.0 122.0 jit_solution(14928066674326836657)
XLA Ops:
  0.7 2.4 %dynamic-slice_bitcast_fusion = (bf16[3,128,512]{2,1,0:T(8,128)(2,1)S(1)}, bf16[3,128,512]{2,1,0:T(8,128)(2,1)}, bf16[3,128,512]{2,1,0:T(8,128)(2,1)}) fusion(bf16[3,3,256,512]{3,2,1,0:T(8,128)(2,1)} %weights.5, s32[]{:T(128)S(6)} %select_n.14), kind=kLoop, calls=%fused_computation | loop fusion | bytes 2359300 | tf_op jit(solution)/shard_map/squeeze | solution.py:466
  3.0 3.0 %collective-permute-start.6 = (bf16[3,128,512]{2,1,0:T(8,128)(2,1)}, bf16[3,128,512]{2,1,0:T(8,128)(2,1)}, u32[]{:S(2)}, u32[]{:S(2)}) collective-permute-start(bf16[3,128,512]{2,1,0:T(8,128)(2,1)} %get-tuple-element.40), channel_id=1, source_target_pairs={{0,16},{16,0},{1,17},{17,1},{2,18},{18,2},{3,19},{19,3},{4,20},{20... | collective-permute-start | bytes 1179656 | tf_op jit(solution)/shard_map/ppermute | solution.py:469
  6.1 2.0 %collective-permute-start.12 = (bf16[3,128,512]{2,1,0:T(8,128)(2,1)S(1)}, bf16[3,128,512]{2,1,0:T(8,128)(2,1)S(1)}, u32[]{:S(2)}, u32[]{:S(2)}) collective-permute-start(bf16[3,128,512]{2,1,0:T(8,128)(2,1)S(1)} %get-tuple-element.38), channel_id=1, source_target_pairs={{0,16},{16,0},{1,17},{17,1},{2,18},{18,2},{3,19},{19,3},{4,20},{20... | collective-permute-start | bytes 1179656 | tf_op jit(solution)/shard_map/ppermute | solution.py:469
  10.8 3.6 %collective-permute-start.4 = (bf16[128,128]{1,0:T(8,128)(2,1)}, bf16[128,128]{1,0:T(8,128)(2,1)}, u32[]{:S(2)}, u32[]{:S(2)}) collective-permute-start(bf16[128,128]{1,0:T(8,128)(2,1)} %get-tuple-element.41), channel_id=1, source_target_pairs={{0,1},{1,2},{2,3},{3,4},{4,5},{5,6},{6,7},{7,8},{8,9},{9,10},{10,1... | collective-permute-start | bytes 98312 | tf_op jit(solution)/shard_map/ppermute | solution.py:457
  16.3 8.3 %collective-permute-done.9.near_w = bf16[3,128,512]{2,1,0:T(8,128)(2,1)S(1)} collective-permute-done((bf16[3,128,512]{2,1,0:T(8,128)(2,1)}, bf16[3,128,512]{2,1,0:T(8,128)(2,1)S(1)}, u32[]{:S(2)}, u32[]{:S(2)}) %collective-permute-start.9) | collective-permute-done | bytes 393248 | tf_op jit(solution)/shard_map/ppermute | solution.py:469
  24.6 7.6 %collective-permute-done.12.near_w = bf16[3,128,512]{2,1,0:T(8,128)(2,1)S(1)} collective-permute-done((bf16[3,128,512]{2,1,0:T(8,128)(2,1)S(1)}, bf16[3,128,512]{2,1,0:T(8,128)(2,1)S(1)}, u32[]{:S(2)}, u32[]{:S(2)}) %collective-permute-start.12) | collective-permute-done | bytes 393248 | tf_op jit(solution)/shard_map/ppermute | solution.py:469
  32.2 1.8 %collective-permute-start.2 = (bf16[128,1024]{1,0:T(8,128)(2,1)}, bf16[128,1024]{1,0:T(8,128)(2,1)}, u32[]{:S(2)}, u32[]{:S(2)}) collective-permute-start(bf16[128,1024]{1,0:T(8,128)(2,1)} %own.1), channel_id=1, source_target_pairs={{0,16},{16,0},{1,17},{17,1},{2,18},{18,2},{3,19},{19,3},{4,20},{20... | collective-permute-start | bytes 786440 | tf_op jit(solution)/shard_map/ppermute | solution.py:450
  35.1 7.5 %collective-permute-done.near_w = bf16[256,128]{1,0:T(8,128)(2,1)S(1)} collective-permute-done((bf16[256,128]{1,0:T(8,128)(2,1)S(1)}, bf16[256,128]{1,0:T(8,128)(2,1)S(1)}, u32[]{:S(2)}, u32[]{:S(2)}) %collective-permute-start) | collective-permute-done | bytes 65568 | tf_op jit(solution)/shard_map/ppermute | solution.py:452
  42.6 1.7 %collective-permute-start.5 = (bf16[128,128]{1,0:T(8,128)(2,1)S(1)}, bf16[128,128]{1,0:T(8,128)(2,1)S(1)}, u32[]{:S(2)}, u32[]{:S(2)}) collective-permute-start(bf16[128,128]{1,0:T(8,128)(2,1)S(1)} %broadcast_select_fusion.own_edge), channel_id=1, source_target_pairs={{0,16},{16,0},{1,17},{17,1},{2,18},{18,2},{3,19},{19,3},{4,20},{20... | collective-permute-start | bytes 98312 | tf_op jit(solution)/shard_map/ppermute | solution.py:463
  49.0 1.7 %collective-permute-start.8 = (f32[3,256]{1,0:T(4,128)}, f32[3,256]{1,0:T(4,128)S(1)}, u32[]{:S(2)}, u32[]{:S(2)}) collective-permute-start(f32[3,256]{1,0:T(4,128)} %biases.5), channel_id=1, source_target_pairs={{0,16},{16,0},{1,17},{17,1},{2,18},{18,2},{3,19},{19,3},{4,20},{20... | collective-permute-start | bytes 9224 | tf_op jit(solution)/shard_map/ppermute | solution.py:464
  57.5 3.7 %shard_map.105 = (bf16[256,1152]{1,0:T(8,128)(2,1)S(1)}, bf16[3,512,1152]{2,1,0:T(8,128)(2,1)S(1)}) custom-call(s32[3]{0:T(128)S(1)} %copy-done.16, s32[1]{0:T(128)} %bitcast.side, s32[1]{0:T(128)} %bitcast.1.place, bf16[256,1152]{1,0:T(8,128)(2,1)S(1)} %get-tuple-element.20.mine, bf16[256,1152]{1,0:T(8,128)(2,1)S(1)} %get-tuple-element.21.theirs, ...), custom_call_target="tpu_custom_call" | custom-call | tf_op jit(solution)/shard_map/pallas_call | solution.py:421
  61.2 2.7 %shard_map.106.theirs = bf16[256,1152]{1,0:T(8,128)(2,1)S(1)} custom-call(s32[1]{0:T(128)S(6)} %and.14.core, s32[1]{0:T(128)} %bitcast.1.place, bf16[256,1152]{1,0:T(8,128)(2,1)S(1)} %get-tuple-element.21.theirs, bf16[3,512,1152]{2,1,0:T(8,128)(2,1)S(1)} %get-tuple-element.23.taps, bf16[3,128,512]{2,1,0:T(8,128)(2,1)} %collective-permute-done.6.near_w, ...), custom_call_target="tpu_custom_call" | custom-call | tf_op jit(solution)/shard_map/pallas_call | solution.py:421
  63.9 3.7 %shard_map.107 = (bf16[256,1152]{1,0:T(8,128)(2,1)S(1)}, bf16[3,512,1152]{2,1,0:T(8,128)(2,1)S(1)}) custom-call(s32[3]{0:T(128)S(1)} %copy-done.16, s32[1]{0:T(128)} %bitcast.side, s32[1]{0:T(128)} %bitcast.1.place, bf16[256,1152]{1,0:T(8,128)(2,1)S(1)} %get-tuple-element.22.mine, bf16[256,1152]{1,0:T(8,128)(2,1)S(1)} %shard_map.106.theirs, ...), custom_call_target="tpu_custom_call" | custom-call | tf_op jit(solution)/shard_map/pallas_call | solution.py:421
  67.6 2.6 %shard_map.108.theirs = bf16[256,1152]{1,0:T(8,128)(2,1)S(1)} custom-call(s32[1]{0:T(128)S(6)} %and.14.core, s32[1]{0:T(128)} %bitcast.1.place, bf16[256,1152]{1,0:T(8,128)(2,1)S(1)} %shard_map.106.theirs, bf16[3,512,1152]{2,1,0:T(8,128)(2,1)S(1)} %get-tuple-element.25.taps, bf16[3,128,512]{2,1,0:T(8,128)(2,1)S(1)} %collective-permute-done.9.near_w, ...), custom_call_target="tpu_custom_call" | custom-call | tf_op jit(solution)/shard_map/pallas_call | solution.py:421
  70.2 4.2 %shard_map.109 = (bf16[256,1024]{1,0:T(8,128)(2,1)}, bf16[3,512,1152]{2,1,0:T(8,128)(2,1)S(1)}) custom-call(s32[3]{0:T(128)S(1)} %copy-done.16, s32[1]{0:T(128)} %bitcast.side, s32[1]{0:T(128)} %bitcast.1.place, bf16[256,1152]{1,0:T(8,128)(2,1)S(1)} %get-tuple-element.24.mine, bf16[256,1152]{1,0:T(8,128)(2,1)S(1)} %shard_map.108.theirs, ...), custom_call_target="tpu_custom_call" | custom-call | tf_op jit(solution)/shard_map/pallas_call | solution.py:421
  75.6 1.9 %shard_map.110 = (bf16[1024,128]{1,0:T(8,128)(2,1)S(1)}, bf16[1024,128]{1,0:T(8,128)(2,1)S(1)}, bf16[128,1024]{1,0:T(8,128)(2,1)S(1)}, bf16[128,1024]{1,0:T(8,128)(2,1)S(1)}) custom-call(s32[1]{0:T(128)} %bitcast.side, s32[1]{0:T(128)S(6)} %and.14.core, bf16[256,1024]{1,0:T(8,128)(2,1)S(1)} %copy-done.2, bf16[256,1152]{1,0:T(8,128)(2,1)S(1)} %shard_map.108.theirs, ...), custom_call_target="tpu_custom_call" | custom-call | tf_op jit(solution)/shard_map/pallas_call | solution.py:421
  79.6 4.0 %attend_send.3 = bf16[72,1024]{1,0:T(8,128)(2,1)S(1)} custom-call(s32[1]{0:T(128)S(6)} %and.14.core, s32[1]{0:T(128)S(6)} %sub.8.which, s32[1]{0:T(128)S(6)} %sub.9.half, s32[1]{0:T(128)S(6)} %copy.11.valid_own, s32[1]{0:T(128)} %collective-permute-done.11.valid_rec, bf16[1024,128]{1,0:T(8,128)(2,1)S(1)} %get-tuple-element.28.key_own, ...), custom_call_target="tpu_custom_call" | custom-call | tf_op jit(solution)/shard_map/attend_send/pallas_call | solution.py:389
  85.2 4.0 %attend_send.2 = bf16[72,1024]{1,0:T(8,128)(2,1)S(1)} custom-call(s32[1]{0:T(128)S(6)} %and.14.core, s32[1]{0:T(128)S(6)} %sub.8.which, s32[1]{0:T(128)S(6)} %and.16.half.lower, s32[1]{0:T(128)S(6)} %copy.11.valid_own, s32[1]{0:T(128)} %collective-permute-done.11.valid_rec, bf16[1024,128]{1,0:T(8,128)(2,1)S(1)} %get-tuple-element.28.key_own, ...), custom_call_target="tpu_custom_call" | custom-call | tf_op jit(solution)/shard_map/attend_send/pallas_call | solution.py:389
  89.8 4.2 %attend_keep.3 = (f32[1,1024]{1,0:T(1,128)S(1)}, f32[1,1024]{1,0:T(1,128)S(1)}, f32[64,1024]{1,0:T(8,128)S(1)}) custom-call(s32[1]{0:T(128)S(6)} %and.14.core, s32[1]{0:T(128)S(6)} %and.15.which.cross, s32[1]{0:T(128)S(6)} %sub.9.half, s32[1]{0:T(128)S(6)} %copy.11.valid_own, s32[1]{0:T(128)} %collective-permute-done.11.valid_rec, ...), custom_call_target="tpu_custom_call" | custom-call | tf_op jit(solution)/shard_map/attend_keep/pallas_call | solution.py:389
  95.8 4.0 %attend_keep.2 = (f32[1,1024]{1,0:T(1,128)S(1)}, f32[1,1024]{1,0:T(1,128)S(1)}, f32[64,1024]{1,0:T(8,128)S(1)}) custom-call(s32[1]{0:T(128)S(6)} %and.14.core, s32[1]{0:T(128)S(6)} %and.15.which.cross, s32[1]{0:T(128)S(6)} %and.16.half.lower, s32[1]{0:T(128)S(6)} %copy.11.valid_own, s32[1]{0:T(128)} %collective-permute-done.11.valid_rec, ...), custom_call_target="tpu_custom_call" | custom-call | tf_op jit(solution)/shard_map/attend_keep/pallas_call | solution.py:389
  100.0 2.7 %collective-permute-start.19 = (bf16[72,1024]{1,0:T(8,128)(2,1)S(1)}, bf16[72,1024]{1,0:T(8,128)(2,1)S(1)}, u32[]{:S(2)}, u32[]{:S(2)}) collective-permute-start(bf16[72,1024]{1,0:T(8,128)(2,1)S(1)} %shard_map.112.mine), channel_id=1, source_target_pairs={{0,8},{1,9},{2,10},{3,11},{4,12},{5,13},{6,14},{7,15},{8,0},{9,1},... | collective-permute-start | bytes 442376 | tf_op jit(solution)/shard_map/ppermute | solution.py:518
  102.7 6.5 %collective-permute-done.19.theirs = bf16[72,1024]{1,0:T(8,128)(2,1)S(1)} collective-permute-done((bf16[72,1024]{1,0:T(8,128)(2,1)S(1)}, bf16[72,1024]{1,0:T(8,128)(2,1)S(1)}, u32[]{:S(2)}, u32[]{:S(2)}) %collective-permute-start.19) | collective-permute-done | bytes 147488 | tf_op jit(solution)/shard_map/ppermute | solution.py:518
  111.0 3.7 %collective-permute-done.20.refs_1_ = bf16[64,1024]{1,0:T(8,128)(2,1)S(1)} collective-permute-done((bf16[64,1024]{1,0:T(8,128)(2,1)S(1)}, bf16[64,1024]{1,0:T(8,128)(2,1)S(1)}, u32[]{:S(2)}, u32[]{:S(2)}) %collective-permute-start.20) | collective-permute-done | bytes 131104 | tf_op jit(solution)/shard_map/ppermute | solution.py:518
  116.7 2.9 %collective-permute-done.22.refs_3_ = bf16[64,1024]{1,0:T(8,128)(2,1)S(1)} collective-permute-done((bf16[64,1024]{1,0:T(8,128)(2,1)S(1)}, bf16[64,1024]{1,0:T(8,128)(2,1)S(1)}, u32[]{:S(2)}, u32[]{:S(2)}) %collective-permute-start.22) | collective-permute-done | bytes 131104 | tf_op jit(solution)/shard_map/ppermute | solution.py:518
  (84 shorter events, 29.9 us)
Async XLA Ops:
  3.0 13.3 %collective-permute-start.6 = (bf16[3,128,512]{2,1,0:T(8,128)(2,1)}, bf16[3,128,512]{2,1,0:T(8,128)(2,1)}, u32[]{:S(2)}, u32[]{:S(2)}) collective-permute-start(bf16[3,128,512]{2,1,0:T(8,128)(2,1)} %get-tuple-element.40), channel_id=1, source_target_pairs={{0,16},{16,0},{1,17},{17,1},{2,18},{18,2},{3,19},{19,3},{4,20},{20... | collective-permute-start | bytes 1179656 | tf_op jit(solution)/shard_map/ppermute | solution.py:469
  6.0 18.6 %collective-permute-start.9 = (bf16[3,128,512]{2,1,0:T(8,128)(2,1)}, bf16[3,128,512]{2,1,0:T(8,128)(2,1)S(1)}, u32[]{:S(2)}, u32[]{:S(2)}) collective-permute-start(bf16[3,128,512]{2,1,0:T(8,128)(2,1)} %get-tuple-element.39), channel_id=1, source_target_pairs={{0,16},{16,0},{1,17},{17,1},{2,18},{18,2},{3,19},{19,3},{4,20},{20... | collective-permute-start | bytes 1179656 | tf_op jit(solution)/shard_map/ppermute | solution.py:469
  6.1 26.1 %collective-permute-start.12 = (bf16[3,128,512]{2,1,0:T(8,128)(2,1)S(1)}, bf16[3,128,512]{2,1,0:T(8,128)(2,1)S(1)}, u32[]{:S(2)}, u32[]{:S(2)}) collective-permute-start(bf16[3,128,512]{2,1,0:T(8,128)(2,1)S(1)} %get-tuple-element.38), channel_id=1, source_target_pairs={{0,16},{16,0},{1,17},{17,1},{2,18},{18,2},{3,19},{19,3},{4,20},{20... | collective-permute-start | bytes 1179656 | tf_op jit(solution)/shard_map/ppermute | solution.py:469
  9.5 22.7 %collective-permute-start.3 = (bf16[128,128]{1,0:T(8,128)(2,1)}, bf16[128,128]{1,0:T(8,128)(2,1)}, u32[]{:S(2)}, u32[]{:S(2)}) collective-permute-start(bf16[128,128]{1,0:T(8,128)(2,1)} %get-tuple-element.42), channel_id=1, source_target_pairs={{1,0},{2,1},{3,2},{4,3},{5,4},{6,5},{7,6},{8,7},{9,8},{10,9},{11,1... | collective-permute-start | bytes 98312 | tf_op jit(solution)/shard_map/ppermute | solution.py:460
  10.8 23.3 %collective-permute-start.4 = (bf16[128,128]{1,0:T(8,128)(2,1)}, bf16[128,128]{1,0:T(8,128)(2,1)}, u32[]{:S(2)}, u32[]{:S(2)}) collective-permute-start(bf16[128,128]{1,0:T(8,128)(2,1)} %get-tuple-element.41), channel_id=1, source_target_pairs={{0,1},{1,2},{2,3},{3,4},{4,5},{5,6},{6,7},{7,8},{8,9},{9,10},{10,1... | collective-permute-start | bytes 98312 | tf_op jit(solution)/shard_map/ppermute | solution.py:457
  16.3 44.9 %collective-permute-start.7 = (bf16[3,128,512]{2,1,0:T(8,128)(2,1)}, bf16[3,128,512]{2,1,0:T(8,128)(2,1)}, u32[]{:S(2)}, u32[]{:S(2)}) collective-permute-start(bf16[3,128,512]{2,1,0:T(8,128)(2,1)} %collective-permute-done.6.near_w), channel_id=1, source_target_pairs={{0,1},{1,0},{2,3},{3,2},{4,5},{5,4},{6,7},{7,6},{8,9},{9,8},{10,11... | collective-permute-start | bytes 1179656 | tf_op jit(solution)/shard_map/ppermute | solution.py:470
  24.6 43.0 %collective-permute-start.10 = (bf16[3,128,512]{2,1,0:T(8,128)(2,1)S(1)}, bf16[3,128,512]{2,1,0:T(8,128)(2,1)}, u32[]{:S(2)}, u32[]{:S(2)}) collective-permute-start(bf16[3,128,512]{2,1,0:T(8,128)(2,1)S(1)} %collective-permute-done.9.near_w), channel_id=1, source_target_pairs={{0,1},{1,0},{2,3},{3,2},{4,5},{5,4},{6,7},{7,6},{8,9},{9,8},{10,11... | collective-permute-start | bytes 1179656 | tf_op jit(solution)/shard_map/ppermute | solution.py:470
  32.2 42.3 %collective-permute-start.13 = (bf16[3,128,512]{2,1,0:T(8,128)(2,1)S(1)}, bf16[3,128,512]{2,1,0:T(8,128)(2,1)S(1)}, u32[]{:S(2)}, u32[]{:S(2)}) collective-permute-start(bf16[3,128,512]{2,1,0:T(8,128)(2,1)S(1)} %collective-permute-done.12.near_w), channel_id=1, source_target_pairs={{0,1},{1,0},{2,3},{3,2},{4,5},{5,4},{6,7},{7,6},{8,9},{9,8},{10,11... | collective-permute-start | bytes 1179656 | tf_op jit(solution)/shard_map/ppermute | solution.py:470
  32.2 18.5 %collective-permute-start.2 = (bf16[128,1024]{1,0:T(8,128)(2,1)}, bf16[128,1024]{1,0:T(8,128)(2,1)}, u32[]{:S(2)}, u32[]{:S(2)}) collective-permute-start(bf16[128,1024]{1,0:T(8,128)(2,1)} %own.1), channel_id=1, source_target_pairs={{0,16},{16,0},{1,17},{17,1},{2,18},{18,2},{3,19},{19,3},{4,20},{20... | collective-permute-start | bytes 786440 | tf_op jit(solution)/shard_map/ppermute | solution.py:450
  34.0 8.5 %collective-permute-start = (bf16[256,128]{1,0:T(8,128)(2,1)S(1)}, bf16[256,128]{1,0:T(8,128)(2,1)S(1)}, u32[]{:S(2)}, u32[]{:S(2)}) collective-permute-start(bf16[256,128]{1,0:T(8,128)(2,1)S(1)} %constant_dynamic-slice_fusion), channel_id=1, source_target_pairs={{0,16},{16,0},{1,17},{17,1},{2,18},{18,2},{3,19},{19,3},{4,20},{20... | collective-permute-start | bytes 196616 | tf_op jit(solution)/shard_map/ppermute | solution.py:452
  42.6 3.9 %collective-permute-start.5 = (bf16[128,128]{1,0:T(8,128)(2,1)S(1)}, bf16[128,128]{1,0:T(8,128)(2,1)S(1)}, u32[]{:S(2)}, u32[]{:S(2)}) collective-permute-start(bf16[128,128]{1,0:T(8,128)(2,1)S(1)} %broadcast_select_fusion.own_edge), channel_id=1, source_target_pairs={{0,16},{16,0},{1,17},{17,1},{2,18},{18,2},{3,19},{19,3},{4,20},{20... | collective-permute-start | bytes 98312 | tf_op jit(solution)/shard_map/ppermute | solution.py:463
  49.0 12.2 %collective-permute-start.8 = (f32[3,256]{1,0:T(4,128)}, f32[3,256]{1,0:T(4,128)S(1)}, u32[]{:S(2)}, u32[]{:S(2)}) collective-permute-start(f32[3,256]{1,0:T(4,128)} %biases.5), channel_id=1, source_target_pairs={{0,16},{16,0},{1,17},{17,1},{2,18},{18,2},{3,19},{19,3},{4,20},{20... | collective-permute-start | bytes 9224 | tf_op jit(solution)/shard_map/ppermute | solution.py:464
  77.6 2.0 %collective-permute-start.14 = (bf16[1024,128]{1,0:T(8,128)(2,1)S(1)}, bf16[1024,128]{1,0:T(8,128)(2,1)S(1)}, u32[]{:S(2)}, u32[]{:S(2)}) collective-permute-start(bf16[1024,128]{1,0:T(8,128)(2,1)S(1)} %get-tuple-element.29), channel_id=1, source_target_pairs={{0,1},{1,0},{2,3},{3,2},{4,5},{5,4},{6,7},{7,6},{8,9},{9,8},{10,11... | collective-permute-start | bytes 786440 | tf_op jit(solution)/shard_map/ppermute | solution.py:514
  77.6 1.9 %collective-permute-start.15 = (bf16[128,1024]{1,0:T(8,128)(2,1)S(1)}, bf16[128,1024]{1,0:T(8,128)(2,1)S(1)}, u32[]{:S(2)}, u32[]{:S(2)}) collective-permute-start(bf16[128,1024]{1,0:T(8,128)(2,1)S(1)} %get-tuple-element.31), channel_id=1, source_target_pairs={{0,1},{1,0},{2,3},{3,2},{4,5},{5,4},{6,7},{7,6},{8,9},{9,8},{10,11... | collective-permute-start | bytes 786440 | tf_op jit(solution)/shard_map/ppermute | solution.py:515
  83.6 10.4 %collective-permute-start.17 = (bf16[72,1024]{1,0:T(8,128)(2,1)S(1)}, bf16[72,1024]{1,0:T(8,128)(2,1)S(1)}, u32[]{:S(2)}, u32[]{:S(2)}) collective-permute-start(bf16[72,1024]{1,0:T(8,128)(2,1)S(1)} %attend_send.3), channel_id=1, source_target_pairs={{0,2},{1,3},{2,0},{3,1},{4,6},{5,7},{6,4},{7,5},{8,10},{9,11},{10,... | collective-permute-start | bytes 442376 | tf_op jit(solution)/shard_map/ppermute | solution.py:518
  89.2 10.6 %collective-permute-start.16 = (bf16[72,1024]{1,0:T(8,128)(2,1)S(1)}, bf16[72,1024]{1,0:T(8,128)(2,1)S(1)}, u32[]{:S(2)}, u32[]{:S(2)}) collective-permute-start(bf16[72,1024]{1,0:T(8,128)(2,1)S(1)} %attend_send.2), channel_id=1, source_target_pairs={{0,2},{1,3},{2,0},{3,1},{4,6},{5,7},{6,4},{7,5},{8,10},{9,11},{10,... | collective-permute-start | bytes 442376 | tf_op jit(solution)/shard_map/ppermute | solution.py:518
  94.2 5.7 %collective-permute-start.18 = (bf16[72,1024]{1,0:T(8,128)(2,1)S(1)}, bf16[72,1024]{1,0:T(8,128)(2,1)S(1)}, u32[]{:S(2)}, u32[]{:S(2)}) collective-permute-start(bf16[72,1024]{1,0:T(8,128)(2,1)S(1)} %shard_map.111), channel_id=1, source_target_pairs={{0,4},{1,5},{2,6},{3,7},{4,0},{5,1},{6,2},{7,3},{8,12},{9,13},{10,... | collective-permute-start | bytes 442376 | tf_op jit(solution)/shard_map/ppermute | solution.py:518
  100.0 9.2 %collective-permute-start.19 = (bf16[72,1024]{1,0:T(8,128)(2,1)S(1)}, bf16[72,1024]{1,0:T(8,128)(2,1)S(1)}, u32[]{:S(2)}, u32[]{:S(2)}) collective-permute-start(bf16[72,1024]{1,0:T(8,128)(2,1)S(1)} %shard_map.112.mine), channel_id=1, source_target_pairs={{0,8},{1,9},{2,10},{3,11},{4,12},{5,13},{6,14},{7,15},{8,0},{9,1},... | collective-permute-start | bytes 442376 | tf_op jit(solution)/shard_map/ppermute | solution.py:518
  109.3 5.4 %collective-permute-start.20 = (bf16[64,1024]{1,0:T(8,128)(2,1)S(1)}, bf16[64,1024]{1,0:T(8,128)(2,1)S(1)}, u32[]{:S(2)}, u32[]{:S(2)}) collective-permute-start(bf16[64,1024]{1,0:T(8,128)(2,1)S(1)} %shard_map.113.refs_0_), channel_id=1, source_target_pairs={{0,4},{1,5},{2,6},{3,7},{4,0},{5,1},{6,2},{7,3},{8,12},{9,13},{10,... | collective-permute-start | bytes 393224 | tf_op jit(solution)/shard_map/ppermute | solution.py:518
  109.4 7.3 %collective-permute-start.21 = (bf16[64,1024]{1,0:T(8,128)(2,1)S(1)}, bf16[64,1024]{1,0:T(8,128)(2,1)S(1)}, u32[]{:S(2)}, u32[]{:S(2)}) collective-permute-start(bf16[64,1024]{1,0:T(8,128)(2,1)S(1)} %shard_map.113.refs_0_), channel_id=1, source_target_pairs={{0,2},{1,3},{2,0},{3,1},{4,6},{5,7},{6,4},{7,5},{8,10},{9,11},{10,... | collective-permute-start | bytes 393224 | tf_op jit(solution)/shard_map/ppermute | solution.py:518
  114.7 5.0 %collective-permute-start.22 = (bf16[64,1024]{1,0:T(8,128)(2,1)S(1)}, bf16[64,1024]{1,0:T(8,128)(2,1)S(1)}, u32[]{:S(2)}, u32[]{:S(2)}) collective-permute-start(bf16[64,1024]{1,0:T(8,128)(2,1)S(1)} %collective-permute-done.20.refs_1_), channel_id=1, source_target_pairs={{0,2},{1,3},{2,0},{3,1},{4,6},{5,7},{6,4},{7,5},{8,10},{9,11},{10,... | collective-permute-start | bytes 393224 | tf_op jit(solution)/shard_map/ppermute | solution.py:518
  116.2 3.5 %collective-permute-start.23 = (bf16[64,1024]{1,0:T(8,128)(2,1)S(1)}, bf16[64,1024]{1,0:T(8,128)(2,1)S(1)}, u32[]{:S(2)}, u32[]{:S(2)}) collective-permute-start(bf16[64,1024]{1,0:T(8,128)(2,1)S(1)} %shard_map.113.refs_0_), channel_id=1, source_target_pairs={{0,1},{1,0},{2,3},{3,2},{4,5},{5,4},{6,7},{7,6},{8,9},{9,8},{10,11... | collective-permute-start | bytes 393224 | tf_op jit(solution)/shard_map/ppermute | solution.py:518
  116.2 3.5 %collective-permute-start.24 = (bf16[64,1024]{1,0:T(8,128)(2,1)S(1)}, bf16[64,1024]{1,0:T(8,128)(2,1)S(1)}, u32[]{:S(2)}, u32[]{:S(2)}) collective-permute-start(bf16[64,1024]{1,0:T(8,128)(2,1)S(1)} %collective-permute-done.20.refs_1_), channel_id=1, source_target_pairs={{0,1},{1,0},{2,3},{3,2},{4,5},{5,4},{6,7},{7,6},{8,9},{9,8},{10,11... | collective-permute-start | bytes 393224 | tf_op jit(solution)/shard_map/ppermute | solution.py:518
  116.7 3.0 %collective-permute-start.25 = (bf16[64,1024]{1,0:T(8,128)(2,1)S(1)}, bf16[64,1024]{1,0:T(8,128)(2,1)S(1)}, u32[]{:S(2)}, u32[]{:S(2)}) collective-permute-start(bf16[64,1024]{1,0:T(8,128)(2,1)S(1)} %collective-permute-done.21.refs_2_), channel_id=1, source_target_pairs={{0,1},{1,0},{2,3},{3,2},{4,5},{5,4},{6,7},{7,6},{8,9},{9,8},{10,11... | collective-permute-start | bytes 393224 | tf_op jit(solution)/shard_map/ppermute | solution.py:518
  (20 other events, 202.1 us)

commit v4 on v3

--- a/solution.py
+++ b/solution.py
@@ -136,16 +136,22 @@
     return jnp.dot(left, right, preferred_element_type=jnp.float32)
 
 
-def first_kernel(
-    side, core, own_w, near_w, far_w, own, other, own_edge, other_edge, mine, theirs, weights
-):
+def first_kernel(side, *refs):
+    sources, (mine, theirs), held, done = refs[:6], refs[6:8], refs[8:14], refs[14]
+    copies = [
+        pltpu.make_async_copy(source, target, done.at[n])
+        for n, (source, target) in enumerate(zip(sources, held))
+    ]
+    for copy in copies:
+        copy.start()
+    for copy in copies:
+        copy.wait()
+    own_w, other_w, own, other, own_edge, other_edge = held
     frames = own.shape[1]
     rows = mine.shape[0]
-    weights[core[0]] = near_w[...]
-    weights[1 - core[0]] = far_w[...]
     for out, part in ((mine, side[0]), (theirs, 1 - side[0])):
-        left = own_w[pl.ds(pl.multiple_of(part * rows, rows), rows), :]
-        right = weights[part]
+        here = pl.ds(pl.multiple_of(part * rows, rows), rows)
+        left, right = own_w[here, :], other_w[here, :]
         out[:, :frames] = (dot(left, own[...]) + dot(right, other[...])).astype(out.dtype)
         out[:, frames:] = (dot(left, own_edge[...]) + dot(right, other_edge[...])).astype(out.dtype)
 
@@ -183,20 +189,31 @@
 
 
 def own_kernel(
-    layer, blocks, last, dilations, side, place, mine, theirs, weights, biases, out, taps, col
+    layer, blocks, last, dilations, side, place, mine, theirs, weights, biases, *refs
 ):
+    outs, taps, col = refs[:-2], refs[-2], refs[-1]
+    out = outs[0]
     rows, span = mine.shape
     shift = dilations[layer]
+    lane = lax.broadcasted_iota(jnp.int32, (rows, EDGE), 1)
+    count = span // EDGE
     for part, source in ((side[0], mine), (1 - side[0], theirs)):
         here = pl.ds(pl.multiple_of(part * rows, rows), rows)
-        wide = source[...].astype(jnp.float32)
-        taps[1, here, :] = source[...]
-        taps[0, here, :] = pltpu.roll(wide, shift, 1).astype(jnp.bfloat16)
-        taps[2, here, :] = pltpu.roll(wide, span - shift, 1).astype(jnp.bfloat16)
+        tiles = [source[:, n * EDGE : (n + 1) * EDGE] for n in range(count)]
+        later = [pltpu.roll(tile, shift, 1) for tile in tiles]
+        sooner = [pltpu.roll(tile, EDGE - shift, 1) for tile in tiles]
+        for n in range(count):
+            cols = slice(n * EDGE, (n + 1) * EDGE)
+            taps[1, here, cols] = tiles[n]
+            taps[0, here, cols] = jnp.where(lane < shift, later[n - 1], later[n])
+            taps[2, here, cols] = jnp.where(
+                lane < EDGE - shift, sooner[n], sooner[(n + 1) % count]
+            )
     column(biases[layer : layer + 1, :], col)
 
     def store(here, value):
-        out[:, here] = value
+        for target in outs:
+            target[:, here] = value
 
     conv_rows(
         taps, lambda here: mine[:, here], weights, col[:, 0:1],
@@ -319,7 +336,7 @@
     frames = key_own.shape[0]
     latents = asked.shape[1]
     tile = score_a.shape[1]
-    chunk = 256
+    chunk = frames
     slot = which[0]
     lane = lax.broadcasted_iota(jnp.int32, (frames, 2 * HD), 1)
     frame = lax.broadcasted_iota(jnp.int32, (frames, 2 * HD), 0)
@@ -330,9 +347,8 @@
         keyed[pl.ds(part * frames, frames), :] = jnp.where(
             lane == spare, bias, source[...].astype(jnp.float32)
         ).astype(jnp.bfloat16)
-    valued[0:HD, 0:frames] = value_own[value_rows, :]
-    valued[0:HD, frames:] = value_rec[value_rows, :]
-    valued[HD:, :] = jnp.ones((valued.shape[0] - HD, 2 * frames), jnp.bfloat16)
+    valued[:, 0:frames] = value_own[value_rows, :]
+    valued[:, frames:] = value_rec[value_rows, :]
     row = lax.broadcasted_iota(jnp.int32, (2 * HD, latents), 0)
     wide = queries[
         pl.ds(pl.multiple_of(core[0] * 2 * HD, 2 * HD), 2 * HD),
@@ -341,33 +357,41 @@
     wide = jnp.where(row // HD == slot, wide, jnp.where(row == spare, 1.0, 0.0))
     asked[...] = wide.astype(jnp.bfloat16)
 
-    buffers = (score_a, score_b)
     count = latents // tile
     peak = None
     for step in range(count + 1):
         cols = slice(step * tile, (step + 1) * tile)
         done = slice((step - 1) * tile, step * tile)
-        top = None
-        weighted = None
-        for start in range(0, 2 * frames, chunk):
-            here = pl.ds(start, chunk)
+        now, before = ((score_a, score_b), (score_b, score_a))[step % 2]
+
+        def body(index, carry, step=step, cols=cols, now=now, before=before, peak=peak):
+            top, total, weighted = carry
+            here = pl.ds(pl.multiple_of(index * chunk, chunk), chunk)
             if step < count:
                 value = dot(keyed[here, :], asked[:, cols])
-                buffers[step % 2][here, :] = value
-                high = jnp.max(value.reshape(chunk // 8, 8, tile), axis=0)
-                top = high if top is None else jnp.maximum(top, high)
+                now[here, :] = value
+                top = jnp.maximum(top, jnp.max(value.reshape(chunk // 8, 8, tile), axis=0))
             if step > 0:
-                probs = jnp.exp2((buffers[(step - 1) % 2][here, :] - peak) * SCALE)
-                term = dot(valued[:, here], probs.astype(jnp.bfloat16))
-                weighted = term if weighted is None else weighted + term
+                probs = jnp.exp2((before[here, :] - peak) * SCALE)
+                total = total + jnp.sum(probs.reshape(chunk // 8, 8, tile), axis=0)
+                weighted = weighted + dot(valued[:, here], probs.astype(jnp.bfloat16))
+            return top, total, weighted
+
+        top, total, weighted = lax.fori_loop(
+            0, 2 * frames // chunk, body,
+            (
+                jnp.full((8, tile), -jnp.inf, jnp.float32), jnp.zeros((8, tile), jnp.float32),
+                jnp.zeros((HD, tile), jnp.float32),
+            ),
+        )
         if step > 0:
-            total = weighted[HD : HD + 1, :]
+            total = jnp.sum(total, axis=0, keepdims=True)
             if packed:
-                pack(outs[0].at[:, done], peak, total, weighted[0:HD, :])
+                pack(outs[0].at[:, done], peak, total, weighted)
             else:
                 outs[0][:, done] = peak
                 outs[1][:, done] = total
-                outs[2][:, done] = weighted[0:HD, :]
+                outs[2][:, done] = weighted
         if step < count:
             peak = jnp.max(top, axis=0, keepdims=True)
 
@@ -394,7 +418,7 @@
         scratch_shapes=[
             VMEM((2 * frames, 2 * HD), jnp.bfloat16),
             VMEM((2 * HD, latents), jnp.bfloat16),
-            VMEM((HD + 16, 2 * frames), jnp.bfloat16),
+            VMEM((HD, 2 * frames), jnp.bfloat16),
             VMEM((2 * frames, tile), jnp.float32),
             VMEM((2 * frames, tile), jnp.float32),
         ],
@@ -448,12 +472,7 @@
     twins = [(i, i ^ 1) for i in range(blocks)]
 
     other_rec = lax.ppermute(recording, "sensor", across)
-    slab = ch // 2
-    near_sp = lax.ppermute(
-        lax.dynamic_slice_in_dim(spatial_w, core[0] * slab, slab, axis=0),
-        "sensor", across,
-    )
-    far_sp = lax.ppermute(near_sp, "tm", twins)
+    other_w = lax.ppermute(spatial_w, "sensor", across)
     tail = lax.ppermute(
         recording[:, frames - EDGE :], "tm", [(i, i + 1) for i in range(blocks - 1)]
     )
@@ -462,22 +481,21 @@
     edge = jnp.where(lane < HALF, head, tail)
     other_edge = lax.ppermute(edge, "sensor", across)
     other_b = lax.ppermute(conv_b, "sensor", across)
+    later_w = lax.optimization_barrier((conv_w, head))[0]
     mine = [
-        lax.dynamic_slice(conv_w, (layer, 0, core[0] * half, 0), (1, 3, half, ch))[0]
+        lax.dynamic_slice(
+            later_w if layer else conv_w, (layer, 0, core[0] * half, 0), (1, 3, half, ch)
+        )[0]
         for layer in range(LAYERS)
     ]
     near = [lax.ppermute(mine[n], "sensor", across) for n in range(LAYERS)]
     far = [lax.ppermute(near[n], "tm", twins) for n in range(LAYERS)]
-    other_valid = lax.ppermute(valid_frames, "tm", twins)
-
     half_shape = jax.ShapeDtypeStruct((ch_loc, span), bf16)
+    parts = (spatial_w, other_w, recording, other_rec, edge, other_edge)
     own_h, other_h = simple(
-        first_kernel,
-        [half_shape, half_shape],
-        (side, core),
-        (spatial_w, near_sp, far_sp, recording, other_rec, edge, other_edge),
-        [VMEM((2, slab, recording.shape[0]), bf16)],
-        mib=48,
+        first_kernel, [half_shape, half_shape], (side,), parts,
+        [VMEM(part.shape, bf16) for part in parts] + [pltpu.SemaphoreType.DMA((len(parts),))],
+        specs=[pl.BlockSpec(memory_space=pltpu.HBM)] * len(parts),
     )
     taps_shape = jax.ShapeDtypeStruct((3, ch, span), bf16)
     col = [VMEM((ch_loc, EDGE), jnp.float32)]
@@ -485,15 +503,15 @@
         last = layer == LAYERS - 1
         specs = whole(4)
         specs[2] = pl.BlockSpec((None, 3, ch_loc, ch), lambda _, layer=layer: (layer, 0, 0, 0))
-        own_next, taps = simple(
-            functools.partial(own_kernel, layer, blocks, last),
-            [jax.ShapeDtypeStruct((ch_loc, frames), bf16) if last else half_shape, taps_shape],
+        made = [jax.ShapeDtypeStruct((ch_loc, frames), bf16)] * 2 if last else [half_shape]
+        *own_next, taps = simple(
+            functools.partial(own_kernel, layer, blocks, last), made + [taps_shape],
             (dilations, side, place), (own_h, other_h, conv_w, conv_b), col,
             mib=24, specs=specs,
         )
         arrays = (other_h, taps, near[layer], far[layer], other_b)
         if last:
-            features = own_next
+            features, kept_features = own_next
             shapes = [
                 jax.ShapeDtypeStruct((frames, half), bf16),
                 jax.ShapeDtypeStruct((frames, half), bf16),
@@ -502,7 +520,7 @@
             ]
             key_keep, key_send, value_keep, value_send = simple(
                 functools.partial(last_kernel, layer), shapes, (side, core),
-                (features,) + arrays + (key_w, value_w), col + [VMEM((ch, frames), bf16)],
+                (kept_features,) + arrays + (key_w, value_w), col + [VMEM((ch, frames), bf16)],
                 mib=24,
             )
         else:
@@ -510,9 +528,10 @@
                 functools.partial(other_kernel, layer, blocks), half_shape, (core, place), arrays,
                 col, mib=24,
             )
-            own_h = own_next
+            own_h = own_next[0]
     keys = (key_keep, lax.ppermute(key_send, "tm", twins))
     values = (value_keep, lax.ppermute(value_send, "tm", twins))
+    other_valid = lax.ppermute(valid_frames, "tm", twins)
 
     def flip(value, bit):
         return lax.ppermute(value, "tm", [(i, i ^ bit) for i in range(blocks)])

time: 123 us -> 120 us (0.976)
  starting transfers between devices: 26.3 us -> 29.6 us
  waiting for transfers between devices: 41.8 us -> 38.9 us
  local copies, waits for them, and re-layouts: 13.3 us -> 11.3 us
  Pallas kernels: 38.3 us -> 36.9 us
    ppermute x2 -> x1, waiting for transfers between devices: 8.08 us -> 3.98 us  [pair_device(): other_w = lax.ppermute(spatial_w, 'sensor', across)]
    ppermute x3, starting transfers between devices: 0.01 us -> 2.96 us  [pair_device(): far = [lax.ppermute(near[n], 'tm', twins) for n in range(LAYERS)]]
    pallas_call x11, Pallas kernels: 21.9 us -> 19.5 us  [simple(): pl.pallas_call(kernel, grid=(1,), out_shape=out_shape, in_specs=smem(len(...]
    ppermute x2 -> x1, starting transfers between devices: 0.29 us -> 2.3 us  [pair_device(): other_w = lax.ppermute(spatial_w, 'sensor', across)]
  transfers between devices with their start and end apart: 27 -> 26, of which waited for: 11 -> 10; matrix products, arithmetic and copies ran while one was open for 3% -> 3% of each run, Pallas kernels for 25% -> 25%
where the time goes in v4:
time: 120 us; the launch traced here: 119 us
  waiting for transfers between devices  38.9 us (32%)
  Pallas kernels  36.9 us (31%)
  starting transfers between devices  29.6 us (25%)
  local copies, waits for them, and re-layouts  11.3 us (9%)
  between operations  1.6 us (1%)
    pallas_call x11, Pallas kernels, simple(): pl.pallas_call(kernel, grid=(1,), out_shape=out_shape, in_specs=smem(len(...  19.5 us
    ppermute x3, waiting for transfers between devices, pair_device(): near = [lax.ppermute(mine[n], 'sensor', across) for n in range(LAYERS)]  17.4 us
    pallas_call x4, Pallas kernels, attend(): pl.pallas_call(functools.partial(attend_kernel, packed), out_shape=out_sh...  17.4 us
    ppermute x11, waiting for transfers between devices, flip(): return lax.ppermute(value, 'tm', [(i, i ^ bit) for i in range(blocks)])  14.5 us
    ppermute x11, starting transfers between devices, flip(): return lax.ppermute(value, 'tm', [(i, i ^ bit) for i in range(blocks)])  10 us
    unnamed x34, local copies, waits for them, and re-layouts  7.52 us
    ppermute x3, starting transfers between devices, pair_device(): near = [lax.ppermute(mine[n], 'sensor', across) for n in range(LAYERS)]  5.15 us
    ppermute x1, waiting for transfers between devices, pair_device(): other_w = lax.ppermute(spatial_w, 'sensor', across)  3.98 us
  transfers between devices with their start and end apart: 26, of which 10 were waited for; matrix products, arithmetic and copies ran while one was open for 3% of the time, Pallas kernels for 25%

profile of v4, /device:TPU:0, one launch (start us, length us, event | category | flops | bytes accessed | tf_op | source)
XLA Modules:
  0.0 119.0 jit_solution(15087432147479486814)
XLA Ops:
  4.5 3.1 %collective-permute-start.5 = (bf16[3,128,512]{2,1,0:T(8,128)(2,1)S(1)}, bf16[3,128,512]{2,1,0:T(8,128)(2,1)}, u32[]{:S(2)}, u32[]{:S(2)}) collective-permute-start(bf16[3,128,512]{2,1,0:T(8,128)(2,1)S(1)} %dynamic-slice_bitcast_fusion.2), channel_id=1, source_target_pairs={{0,16},{16,0},{1,17},{17,1},{2,18},{18,2},{3,19},{19,3},{4,20},{20... | collective-permute-start | bytes 1179656 | tf_op jit(solution)/shard_map/ppermute | solution.py:491
  11.6 3.1 %collective-permute-start.3 = (bf16[128,128]{1,0:T(8,128)(2,1)}, bf16[128,128]{1,0:T(8,128)(2,1)S(1)}, u32[]{:S(2)}, u32[]{:S(2)}) collective-permute-start(bf16[128,128]{1,0:T(8,128)(2,1)} %get-tuple-element.44), channel_id=1, source_target_pairs={{0,1},{1,2},{2,3},{3,4},{4,5},{5,6},{6,7},{7,8},{8,9},{9,10},{10,1... | collective-permute-start | bytes 98312 | tf_op jit(solution)/shard_map/ppermute | solution.py:476
  14.7 2.6 %collective-permute-done.5.near_w = bf16[3,128,512]{2,1,0:T(8,128)(2,1)} collective-permute-done((bf16[3,128,512]{2,1,0:T(8,128)(2,1)S(1)}, bf16[3,128,512]{2,1,0:T(8,128)(2,1)}, u32[]{:S(2)}, u32[]{:S(2)}) %collective-permute-start.5) | collective-permute-done | bytes 393248 | tf_op jit(solution)/shard_map/ppermute | solution.py:491
  18.1 7.4 %collective-permute-done.8.near_w = bf16[3,128,512]{2,1,0:T(8,128)(2,1)S(1)} collective-permute-done((bf16[3,128,512]{2,1,0:T(8,128)(2,1)S(1)}, bf16[3,128,512]{2,1,0:T(8,128)(2,1)S(1)}, u32[]{:S(2)}, u32[]{:S(2)}) %collective-permute-start.8) | collective-permute-done | bytes 393248 | tf_op jit(solution)/shard_map/ppermute | solution.py:491
  26.5 7.4 %collective-permute-done.11.near_w = bf16[3,128,512]{2,1,0:T(8,128)(2,1)S(1)} collective-permute-done((bf16[3,128,512]{2,1,0:T(8,128)(2,1)S(1)}, bf16[3,128,512]{2,1,0:T(8,128)(2,1)S(1)}, u32[]{:S(2)}, u32[]{:S(2)}) %collective-permute-start.11) | collective-permute-done | bytes 393248 | tf_op jit(solution)/shard_map/ppermute | solution.py:491
  38.2 2.1 %collective-permute-done.4.refs_5_ = bf16[128,128]{1,0:T(8,128)(2,1)S(1)} collective-permute-done((bf16[128,128]{1,0:T(8,128)(2,1)S(1)}, bf16[128,128]{1,0:T(8,128)(2,1)S(1)}, u32[]{:S(2)}, u32[]{:S(2)}) %collective-permute-start.4) | collective-permute-done | bytes 32800 | tf_op jit(solution)/shard_map/ppermute | solution.py:482
  40.9 2.3 %collective-permute-start = (bf16[512,128]{1,0:T(8,128)(2,1)}, bf16[512,128]{1,0:T(8,128)(2,1)S(1)}, u32[]{:S(2)}, u32[]{:S(2)}) collective-permute-start(bf16[512,128]{1,0:T(8,128)(2,1)} %refs_0_.1), channel_id=1, source_target_pairs={{0,16},{16,0},{1,17},{17,1},{2,18},{18,2},{3,19},{19,3},{4,20},{20... | collective-permute-start | bytes 393224 | tf_op jit(solution)/shard_map/ppermute | solution.py:475
  43.2 4.0 %collective-permute-done.refs_1_ = bf16[512,128]{1,0:T(8,128)(2,1)S(1)} collective-permute-done((bf16[512,128]{1,0:T(8,128)(2,1)}, bf16[512,128]{1,0:T(8,128)(2,1)S(1)}, u32[]{:S(2)}, u32[]{:S(2)}) %collective-permute-start) | collective-permute-done | bytes 131104 | tf_op jit(solution)/shard_map/ppermute | solution.py:475
  47.8 1.7 %collective-permute-start.7 = (f32[3,256]{1,0:T(4,128)}, f32[3,256]{1,0:T(4,128)S(1)}, u32[]{:S(2)}, u32[]{:S(2)}) collective-permute-start(f32[3,256]{1,0:T(4,128)} %biases.5), channel_id=1, source_target_pairs={{0,16},{16,0},{1,17},{17,1},{2,18},{18,2},{3,19},{19,3},{4,20},{20... | collective-permute-start | bytes 9224 | tf_op jit(solution)/shard_map/ppermute | solution.py:483
  53.9 2.1 %shard_map.104 = (bf16[256,1152]{1,0:T(8,128)(2,1)S(1)}, bf16[256,1152]{1,0:T(8,128)(2,1)S(1)}) custom-call(s32[1]{0:T(128)} %bitcast.side, bf16[512,128]{1,0:T(8,128)(2,1)S(1)} %copy-done.7, bf16[512,128]{1,0:T(8,128)(2,1)S(1)} %copy-done.9, bf16[128,1024]{1,0:T(8,128)(2,1)S(1)} %copy-done.2, bf16[128,1024]{1,0:T(8,128)(2,1)} %collective-permute-done.1.refs_3_, ...), custom_call_target="tpu_custom_call" | custom-call | tf_op jit(solution)/shard_map/pallas_call | solution.py:445
  57.3 2.9 %shard_map.105 = (bf16[256,1152]{1,0:T(8,128)(2,1)S(1)}, bf16[3,512,1152]{2,1,0:T(8,128)(2,1)S(1)}) custom-call(s32[3]{0:T(128)S(1)} %copy-done.14, s32[1]{0:T(128)} %bitcast.side, s32[1]{0:T(128)} %bitcast.1.place, bf16[256,1152]{1,0:T(8,128)(2,1)S(1)} %get-tuple-element.22.mine, bf16[256,1152]{1,0:T(8,128)(2,1)S(1)} %get-tuple-element.23.theirs, ...), custom_call_target="tpu_custom_call" | custom-call | tf_op jit(solution)/shard_map/pallas_call | solution.py:445
  60.2 2.6 %shard_map.106.theirs = bf16[256,1152]{1,0:T(8,128)(2,1)S(1)} custom-call(s32[1]{0:T(128)S(6)} %and.14.core, s32[1]{0:T(128)} %bitcast.1.place, bf16[256,1152]{1,0:T(8,128)(2,1)S(1)} %get-tuple-element.23.theirs, bf16[3,512,1152]{2,1,0:T(8,128)(2,1)S(1)} %get-tuple-element.25.taps, bf16[3,128,512]{2,1,0:T(8,128)(2,1)} %collective-permute-done.5.near_w, ...), custom_call_target="tpu_custom_call" | custom-call | tf_op jit(solution)/shard_map/pallas_call | solution.py:445
  62.8 2.9 %shard_map.107 = (bf16[256,1152]{1,0:T(8,128)(2,1)S(1)}, bf16[3,512,1152]{2,1,0:T(8,128)(2,1)S(1)}) custom-call(s32[3]{0:T(128)S(1)} %copy-done.15, s32[1]{0:T(128)} %bitcast.side, s32[1]{0:T(128)} %bitcast.1.place, bf16[256,1152]{1,0:T(8,128)(2,1)S(1)} %get-tuple-element.24.mine, bf16[256,1152]{1,0:T(8,128)(2,1)S(1)} %shard_map.106.theirs, ...), custom_call_target="tpu_custom_call" | custom-call | tf_op jit(solution)/shard_map/pallas_call | solution.py:445
  65.8 2.5 %shard_map.108.theirs = bf16[256,1152]{1,0:T(8,128)(2,1)S(1)} custom-call(s32[1]{0:T(128)S(6)} %and.14.core, s32[1]{0:T(128)} %bitcast.1.place, bf16[256,1152]{1,0:T(8,128)(2,1)S(1)} %shard_map.106.theirs, bf16[3,512,1152]{2,1,0:T(8,128)(2,1)S(1)} %get-tuple-element.27.taps, bf16[3,128,512]{2,1,0:T(8,128)(2,1)S(1)} %collective-permute-done.8.near_w, ...), custom_call_target="tpu_custom_call" | custom-call | tf_op jit(solution)/shard_map/pallas_call | solution.py:445
  68.3 3.3 %shard_map.109 = (bf16[256,1024]{1,0:T(8,128)(2,1)}, bf16[256,1024]{1,0:T(8,128)(2,1)S(1)}, bf16[3,512,1152]{2,1,0:T(8,128)(2,1)S(1)}) custom-call(s32[3]{0:T(128)S(1)} %copy-done.15, s32[1]{0:T(128)} %bitcast.side, s32[1]{0:T(128)} %bitcast.1.place, bf16[256,1152]{1,0:T(8,128)(2,1)S(1)} %get-tuple-element.26.mine, bf16[256,1152]{1,0:T(8,128)(2,1)S(1)} %shard_map.108.theirs, ...), custom_call_target="tpu_custom_call" | custom-call | tf_op jit(solution)/shard_map/pallas_call | solution.py:445
  71.6 1.8 %shard_map.110 = (bf16[1024,128]{1,0:T(8,128)(2,1)S(1)}, bf16[1024,128]{1,0:T(8,128)(2,1)S(1)}, bf16[128,1024]{1,0:T(8,128)(2,1)S(1)}, bf16[128,1024]{1,0:T(8,128)(2,1)S(1)}) custom-call(s32[1]{0:T(128)} %bitcast.side, s32[1]{0:T(128)S(6)} %and.14.core, bf16[256,1024]{1,0:T(8,128)(2,1)S(1)} %get-tuple-element.30.features, ...), custom_call_target="tpu_custom_call" | custom-call | tf_op jit(solution)/shard_map/pallas_call | solution.py:445
  75.5 4.5 %attend_send.3 = bf16[72,1024]{1,0:T(8,128)(2,1)S(1)} custom-call(s32[1]{0:T(128)S(6)} %and.14.core, s32[1]{0:T(128)S(6)} %sub.8.which, s32[1]{0:T(128)S(6)} %sub.9.half, s32[1]{0:T(128)S(6)} %copy.11.valid_own, s32[1]{0:T(128)} %collective-permute-done.10.valid_rec, bf16[1024,128]{1,0:T(8,128)(2,1)S(1)} %get-tuple-element.32.key_own, ...), custom_call_target="tpu_custom_call" | custom-call | tf_op jit(solution)/shard_map/attend_send/pallas_call | solution.py:413
  81.6 4.3 %attend_send.2 = bf16[72,1024]{1,0:T(8,128)(2,1)S(1)} custom-call(s32[1]{0:T(128)S(6)} %and.14.core, s32[1]{0:T(128)S(6)} %sub.8.which, s32[1]{0:T(128)S(6)} %and.16.half.lower, s32[1]{0:T(128)S(6)} %copy.11.valid_own, s32[1]{0:T(128)} %collective-permute-done.10.valid_rec, bf16[1024,128]{1,0:T(8,128)(2,1)S(1)} %get-tuple-element.32.key_own, ...), custom_call_target="tpu_custom_call" | custom-call | tf_op jit(solution)/shard_map/attend_send/pallas_call | solution.py:413
  86.5 4.3 %attend_keep.3 = (f32[1,1024]{1,0:T(1,128)S(1)}, f32[1,1024]{1,0:T(1,128)S(1)}, f32[64,1024]{1,0:T(8,128)S(1)}) custom-call(s32[1]{0:T(128)S(6)} %and.14.core, s32[1]{0:T(128)S(6)} %and.15.which.cross, s32[1]{0:T(128)S(6)} %sub.9.half, s32[1]{0:T(128)S(6)} %copy.11.valid_own, s32[1]{0:T(128)} %collective-permute-done.10.valid_rec, ...), custom_call_target="tpu_custom_call" | custom-call | tf_op jit(solution)/shard_map/attend_keep/pallas_call | solution.py:413
  92.6 4.3 %attend_keep.2 = (f32[1,1024]{1,0:T(1,128)S(1)}, f32[1,1024]{1,0:T(1,128)S(1)}, f32[64,1024]{1,0:T(8,128)S(1)}) custom-call(s32[1]{0:T(128)S(6)} %and.14.core, s32[1]{0:T(128)S(6)} %and.15.which.cross, s32[1]{0:T(128)S(6)} %and.16.half.lower, s32[1]{0:T(128)S(6)} %copy.11.valid_own, s32[1]{0:T(128)} %collective-permute-done.10.valid_rec, ...), custom_call_target="tpu_custom_call" | custom-call | tf_op jit(solution)/shard_map/attend_keep/pallas_call | solution.py:413
  97.0 2.7 %collective-permute-start.18 = (bf16[72,1024]{1,0:T(8,128)(2,1)S(1)}, bf16[72,1024]{1,0:T(8,128)(2,1)S(1)}, u32[]{:S(2)}, u32[]{:S(2)}) collective-permute-start(bf16[72,1024]{1,0:T(8,128)(2,1)S(1)} %shard_map.112.mine), channel_id=1, source_target_pairs={{0,8},{1,9},{2,10},{3,11},{4,12},{5,13},{6,14},{7,15},{8,0},{9,1},... | collective-permute-start | bytes 442376 | tf_op jit(solution)/shard_map/ppermute | solution.py:537
  99.7 6.4 %collective-permute-done.18.theirs = bf16[72,1024]{1,0:T(8,128)(2,1)S(1)} collective-permute-done((bf16[72,1024]{1,0:T(8,128)(2,1)S(1)}, bf16[72,1024]{1,0:T(8,128)(2,1)S(1)}, u32[]{:S(2)}, u32[]{:S(2)}) %collective-permute-start.18) | collective-permute-done | bytes 147488 | tf_op jit(solution)/shard_map/ppermute | solution.py:537
  107.8 3.8 %collective-permute-done.19.refs_1_ = bf16[64,1024]{1,0:T(8,128)(2,1)S(1)} collective-permute-done((bf16[64,1024]{1,0:T(8,128)(2,1)S(1)}, bf16[64,1024]{1,0:T(8,128)(2,1)S(1)}, u32[]{:S(2)}, u32[]{:S(2)}) %collective-permute-start.19) | collective-permute-done | bytes 131104 | tf_op jit(solution)/shard_map/ppermute | solution.py:537
  113.6 3.0 %collective-permute-done.21.refs_3_ = bf16[64,1024]{1,0:T(8,128)(2,1)S(1)} collective-permute-done((bf16[64,1024]{1,0:T(8,128)(2,1)S(1)}, bf16[64,1024]{1,0:T(8,128)(2,1)S(1)}, u32[]{:S(2)}, u32[]{:S(2)}) %collective-permute-start.21) | collective-permute-done | bytes 131104 | tf_op jit(solution)/shard_map/ppermute | solution.py:537
  (82 shorter events, 32.4 us)
Async XLA Ops:
  2.2 5.4 %collective-permute-start.2 = (bf16[128,128]{1,0:T(8,128)(2,1)S(1)}, bf16[128,128]{1,0:T(8,128)(2,1)S(1)}, u32[]{:S(2)}, u32[]{:S(2)}) collective-permute-start(bf16[128,128]{1,0:T(8,128)(2,1)S(1)} %get-tuple-element.45), channel_id=1, source_target_pairs={{1,0},{2,1},{3,2},{4,3},{5,4},{6,5},{7,6},{8,7},{9,8},{10,9},{11,1... | collective-permute-start | bytes 98312 | tf_op jit(solution)/shard_map/ppermute | solution.py:479
  4.5 12.7 %collective-permute-start.5 = (bf16[3,128,512]{2,1,0:T(8,128)(2,1)S(1)}, bf16[3,128,512]{2,1,0:T(8,128)(2,1)}, u32[]{:S(2)}, u32[]{:S(2)}) collective-permute-start(bf16[3,128,512]{2,1,0:T(8,128)(2,1)S(1)} %dynamic-slice_bitcast_fusion.2), channel_id=1, source_target_pairs={{0,16},{16,0},{1,17},{17,1},{2,18},{18,2},{3,19},{19,3},{4,20},{20... | collective-permute-start | bytes 1179656 | tf_op jit(solution)/shard_map/ppermute | solution.py:491
  8.8 16.7 %collective-permute-start.8 = (bf16[3,128,512]{2,1,0:T(8,128)(2,1)S(1)}, bf16[3,128,512]{2,1,0:T(8,128)(2,1)S(1)}, u32[]{:S(2)}, u32[]{:S(2)}) collective-permute-start(bf16[3,128,512]{2,1,0:T(8,128)(2,1)S(1)} %get-tuple-element.43), channel_id=1, source_target_pairs={{0,16},{16,0},{1,17},{17,1},{2,18},{18,2},{3,19},{19,3},{4,20},{20... | collective-permute-start | bytes 1179656 | tf_op jit(solution)/shard_map/ppermute | solution.py:491
  9.6 24.4 %collective-permute-start.11 = (bf16[3,128,512]{2,1,0:T(8,128)(2,1)S(1)}, bf16[3,128,512]{2,1,0:T(8,128)(2,1)S(1)}, u32[]{:S(2)}, u32[]{:S(2)}) collective-permute-start(bf16[3,128,512]{2,1,0:T(8,128)(2,1)S(1)} %get-tuple-element.42), channel_id=1, source_target_pairs={{0,16},{16,0},{1,17},{17,1},{2,18},{18,2},{3,19},{19,3},{4,20},{20... | collective-permute-start | bytes 1179656 | tf_op jit(solution)/shard_map/ppermute | solution.py:491
  10.9 38.7 %collective-permute-start.1 = (bf16[128,1024]{1,0:T(8,128)(2,1)}, bf16[128,1024]{1,0:T(8,128)(2,1)}, u32[]{:S(2)}, u32[]{:S(2)}) collective-permute-start(bf16[128,1024]{1,0:T(8,128)(2,1)} %refs_2_.1), channel_id=1, source_target_pairs={{0,16},{16,0},{1,17},{17,1},{2,18},{18,2},{3,19},{19,3},{4,20},{20... | collective-permute-start | bytes 786440 | tf_op jit(solution)/shard_map/ppermute | solution.py:474
  11.6 23.5 %collective-permute-start.3 = (bf16[128,128]{1,0:T(8,128)(2,1)}, bf16[128,128]{1,0:T(8,128)(2,1)S(1)}, u32[]{:S(2)}, u32[]{:S(2)}) collective-permute-start(bf16[128,128]{1,0:T(8,128)(2,1)} %get-tuple-element.44), channel_id=1, source_target_pairs={{0,1},{1,2},{2,3},{3,4},{4,5},{5,6},{6,7},{7,8},{8,9},{9,10},{10,1... | collective-permute-start | bytes 98312 | tf_op jit(solution)/shard_map/ppermute | solution.py:476
  17.2 43.0 %collective-permute-start.6 = (bf16[3,128,512]{2,1,0:T(8,128)(2,1)}, bf16[3,128,512]{2,1,0:T(8,128)(2,1)}, u32[]{:S(2)}, u32[]{:S(2)}) collective-permute-start(bf16[3,128,512]{2,1,0:T(8,128)(2,1)} %collective-permute-done.5.near_w), channel_id=1, source_target_pairs={{0,1},{1,0},{2,3},{3,2},{4,5},{5,4},{6,7},{7,6},{8,9},{9,8},{10,11... | collective-permute-start | bytes 1179656 | tf_op jit(solution)/shard_map/ppermute | solution.py:492
  25.5 40.2 %collective-permute-start.9 = (bf16[3,128,512]{2,1,0:T(8,128)(2,1)S(1)}, bf16[3,128,512]{2,1,0:T(8,128)(2,1)}, u32[]{:S(2)}, u32[]{:S(2)}) collective-permute-start(bf16[3,128,512]{2,1,0:T(8,128)(2,1)S(1)} %collective-permute-done.8.near_w), channel_id=1, source_target_pairs={{0,1},{1,0},{2,3},{3,2},{4,5},{5,4},{6,7},{7,6},{8,9},{9,8},{10,11... | collective-permute-start | bytes 1179656 | tf_op jit(solution)/shard_map/ppermute | solution.py:492
  34.0 37.6 %collective-permute-start.12 = (bf16[3,128,512]{2,1,0:T(8,128)(2,1)S(1)}, bf16[3,128,512]{2,1,0:T(8,128)(2,1)S(1)}, u32[]{:S(2)}, u32[]{:S(2)}) collective-permute-start(bf16[3,128,512]{2,1,0:T(8,128)(2,1)S(1)} %collective-permute-done.11.near_w), channel_id=1, source_target_pairs={{0,1},{1,0},{2,3},{3,2},{4,5},{5,4},{6,7},{7,6},{8,9},{9,8},{10,11... | collective-permute-start | bytes 1179656 | tf_op jit(solution)/shard_map/ppermute | solution.py:492
  35.8 4.5 %collective-permute-start.4 = (bf16[128,128]{1,0:T(8,128)(2,1)S(1)}, bf16[128,128]{1,0:T(8,128)(2,1)S(1)}, u32[]{:S(2)}, u32[]{:S(2)}) collective-permute-start(bf16[128,128]{1,0:T(8,128)(2,1)S(1)} %broadcast_select_fusion.refs_4_), channel_id=1, source_target_pairs={{0,16},{16,0},{1,17},{17,1},{2,18},{18,2},{3,19},{19,3},{4,20},{20... | collective-permute-start | bytes 98312 | tf_op jit(solution)/shard_map/ppermute | solution.py:482
  40.9 6.3 %collective-permute-start = (bf16[512,128]{1,0:T(8,128)(2,1)}, bf16[512,128]{1,0:T(8,128)(2,1)S(1)}, u32[]{:S(2)}, u32[]{:S(2)}) collective-permute-start(bf16[512,128]{1,0:T(8,128)(2,1)} %refs_0_.1), channel_id=1, source_target_pairs={{0,16},{16,0},{1,17},{17,1},{2,18},{18,2},{3,19},{19,3},{4,20},{20... | collective-permute-start | bytes 393224 | tf_op jit(solution)/shard_map/ppermute | solution.py:475
  47.8 12.4 %collective-permute-start.7 = (f32[3,256]{1,0:T(4,128)}, f32[3,256]{1,0:T(4,128)S(1)}, u32[]{:S(2)}, u32[]{:S(2)}) collective-permute-start(f32[3,256]{1,0:T(4,128)} %biases.5), channel_id=1, source_target_pairs={{0,16},{16,0},{1,17},{17,1},{2,18},{18,2},{3,19},{19,3},{4,20},{20... | collective-permute-start | bytes 9224 | tf_op jit(solution)/shard_map/ppermute | solution.py:483
  73.4 2.1 %collective-permute-start.13 = (bf16[1024,128]{1,0:T(8,128)(2,1)S(1)}, bf16[1024,128]{1,0:T(8,128)(2,1)S(1)}, u32[]{:S(2)}, u32[]{:S(2)}) collective-permute-start(bf16[1024,128]{1,0:T(8,128)(2,1)S(1)} %get-tuple-element.33), channel_id=1, source_target_pairs={{0,1},{1,0},{2,3},{3,2},{4,5},{5,4},{6,7},{7,6},{8,9},{9,8},{10,11... | collective-permute-start | bytes 786440 | tf_op jit(solution)/shard_map/ppermute | solution.py:532
  73.5 2.0 %collective-permute-start.14 = (bf16[128,1024]{1,0:T(8,128)(2,1)S(1)}, bf16[128,1024]{1,0:T(8,128)(2,1)S(1)}, u32[]{:S(2)}, u32[]{:S(2)}) collective-permute-start(bf16[128,1024]{1,0:T(8,128)(2,1)S(1)} %get-tuple-element.35), channel_id=1, source_target_pairs={{0,1},{1,0},{2,3},{3,2},{4,5},{5,4},{6,7},{7,6},{8,9},{9,8},{10,11... | collective-permute-start | bytes 786440 | tf_op jit(solution)/shard_map/ppermute | solution.py:533
  80.0 10.8 %collective-permute-start.16 = (bf16[72,1024]{1,0:T(8,128)(2,1)S(1)}, bf16[72,1024]{1,0:T(8,128)(2,1)S(1)}, u32[]{:S(2)}, u32[]{:S(2)}) collective-permute-start(bf16[72,1024]{1,0:T(8,128)(2,1)S(1)} %attend_send.3), channel_id=1, source_target_pairs={{0,2},{1,3},{2,0},{3,1},{4,6},{5,7},{6,4},{7,5},{8,10},{9,11},{10,... | collective-permute-start | bytes 442376 | tf_op jit(solution)/shard_map/ppermute | solution.py:537
  85.9 11.0 %collective-permute-start.15 = (bf16[72,1024]{1,0:T(8,128)(2,1)S(1)}, bf16[72,1024]{1,0:T(8,128)(2,1)S(1)}, u32[]{:S(2)}, u32[]{:S(2)}) collective-permute-start(bf16[72,1024]{1,0:T(8,128)(2,1)S(1)} %attend_send.2), channel_id=1, source_target_pairs={{0,2},{1,3},{2,0},{3,1},{4,6},{5,7},{6,4},{7,5},{8,10},{9,11},{10,... | collective-permute-start | bytes 442376 | tf_op jit(solution)/shard_map/ppermute | solution.py:537
  91.0 5.9 %collective-permute-start.17 = (bf16[72,1024]{1,0:T(8,128)(2,1)S(1)}, bf16[72,1024]{1,0:T(8,128)(2,1)S(1)}, u32[]{:S(2)}, u32[]{:S(2)}) collective-permute-start(bf16[72,1024]{1,0:T(8,128)(2,1)S(1)} %shard_map.111), channel_id=1, source_target_pairs={{0,4},{1,5},{2,6},{3,7},{4,0},{5,1},{6,2},{7,3},{8,12},{9,13},{10,... | collective-permute-start | bytes 442376 | tf_op jit(solution)/shard_map/ppermute | solution.py:537
  97.0 9.1 %collective-permute-start.18 = (bf16[72,1024]{1,0:T(8,128)(2,1)S(1)}, bf16[72,1024]{1,0:T(8,128)(2,1)S(1)}, u32[]{:S(2)}, u32[]{:S(2)}) collective-permute-start(bf16[72,1024]{1,0:T(8,128)(2,1)S(1)} %shard_map.112.mine), channel_id=1, source_target_pairs={{0,8},{1,9},{2,10},{3,11},{4,12},{5,13},{6,14},{7,15},{8,0},{9,1},... | collective-permute-start | bytes 442376 | tf_op jit(solution)/shard_map/ppermute | solution.py:537
  106.2 5.4 %collective-permute-start.19 = (bf16[64,1024]{1,0:T(8,128)(2,1)S(1)}, bf16[64,1024]{1,0:T(8,128)(2,1)S(1)}, u32[]{:S(2)}, u32[]{:S(2)}) collective-permute-start(bf16[64,1024]{1,0:T(8,128)(2,1)S(1)} %shard_map.113.refs_0_), channel_id=1, source_target_pairs={{0,4},{1,5},{2,6},{3,7},{4,0},{5,1},{6,2},{7,3},{8,12},{9,13},{10,... | collective-permute-start | bytes 393224 | tf_op jit(solution)/shard_map/ppermute | solution.py:537
  106.3 7.3 %collective-permute-start.20 = (bf16[64,1024]{1,0:T(8,128)(2,1)S(1)}, bf16[64,1024]{1,0:T(8,128)(2,1)S(1)}, u32[]{:S(2)}, u32[]{:S(2)}) collective-permute-start(bf16[64,1024]{1,0:T(8,128)(2,1)S(1)} %shard_map.113.refs_0_), channel_id=1, source_target_pairs={{0,2},{1,3},{2,0},{3,1},{4,6},{5,7},{6,4},{7,5},{8,10},{9,11},{10,... | collective-permute-start | bytes 393224 | tf_op jit(solution)/shard_map/ppermute | solution.py:537
  111.6 5.0 %collective-permute-start.21 = (bf16[64,1024]{1,0:T(8,128)(2,1)S(1)}, bf16[64,1024]{1,0:T(8,128)(2,1)S(1)}, u32[]{:S(2)}, u32[]{:S(2)}) collective-permute-start(bf16[64,1024]{1,0:T(8,128)(2,1)S(1)} %collective-permute-done.19.refs_1_), channel_id=1, source_target_pairs={{0,2},{1,3},{2,0},{3,1},{4,6},{5,7},{6,4},{7,5},{8,10},{9,11},{10,... | collective-permute-start | bytes 393224 | tf_op jit(solution)/shard_map/ppermute | solution.py:537
  113.1 3.5 %collective-permute-start.22 = (bf16[64,1024]{1,0:T(8,128)(2,1)S(1)}, bf16[64,1024]{1,0:T(8,128)(2,1)S(1)}, u32[]{:S(2)}, u32[]{:S(2)}) collective-permute-start(bf16[64,1024]{1,0:T(8,128)(2,1)S(1)} %shard_map.113.refs_0_), channel_id=1, source_target_pairs={{0,1},{1,0},{2,3},{3,2},{4,5},{5,4},{6,7},{7,6},{8,9},{9,8},{10,11... | collective-permute-start | bytes 393224 | tf_op jit(solution)/shard_map/ppermute | solution.py:537
  113.1 3.5 %collective-permute-start.23 = (bf16[64,1024]{1,0:T(8,128)(2,1)S(1)}, bf16[64,1024]{1,0:T(8,128)(2,1)S(1)}, u32[]{:S(2)}, u32[]{:S(2)}) collective-permute-start(bf16[64,1024]{1,0:T(8,128)(2,1)S(1)} %collective-permute-done.19.refs_1_), channel_id=1, source_target_pairs={{0,1},{1,0},{2,3},{3,2},{4,5},{5,4},{6,7},{7,6},{8,9},{9,8},{10,11... | collective-permute-start | bytes 393224 | tf_op jit(solution)/shard_map/ppermute | solution.py:537
  113.6 3.0 %collective-permute-start.24 = (bf16[64,1024]{1,0:T(8,128)(2,1)S(1)}, bf16[64,1024]{1,0:T(8,128)(2,1)S(1)}, u32[]{:S(2)}, u32[]{:S(2)}) collective-permute-start(bf16[64,1024]{1,0:T(8,128)(2,1)S(1)} %collective-permute-done.20.refs_2_), channel_id=1, source_target_pairs={{0,1},{1,0},{2,3},{3,2},{4,5},{5,4},{6,7},{7,6},{8,9},{9,8},{10,11... | collective-permute-start | bytes 393224 | tf_op jit(solution)/shard_map/ppermute | solution.py:537
  (19 other events, 88.6 us)

commit v5 on v4

--- a/solution.py
+++ b/solution.py
@@ -267,8 +267,8 @@
         (key_send, value_send, 1 - core[0]), (key_keep, value_keep, core[0])
     ):
         here = pl.ds(pl.multiple_of(part * half, half), half)
-        key_out[...] = dot(key_w[here, :], full[...]).T.astype(jnp.bfloat16)
-        value_out[...] = dot(value_w[here, :], full[...]).astype(jnp.bfloat16)
+        key_out[...] = dot(key_w[here, :], full[...]).astype(jnp.bfloat16)
+        value_out[...] = dot(value_w[here, :], full[...]).T.astype(jnp.bfloat16)
 
 
 def thirds(value):
@@ -327,79 +327,79 @@
     out[...] = (weighted / total).astype(out.dtype)
 
 
+def ask_kernel(core, queries, out):
+    rows = 2 * HD
+    wide = queries[pl.ds(pl.multiple_of(core[0] * rows, rows), rows), :].astype(jnp.float32)
+    out[...] = wide.T.astype(out.dtype)
+
+
 def attend_kernel(
-    packed, core, which, half, valid_own, valid_rec, key_own, key_rec, value_own, value_rec,
-    queries, *refs
+    packed, which, half, valid_own, valid_rec, key_own, key_rec, value_own, value_rec, queries,
+    *refs
 ):
-    outs = refs[:-5]
-    keyed, asked, valued, score_a, score_b = refs[-5:]
-    frames = key_own.shape[0]
-    latents = asked.shape[1]
-    tile = score_a.shape[1]
-    chunk = frames
+    outs = refs[:-6]
+    asked, keyed, values, score_a, score_b, probs_ref = refs[-6:]
+    frames = key_own.shape[1]
+    latents = asked.shape[0]
+    rows = score_a.shape[0]
+    chunk = frames // 2
     slot = which[0]
-    lane = lax.broadcasted_iota(jnp.int32, (frames, 2 * HD), 1)
-    frame = lax.broadcasted_iota(jnp.int32, (frames, 2 * HD), 0)
     spare = (1 - slot) * HD
-    value_rows = pl.ds(pl.multiple_of(slot * HD, HD), HD)
+    row = lax.broadcasted_iota(jnp.int32, (2 * HD, frames), 0)
+    frame = lax.broadcasted_iota(jnp.int32, (2 * HD, frames), 1)
     for part, (source, valid) in enumerate(((key_own, valid_own), (key_rec, valid_rec))):
-        bias = jnp.where(frame < valid[0], 0.0, MASKED)
-        keyed[pl.ds(part * frames, frames), :] = jnp.where(
-            lane == spare, bias, source[...].astype(jnp.float32)
-        ).astype(jnp.bfloat16)
-    valued[:, 0:frames] = value_own[value_rows, :]
-    valued[:, frames:] = value_rec[value_rows, :]
-    row = lax.broadcasted_iota(jnp.int32, (2 * HD, latents), 0)
-    wide = queries[
-        pl.ds(pl.multiple_of(core[0] * 2 * HD, 2 * HD), 2 * HD),
-        pl.ds(pl.multiple_of(half[0] * latents, latents), latents),
-    ].astype(jnp.float32)
-    wide = jnp.where(row // HD == slot, wide, jnp.where(row == spare, 1.0, 0.0))
-    asked[...] = wide.astype(jnp.bfloat16)
-
-    count = latents // tile
+        bias = jnp.where(frame < valid[0], 0.0, MASKED).astype(jnp.bfloat16)
+        keyed[:, part * frames : (part + 1) * frames] = jnp.where(row == spare, bias, source[...])
+    values[0:frames, :] = value_own[...]
+    values[frames:, :] = value_rec[...]
+    lane = lax.broadcasted_iota(jnp.int32, (latents, 2 * HD), 1)
+    fill = jnp.where(lane == spare, 1.0, 0.0).astype(jnp.bfloat16)
+    mine = queries[pl.ds(pl.multiple_of(half[0] * latents, latents), latents), :]
+    asked[...] = jnp.where(lane // HD == slot, mine, fill)
+    lane = lax.broadcasted_iota(jnp.int32, (rows, 2 * HD), 1)
+    count = latents // rows
     peak = None
     for step in range(count + 1):
-        cols = slice(step * tile, (step + 1) * tile)
-        done = slice((step - 1) * tile, step * tile)
         now, before = ((score_a, score_b), (score_b, score_a))[step % 2]
-
-        def body(index, carry, step=step, cols=cols, now=now, before=before, peak=peak):
-            top, total, weighted = carry
-            here = pl.ds(pl.multiple_of(index * chunk, chunk), chunk)
+        top = None
+        total = None
+        for start in range(0, 2 * frames, chunk):
+            here = slice(start, start + chunk)
             if step < count:
-                value = dot(keyed[here, :], asked[:, cols])
-                now[here, :] = value
-                top = jnp.maximum(top, jnp.max(value.reshape(chunk // 8, 8, tile), axis=0))
+                value = dot(asked[step * rows : (step + 1) * rows, :], keyed[:, here])
+                now[:, here] = value
+                for n in range(0, chunk, EDGE):
+                    part = value[:, n : n + EDGE]
+                    top = part if top is None else jnp.maximum(top, part)
             if step > 0:
-                probs = jnp.exp2((before[here, :] - peak) * SCALE)
-                total = total + jnp.sum(probs.reshape(chunk // 8, 8, tile), axis=0)
-                weighted = weighted + dot(valued[:, here], probs.astype(jnp.bfloat16))
-            return top, total, weighted
-
-        top, total, weighted = lax.fori_loop(
-            0, 2 * frames // chunk, body,
-            (
-                jnp.full((8, tile), -jnp.inf, jnp.float32), jnp.zeros((8, tile), jnp.float32),
-                jnp.zeros((HD, tile), jnp.float32),
-            ),
-        )
+                probs = jnp.exp2((before[:, here] - peak) * SCALE)
+                for n in range(0, chunk, EDGE):
+                    part = probs[:, n : n + EDGE]
+                    total = part if total is None else total + part
+                probs_ref[:, here] = probs.astype(jnp.bfloat16)
         if step > 0:
-            total = jnp.sum(total, axis=0, keepdims=True)
+            weighted = dot(probs_ref[...], values[...])
+            total = jnp.sum(total, axis=1, keepdims=True)
+            both = jnp.where(
+                lane == spare, peak, jnp.where(lane == spare + 1, total, weighted)
+            ).T
+            kept = jnp.where(slot == 0, both[0:HD, :], both[HD:, :])
+            rest = jnp.where(slot == 0, both[HD : HD + 8, :], both[0:8, :])
+            done = slice((step - 1) * rows, step * rows)
             if packed:
-                pack(outs[0].at[:, done], peak, total, weighted)
+                pack(outs[0].at[:, done], rest[0:1], rest[1:2], kept)
             else:
-                outs[0][:, done] = peak
-                outs[1][:, done] = total
-                outs[2][:, done] = weighted
+                outs[0][:, done] = rest[0:1]
+                outs[1][:, done] = rest[1:2]
+                outs[2][:, done] = kept
         if step < count:
-            peak = jnp.max(top, axis=0, keepdims=True)
+            peak = jnp.max(top, axis=1, keepdims=True)
 
 
 def attend(packed, scalars, keys, values, queries):
-    latents = queries.shape[1] // 2
-    frames = keys[0].shape[0]
-    tile = min(256, latents)
+    latents = queries.shape[0] // 2
+    frames = keys[0].shape[1]
+    rows = min(EDGE, latents)
     if packed:
         out_shape = jax.ShapeDtypeStruct((HD + 8, latents), jnp.bfloat16)
         out_specs = pl.BlockSpec(memory_space=pltpu.VMEM)
@@ -413,14 +413,15 @@
     return pl.pallas_call(
         functools.partial(attend_kernel, packed),
         out_shape=out_shape,
-        in_specs=smem(5) + whole(5),
+        in_specs=smem(4) + whole(5),
         out_specs=out_specs,
         scratch_shapes=[
+            VMEM((latents, 2 * HD), jnp.bfloat16),
+            VMEM((2 * HD, 2 * frames), jnp.bfloat16),
             VMEM((2 * frames, 2 * HD), jnp.bfloat16),
-            VMEM((2 * HD, latents), jnp.bfloat16),
-            VMEM((HD, 2 * frames), jnp.bfloat16),
-            VMEM((2 * frames, tile), jnp.float32),
-            VMEM((2 * frames, tile), jnp.float32),
+            VMEM((rows, 2 * frames), jnp.float32),
+            VMEM((rows, 2 * frames), jnp.float32),
+            VMEM((rows, 2 * frames), jnp.bfloat16),
         ],
         compiler_params=params(20),
         name="attend_send" if packed else "attend_keep",
@@ -490,6 +491,7 @@
     ]
     near = [lax.ppermute(mine[n], "sensor", across) for n in range(LAYERS)]
     far = [lax.ppermute(near[n], "tm", twins) for n in range(LAYERS)]
+    asked = simple(ask_kernel, jax.ShapeDtypeStruct((latents, half), bf16), (core,), (queries,))
     half_shape = jax.ShapeDtypeStruct((ch_loc, span), bf16)
     parts = (spatial_w, other_w, recording, other_rec, edge, other_edge)
     own_h, other_h = simple(
@@ -513,10 +515,10 @@
         if last:
             features, kept_features = own_next
             shapes = [
+                jax.ShapeDtypeStruct((half, frames), bf16),
+                jax.ShapeDtypeStruct((half, frames), bf16),
                 jax.ShapeDtypeStruct((frames, half), bf16),
                 jax.ShapeDtypeStruct((frames, half), bf16),
-                jax.ShapeDtypeStruct((half, frames), bf16),
-                jax.ShapeDtypeStruct((half, frames), bf16),
             ]
             key_keep, key_send, value_keep, value_send = simple(
                 functools.partial(last_kernel, layer), shapes, (side, core),
@@ -539,8 +541,8 @@
     lower = (place >> 2) & 1
 
     def run(packed, slot, part):
-        scalars = (core, slot, part, valid_frames, other_valid)
-        return attend(packed, scalars, keys, values, queries)
+        scalars = (slot, part, valid_frames, other_valid)
+        return attend(packed, scalars, keys, values, asked)
 
     sent = flip(run(True, 1 - cross, 1 - lower), 2)
     kept = flip(run(True, 1 - cross, lower), 2)

time: 120 us -> 116 us (0.967)
  Pallas kernels: 36.9 us -> 33.8 us
    pallas_call x4, Pallas kernels: 17.4 us -> 14.1 us  [attend(): pl.pallas_call(functools.partial(attend_kernel, packed), out_shape=out_sh...]
    pallas_call x11 -> x12, Pallas kernels: 19.5 us -> 19.7 us  [simple(): pl.pallas_call(kernel, grid=(1,), out_shape=out_shape, in_specs=smem(len(...]
  transfers between devices with their start and end apart: 26 -> 26, of which waited for: 10 -> 11; matrix products, arithmetic and copies ran while one was open for 3% -> 3% of each run, Pallas kernels for 25% -> 23%
where the time goes in v5:
time: 116 us
  waiting for transfers between devices  38 us (33%)
  Pallas kernels  33.8 us (29%)
  starting transfers between devices  30 us (26%)
  local copies, waits for them, and re-layouts  11.3 us (10%)
  between operations  1.6 us (1%)
    pallas_call x12, Pallas kernels, simple(): pl.pallas_call(kernel, grid=(1,), out_shape=out_shape, in_specs=smem(len(...  19.7 us
    ppermute x3, waiting for transfers between devices, pair_device(): near = [lax.ppermute(mine[n], 'sensor', across) for n in range(LAYERS)]  17.4 us
    pallas_call x4, Pallas kernels, attend(): pl.pallas_call(functools.partial(attend_kernel, packed), out_shape=out_sh...  14.1 us
    ppermute x11, waiting for transfers between devices, flip(): return lax.ppermute(value, 'tm', [(i, i ^ bit) for i in range(blocks)])  13.9 us
    ppermute x11, starting transfers between devices, flip(): return lax.ppermute(value, 'tm', [(i, i ^ bit) for i in range(blocks)])  10.4 us
    unnamed x34, local copies, waits for them, and re-layouts  7.52 us
    ppermute x3, starting transfers between devices, pair_device(): near = [lax.ppermute(mine[n], 'sensor', across) for n in range(LAYERS)]  5.15 us
    ppermute x1, waiting for transfers between devices, pair_device(): other_w = lax.ppermute(spatial_w, 'sensor', across)  3.98 us
  transfers between devices with their start and end apart: 26, of which 11 were waited for; matrix products, arithmetic and copies ran while one was open for 3% of the time, Pallas kernels for 23%

profile of v5, /device:TPU:0, one launch (start us, length us, event | category | flops | bytes accessed | tf_op | source)
XLA Modules:
  0.0 115.5 jit_solution(18019255986780260643)
XLA Ops:
  4.5 3.1 %collective-permute-start.5 = (bf16[3,128,512]{2,1,0:T(8,128)(2,1)S(1)}, bf16[3,128,512]{2,1,0:T(8,128)(2,1)}, u32[]{:S(2)}, u32[]{:S(2)}) collective-permute-start(bf16[3,128,512]{2,1,0:T(8,128)(2,1)S(1)} %dynamic-slice_bitcast_fusion.2), channel_id=1, source_target_pairs={{0,16},{16,0},{1,17},{17,1},{2,18},{18,2},{3,19},{19,3},{4,20},{20... | collective-permute-start | bytes 1179656 | tf_op jit(solution)/shard_map/ppermute | solution.py:492
  11.6 3.1 %collective-permute-start.3 = (bf16[128,128]{1,0:T(8,128)(2,1)}, bf16[128,128]{1,0:T(8,128)(2,1)S(1)}, u32[]{:S(2)}, u32[]{:S(2)}) collective-permute-start(bf16[128,128]{1,0:T(8,128)(2,1)} %get-tuple-element.44), channel_id=1, source_target_pairs={{0,1},{1,2},{2,3},{3,4},{4,5},{5,6},{6,7},{7,8},{8,9},{9,10},{10,1... | collective-permute-start | bytes 98312 | tf_op jit(solution)/shard_map/ppermute | solution.py:477
  14.7 2.6 %collective-permute-done.5.near_w = bf16[3,128,512]{2,1,0:T(8,128)(2,1)} collective-permute-done((bf16[3,128,512]{2,1,0:T(8,128)(2,1)S(1)}, bf16[3,128,512]{2,1,0:T(8,128)(2,1)}, u32[]{:S(2)}, u32[]{:S(2)}) %collective-permute-start.5) | collective-permute-done | bytes 393248 | tf_op jit(solution)/shard_map/ppermute | solution.py:492
  18.1 7.4 %collective-permute-done.8.near_w = bf16[3,128,512]{2,1,0:T(8,128)(2,1)S(1)} collective-permute-done((bf16[3,128,512]{2,1,0:T(8,128)(2,1)S(1)}, bf16[3,128,512]{2,1,0:T(8,128)(2,1)S(1)}, u32[]{:S(2)}, u32[]{:S(2)}) %collective-permute-start.8) | collective-permute-done | bytes 393248 | tf_op jit(solution)/shard_map/ppermute | solution.py:492
  26.5 7.4 %collective-permute-done.11.near_w = bf16[3,128,512]{2,1,0:T(8,128)(2,1)S(1)} collective-permute-done((bf16[3,128,512]{2,1,0:T(8,128)(2,1)S(1)}, bf16[3,128,512]{2,1,0:T(8,128)(2,1)S(1)}, u32[]{:S(2)}, u32[]{:S(2)}) %collective-permute-start.11) | collective-permute-done | bytes 393248 | tf_op jit(solution)/shard_map/ppermute | solution.py:492
  38.2 2.1 %collective-permute-done.4.refs_5_ = bf16[128,128]{1,0:T(8,128)(2,1)S(1)} collective-permute-done((bf16[128,128]{1,0:T(8,128)(2,1)S(1)}, bf16[128,128]{1,0:T(8,128)(2,1)S(1)}, u32[]{:S(2)}, u32[]{:S(2)}) %collective-permute-start.4) | collective-permute-done | bytes 32800 | tf_op jit(solution)/shard_map/ppermute | solution.py:483
  40.9 2.3 %collective-permute-start = (bf16[512,128]{1,0:T(8,128)(2,1)}, bf16[512,128]{1,0:T(8,128)(2,1)S(1)}, u32[]{:S(2)}, u32[]{:S(2)}) collective-permute-start(bf16[512,128]{1,0:T(8,128)(2,1)} %refs_0_.1), channel_id=1, source_target_pairs={{0,16},{16,0},{1,17},{17,1},{2,18},{18,2},{3,19},{19,3},{4,20},{20... | collective-permute-start | bytes 393224 | tf_op jit(solution)/shard_map/ppermute | solution.py:476
  43.2 4.0 %collective-permute-done.refs_1_ = bf16[512,128]{1,0:T(8,128)(2,1)S(1)} collective-permute-done((bf16[512,128]{1,0:T(8,128)(2,1)}, bf16[512,128]{1,0:T(8,128)(2,1)S(1)}, u32[]{:S(2)}, u32[]{:S(2)}) %collective-permute-start) | collective-permute-done | bytes 131104 | tf_op jit(solution)/shard_map/ppermute | solution.py:476
  47.8 1.7 %collective-permute-start.7 = (f32[3,256]{1,0:T(4,128)}, f32[3,256]{1,0:T(4,128)S(1)}, u32[]{:S(2)}, u32[]{:S(2)}) collective-permute-start(f32[3,256]{1,0:T(4,128)} %biases.5), channel_id=1, source_target_pairs={{0,16},{16,0},{1,17},{17,1},{2,18},{18,2},{3,19},{19,3},{4,20},{20... | collective-permute-start | bytes 9224 | tf_op jit(solution)/shard_map/ppermute | solution.py:484
  53.9 2.1 %shard_map.104 = (bf16[256,1152]{1,0:T(8,128)(2,1)S(1)}, bf16[256,1152]{1,0:T(8,128)(2,1)S(1)}) custom-call(s32[1]{0:T(128)} %bitcast.side, bf16[512,128]{1,0:T(8,128)(2,1)S(1)} %copy-done.7, bf16[512,128]{1,0:T(8,128)(2,1)S(1)} %copy-done.9, bf16[128,1024]{1,0:T(8,128)(2,1)S(1)} %copy-done.2, bf16[128,1024]{1,0:T(8,128)(2,1)} %collective-permute-done.1.refs_3_, ...), custom_call_target="tpu_custom_call" | custom-call | tf_op jit(solution)/shard_map/pallas_call | solution.py:446
  57.3 2.9 %shard_map.105 = (bf16[256,1152]{1,0:T(8,128)(2,1)S(1)}, bf16[3,512,1152]{2,1,0:T(8,128)(2,1)S(1)}) custom-call(s32[3]{0:T(128)S(1)} %copy-done.14, s32[1]{0:T(128)} %bitcast.side, s32[1]{0:T(128)} %bitcast.1.place, bf16[256,1152]{1,0:T(8,128)(2,1)S(1)} %get-tuple-element.22.mine, bf16[256,1152]{1,0:T(8,128)(2,1)S(1)} %get-tuple-element.23.theirs, ...), custom_call_target="tpu_custom_call" | custom-call | tf_op jit(solution)/shard_map/pallas_call | solution.py:446
  60.2 2.6 %shard_map.106.theirs = bf16[256,1152]{1,0:T(8,128)(2,1)S(1)} custom-call(s32[1]{0:T(128)S(6)} %and.14.core, s32[1]{0:T(128)} %bitcast.1.place, bf16[256,1152]{1,0:T(8,128)(2,1)S(1)} %get-tuple-element.23.theirs, bf16[3,512,1152]{2,1,0:T(8,128)(2,1)S(1)} %get-tuple-element.25.taps, bf16[3,128,512]{2,1,0:T(8,128)(2,1)} %collective-permute-done.5.near_w, ...), custom_call_target="tpu_custom_call" | custom-call | tf_op jit(solution)/shard_map/pallas_call | solution.py:446
  62.8 2.9 %shard_map.107 = (bf16[256,1152]{1,0:T(8,128)(2,1)S(1)}, bf16[3,512,1152]{2,1,0:T(8,128)(2,1)S(1)}) custom-call(s32[3]{0:T(128)S(1)} %copy-done.15, s32[1]{0:T(128)} %bitcast.side, s32[1]{0:T(128)} %bitcast.1.place, bf16[256,1152]{1,0:T(8,128)(2,1)S(1)} %get-tuple-element.24.mine, bf16[256,1152]{1,0:T(8,128)(2,1)S(1)} %shard_map.106.theirs, ...), custom_call_target="tpu_custom_call" | custom-call | tf_op jit(solution)/shard_map/pallas_call | solution.py:446
  65.8 2.5 %shard_map.108.theirs = bf16[256,1152]{1,0:T(8,128)(2,1)S(1)} custom-call(s32[1]{0:T(128)S(6)} %and.14.core, s32[1]{0:T(128)} %bitcast.1.place, bf16[256,1152]{1,0:T(8,128)(2,1)S(1)} %shard_map.106.theirs, bf16[3,512,1152]{2,1,0:T(8,128)(2,1)S(1)} %get-tuple-element.27.taps, bf16[3,128,512]{2,1,0:T(8,128)(2,1)S(1)} %collective-permute-done.8.near_w, ...), custom_call_target="tpu_custom_call" | custom-call | tf_op jit(solution)/shard_map/pallas_call | solution.py:446
  68.3 3.3 %shard_map.109 = (bf16[256,1024]{1,0:T(8,128)(2,1)}, bf16[256,1024]{1,0:T(8,128)(2,1)S(1)}, bf16[3,512,1152]{2,1,0:T(8,128)(2,1)S(1)}) custom-call(s32[3]{0:T(128)S(1)} %copy-done.15, s32[1]{0:T(128)} %bitcast.side, s32[1]{0:T(128)} %bitcast.1.place, bf16[256,1152]{1,0:T(8,128)(2,1)S(1)} %get-tuple-element.26.mine, bf16[256,1152]{1,0:T(8,128)(2,1)S(1)} %shard_map.108.theirs, ...), custom_call_target="tpu_custom_call" | custom-call | tf_op jit(solution)/shard_map/pallas_call | solution.py:446
  71.6 1.9 %shard_map.110 = (bf16[128,1024]{1,0:T(8,128)(2,1)S(1)}, bf16[128,1024]{1,0:T(8,128)(2,1)S(1)}, bf16[1024,128]{1,0:T(8,128)(2,1)S(1)}, bf16[1024,128]{1,0:T(8,128)(2,1)S(1)}) custom-call(s32[1]{0:T(128)} %bitcast.side, s32[1]{0:T(128)S(6)} %and.14.core, bf16[256,1024]{1,0:T(8,128)(2,1)S(1)} %get-tuple-element.30.features, ...), custom_call_target="tpu_custom_call" | custom-call | tf_op jit(solution)/shard_map/pallas_call | solution.py:446
  75.6 3.7 %attend_send.3 = bf16[72,1024]{1,0:T(8,128)(2,1)S(1)} custom-call(s32[1]{0:T(128)S(6)} %sub.8.which, s32[1]{0:T(128)S(6)} %sub.9.half, s32[1]{0:T(128)S(6)} %copy.11.valid_own, s32[1]{0:T(128)} %collective-permute-done.10.valid_rec, bf16[128,1024]{1,0:T(8,128)(2,1)S(1)} %get-tuple-element.32.key_own, bf16[128,1024]{1,0:T(8,128)(2,1)S(1)} %collective-permute-done.13.key_rec, ...), custom_call_target="tpu_custom_call" | custom-call | tf_op jit(solution)/shard_map/attend_send/pallas_call | solution.py:413
  80.8 3.5 %attend_send.2 = bf16[72,1024]{1,0:T(8,128)(2,1)S(1)} custom-call(s32[1]{0:T(128)S(6)} %sub.8.which, s32[1]{0:T(128)S(6)} %and.16.half.lower, s32[1]{0:T(128)S(6)} %copy.11.valid_own, s32[1]{0:T(128)} %collective-permute-done.10.valid_rec, bf16[128,1024]{1,0:T(8,128)(2,1)S(1)} %get-tuple-element.32.key_own, ...), custom_call_target="tpu_custom_call" | custom-call | tf_op jit(solution)/shard_map/attend_send/pallas_call | solution.py:413
  84.9 3.5 %attend_keep.3 = (f32[1,1024]{1,0:T(1,128)S(1)}, f32[1,1024]{1,0:T(1,128)S(1)}, f32[64,1024]{1,0:T(8,128)S(1)}) custom-call(s32[1]{0:T(128)S(6)} %and.15.which.cross, s32[1]{0:T(128)S(6)} %sub.9.half, s32[1]{0:T(128)S(6)} %copy.11.valid_own, s32[1]{0:T(128)} %collective-permute-done.10.valid_rec, bf16[128,1024]{1,0:T(8,128)(2,1)S(1)} %get-tuple-element.32.key_own, ...), custom_call_target="tpu_custom_call" | custom-call | tf_op jit(solution)/shard_map/attend_keep/pallas_call | solution.py:413
  90.1 3.5 %attend_keep.2 = (f32[1,1024]{1,0:T(1,128)S(1)}, f32[1,1024]{1,0:T(1,128)S(1)}, f32[64,1024]{1,0:T(8,128)S(1)}) custom-call(s32[1]{0:T(128)S(6)} %and.15.which.cross, s32[1]{0:T(128)S(6)} %and.16.half.lower, s32[1]{0:T(128)S(6)} %copy.11.valid_own, s32[1]{0:T(128)} %collective-permute-done.10.valid_rec, bf16[128,1024]{1,0:T(8,128)(2,1)S(1)} %get-tuple-element.32.key_own, ...), custom_call_target="tpu_custom_call" | custom-call | tf_op jit(solution)/shard_map/attend_keep/pallas_call | solution.py:413
  94.1 2.6 %collective-permute-start.18 = (bf16[72,1024]{1,0:T(8,128)(2,1)S(1)}, bf16[72,1024]{1,0:T(8,128)(2,1)S(1)}, u32[]{:S(2)}, u32[]{:S(2)}) collective-permute-start(bf16[72,1024]{1,0:T(8,128)(2,1)S(1)} %shard_map.113.mine), channel_id=1, source_target_pairs={{0,8},{1,9},{2,10},{3,11},{4,12},{5,13},{6,14},{7,15},{8,0},{9,1},... | collective-permute-start | bytes 442376 | tf_op jit(solution)/shard_map/ppermute | solution.py:539
  96.7 6.3 %collective-permute-done.18.theirs = bf16[72,1024]{1,0:T(8,128)(2,1)S(1)} collective-permute-done((bf16[72,1024]{1,0:T(8,128)(2,1)S(1)}, bf16[72,1024]{1,0:T(8,128)(2,1)S(1)}, u32[]{:S(2)}, u32[]{:S(2)}) %collective-permute-start.18) | collective-permute-done | bytes 147488 | tf_op jit(solution)/shard_map/ppermute | solution.py:539
  105.2 3.0 %collective-permute-done.19.refs_1_ = bf16[64,1024]{1,0:T(8,128)(2,1)S(1)} collective-permute-done((bf16[64,1024]{1,0:T(8,128)(2,1)S(1)}, bf16[64,1024]{1,0:T(8,128)(2,1)S(1)}, u32[]{:S(2)}, u32[]{:S(2)}) %collective-permute-start.19) | collective-permute-done | bytes 131104 | tf_op jit(solution)/shard_map/ppermute | solution.py:539
  110.2 3.0 %collective-permute-done.21.refs_3_ = bf16[64,1024]{1,0:T(8,128)(2,1)S(1)} collective-permute-done((bf16[64,1024]{1,0:T(8,128)(2,1)S(1)}, bf16[64,1024]{1,0:T(8,128)(2,1)S(1)}, u32[]{:S(2)}, u32[]{:S(2)}) %collective-permute-start.21) | collective-permute-done | bytes 131104 | tf_op jit(solution)/shard_map/ppermute | solution.py:539
  (83 shorter events, 33.2 us)
Async XLA Ops:
  2.2 5.4 %collective-permute-start.2 = (bf16[128,128]{1,0:T(8,128)(2,1)S(1)}, bf16[128,128]{1,0:T(8,128)(2,1)S(1)}, u32[]{:S(2)}, u32[]{:S(2)}) collective-permute-start(bf16[128,128]{1,0:T(8,128)(2,1)S(1)} %get-tuple-element.45), channel_id=1, source_target_pairs={{1,0},{2,1},{3,2},{4,3},{5,4},{6,5},{7,6},{8,7},{9,8},{10,9},{11,1... | collective-permute-start | bytes 98312 | tf_op jit(solution)/shard_map/ppermute | solution.py:480
  4.5 12.7 %collective-permute-start.5 = (bf16[3,128,512]{2,1,0:T(8,128)(2,1)S(1)}, bf16[3,128,512]{2,1,0:T(8,128)(2,1)}, u32[]{:S(2)}, u32[]{:S(2)}) collective-permute-start(bf16[3,128,512]{2,1,0:T(8,128)(2,1)S(1)} %dynamic-slice_bitcast_fusion.2), channel_id=1, source_target_pairs={{0,16},{16,0},{1,17},{17,1},{2,18},{18,2},{3,19},{19,3},{4,20},{20... | collective-permute-start | bytes 1179656 | tf_op jit(solution)/shard_map/ppermute | solution.py:492
  8.8 16.7 %collective-permute-start.8 = (bf16[3,128,512]{2,1,0:T(8,128)(2,1)S(1)}, bf16[3,128,512]{2,1,0:T(8,128)(2,1)S(1)}, u32[]{:S(2)}, u32[]{:S(2)}) collective-permute-start(bf16[3,128,512]{2,1,0:T(8,128)(2,1)S(1)} %get-tuple-element.43), channel_id=1, source_target_pairs={{0,16},{16,0},{1,17},{17,1},{2,18},{18,2},{3,19},{19,3},{4,20},{20... | collective-permute-start | bytes 1179656 | tf_op jit(solution)/shard_map/ppermute | solution.py:492
  9.6 24.4 %collective-permute-start.11 = (bf16[3,128,512]{2,1,0:T(8,128)(2,1)S(1)}, bf16[3,128,512]{2,1,0:T(8,128)(2,1)S(1)}, u32[]{:S(2)}, u32[]{:S(2)}) collective-permute-start(bf16[3,128,512]{2,1,0:T(8,128)(2,1)S(1)} %get-tuple-element.42), channel_id=1, source_target_pairs={{0,16},{16,0},{1,17},{17,1},{2,18},{18,2},{3,19},{19,3},{4,20},{20... | collective-permute-start | bytes 1179656 | tf_op jit(solution)/shard_map/ppermute | solution.py:492
  10.9 38.7 %collective-permute-start.1 = (bf16[128,1024]{1,0:T(8,128)(2,1)}, bf16[128,1024]{1,0:T(8,128)(2,1)}, u32[]{:S(2)}, u32[]{:S(2)}) collective-permute-start(bf16[128,1024]{1,0:T(8,128)(2,1)} %refs_2_.1), channel_id=1, source_target_pairs={{0,16},{16,0},{1,17},{17,1},{2,18},{18,2},{3,19},{19,3},{4,20},{20... | collective-permute-start | bytes 786440 | tf_op jit(solution)/shard_map/ppermute | solution.py:475
  11.6 23.5 %collective-permute-start.3 = (bf16[128,128]{1,0:T(8,128)(2,1)}, bf16[128,128]{1,0:T(8,128)(2,1)S(1)}, u32[]{:S(2)}, u32[]{:S(2)}) collective-permute-start(bf16[128,128]{1,0:T(8,128)(2,1)} %get-tuple-element.44), channel_id=1, source_target_pairs={{0,1},{1,2},{2,3},{3,4},{4,5},{5,6},{6,7},{7,8},{8,9},{9,10},{10,1... | collective-permute-start | bytes 98312 | tf_op jit(solution)/shard_map/ppermute | solution.py:477
  17.2 43.0 %collective-permute-start.6 = (bf16[3,128,512]{2,1,0:T(8,128)(2,1)}, bf16[3,128,512]{2,1,0:T(8,128)(2,1)}, u32[]{:S(2)}, u32[]{:S(2)}) collective-permute-start(bf16[3,128,512]{2,1,0:T(8,128)(2,1)} %collective-permute-done.5.near_w), channel_id=1, source_target_pairs={{0,1},{1,0},{2,3},{3,2},{4,5},{5,4},{6,7},{7,6},{8,9},{9,8},{10,11... | collective-permute-start | bytes 1179656 | tf_op jit(solution)/shard_map/ppermute | solution.py:493
  25.5 40.2 %collective-permute-start.9 = (bf16[3,128,512]{2,1,0:T(8,128)(2,1)S(1)}, bf16[3,128,512]{2,1,0:T(8,128)(2,1)}, u32[]{:S(2)}, u32[]{:S(2)}) collective-permute-start(bf16[3,128,512]{2,1,0:T(8,128)(2,1)S(1)} %collective-permute-done.8.near_w), channel_id=1, source_target_pairs={{0,1},{1,0},{2,3},{3,2},{4,5},{5,4},{6,7},{7,6},{8,9},{9,8},{10,11... | collective-permute-start | bytes 1179656 | tf_op jit(solution)/shard_map/ppermute | solution.py:493
  34.0 37.6 %collective-permute-start.12 = (bf16[3,128,512]{2,1,0:T(8,128)(2,1)S(1)}, bf16[3,128,512]{2,1,0:T(8,128)(2,1)S(1)}, u32[]{:S(2)}, u32[]{:S(2)}) collective-permute-start(bf16[3,128,512]{2,1,0:T(8,128)(2,1)S(1)} %collective-permute-done.11.near_w), channel_id=1, source_target_pairs={{0,1},{1,0},{2,3},{3,2},{4,5},{5,4},{6,7},{7,6},{8,9},{9,8},{10,11... | collective-permute-start | bytes 1179656 | tf_op jit(solution)/shard_map/ppermute | solution.py:493
  35.8 4.5 %collective-permute-start.4 = (bf16[128,128]{1,0:T(8,128)(2,1)S(1)}, bf16[128,128]{1,0:T(8,128)(2,1)S(1)}, u32[]{:S(2)}, u32[]{:S(2)}) collective-permute-start(bf16[128,128]{1,0:T(8,128)(2,1)S(1)} %broadcast_select_fusion.refs_4_), channel_id=1, source_target_pairs={{0,16},{16,0},{1,17},{17,1},{2,18},{18,2},{3,19},{19,3},{4,20},{20... | collective-permute-start | bytes 98312 | tf_op jit(solution)/shard_map/ppermute | solution.py:483
  40.9 6.3 %collective-permute-start = (bf16[512,128]{1,0:T(8,128)(2,1)}, bf16[512,128]{1,0:T(8,128)(2,1)S(1)}, u32[]{:S(2)}, u32[]{:S(2)}) collective-permute-start(bf16[512,128]{1,0:T(8,128)(2,1)} %refs_0_.1), channel_id=1, source_target_pairs={{0,16},{16,0},{1,17},{17,1},{2,18},{18,2},{3,19},{19,3},{4,20},{20... | collective-permute-start | bytes 393224 | tf_op jit(solution)/shard_map/ppermute | solution.py:476
  47.8 12.4 %collective-permute-start.7 = (f32[3,256]{1,0:T(4,128)}, f32[3,256]{1,0:T(4,128)S(1)}, u32[]{:S(2)}, u32[]{:S(2)}) collective-permute-start(f32[3,256]{1,0:T(4,128)} %biases.5), channel_id=1, source_target_pairs={{0,16},{16,0},{1,17},{17,1},{2,18},{18,2},{3,19},{19,3},{4,20},{20... | collective-permute-start | bytes 9224 | tf_op jit(solution)/shard_map/ppermute | solution.py:484
  73.5 2.1 %collective-permute-start.13 = (bf16[128,1024]{1,0:T(8,128)(2,1)S(1)}, bf16[128,1024]{1,0:T(8,128)(2,1)S(1)}, u32[]{:S(2)}, u32[]{:S(2)}) collective-permute-start(bf16[128,1024]{1,0:T(8,128)(2,1)S(1)} %get-tuple-element.33), channel_id=1, source_target_pairs={{0,1},{1,0},{2,3},{3,2},{4,5},{5,4},{6,7},{7,6},{8,9},{9,8},{10,11... | collective-permute-start | bytes 786440 | tf_op jit(solution)/shard_map/ppermute | solution.py:534
  73.6 2.0 %collective-permute-start.14 = (bf16[1024,128]{1,0:T(8,128)(2,1)S(1)}, bf16[1024,128]{1,0:T(8,128)(2,1)S(1)}, u32[]{:S(2)}, u32[]{:S(2)}) collective-permute-start(bf16[1024,128]{1,0:T(8,128)(2,1)S(1)} %get-tuple-element.35), channel_id=1, source_target_pairs={{0,1},{1,0},{2,3},{3,2},{4,5},{5,4},{6,7},{7,6},{8,9},{9,8},{10,11... | collective-permute-start | bytes 786440 | tf_op jit(solution)/shard_map/ppermute | solution.py:535
  79.3 9.1 %collective-permute-start.16 = (bf16[72,1024]{1,0:T(8,128)(2,1)S(1)}, bf16[72,1024]{1,0:T(8,128)(2,1)S(1)}, u32[]{:S(2)}, u32[]{:S(2)}) collective-permute-start(bf16[72,1024]{1,0:T(8,128)(2,1)S(1)} %attend_send.3), channel_id=1, source_target_pairs={{0,2},{1,3},{2,0},{3,1},{4,6},{5,7},{6,4},{7,5},{8,10},{9,11},{10,... | collective-permute-start | bytes 442376 | tf_op jit(solution)/shard_map/ppermute | solution.py:539
  84.3 9.3 %collective-permute-start.15 = (bf16[72,1024]{1,0:T(8,128)(2,1)S(1)}, bf16[72,1024]{1,0:T(8,128)(2,1)S(1)}, u32[]{:S(2)}, u32[]{:S(2)}) collective-permute-start(bf16[72,1024]{1,0:T(8,128)(2,1)S(1)} %attend_send.2), channel_id=1, source_target_pairs={{0,2},{1,3},{2,0},{3,1},{4,6},{5,7},{6,4},{7,5},{8,10},{9,11},{10,... | collective-permute-start | bytes 442376 | tf_op jit(solution)/shard_map/ppermute | solution.py:539
  88.5 5.4 %collective-permute-start.17 = (bf16[72,1024]{1,0:T(8,128)(2,1)S(1)}, bf16[72,1024]{1,0:T(8,128)(2,1)S(1)}, u32[]{:S(2)}, u32[]{:S(2)}) collective-permute-start(bf16[72,1024]{1,0:T(8,128)(2,1)S(1)} %shard_map.112), channel_id=1, source_target_pairs={{0,4},{1,5},{2,6},{3,7},{4,0},{5,1},{6,2},{7,3},{8,12},{9,13},{10,... | collective-permute-start | bytes 442376 | tf_op jit(solution)/shard_map/ppermute | solution.py:539
  94.1 8.9 %collective-permute-start.18 = (bf16[72,1024]{1,0:T(8,128)(2,1)S(1)}, bf16[72,1024]{1,0:T(8,128)(2,1)S(1)}, u32[]{:S(2)}, u32[]{:S(2)}) collective-permute-start(bf16[72,1024]{1,0:T(8,128)(2,1)S(1)} %shard_map.113.mine), channel_id=1, source_target_pairs={{0,8},{1,9},{2,10},{3,11},{4,12},{5,13},{6,14},{7,15},{8,0},{9,1},... | collective-permute-start | bytes 442376 | tf_op jit(solution)/shard_map/ppermute | solution.py:539
  103.1 5.0 %collective-permute-start.19 = (bf16[64,1024]{1,0:T(8,128)(2,1)S(1)}, bf16[64,1024]{1,0:T(8,128)(2,1)S(1)}, u32[]{:S(2)}, u32[]{:S(2)}) collective-permute-start(bf16[64,1024]{1,0:T(8,128)(2,1)S(1)} %shard_map.114.refs_0_), channel_id=1, source_target_pairs={{0,4},{1,5},{2,6},{3,7},{4,0},{5,1},{6,2},{7,3},{8,12},{9,13},{10,... | collective-permute-start | bytes 393224 | tf_op jit(solution)/shard_map/ppermute | solution.py:539
  103.7 6.5 %collective-permute-start.20 = (bf16[64,1024]{1,0:T(8,128)(2,1)S(1)}, bf16[64,1024]{1,0:T(8,128)(2,1)S(1)}, u32[]{:S(2)}, u32[]{:S(2)}) collective-permute-start(bf16[64,1024]{1,0:T(8,128)(2,1)S(1)} %shard_map.114.refs_0_), channel_id=1, source_target_pairs={{0,2},{1,3},{2,0},{3,1},{4,6},{5,7},{6,4},{7,5},{8,10},{9,11},{10,... | collective-permute-start | bytes 393224 | tf_op jit(solution)/shard_map/ppermute | solution.py:539
  108.1 5.0 %collective-permute-start.21 = (bf16[64,1024]{1,0:T(8,128)(2,1)S(1)}, bf16[64,1024]{1,0:T(8,128)(2,1)S(1)}, u32[]{:S(2)}, u32[]{:S(2)}) collective-permute-start(bf16[64,1024]{1,0:T(8,128)(2,1)S(1)} %collective-permute-done.19.refs_1_), channel_id=1, source_target_pairs={{0,2},{1,3},{2,0},{3,1},{4,6},{5,7},{6,4},{7,5},{8,10},{9,11},{10,... | collective-permute-start | bytes 393224 | tf_op jit(solution)/shard_map/ppermute | solution.py:539
  109.6 3.5 %collective-permute-start.22 = (bf16[64,1024]{1,0:T(8,128)(2,1)S(1)}, bf16[64,1024]{1,0:T(8,128)(2,1)S(1)}, u32[]{:S(2)}, u32[]{:S(2)}) collective-permute-start(bf16[64,1024]{1,0:T(8,128)(2,1)S(1)} %shard_map.114.refs_0_), channel_id=1, source_target_pairs={{0,1},{1,0},{2,3},{3,2},{4,5},{5,4},{6,7},{7,6},{8,9},{9,8},{10,11... | collective-permute-start | bytes 393224 | tf_op jit(solution)/shard_map/ppermute | solution.py:539
  109.6 3.5 %collective-permute-start.23 = (bf16[64,1024]{1,0:T(8,128)(2,1)S(1)}, bf16[64,1024]{1,0:T(8,128)(2,1)S(1)}, u32[]{:S(2)}, u32[]{:S(2)}) collective-permute-start(bf16[64,1024]{1,0:T(8,128)(2,1)S(1)} %collective-permute-done.19.refs_1_), channel_id=1, source_target_pairs={{0,1},{1,0},{2,3},{3,2},{4,5},{5,4},{6,7},{7,6},{8,9},{9,8},{10,11... | collective-permute-start | bytes 393224 | tf_op jit(solution)/shard_map/ppermute | solution.py:539
  110.2 3.0 %collective-permute-start.24 = (bf16[64,1024]{1,0:T(8,128)(2,1)S(1)}, bf16[64,1024]{1,0:T(8,128)(2,1)S(1)}, u32[]{:S(2)}, u32[]{:S(2)}) collective-permute-start(bf16[64,1024]{1,0:T(8,128)(2,1)S(1)} %collective-permute-done.20.refs_2_), channel_id=1, source_target_pairs={{0,1},{1,0},{2,3},{3,2},{4,5},{5,4},{6,7},{7,6},{8,9},{9,8},{10,11... | collective-permute-start | bytes 393224 | tf_op jit(solution)/shard_map/ppermute | solution.py:539
  (19 other events, 87.8 us)

commit v6 on v5

--- a/solution.py
+++ b/solution.py
@@ -137,7 +137,7 @@
 
 
 def first_kernel(side, *refs):
-    sources, (mine, theirs), held, done = refs[:6], refs[6:8], refs[8:14], refs[14]
+    sources, (mine, theirs), held, done = refs[:8], refs[8:10], refs[10:18], refs[18]
     copies = [
         pltpu.make_async_copy(source, target, done.at[n])
         for n, (source, target) in enumerate(zip(sources, held))
@@ -146,14 +146,17 @@
         copy.start()
     for copy in copies:
         copy.wait()
-    own_w, other_w, own, other, own_edge, other_edge = held
+    own_w, other_w, own, other, own_head, own_tail, other_head, other_tail = held
     frames = own.shape[1]
     rows = mine.shape[0]
+    lane = lax.broadcasted_iota(jnp.int32, own_head.shape, 1)
+    own_edge = jnp.where(lane < HALF, own_head[...], own_tail[...])
+    other_edge = jnp.where(lane < HALF, other_head[...], other_tail[...])
     for out, part in ((mine, side[0]), (theirs, 1 - side[0])):
         here = pl.ds(pl.multiple_of(part * rows, rows), rows)
         left, right = own_w[here, :], other_w[here, :]
         out[:, :frames] = (dot(left, own[...]) + dot(right, other[...])).astype(out.dtype)
-        out[:, frames:] = (dot(left, own_edge[...]) + dot(right, other_edge[...])).astype(out.dtype)
+        out[:, frames:] = (dot(left, own_edge) + dot(right, other_edge)).astype(out.dtype)
 
 
 def gelu(value):
@@ -474,15 +477,21 @@
 
     other_rec = lax.ppermute(recording, "sensor", across)
     other_w = lax.ppermute(spatial_w, "sensor", across)
-    tail = lax.ppermute(
-        recording[:, frames - EDGE :], "tm", [(i, i + 1) for i in range(blocks - 1)]
-    )
-    head = lax.ppermute(recording[:, :EDGE], "tm", [(i + 1, i) for i in range(blocks - 1)])
-    lane = jnp.arange(EDGE, dtype=jnp.int32)[None, :]
-    edge = jnp.where(lane < HALF, head, tail)
-    other_edge = lax.ppermute(edge, "sensor", across)
+    ends = blocks - 1
+    last_part, first_part = recording[:, frames - EDGE :], recording[:, :EDGE]
+    tail = lax.ppermute(last_part, "tm", [(i, i + 1) for i in range(ends)])
+    head = lax.ppermute(first_part, "tm", [(i + 1, i) for i in range(ends)])
+    planes = ("sensor", "tm")
+    other_tail = lax.ppermute(
+        last_part, planes,
+        [(s * blocks + i, (1 - s) * blocks + i + 1) for s in range(2) for i in range(ends)],
+    )
+    other_head = lax.ppermute(
+        first_part, planes,
+        [(s * blocks + i + 1, (1 - s) * blocks + i) for s in range(2) for i in range(ends)],
+    )
     other_b = lax.ppermute(conv_b, "sensor", across)
-    later_w = lax.optimization_barrier((conv_w, head))[0]
+    later_w = lax.optimization_barrier((conv_w, other_head))[0]
     mine = [
         lax.dynamic_slice(
             later_w if layer else conv_w, (layer, 0, core[0] * half, 0), (1, 3, half, ch)
@@ -493,7 +502,7 @@
     far = [lax.ppermute(near[n], "tm", twins) for n in range(LAYERS)]
     asked = simple(ask_kernel, jax.ShapeDtypeStruct((latents, half), bf16), (core,), (queries,))
     half_shape = jax.ShapeDtypeStruct((ch_loc, span), bf16)
-    parts = (spatial_w, other_w, recording, other_rec, edge, other_edge)
+    parts = (spatial_w, other_w, recording, other_rec, head, tail, other_head, other_tail)
     own_h, other_h = simple(
         first_kernel, [half_shape, half_shape], (side,), parts,
         [VMEM(part.shape, bf16) for part in parts] + [pltpu.SemaphoreType.DMA((len(parts),))],
@@ -564,7 +573,7 @@
         bit *= 2
     above = flip(done, 4)
     beside = flip(done, 2)
-    corner = flip(above, 2)
+    corner = flip(done, 6)
     pieces = [done, above, beside, corner]
     pieces += [flip(piece, 1) for piece in pieces]
     attended = simple(

time: 116 us -> 131 us (1.13)
  starting transfers between devices: 30 us -> 40.1 us
  waiting for transfers between devices: 38 us -> 41.1 us
  local copies, waits for them, and re-layouts: 11.3 us -> 13.4 us
    ppermute x11, starting transfers between devices: 10.4 us -> 15 us  [flip(): return lax.ppermute(value, 'tm', [(i, i ^ bit) for i in range(blocks)])]
    ppermute x3 -> x4, starting transfers between devices: 6.08 us -> 10.2 us  [the longest x1 4.63 us: pair_device(): tail = lax.ppermute(last_part, 'tm', [(i, i + 1) for i in range(ends)])]
    ppermute x3 -> x4, waiting for transfers between devices: 2.1 us -> 5.49 us  [the longest x1 2.01 us: pair_device(): head = lax.ppermute(first_part, 'tm', [(i + 1, i) for i in range(ends)])]
    unnamed x34 -> x42, local copies, waits for them, and re-layouts: 7.52 us -> 9.65 us
    ppermute x11, waiting for transfers between devices: 13.9 us -> 11.9 us  [flip(): return lax.ppermute(value, 'tm', [(i, i ^ bit) for i in range(blocks)])]
    ppermute x3, starting transfers between devices: 2.96 us -> 4.83 us  [pair_device(): far = [lax.ppermute(near[n], 'tm', twins) for n in range(LAYERS)]]
    ppermute x1, starting transfers between devices: 0.69 us -> 2.13 us  [pair_device(): other_rec = lax.ppermute(recording, 'sensor', across)]
    ppermute x1, starting transfers between devices: 2.3 us -> 0.86 us  [pair_device(): other_w = lax.ppermute(spatial_w, 'sensor', across)]
  transfers between devices with their start and end apart: 26 -> 27, of which waited for: 11 -> 15; matrix products, arithmetic and copies ran while one was open for 3% -> 2% of each run, Pallas kernels for 23% -> 21%
where the time goes in v6:
time: 131 us; the launch traced here: 130 us
  waiting for transfers between devices  41.1 us (31%)
  starting transfers between devices  40.1 us (31%)
  Pallas kernels  34 us (26%)
  local copies, waits for them, and re-layouts  13.4 us (10%)
  between operations  1.6 us (1%)
    pallas_call x12, Pallas kernels, simple(): pl.pallas_call(kernel, grid=(1,), out_shape=out_shape, in_specs=smem(len(...  19.8 us
    ppermute x3, waiting for transfers between devices, pair_device(): near = [lax.ppermute(mine[n], 'sensor', across) for n in range(LAYERS)]  18 us
    ppermute x11, starting transfers between devices, flip(): return lax.ppermute(value, 'tm', [(i, i ^ bit) for i in range(blocks)])  15 us
    pallas_call x4, Pallas kernels, attend(): pl.pallas_call(functools.partial(attend_kernel, packed), out_shape=out_sh...  14.3 us
    ppermute x11, waiting for transfers between devices, flip(): return lax.ppermute(value, 'tm', [(i, i ^ bit) for i in range(blocks)])  11.9 us
    unnamed x42, local copies, waits for them, and re-layouts  9.65 us
    ppermute x3, starting transfers between devices, pair_device(): near = [lax.ppermute(mine[n], 'sensor', across) for n in range(LAYERS)]  5.51 us
    ppermute x1, waiting for transfers between devices, pair_device(): other_w = lax.ppermute(spatial_w, 'sensor', across)  5.29 us
  transfers between devices with their start and end apart: 27, of which 15 were waited for; matrix products, arithmetic and copies ran while one was open for 2% of the time, Pallas kernels for 21%

profile of v6, /device:TPU:0, one launch (start us, length us, event | category | flops | bytes accessed | tf_op | source)
XLA Modules:
  0.0 130.3 jit_solution(15308086547043568619)
XLA Ops:
  4.5 3.1 %collective-permute-start.6 = (bf16[3,128,512]{2,1,0:T(8,128)(2,1)S(1)}, bf16[3,128,512]{2,1,0:T(8,128)(2,1)}, u32[]{:S(2)}, u32[]{:S(2)}) collective-permute-start(bf16[3,128,512]{2,1,0:T(8,128)(2,1)S(1)} %dynamic-slice_bitcast_fusion.2), channel_id=1, source_target_pairs={{0,16},{16,0},{1,17},{17,1},{2,18},{18,2},{3,19},{19,3},{4,20},{20... | collective-permute-start | bytes 1179656 | tf_op jit(solution)/shard_map/ppermute | solution.py:501
  9.3 2.4 %collective-permute-start.9 = (bf16[3,128,512]{2,1,0:T(8,128)(2,1)S(1)}, bf16[3,128,512]{2,1,0:T(8,128)(2,1)S(1)}, u32[]{:S(2)}, u32[]{:S(2)}) collective-permute-start(bf16[3,128,512]{2,1,0:T(8,128)(2,1)S(1)} %get-tuple-element.43), channel_id=1, source_target_pairs={{0,16},{16,0},{1,17},{17,1},{2,18},{18,2},{3,19},{19,3},{4,20},{20... | collective-permute-start | bytes 1179656 | tf_op jit(solution)/shard_map/ppermute | solution.py:501
  11.8 5.5 %collective-permute-done.6.near_w = bf16[3,128,512]{2,1,0:T(8,128)(2,1)} collective-permute-done((bf16[3,128,512]{2,1,0:T(8,128)(2,1)S(1)}, bf16[3,128,512]{2,1,0:T(8,128)(2,1)}, u32[]{:S(2)}, u32[]{:S(2)}) %collective-permute-start.6) | collective-permute-done | bytes 393248 | tf_op jit(solution)/shard_map/ppermute | solution.py:501
  19.4 6.2 %collective-permute-done.9.near_w = bf16[3,128,512]{2,1,0:T(8,128)(2,1)S(1)} collective-permute-done((bf16[3,128,512]{2,1,0:T(8,128)(2,1)S(1)}, bf16[3,128,512]{2,1,0:T(8,128)(2,1)S(1)}, u32[]{:S(2)}, u32[]{:S(2)}) %collective-permute-start.9) | collective-permute-done | bytes 393248 | tf_op jit(solution)/shard_map/ppermute | solution.py:501
  25.7 2.2 %collective-permute-start.10 = (bf16[3,128,512]{2,1,0:T(8,128)(2,1)S(1)}, bf16[3,128,512]{2,1,0:T(8,128)(2,1)}, u32[]{:S(2)}, u32[]{:S(2)}) collective-permute-start(bf16[3,128,512]{2,1,0:T(8,128)(2,1)S(1)} %collective-permute-done.9.near_w), channel_id=1, source_target_pairs={{0,1},{1,0},{2,3},{3,2},{4,5},{5,4},{6,7},{7,6},{8,9},{9,8},{10,11... | collective-permute-start | bytes 1179656 | tf_op jit(solution)/shard_map/ppermute | solution.py:502
  27.9 6.2 %collective-permute-done.12.near_w = bf16[3,128,512]{2,1,0:T(8,128)(2,1)S(1)} collective-permute-done((bf16[3,128,512]{2,1,0:T(8,128)(2,1)S(1)}, bf16[3,128,512]{2,1,0:T(8,128)(2,1)S(1)}, u32[]{:S(2)}, u32[]{:S(2)}) %collective-permute-start.12) | collective-permute-done | bytes 393248 | tf_op jit(solution)/shard_map/ppermute | solution.py:501
  40.6 4.6 %collective-permute-start.3 = (bf16[128,128]{1,0:T(8,128)(2,1)}, bf16[128,128]{1,0:T(8,128)(2,1)S(1)}, u32[]{:S(2)}, u32[]{:S(2)}) collective-permute-start(bf16[128,128]{1,0:T(8,128)(2,1)} %get-tuple-element.44), channel_id=1, source_target_pairs={{0,1},{1,2},{2,3},{3,4},{4,5},{5,6},{6,7},{7,8},{8,9},{9,10},{10,1... | collective-permute-start | bytes 98312 | tf_op jit(solution)/shard_map/ppermute | solution.py:482
  46.9 3.0 %collective-permute-start.5 = (bf16[128,128]{1,0:T(8,128)(2,1)}, bf16[128,128]{1,0:T(8,128)(2,1)S(1)}, u32[]{:S(2)}, u32[]{:S(2)}) collective-permute-start(bf16[128,128]{1,0:T(8,128)(2,1)} %get-tuple-element.44), channel_id=1, source_target_pairs={{0,17},{1,18},{2,19},{3,20},{4,21},{5,22},{6,23},{7,24},{8,25},{9,... | collective-permute-start | bytes 98312 | tf_op jit(solution)/shard_map/ppermute | solution.py:485
  53.3 5.3 %collective-permute-done.refs_1_ = bf16[512,128]{1,0:T(8,128)(2,1)S(1)} collective-permute-done((bf16[512,128]{1,0:T(8,128)(2,1)}, bf16[512,128]{1,0:T(8,128)(2,1)S(1)}, u32[]{:S(2)}, u32[]{:S(2)}) %collective-permute-start) | collective-permute-done | bytes 131104 | tf_op jit(solution)/shard_map/ppermute | solution.py:479
  69.4 2.9 %shard_map.105 = (bf16[256,1152]{1,0:T(8,128)(2,1)S(1)}, bf16[3,512,1152]{2,1,0:T(8,128)(2,1)S(1)}) custom-call(s32[3]{0:T(128)S(1)} %copy-done.18, s32[1]{0:T(128)} %bitcast.side, s32[1]{0:T(128)} %bitcast.1.place, bf16[256,1152]{1,0:T(8,128)(2,1)S(1)} %get-tuple-element.22.mine, bf16[256,1152]{1,0:T(8,128)(2,1)S(1)} %get-tuple-element.23.theirs, ...), custom_call_target="tpu_custom_call" | custom-call | tf_op jit(solution)/shard_map/pallas_call | solution.py:449
  72.3 2.6 %shard_map.106.theirs = bf16[256,1152]{1,0:T(8,128)(2,1)S(1)} custom-call(s32[1]{0:T(128)S(6)} %and.14.core, s32[1]{0:T(128)} %bitcast.1.place, bf16[256,1152]{1,0:T(8,128)(2,1)S(1)} %get-tuple-element.23.theirs, bf16[3,512,1152]{2,1,0:T(8,128)(2,1)S(1)} %get-tuple-element.25.taps, bf16[3,128,512]{2,1,0:T(8,128)(2,1)} %collective-permute-done.6.near_w, ...), custom_call_target="tpu_custom_call" | custom-call | tf_op jit(solution)/shard_map/pallas_call | solution.py:449
  74.9 2.9 %shard_map.107 = (bf16[256,1152]{1,0:T(8,128)(2,1)S(1)}, bf16[3,512,1152]{2,1,0:T(8,128)(2,1)S(1)}) custom-call(s32[3]{0:T(128)S(1)} %copy-done.19, s32[1]{0:T(128)} %bitcast.side, s32[1]{0:T(128)} %bitcast.1.place, bf16[256,1152]{1,0:T(8,128)(2,1)S(1)} %get-tuple-element.24.mine, bf16[256,1152]{1,0:T(8,128)(2,1)S(1)} %shard_map.106.theirs, ...), custom_call_target="tpu_custom_call" | custom-call | tf_op jit(solution)/shard_map/pallas_call | solution.py:449
  77.9 2.5 %shard_map.108.theirs = bf16[256,1152]{1,0:T(8,128)(2,1)S(1)} custom-call(s32[1]{0:T(128)S(6)} %and.14.core, s32[1]{0:T(128)} %bitcast.1.place, bf16[256,1152]{1,0:T(8,128)(2,1)S(1)} %shard_map.106.theirs, bf16[3,512,1152]{2,1,0:T(8,128)(2,1)S(1)} %get-tuple-element.27.taps, bf16[3,128,512]{2,1,0:T(8,128)(2,1)S(1)} %collective-permute-done.9.near_w, ...), custom_call_target="tpu_custom_call" | custom-call | tf_op jit(solution)/shard_map/pallas_call | solution.py:449
  80.4 3.3 %shard_map.109 = (bf16[256,1024]{1,0:T(8,128)(2,1)}, bf16[256,1024]{1,0:T(8,128)(2,1)S(1)}, bf16[3,512,1152]{2,1,0:T(8,128)(2,1)S(1)}) custom-call(s32[3]{0:T(128)S(1)} %copy-done.19, s32[1]{0:T(128)} %bitcast.side, s32[1]{0:T(128)} %bitcast.1.place, bf16[256,1152]{1,0:T(8,128)(2,1)S(1)} %get-tuple-element.26.mine, bf16[256,1152]{1,0:T(8,128)(2,1)S(1)} %shard_map.108.theirs, ...), custom_call_target="tpu_custom_call" | custom-call | tf_op jit(solution)/shard_map/pallas_call | solution.py:449
  87.6 3.7 %attend_send.3 = bf16[72,1024]{1,0:T(8,128)(2,1)S(1)} custom-call(s32[1]{0:T(128)S(6)} %sub.8.which, s32[1]{0:T(128)S(6)} %sub.9.half, s32[1]{0:T(128)S(6)} %copy.11.valid_own, s32[1]{0:T(128)} %collective-permute-done.11.valid_rec, bf16[128,1024]{1,0:T(8,128)(2,1)S(1)} %get-tuple-element.32.key_own, bf16[128,1024]{1,0:T(8,128)(2,1)S(1)} %collective-permute-done.14.key_rec, ...), custom_call_target="tpu_custom_call" | custom-call | tf_op jit(solution)/shard_map/attend_send/pallas_call | solution.py:416
  91.3 4.2 %collective-permute-start.17 = (bf16[72,1024]{1,0:T(8,128)(2,1)S(1)}, bf16[72,1024]{1,0:T(8,128)(2,1)S(1)}, u32[]{:S(2)}, u32[]{:S(2)}) collective-permute-start(bf16[72,1024]{1,0:T(8,128)(2,1)S(1)} %attend_send.3), channel_id=1, source_target_pairs={{0,2},{1,3},{2,0},{3,1},{4,6},{5,7},{6,4},{7,5},{8,10},{9,11},{10,... | collective-permute-start | bytes 442376 | tf_op jit(solution)/shard_map/ppermute | solution.py:548
  95.6 3.5 %attend_send.2 = bf16[72,1024]{1,0:T(8,128)(2,1)S(1)} custom-call(s32[1]{0:T(128)S(6)} %sub.8.which, s32[1]{0:T(128)S(6)} %and.16.half.lower, s32[1]{0:T(128)S(6)} %copy.11.valid_own, s32[1]{0:T(128)} %collective-permute-done.11.valid_rec, bf16[128,1024]{1,0:T(8,128)(2,1)S(1)} %get-tuple-element.32.key_own, ...), custom_call_target="tpu_custom_call" | custom-call | tf_op jit(solution)/shard_map/attend_send/pallas_call | solution.py:416
  99.2 3.5 %attend_keep.3 = (f32[1,1024]{1,0:T(1,128)S(1)}, f32[1,1024]{1,0:T(1,128)S(1)}, f32[64,1024]{1,0:T(8,128)S(1)}) custom-call(s32[1]{0:T(128)S(6)} %and.15.which.cross, s32[1]{0:T(128)S(6)} %sub.9.half, s32[1]{0:T(128)S(6)} %copy.11.valid_own, s32[1]{0:T(128)} %collective-permute-done.11.valid_rec, bf16[128,1024]{1,0:T(8,128)(2,1)S(1)} %get-tuple-element.32.key_own, ...), custom_call_target="tpu_custom_call" | custom-call | tf_op jit(solution)/shard_map/attend_keep/pallas_call | solution.py:416
  102.8 3.8 %collective-permute-start.18 = (bf16[72,1024]{1,0:T(8,128)(2,1)S(1)}, bf16[72,1024]{1,0:T(8,128)(2,1)S(1)}, u32[]{:S(2)}, u32[]{:S(2)}) collective-permute-start(bf16[72,1024]{1,0:T(8,128)(2,1)S(1)} %shard_map.112), channel_id=1, source_target_pairs={{0,4},{1,5},{2,6},{3,7},{4,0},{5,1},{6,2},{7,3},{8,12},{9,13},{10,... | collective-permute-start | bytes 442376 | tf_op jit(solution)/shard_map/ppermute | solution.py:548
  106.6 3.5 %attend_keep.2 = (f32[1,1024]{1,0:T(1,128)S(1)}, f32[1,1024]{1,0:T(1,128)S(1)}, f32[64,1024]{1,0:T(8,128)S(1)}) custom-call(s32[1]{0:T(128)S(6)} %and.15.which.cross, s32[1]{0:T(128)S(6)} %and.16.half.lower, s32[1]{0:T(128)S(6)} %copy.11.valid_own, s32[1]{0:T(128)} %collective-permute-done.11.valid_rec, bf16[128,1024]{1,0:T(8,128)(2,1)S(1)} %get-tuple-element.32.key_own, ...), custom_call_target="tpu_custom_call" | custom-call | tf_op jit(solution)/shard_map/attend_keep/pallas_call | solution.py:416
  110.4 2.8 %collective-permute-start.19 = (bf16[72,1024]{1,0:T(8,128)(2,1)S(1)}, bf16[72,1024]{1,0:T(8,128)(2,1)S(1)}, u32[]{:S(2)}, u32[]{:S(2)}) collective-permute-start(bf16[72,1024]{1,0:T(8,128)(2,1)S(1)} %shard_map.113.mine), channel_id=1, source_target_pairs={{0,8},{1,9},{2,10},{3,11},{4,12},{5,13},{6,14},{7,15},{8,0},{9,1},... | collective-permute-start | bytes 442376 | tf_op jit(solution)/shard_map/ppermute | solution.py:548
  113.2 6.3 %collective-permute-done.19.theirs = bf16[72,1024]{1,0:T(8,128)(2,1)S(1)} collective-permute-done((bf16[72,1024]{1,0:T(8,128)(2,1)S(1)}, bf16[72,1024]{1,0:T(8,128)(2,1)S(1)}, u32[]{:S(2)}, u32[]{:S(2)}) %collective-permute-start.19) | collective-permute-done | bytes 147488 | tf_op jit(solution)/shard_map/ppermute | solution.py:548
  120.6 2.5 %collective-permute-start.22 = (bf16[64,1024]{1,0:T(8,128)(2,1)S(1)}, bf16[64,1024]{1,0:T(8,128)(2,1)S(1)}, u32[]{:S(2)}, u32[]{:S(2)}) collective-permute-start(bf16[64,1024]{1,0:T(8,128)(2,1)S(1)} %shard_map.114.refs_0_), channel_id=1, source_target_pairs={{0,6},{1,7},{2,4},{3,5},{4,2},{5,3},{6,0},{7,1},{8,14},{9,15},{10,... | collective-permute-start | bytes 393224 | tf_op jit(solution)/shard_map/ppermute | solution.py:548
  123.2 2.8 %collective-permute-done.20.refs_1_ = bf16[64,1024]{1,0:T(8,128)(2,1)S(1)} collective-permute-done((bf16[64,1024]{1,0:T(8,128)(2,1)S(1)}, bf16[64,1024]{1,0:T(8,128)(2,1)S(1)}, u32[]{:S(2)}, u32[]{:S(2)}) %collective-permute-start.20) | collective-permute-done | bytes 131104 | tf_op jit(solution)/shard_map/ppermute | solution.py:548
  (91 shorter events, 39.3 us)
Async XLA Ops:
  2.2 5.9 %collective-permute-start.4 = (bf16[128,128]{1,0:T(8,128)(2,1)S(1)}, bf16[128,128]{1,0:T(8,128)(2,1)S(1)}, u32[]{:S(2)}, u32[]{:S(2)}) collective-permute-start(bf16[128,128]{1,0:T(8,128)(2,1)S(1)} %get-tuple-element.45), channel_id=1, source_target_pairs={{1,16},{2,17},{3,18},{4,19},{5,20},{6,21},{7,22},{8,23},{9,24},{10... | collective-permute-start | bytes 98312 | tf_op jit(solution)/shard_map/ppermute | solution.py:489
  4.5 12.7 %collective-permute-start.6 = (bf16[3,128,512]{2,1,0:T(8,128)(2,1)S(1)}, bf16[3,128,512]{2,1,0:T(8,128)(2,1)}, u32[]{:S(2)}, u32[]{:S(2)}) collective-permute-start(bf16[3,128,512]{2,1,0:T(8,128)(2,1)S(1)} %dynamic-slice_bitcast_fusion.2), channel_id=1, source_target_pairs={{0,16},{16,0},{1,17},{17,1},{2,18},{18,2},{3,19},{19,3},{4,20},{20... | collective-permute-start | bytes 1179656 | tf_op jit(solution)/shard_map/ppermute | solution.py:501
  9.3 16.4 %collective-permute-start.9 = (bf16[3,128,512]{2,1,0:T(8,128)(2,1)S(1)}, bf16[3,128,512]{2,1,0:T(8,128)(2,1)S(1)}, u32[]{:S(2)}, u32[]{:S(2)}) collective-permute-start(bf16[3,128,512]{2,1,0:T(8,128)(2,1)S(1)} %get-tuple-element.43), channel_id=1, source_target_pairs={{0,16},{16,0},{1,17},{17,1},{2,18},{18,2},{3,19},{19,3},{4,20},{20... | collective-permute-start | bytes 1179656 | tf_op jit(solution)/shard_map/ppermute | solution.py:501
  11.7 22.4 %collective-permute-start.12 = (bf16[3,128,512]{2,1,0:T(8,128)(2,1)S(1)}, bf16[3,128,512]{2,1,0:T(8,128)(2,1)S(1)}, u32[]{:S(2)}, u32[]{:S(2)}) collective-permute-start(bf16[3,128,512]{2,1,0:T(8,128)(2,1)S(1)} %get-tuple-element.42), channel_id=1, source_target_pairs={{0,16},{16,0},{1,17},{17,1},{2,18},{18,2},{3,19},{19,3},{4,20},{20... | collective-permute-start | bytes 1179656 | tf_op jit(solution)/shard_map/ppermute | solution.py:501
  17.3 55.1 %collective-permute-start.7 = (bf16[3,128,512]{2,1,0:T(8,128)(2,1)}, bf16[3,128,512]{2,1,0:T(8,128)(2,1)}, u32[]{:S(2)}, u32[]{:S(2)}) collective-permute-start(bf16[3,128,512]{2,1,0:T(8,128)(2,1)} %collective-permute-done.6.near_w), channel_id=1, source_target_pairs={{0,1},{1,0},{2,3},{3,2},{4,5},{5,4},{6,7},{7,6},{8,9},{9,8},{10,11... | collective-permute-start | bytes 1179656 | tf_op jit(solution)/shard_map/ppermute | solution.py:502
  25.7 52.1 %collective-permute-start.10 = (bf16[3,128,512]{2,1,0:T(8,128)(2,1)S(1)}, bf16[3,128,512]{2,1,0:T(8,128)(2,1)}, u32[]{:S(2)}, u32[]{:S(2)}) collective-permute-start(bf16[3,128,512]{2,1,0:T(8,128)(2,1)S(1)} %collective-permute-done.9.near_w), channel_id=1, source_target_pairs={{0,1},{1,0},{2,3},{3,2},{4,5},{5,4},{6,7},{7,6},{8,9},{9,8},{10,11... | collective-permute-start | bytes 1179656 | tf_op jit(solution)/shard_map/ppermute | solution.py:502
  34.1 49.5 %collective-permute-start.13 = (bf16[3,128,512]{2,1,0:T(8,128)(2,1)S(1)}, bf16[3,128,512]{2,1,0:T(8,128)(2,1)S(1)}, u32[]{:S(2)}, u32[]{:S(2)}) collective-permute-start(bf16[3,128,512]{2,1,0:T(8,128)(2,1)S(1)} %collective-permute-done.12.near_w), channel_id=1, source_target_pairs={{0,1},{1,0},{2,3},{3,2},{4,5},{5,4},{6,7},{7,6},{8,9},{9,8},{10,11... | collective-permute-start | bytes 1179656 | tf_op jit(solution)/shard_map/ppermute | solution.py:502
  34.6 25.5 %collective-permute-start.1 = (bf16[128,1024]{1,0:T(8,128)(2,1)}, bf16[128,1024]{1,0:T(8,128)(2,1)}, u32[]{:S(2)}, u32[]{:S(2)}) collective-permute-start(bf16[128,1024]{1,0:T(8,128)(2,1)} %refs_2_.1), channel_id=1, source_target_pairs={{0,16},{16,0},{1,17},{17,1},{2,18},{18,2},{3,19},{19,3},{4,20},{20... | collective-permute-start | bytes 786440 | tf_op jit(solution)/shard_map/ppermute | solution.py:478
  36.7 3.3 %collective-permute-start.2 = (bf16[128,128]{1,0:T(8,128)(2,1)}, bf16[128,128]{1,0:T(8,128)(2,1)S(1)}, u32[]{:S(2)}, u32[]{:S(2)}) collective-permute-start(bf16[128,128]{1,0:T(8,128)(2,1)} %copy-done.20), channel_id=1, source_target_pairs={{1,0},{2,1},{3,2},{4,3},{5,4},{6,5},{7,6},{8,7},{9,8},{10,9},{11,1... | collective-permute-start | bytes 98312 | tf_op jit(solution)/shard_map/ppermute | solution.py:483
  40.6 5.7 %collective-permute-start.3 = (bf16[128,128]{1,0:T(8,128)(2,1)}, bf16[128,128]{1,0:T(8,128)(2,1)S(1)}, u32[]{:S(2)}, u32[]{:S(2)}) collective-permute-start(bf16[128,128]{1,0:T(8,128)(2,1)} %get-tuple-element.44), channel_id=1, source_target_pairs={{0,1},{1,2},{2,3},{3,4},{4,5},{5,6},{6,7},{7,8},{8,9},{9,10},{10,1... | collective-permute-start | bytes 98312 | tf_op jit(solution)/shard_map/ppermute | solution.py:482
  46.9 4.9 %collective-permute-start.5 = (bf16[128,128]{1,0:T(8,128)(2,1)}, bf16[128,128]{1,0:T(8,128)(2,1)S(1)}, u32[]{:S(2)}, u32[]{:S(2)}) collective-permute-start(bf16[128,128]{1,0:T(8,128)(2,1)} %get-tuple-element.44), channel_id=1, source_target_pairs={{0,17},{1,18},{2,19},{3,20},{4,21},{5,22},{6,23},{7,24},{8,25},{9,... | collective-permute-start | bytes 98312 | tf_op jit(solution)/shard_map/ppermute | solution.py:485
  52.5 6.1 %collective-permute-start = (bf16[512,128]{1,0:T(8,128)(2,1)}, bf16[512,128]{1,0:T(8,128)(2,1)S(1)}, u32[]{:S(2)}, u32[]{:S(2)}) collective-permute-start(bf16[512,128]{1,0:T(8,128)(2,1)} %refs_0_.1), channel_id=1, source_target_pairs={{0,16},{16,0},{1,17},{17,1},{2,18},{18,2},{3,19},{19,3},{4,20},{20... | collective-permute-start | bytes 393224 | tf_op jit(solution)/shard_map/ppermute | solution.py:479
  59.3 13.1 %collective-permute-start.8 = (f32[3,256]{1,0:T(4,128)}, f32[3,256]{1,0:T(4,128)S(1)}, u32[]{:S(2)}, u32[]{:S(2)}) collective-permute-start(f32[3,256]{1,0:T(4,128)} %biases.5), channel_id=1, source_target_pairs={{0,16},{16,0},{1,17},{17,1},{2,18},{18,2},{3,19},{19,3},{4,20},{20... | collective-permute-start | bytes 9224 | tf_op jit(solution)/shard_map/ppermute | solution.py:493
  85.6 2.0 %collective-permute-start.14 = (bf16[128,1024]{1,0:T(8,128)(2,1)S(1)}, bf16[128,1024]{1,0:T(8,128)(2,1)S(1)}, u32[]{:S(2)}, u32[]{:S(2)}) collective-permute-start(bf16[128,1024]{1,0:T(8,128)(2,1)S(1)} %get-tuple-element.33), channel_id=1, source_target_pairs={{0,1},{1,0},{2,3},{3,2},{4,5},{5,4},{6,7},{7,6},{8,9},{9,8},{10,11... | collective-permute-start | bytes 786440 | tf_op jit(solution)/shard_map/ppermute | solution.py:543
  85.7 1.9 %collective-permute-start.15 = (bf16[1024,128]{1,0:T(8,128)(2,1)S(1)}, bf16[1024,128]{1,0:T(8,128)(2,1)S(1)}, u32[]{:S(2)}, u32[]{:S(2)}) collective-permute-start(bf16[1024,128]{1,0:T(8,128)(2,1)S(1)} %get-tuple-element.35), channel_id=1, source_target_pairs={{0,1},{1,0},{2,3},{3,2},{4,5},{5,4},{6,7},{7,6},{8,9},{9,8},{10,11... | collective-permute-start | bytes 786440 | tf_op jit(solution)/shard_map/ppermute | solution.py:544
  91.3 11.4 %collective-permute-start.17 = (bf16[72,1024]{1,0:T(8,128)(2,1)S(1)}, bf16[72,1024]{1,0:T(8,128)(2,1)S(1)}, u32[]{:S(2)}, u32[]{:S(2)}) collective-permute-start(bf16[72,1024]{1,0:T(8,128)(2,1)S(1)} %attend_send.3), channel_id=1, source_target_pairs={{0,2},{1,3},{2,0},{3,1},{4,6},{5,7},{6,4},{7,5},{8,10},{9,11},{10,... | collective-permute-start | bytes 442376 | tf_op jit(solution)/shard_map/ppermute | solution.py:548
  99.1 11.1 %collective-permute-start.16 = (bf16[72,1024]{1,0:T(8,128)(2,1)S(1)}, bf16[72,1024]{1,0:T(8,128)(2,1)S(1)}, u32[]{:S(2)}, u32[]{:S(2)}) collective-permute-start(bf16[72,1024]{1,0:T(8,128)(2,1)S(1)} %attend_send.2), channel_id=1, source_target_pairs={{0,2},{1,3},{2,0},{3,1},{4,6},{5,7},{6,4},{7,5},{8,10},{9,11},{10,... | collective-permute-start | bytes 442376 | tf_op jit(solution)/shard_map/ppermute | solution.py:548
  102.8 7.4 %collective-permute-start.18 = (bf16[72,1024]{1,0:T(8,128)(2,1)S(1)}, bf16[72,1024]{1,0:T(8,128)(2,1)S(1)}, u32[]{:S(2)}, u32[]{:S(2)}) collective-permute-start(bf16[72,1024]{1,0:T(8,128)(2,1)S(1)} %shard_map.112), channel_id=1, source_target_pairs={{0,4},{1,5},{2,6},{3,7},{4,0},{5,1},{6,2},{7,3},{8,12},{9,13},{10,... | collective-permute-start | bytes 442376 | tf_op jit(solution)/shard_map/ppermute | solution.py:548
  110.4 9.1 %collective-permute-start.19 = (bf16[72,1024]{1,0:T(8,128)(2,1)S(1)}, bf16[72,1024]{1,0:T(8,128)(2,1)S(1)}, u32[]{:S(2)}, u32[]{:S(2)}) collective-permute-start(bf16[72,1024]{1,0:T(8,128)(2,1)S(1)} %shard_map.113.mine), channel_id=1, source_target_pairs={{0,8},{1,9},{2,10},{3,11},{4,12},{5,13},{6,14},{7,15},{8,0},{9,1},... | collective-permute-start | bytes 442376 | tf_op jit(solution)/shard_map/ppermute | solution.py:548
  119.6 6.3 %collective-permute-start.20 = (bf16[64,1024]{1,0:T(8,128)(2,1)S(1)}, bf16[64,1024]{1,0:T(8,128)(2,1)S(1)}, u32[]{:S(2)}, u32[]{:S(2)}) collective-permute-start(bf16[64,1024]{1,0:T(8,128)(2,1)S(1)} %shard_map.114.refs_0_), channel_id=1, source_target_pairs={{0,4},{1,5},{2,6},{3,7},{4,0},{5,1},{6,2},{7,3},{8,12},{9,13},{10,... | collective-permute-start | bytes 393224 | tf_op jit(solution)/shard_map/ppermute | solution.py:548
  120.1 7.6 %collective-permute-start.21 = (bf16[64,1024]{1,0:T(8,128)(2,1)S(1)}, bf16[64,1024]{1,0:T(8,128)(2,1)S(1)}, u32[]{:S(2)}, u32[]{:S(2)}) collective-permute-start(bf16[64,1024]{1,0:T(8,128)(2,1)S(1)} %shard_map.114.refs_0_), channel_id=1, source_target_pairs={{0,2},{1,3},{2,0},{3,1},{4,6},{5,7},{6,4},{7,5},{8,10},{9,11},{10,... | collective-permute-start | bytes 393224 | tf_op jit(solution)/shard_map/ppermute | solution.py:548
  120.6 7.1 %collective-permute-start.22 = (bf16[64,1024]{1,0:T(8,128)(2,1)S(1)}, bf16[64,1024]{1,0:T(8,128)(2,1)S(1)}, u32[]{:S(2)}, u32[]{:S(2)}) collective-permute-start(bf16[64,1024]{1,0:T(8,128)(2,1)S(1)} %shard_map.114.refs_0_), channel_id=1, source_target_pairs={{0,6},{1,7},{2,4},{3,5},{4,2},{5,3},{6,0},{7,1},{8,14},{9,15},{10,... | collective-permute-start | bytes 393224 | tf_op jit(solution)/shard_map/ppermute | solution.py:548
  123.2 5.1 %collective-permute-start.23 = (bf16[64,1024]{1,0:T(8,128)(2,1)S(1)}, bf16[64,1024]{1,0:T(8,128)(2,1)S(1)}, u32[]{:S(2)}, u32[]{:S(2)}) collective-permute-start(bf16[64,1024]{1,0:T(8,128)(2,1)S(1)} %shard_map.114.refs_0_), channel_id=1, source_target_pairs={{0,1},{1,0},{2,3},{3,2},{4,5},{5,4},{6,7},{7,6},{8,9},{9,8},{10,11... | collective-permute-start | bytes 393224 | tf_op jit(solution)/shard_map/ppermute | solution.py:548
  125.9 2.3 %collective-permute-start.24 = (bf16[64,1024]{1,0:T(8,128)(2,1)S(1)}, bf16[64,1024]{1,0:T(8,128)(2,1)S(1)}, u32[]{:S(2)}, u32[]{:S(2)}) collective-permute-start(bf16[64,1024]{1,0:T(8,128)(2,1)S(1)} %collective-permute-done.20.refs_1_), channel_id=1, source_target_pairs={{0,1},{1,0},{2,3},{3,2},{4,5},{5,4},{6,7},{7,6},{8,9},{9,8},{10,11... | collective-permute-start | bytes 393224 | tf_op jit(solution)/shard_map/ppermute | solution.py:548
  (24 other events, 114.6 us)

commit v7 on v5

--- a/solution.py
+++ b/solution.py
@@ -136,24 +136,64 @@
     return jnp.dot(left, right, preferred_element_type=jnp.float32)
 
 
-def first_kernel(side, *refs):
-    sources, (mine, theirs), held, done = refs[:6], refs[6:8], refs[8:14], refs[14]
+def move_all(pairs, done):
     copies = [
         pltpu.make_async_copy(source, target, done.at[n])
-        for n, (source, target) in enumerate(zip(sources, held))
+        for n, (source, target) in enumerate(pairs)
     ]
     for copy in copies:
         copy.start()
     for copy in copies:
         copy.wait()
-    own_w, other_w, own, other, own_edge, other_edge = held
+
+
+def rows_of(part, count):
+    return pl.ds(pl.multiple_of(part * count, count), count)
+
+
+def early_kernel(core, recording, spatial, weights, outer, inner, slab, near, done):
+    width = outer.shape[1]
+    far = recording.shape[1] - width
+    here = pl.ds(pl.multiple_of(core[0] * far, width), width)
+    there = pl.ds(pl.multiple_of((1 - core[0]) * far, width), width)
+    move_all(
+        (
+            (recording.at[:, here], outer),
+            (recording.at[:, there], inner),
+            (spatial.at[rows_of(core[0], slab.shape[0]), :], slab),
+            (weights.at[0, :, rows_of(core[0], near.shape[1]), :], near),
+        ),
+        done,
+    )
+
+
+def later_kernel(core, weights, *refs):
+    pairs = []
+    for layer, near in enumerate(refs[:-1]):
+        pairs.append((weights.at[layer + 1, :, rows_of(core[0], near.shape[1]), :], near))
+    move_all(pairs, refs[-1])
+
+
+def first_kernel(side, core, *refs):
+    sources, (mine, theirs), kept, done = refs[:7], refs[7:9], refs[9:15], refs[15]
+    near_w, far_w = sources[:2]
+    own_w, own, own_edge, held_w, held, held_edge = kept
+    slab = near_w.shape[0]
+    move_all(
+        (
+            (near_w, held_w.at[rows_of(core[0], slab), :]),
+            (far_w, held_w.at[rows_of(1 - core[0], slab), :]),
+            *zip(sources[2:], (own_w, own, own_edge, held, held_edge)),
+        ),
+        done,
+    )
     frames = own.shape[1]
     rows = mine.shape[0]
     for out, part in ((mine, side[0]), (theirs, 1 - side[0])):
-        here = pl.ds(pl.multiple_of(part * rows, rows), rows)
-        left, right = own_w[here, :], other_w[here, :]
-        out[:, :frames] = (dot(left, own[...]) + dot(right, other[...])).astype(out.dtype)
-        out[:, frames:] = (dot(left, own_edge[...]) + dot(right, other_edge[...])).astype(out.dtype)
+        here = rows_of(part, rows)
+        left, right = own_w[here, :], held_w[here, :]
+        out[:, :frames] = (dot(left, own[...]) + dot(right, held[...])).astype(out.dtype)
+        out[:, frames:] = (dot(left, own_edge[...]) + dot(right, held_edge[...])).astype(out.dtype)
 
 
 def gelu(value):
@@ -429,26 +469,28 @@
 
 
 def assemble_kernel(core, cross, lower, *refs):
-    out = refs[-1]
-    latents = refs[0].shape[1]
+    pieces, out, done = refs[:-2], refs[-2], refs[-1]
+    latents = pieces[0].shape[1]
     mine, theirs = 2 * core[0], 2 - 2 * core[0]
     heads = (mine + cross[0], mine + 1 - cross[0], theirs + cross[0], theirs + 1 - cross[0])
-    for index, piece in enumerate(refs[:-1]):
+    pairs = []
+    for index, piece in enumerate(pieces):
         part = lower[0] if index % 2 == 0 else 1 - lower[0]
-        out[
-            pl.ds(pl.multiple_of(heads[index // 2] * HD, HD), HD),
-            pl.ds(pl.multiple_of(part * latents, latents), latents),
-        ] = piece[...]
-
-
-def simple(kernel, out_shape, scalars, arrays, scratch=(), mib=16, specs=None):
+        cols = pl.ds(pl.multiple_of(part * latents, latents), latents)
+        pairs.append((piece, out.at[rows_of(heads[index // 2], HD), cols]))
+    move_all(pairs, done)
+
+
+def simple(
+    kernel, out_shape, scalars, arrays, scratch=(), mib=16, specs=None, out_space=pltpu.VMEM
+):
     many = isinstance(out_shape, (list, tuple))
     return pl.pallas_call(
         kernel,
         grid=(1,),
         out_shape=out_shape,
         in_specs=smem(len(scalars)) + (specs or whole(len(arrays))),
-        out_specs=whole(len(out_shape)) if many else pl.BlockSpec(memory_space=pltpu.VMEM),
+        out_specs=whole(len(out_shape)) if many else pl.BlockSpec(memory_space=out_space),
         scratch_shapes=list(scratch),
         compiler_params=params(mib),
     )(*scalars, *arrays)
@@ -473,31 +515,40 @@
     twins = [(i, i ^ 1) for i in range(blocks)]
 
     other_rec = lax.ppermute(recording, "sensor", across)
-    other_w = lax.ppermute(spatial_w, "sensor", across)
-    tail = lax.ppermute(
-        recording[:, frames - EDGE :], "tm", [(i, i + 1) for i in range(blocks - 1)]
-    )
-    head = lax.ppermute(recording[:, :EDGE], "tm", [(i + 1, i) for i in range(blocks - 1)])
+    even = core[0] == 0
+    slab = ch // 2
+    params_in = (recording, spatial_w, conv_w)
+    hbm = [pl.BlockSpec(memory_space=pltpu.HBM)]
+    near_shape = jax.ShapeDtypeStruct((3, half, ch), bf16)
+    edge_shape = jax.ShapeDtypeStruct((recording.shape[0], EDGE), bf16)
+    outer, inner, slab_w, *mine = simple(
+        early_kernel,
+        [edge_shape, edge_shape, jax.ShapeDtypeStruct((slab, spatial_w.shape[1]), bf16), near_shape],
+        (core,), params_in, [pltpu.SemaphoreType.DMA((4,))], mib=62, specs=hbm * 3,
+    )
+    mine += simple(
+        later_kernel, [near_shape] * (LAYERS - 1), (core,), (conv_w,),
+        [pltpu.SemaphoreType.DMA((LAYERS - 1,))], mib=62, specs=hbm,
+    )
+    near_sp = lax.ppermute(slab_w, "sensor", across)
+    far_sp = lax.ppermute(near_sp, "tm", twins)
+    links = [(i, i + 1) for i in range(1, blocks - 1, 2)]
+    outer = lax.ppermute(outer, "tm", links + [(j, i) for i, j in links])
+    inner = lax.ppermute(inner, "tm", twins)
     lane = jnp.arange(EDGE, dtype=jnp.int32)[None, :]
-    edge = jnp.where(lane < HALF, head, tail)
+    edge = jnp.where((lane < HALF) == even, inner, outer)
     other_edge = lax.ppermute(edge, "sensor", across)
     other_b = lax.ppermute(conv_b, "sensor", across)
-    later_w = lax.optimization_barrier((conv_w, head))[0]
-    mine = [
-        lax.dynamic_slice(
-            later_w if layer else conv_w, (layer, 0, core[0] * half, 0), (1, 3, half, ch)
-        )[0]
-        for layer in range(LAYERS)
-    ]
     near = [lax.ppermute(mine[n], "sensor", across) for n in range(LAYERS)]
     far = [lax.ppermute(near[n], "tm", twins) for n in range(LAYERS)]
     asked = simple(ask_kernel, jax.ShapeDtypeStruct((latents, half), bf16), (core,), (queries,))
     half_shape = jax.ShapeDtypeStruct((ch_loc, span), bf16)
-    parts = (spatial_w, other_w, recording, other_rec, edge, other_edge)
     own_h, other_h = simple(
-        first_kernel, [half_shape, half_shape], (side,), parts,
-        [VMEM(part.shape, bf16) for part in parts] + [pltpu.SemaphoreType.DMA((len(parts),))],
-        specs=[pl.BlockSpec(memory_space=pltpu.HBM)] * len(parts),
+        first_kernel, [half_shape, half_shape], (side, core),
+        (near_sp, far_sp, spatial_w, recording, edge, other_rec, other_edge),
+        [VMEM(part.shape, bf16) for part in (spatial_w, recording, edge) * 2]
+        + [pltpu.SemaphoreType.DMA((7,))],
+        specs=hbm * 7,
     )
     taps_shape = jax.ShapeDtypeStruct((3, ch, span), bf16)
     col = [VMEM((ch_loc, EDGE), jnp.float32)]
@@ -564,12 +615,12 @@
         bit *= 2
     above = flip(done, 4)
     beside = flip(done, 2)
-    corner = flip(above, 2)
+    corner = flip(done, 6)
     pieces = [done, above, beside, corner]
     pieces += [flip(piece, 1) for piece in pieces]
     attended = simple(
         assemble_kernel, jax.ShapeDtypeStruct((ch_loc, latents), bf16), (core, cross, lower),
-        pieces,
+        pieces, [pltpu.SemaphoreType.DMA((len(pieces),))], out_space=pltpu.HBM,
     )
     return (features, attended)
 

time: 116 us -> 104 us (0.90)
  local copies, waits for them, and re-layouts: 11.3 us -> 1.88 us
  starting transfers between devices: 30 us -> 22.1 us
  waiting for transfers between devices: 38 us -> 43.2 us
    unnamed x34 -> x18, local copies, waits for them, and re-layouts: 7.52 us -> 1.88 us
    ppermute x3 -> x4, starting transfers between devices: 6.64 us -> 2.4 us  [the longest x1 1.74 us: pair_device(): near_sp = lax.ppermute(slab_w, 'sensor', across)]
    ppermute x3, waiting for transfers between devices: 17.4 us -> 21.4 us  [pair_device(): near = [lax.ppermute(mine[n], 'sensor', across) for n in range(LAYERS)]]
    ppermute x3, starting transfers between devices: 2.96 us -> 0.01 us  [pair_device(): far = [lax.ppermute(near[n], 'tm', twins) for n in range(LAYERS)]]
    squeeze x2 -> x0, local copies, waits for them, and re-layouts: 2.23 us -> none  [pair_device(): lax.dynamic_slice(later_w if layer else conv_w, (layer, 0, core[0] * half...]
    slice x1 -> x0, local copies, waits for them, and re-layouts: 1.55 us -> none  [pair_device(): recording[:, frames - EDGE:]]
    ppermute x1, waiting for transfers between devices: 2.1 us -> 3.37 us  [pair_device(): other_edge = lax.ppermute(edge, 'sensor', across)]
    pallas_call x12 -> x14, Pallas kernels: 19.7 us -> 20.6 us  [simple(): pl.pallas_call(kernel, grid=(1,), out_shape=out_shape, in_specs=smem(len(...]
  transfers between devices with their start and end apart: 26 -> 27, of which waited for: 11 -> 14; matrix products, arithmetic and copies ran while one was open for 3% -> 0% of each run, Pallas kernels for 23% -> 25%
where the time goes in v7:
time: 104 us
  waiting for transfers between devices  43.2 us (42%)
  Pallas kernels  34.7 us (33%)
  starting transfers between devices  22.1 us (21%)
  local copies, waits for them, and re-layouts  1.88 us (2%)
  between operations  1.76 us (2%)
    ppermute x3, waiting for transfers between devices, pair_device(): near = [lax.ppermute(mine[n], 'sensor', across) for n in range(LAYERS)]  21.4 us
    pallas_call x14, Pallas kernels, simple(): pl.pallas_call(kernel, grid=(1,), out_shape=out_shape, in_specs=smem(len(...  20.6 us
    pallas_call x4, Pallas kernels, attend(): pl.pallas_call(functools.partial(attend_kernel, packed), out_shape=out_sh...  14.1 us
    ppermute x11, waiting for transfers between devices, flip(): return lax.ppermute(value, 'tm', [(i, i ^ bit) for i in range(blocks)])  13.1 us
    ppermute x11, starting transfers between devices, flip(): return lax.ppermute(value, 'tm', [(i, i ^ bit) for i in range(blocks)])  10 us
    ppermute x3, starting transfers between devices, pair_device(): near = [lax.ppermute(mine[n], 'sensor', across) for n in range(LAYERS)]  5.15 us
    ppermute x1, waiting for transfers between devices, pair_device(): other_edge = lax.ppermute(edge, 'sensor', across)  3.37 us
    ppermute x1, waiting for transfers between devices, pair_device(): near_sp = lax.ppermute(slab_w, 'sensor', across)  2.74 us
  transfers between devices with their start and end apart: 27, of which 14 were waited for; matrix products, arithmetic and copies ran while one was open for 0% of the time, Pallas kernels for 25%

profile of v7, /device:TPU:0, one launch (start us, length us, event | category | flops | bytes accessed | tf_op | source)
XLA Modules:
  0.0 103.7 jit_solution(14682770599733545052)
XLA Ops:
  0.7 1.9 %shard_map.104 = (bf16[128,128]{1,0:T(8,128)(2,1)}, bf16[128,128]{1,0:T(8,128)(2,1)}, bf16[256,128]{1,0:T(8,128)(2,1)}, bf16[3,128,512]{2,1,0:T(8,128)(2,1)}) custom-call(s32[1]{0:T(128)S(6)} %and.14.core, bf16[128,1024]{1,0:T(8,128)(2,1)} %refs_3_.1, bf16[512,128]{1,0:T(8,128)(2,1)} %refs_2_.1, bf16[3,3,256,512]{3,2,1,0:T(8,128)(2,1)} %weights.9), custom_call_target="tpu_custom_call" | custom-call | tf_op jit(solution)/shard_map/pallas_call | solution.py:488
  2.6 3.1 %collective-permute-start.6 = (bf16[3,128,512]{2,1,0:T(8,128)(2,1)}, bf16[3,128,512]{2,1,0:T(8,128)(2,1)S(1)}, u32[]{:S(2)}, u32[]{:S(2)}) collective-permute-start(bf16[3,128,512]{2,1,0:T(8,128)(2,1)} %get-tuple-element.34), channel_id=1, source_target_pairs={{0,16},{16,0},{1,17},{17,1},{2,18},{18,2},{3,19},{19,3},{4,20},{20... | collective-permute-start | bytes 1179656 | tf_op jit(solution)/shard_map/ppermute | solution.py:542
  5.7 2.0 %shard_map.109 = (bf16[3,128,512]{2,1,0:T(8,128)(2,1)}, bf16[3,128,512]{2,1,0:T(8,128)(2,1)}) custom-call(s32[1]{0:T(128)S(6)} %and.14.core, bf16[3,3,256,512]{3,2,1,0:T(8,128)(2,1)} %weights.9), custom_call_target="tpu_custom_call" | custom-call | tf_op jit(solution)/shard_map/pallas_call | solution.py:488
  7.8 2.0 %collective-permute-start.12 = (bf16[3,128,512]{2,1,0:T(8,128)(2,1)}, bf16[3,128,512]{2,1,0:T(8,128)(2,1)S(1)}, u32[]{:S(2)}, u32[]{:S(2)}) collective-permute-start(bf16[3,128,512]{2,1,0:T(8,128)(2,1)} %get-tuple-element.41), channel_id=1, source_target_pairs={{0,16},{16,0},{1,17},{17,1},{2,18},{18,2},{3,19},{19,3},{4,20},{20... | collective-permute-start | bytes 1179656 | tf_op jit(solution)/shard_map/ppermute | solution.py:542
  11.3 4.6 %collective-permute-done.6.near_w = bf16[3,128,512]{2,1,0:T(8,128)(2,1)S(1)} collective-permute-done((bf16[3,128,512]{2,1,0:T(8,128)(2,1)}, bf16[3,128,512]{2,1,0:T(8,128)(2,1)S(1)}, u32[]{:S(2)}, u32[]{:S(2)}) %collective-permute-start.6) | collective-permute-done | bytes 393248 | tf_op jit(solution)/shard_map/ppermute | solution.py:542
  15.9 8.4 %collective-permute-done.9.near_w = bf16[3,128,512]{2,1,0:T(8,128)(2,1)S(1)} collective-permute-done((bf16[3,128,512]{2,1,0:T(8,128)(2,1)}, bf16[3,128,512]{2,1,0:T(8,128)(2,1)S(1)}, u32[]{:S(2)}, u32[]{:S(2)}) %collective-permute-start.9) | collective-permute-done | bytes 393248 | tf_op jit(solution)/shard_map/ppermute | solution.py:542
  24.3 8.4 %collective-permute-done.12.near_w = bf16[3,128,512]{2,1,0:T(8,128)(2,1)S(1)} collective-permute-done((bf16[3,128,512]{2,1,0:T(8,128)(2,1)}, bf16[3,128,512]{2,1,0:T(8,128)(2,1)S(1)}, u32[]{:S(2)}, u32[]{:S(2)}) %collective-permute-start.12) | collective-permute-done | bytes 393248 | tf_op jit(solution)/shard_map/ppermute | solution.py:542
  32.7 2.1 %collective-permute-start.5 = (bf16[128,128]{1,0:T(8,128)(2,1)S(1)}, bf16[128,128]{1,0:T(8,128)(2,1)S(1)}, u32[]{:S(2)}, u32[]{:S(2)}) collective-permute-start(bf16[128,128]{1,0:T(8,128)(2,1)S(1)} %broadcast_select_fusion.refs_4_), channel_id=1, source_target_pairs={{0,16},{16,0},{1,17},{17,1},{2,18},{18,2},{3,19},{19,3},{4,20},{20... | collective-permute-start | bytes 98312 | tf_op jit(solution)/shard_map/ppermute | solution.py:540
  34.8 3.4 %collective-permute-done.5.refs_6_ = bf16[128,128]{1,0:T(8,128)(2,1)S(1)} collective-permute-done((bf16[128,128]{1,0:T(8,128)(2,1)S(1)}, bf16[128,128]{1,0:T(8,128)(2,1)S(1)}, u32[]{:S(2)}, u32[]{:S(2)}) %collective-permute-start.5) | collective-permute-done | bytes 32800 | tf_op jit(solution)/shard_map/ppermute | solution.py:540
  38.2 1.7 %collective-permute-start = (bf16[256,128]{1,0:T(8,128)(2,1)}, bf16[256,128]{1,0:T(8,128)(2,1)S(1)}, u32[]{:S(2)}, u32[]{:S(2)}) collective-permute-start(bf16[256,128]{1,0:T(8,128)(2,1)} %get-tuple-element.27), channel_id=1, source_target_pairs={{0,16},{16,0},{1,17},{17,1},{2,18},{18,2},{3,19},{19,3},{4,20},{20... | collective-permute-start | bytes 196616 | tf_op jit(solution)/shard_map/ppermute | solution.py:533
  39.9 2.7 %collective-permute-done.refs_0_ = bf16[256,128]{1,0:T(8,128)(2,1)S(1)} collective-permute-done((bf16[256,128]{1,0:T(8,128)(2,1)}, bf16[256,128]{1,0:T(8,128)(2,1)S(1)}, u32[]{:S(2)}, u32[]{:S(2)}) %collective-permute-start) | collective-permute-done | bytes 65568 | tf_op jit(solution)/shard_map/ppermute | solution.py:533
  43.9 1.7 %collective-permute-start.8 = (f32[3,256]{1,0:T(4,128)S(1)}, f32[3,256]{1,0:T(4,128)S(1)}, u32[]{:S(2)}, u32[]{:S(2)}) collective-permute-start(f32[3,256]{1,0:T(4,128)S(1)} %copy-done.7), channel_id=1, source_target_pairs={{0,16},{16,0},{1,17},{17,1},{2,18},{18,2},{3,19},{19,3},{4,20},{20... | collective-permute-start | bytes 9224 | tf_op jit(solution)/shard_map/ppermute | solution.py:541
  48.6 2.9 %shard_map.106 = (bf16[256,1152]{1,0:T(8,128)(2,1)S(1)}, bf16[3,512,1152]{2,1,0:T(8,128)(2,1)S(1)}) custom-call(s32[3]{0:T(128)S(1)} %copy-done.8, s32[1]{0:T(128)} %bitcast.side, s32[1]{0:T(128)} %bitcast.1.place, bf16[256,1152]{1,0:T(8,128)(2,1)S(1)} %get-tuple-element.30.mine, bf16[256,1152]{1,0:T(8,128)(2,1)S(1)} %get-tuple-element.31.theirs, ...), custom_call_target="tpu_custom_call" | custom-call | tf_op jit(solution)/shard_map/pallas_call | solution.py:488
  53.2 2.9 %shard_map.108 = (bf16[256,1152]{1,0:T(8,128)(2,1)S(1)}, bf16[3,512,1152]{2,1,0:T(8,128)(2,1)S(1)}) custom-call(s32[3]{0:T(128)S(1)} %copy-done.8, s32[1]{0:T(128)} %bitcast.side, s32[1]{0:T(128)} %bitcast.1.place, bf16[256,1152]{1,0:T(8,128)(2,1)S(1)} %get-tuple-element.32.mine, bf16[256,1152]{1,0:T(8,128)(2,1)S(1)} %shard_map.107.theirs, ...), custom_call_target="tpu_custom_call" | custom-call | tf_op jit(solution)/shard_map/pallas_call | solution.py:488
  57.5 3.3 %shard_map.111 = (bf16[256,1024]{1,0:T(8,128)(2,1)}, bf16[256,1024]{1,0:T(8,128)(2,1)S(1)}, bf16[3,512,1152]{2,1,0:T(8,128)(2,1)S(1)}) custom-call(s32[3]{0:T(128)S(1)} %copy-done.8, s32[1]{0:T(128)} %bitcast.side, s32[1]{0:T(128)} %bitcast.1.place, bf16[256,1152]{1,0:T(8,128)(2,1)S(1)} %get-tuple-element.35.mine, bf16[256,1152]{1,0:T(8,128)(2,1)S(1)} %shard_map.110.theirs, ...), custom_call_target="tpu_custom_call" | custom-call | tf_op jit(solution)/shard_map/pallas_call | solution.py:488
  60.8 1.9 %shard_map.112 = (bf16[128,1024]{1,0:T(8,128)(2,1)S(1)}, bf16[128,1024]{1,0:T(8,128)(2,1)S(1)}, bf16[1024,128]{1,0:T(8,128)(2,1)S(1)}, bf16[1024,128]{1,0:T(8,128)(2,1)S(1)}) custom-call(s32[1]{0:T(128)} %bitcast.side, s32[1]{0:T(128)S(6)} %and.14.core, bf16[256,1024]{1,0:T(8,128)(2,1)S(1)} %get-tuple-element.39.features, ...), custom_call_target="tpu_custom_call" | custom-call | tf_op jit(solution)/shard_map/pallas_call | solution.py:488
  64.9 3.7 %attend_send.3 = bf16[72,1024]{1,0:T(8,128)(2,1)S(1)} custom-call(s32[1]{0:T(128)S(6)} %sub.8.which, s32[1]{0:T(128)S(6)} %sub.9.half, s32[1]{0:T(128)S(6)} %copy.11.valid_own, s32[1]{0:T(128)} %collective-permute-done.11.valid_rec, bf16[128,1024]{1,0:T(8,128)(2,1)S(1)} %get-tuple-element.42.key_own, bf16[128,1024]{1,0:T(8,128)(2,1)S(1)} %collective-permute-done.14.key_rec, ...), custom_call_target="tpu_custom_call" | custom-call | tf_op jit(solution)/shard_map/attend_send/pallas_call | solution.py:453
  70.1 3.5 %attend_send.2 = bf16[72,1024]{1,0:T(8,128)(2,1)S(1)} custom-call(s32[1]{0:T(128)S(6)} %sub.8.which, s32[1]{0:T(128)S(6)} %and.16.half.lower, s32[1]{0:T(128)S(6)} %copy.11.valid_own, s32[1]{0:T(128)} %collective-permute-done.11.valid_rec, bf16[128,1024]{1,0:T(8,128)(2,1)S(1)} %get-tuple-element.42.key_own, ...), custom_call_target="tpu_custom_call" | custom-call | tf_op jit(solution)/shard_map/attend_send/pallas_call | solution.py:453
  74.2 3.5 %attend_keep.3 = (f32[1,1024]{1,0:T(1,128)S(1)}, f32[1,1024]{1,0:T(1,128)S(1)}, f32[64,1024]{1,0:T(8,128)S(1)}) custom-call(s32[1]{0:T(128)S(6)} %and.15.which.cross, s32[1]{0:T(128)S(6)} %sub.9.half, s32[1]{0:T(128)S(6)} %copy.11.valid_own, s32[1]{0:T(128)} %collective-permute-done.11.valid_rec, bf16[128,1024]{1,0:T(8,128)(2,1)S(1)} %get-tuple-element.42.key_own, ...), custom_call_target="tpu_custom_call" | custom-call | tf_op jit(solution)/shard_map/attend_keep/pallas_call | solution.py:453
  79.4 3.5 %attend_keep.2 = (f32[1,1024]{1,0:T(1,128)S(1)}, f32[1,1024]{1,0:T(1,128)S(1)}, f32[64,1024]{1,0:T(8,128)S(1)}) custom-call(s32[1]{0:T(128)S(6)} %and.15.which.cross, s32[1]{0:T(128)S(6)} %and.16.half.lower, s32[1]{0:T(128)S(6)} %copy.11.valid_own, s32[1]{0:T(128)} %collective-permute-done.11.valid_rec, bf16[128,1024]{1,0:T(8,128)(2,1)S(1)} %get-tuple-element.42.key_own, ...), custom_call_target="tpu_custom_call" | custom-call | tf_op jit(solution)/shard_map/attend_keep/pallas_call | solution.py:453
  83.3 2.6 %collective-permute-start.19 = (bf16[72,1024]{1,0:T(8,128)(2,1)S(1)}, bf16[72,1024]{1,0:T(8,128)(2,1)S(1)}, u32[]{:S(2)}, u32[]{:S(2)}) collective-permute-start(bf16[72,1024]{1,0:T(8,128)(2,1)S(1)} %shard_map.115.mine), channel_id=1, source_target_pairs={{0,8},{1,9},{2,10},{3,11},{4,12},{5,13},{6,14},{7,15},{8,0},{9,1},... | collective-permute-start | bytes 442376 | tf_op jit(solution)/shard_map/ppermute | solution.py:590
  86.0 6.3 %collective-permute-done.19.theirs = bf16[72,1024]{1,0:T(8,128)(2,1)S(1)} collective-permute-done((bf16[72,1024]{1,0:T(8,128)(2,1)S(1)}, bf16[72,1024]{1,0:T(8,128)(2,1)S(1)}, u32[]{:S(2)}, u32[]{:S(2)}) %collective-permute-start.19) | collective-permute-done | bytes 147488 | tf_op jit(solution)/shard_map/ppermute | solution.py:590
  95.9 2.9 %collective-permute-done.20.refs_1_ = bf16[64,1024]{1,0:T(8,128)(2,1)S(1)} collective-permute-done((bf16[64,1024]{1,0:T(8,128)(2,1)S(1)}, bf16[64,1024]{1,0:T(8,128)(2,1)S(1)}, u32[]{:S(2)}, u32[]{:S(2)}) %collective-permute-start.20) | collective-permute-done | bytes 131104 | tf_op jit(solution)/shard_map/ppermute | solution.py:590
  99.5 1.7 %collective-permute-done.22.refs_3_ = bf16[64,1024]{1,0:T(8,128)(2,1)S(1)} collective-permute-done((bf16[64,1024]{1,0:T(8,128)(2,1)S(1)}, bf16[64,1024]{1,0:T(8,128)(2,1)S(1)}, u32[]{:S(2)}, u32[]{:S(2)}) %collective-permute-start.22) | collective-permute-done | bytes 131104 | tf_op jit(solution)/shard_map/ppermute | solution.py:590
  (68 shorter events, 21.4 us)
Async XLA Ops:
  2.6 13.2 %collective-permute-start.6 = (bf16[3,128,512]{2,1,0:T(8,128)(2,1)}, bf16[3,128,512]{2,1,0:T(8,128)(2,1)S(1)}, u32[]{:S(2)}, u32[]{:S(2)}) collective-permute-start(bf16[3,128,512]{2,1,0:T(8,128)(2,1)} %get-tuple-element.34), channel_id=1, source_target_pairs={{0,16},{16,0},{1,17},{17,1},{2,18},{18,2},{3,19},{19,3},{4,20},{20... | collective-permute-start | bytes 1179656 | tf_op jit(solution)/shard_map/ppermute | solution.py:542
  7.7 16.6 %collective-permute-start.9 = (bf16[3,128,512]{2,1,0:T(8,128)(2,1)}, bf16[3,128,512]{2,1,0:T(8,128)(2,1)S(1)}, u32[]{:S(2)}, u32[]{:S(2)}) collective-permute-start(bf16[3,128,512]{2,1,0:T(8,128)(2,1)} %get-tuple-element.37), channel_id=1, source_target_pairs={{0,16},{16,0},{1,17},{17,1},{2,18},{18,2},{3,19},{19,3},{4,20},{20... | collective-permute-start | bytes 1179656 | tf_op jit(solution)/shard_map/ppermute | solution.py:542
  7.8 24.9 %collective-permute-start.12 = (bf16[3,128,512]{2,1,0:T(8,128)(2,1)}, bf16[3,128,512]{2,1,0:T(8,128)(2,1)S(1)}, u32[]{:S(2)}, u32[]{:S(2)}) collective-permute-start(bf16[3,128,512]{2,1,0:T(8,128)(2,1)} %get-tuple-element.41), channel_id=1, source_target_pairs={{0,16},{16,0},{1,17},{17,1},{2,18},{18,2},{3,19},{19,3},{4,20},{20... | collective-permute-start | bytes 1179656 | tf_op jit(solution)/shard_map/ppermute | solution.py:542
  9.8 22.9 %collective-permute-start.3 = (bf16[128,128]{1,0:T(8,128)(2,1)}, bf16[128,128]{1,0:T(8,128)(2,1)S(1)}, u32[]{:S(2)}, u32[]{:S(2)}) collective-permute-start(bf16[128,128]{1,0:T(8,128)(2,1)} %get-tuple-element.29), channel_id=1, source_target_pairs={{1,2},{3,4},{5,6},{7,8},{9,10},{11,12},{13,14},{2,1},{4,3},{6,5},{... | collective-permute-start | bytes 98312 | tf_op jit(solution)/shard_map/ppermute | solution.py:536
  11.2 34.5 %collective-permute-start.4 = (bf16[128,1024]{1,0:T(8,128)(2,1)S(1)}, bf16[128,1024]{1,0:T(8,128)(2,1)S(1)}, u32[]{:S(2)}, u32[]{:S(2)}) collective-permute-start(bf16[128,1024]{1,0:T(8,128)(2,1)S(1)} %copy-done.3), channel_id=1, source_target_pairs={{0,16},{16,0},{1,17},{17,1},{2,18},{18,2},{3,19},{19,3},{4,20},{20... | collective-permute-start | bytes 786440 | tf_op jit(solution)/shard_map/ppermute | solution.py:517
  15.9 35.7 %collective-permute-start.7 = (bf16[3,128,512]{2,1,0:T(8,128)(2,1)S(1)}, bf16[3,128,512]{2,1,0:T(8,128)(2,1)S(1)}, u32[]{:S(2)}, u32[]{:S(2)}) collective-permute-start(bf16[3,128,512]{2,1,0:T(8,128)(2,1)S(1)} %collective-permute-done.6.near_w), channel_id=1, source_target_pairs={{0,1},{1,0},{2,3},{3,2},{4,5},{5,4},{6,7},{7,6},{8,9},{9,8},{10,11... | collective-permute-start | bytes 1179656 | tf_op jit(solution)/shard_map/ppermute | solution.py:543
  24.3 31.8 %collective-permute-start.10 = (bf16[3,128,512]{2,1,0:T(8,128)(2,1)S(1)}, bf16[3,128,512]{2,1,0:T(8,128)(2,1)S(1)}, u32[]{:S(2)}, u32[]{:S(2)}) collective-permute-start(bf16[3,128,512]{2,1,0:T(8,128)(2,1)S(1)} %collective-permute-done.9.near_w), channel_id=1, source_target_pairs={{0,1},{1,0},{2,3},{3,2},{4,5},{5,4},{6,7},{7,6},{8,9},{9,8},{10,11... | collective-permute-start | bytes 1179656 | tf_op jit(solution)/shard_map/ppermute | solution.py:543
  32.7 28.1 %collective-permute-start.13 = (bf16[3,128,512]{2,1,0:T(8,128)(2,1)S(1)}, bf16[3,128,512]{2,1,0:T(8,128)(2,1)S(1)}, u32[]{:S(2)}, u32[]{:S(2)}) collective-permute-start(bf16[3,128,512]{2,1,0:T(8,128)(2,1)S(1)} %collective-permute-done.12.near_w), channel_id=1, source_target_pairs={{0,1},{1,0},{2,3},{3,2},{4,5},{5,4},{6,7},{7,6},{8,9},{9,8},{10,11... | collective-permute-start | bytes 1179656 | tf_op jit(solution)/shard_map/ppermute | solution.py:543
  32.7 5.5 %collective-permute-start.5 = (bf16[128,128]{1,0:T(8,128)(2,1)S(1)}, bf16[128,128]{1,0:T(8,128)(2,1)S(1)}, u32[]{:S(2)}, u32[]{:S(2)}) collective-permute-start(bf16[128,128]{1,0:T(8,128)(2,1)S(1)} %broadcast_select_fusion.refs_4_), channel_id=1, source_target_pairs={{0,16},{16,0},{1,17},{17,1},{2,18},{18,2},{3,19},{19,3},{4,20},{20... | collective-permute-start | bytes 98312 | tf_op jit(solution)/shard_map/ppermute | solution.py:540
  38.2 4.5 %collective-permute-start = (bf16[256,128]{1,0:T(8,128)(2,1)}, bf16[256,128]{1,0:T(8,128)(2,1)S(1)}, u32[]{:S(2)}, u32[]{:S(2)}) collective-permute-start(bf16[256,128]{1,0:T(8,128)(2,1)} %get-tuple-element.27), channel_id=1, source_target_pairs={{0,16},{16,0},{1,17},{17,1},{2,18},{18,2},{3,19},{19,3},{4,20},{20... | collective-permute-start | bytes 196616 | tf_op jit(solution)/shard_map/ppermute | solution.py:533
  43.9 7.6 %collective-permute-start.8 = (f32[3,256]{1,0:T(4,128)S(1)}, f32[3,256]{1,0:T(4,128)S(1)}, u32[]{:S(2)}, u32[]{:S(2)}) collective-permute-start(f32[3,256]{1,0:T(4,128)S(1)} %copy-done.7), channel_id=1, source_target_pairs={{0,16},{16,0},{1,17},{17,1},{2,18},{18,2},{3,19},{19,3},{4,20},{20... | collective-permute-start | bytes 9224 | tf_op jit(solution)/shard_map/ppermute | solution.py:541
  62.7 2.1 %collective-permute-start.14 = (bf16[128,1024]{1,0:T(8,128)(2,1)S(1)}, bf16[128,1024]{1,0:T(8,128)(2,1)S(1)}, u32[]{:S(2)}, u32[]{:S(2)}) collective-permute-start(bf16[128,1024]{1,0:T(8,128)(2,1)S(1)} %get-tuple-element.43), channel_id=1, source_target_pairs={{0,1},{1,0},{2,3},{3,2},{4,5},{5,4},{6,7},{7,6},{8,9},{9,8},{10,11... | collective-permute-start | bytes 786440 | tf_op jit(solution)/shard_map/ppermute | solution.py:585
  62.8 2.0 %collective-permute-start.15 = (bf16[1024,128]{1,0:T(8,128)(2,1)S(1)}, bf16[1024,128]{1,0:T(8,128)(2,1)S(1)}, u32[]{:S(2)}, u32[]{:S(2)}) collective-permute-start(bf16[1024,128]{1,0:T(8,128)(2,1)S(1)} %get-tuple-element.45), channel_id=1, source_target_pairs={{0,1},{1,0},{2,3},{3,2},{4,5},{5,4},{6,7},{7,6},{8,9},{9,8},{10,11... | collective-permute-start | bytes 786440 | tf_op jit(solution)/shard_map/ppermute | solution.py:586
  63.3 1.5 %collective-permute-start.11 = (s32[1]{0:T(128)}, s32[1]{0:T(128)}, u32[]{:S(2)}, u32[]{:S(2)}) collective-permute-start(s32[1]{0:T(128)} %param.14), channel_id=1, source_target_pairs={{0,1},{1,0},{2,3},{3,2},{4,5},{5,4},{6,7},{7,6},{8,9},{9,8},{10,11... | collective-permute-start | bytes 20 | tf_op jit(solution)/shard_map/ppermute | solution.py:587
  68.5 9.1 %collective-permute-start.17 = (bf16[72,1024]{1,0:T(8,128)(2,1)S(1)}, bf16[72,1024]{1,0:T(8,128)(2,1)S(1)}, u32[]{:S(2)}, u32[]{:S(2)}) collective-permute-start(bf16[72,1024]{1,0:T(8,128)(2,1)S(1)} %attend_send.3), channel_id=1, source_target_pairs={{0,2},{1,3},{2,0},{3,1},{4,6},{5,7},{6,4},{7,5},{8,10},{9,11},{10,... | collective-permute-start | bytes 442376 | tf_op jit(solution)/shard_map/ppermute | solution.py:590
  73.6 9.3 %collective-permute-start.16 = (bf16[72,1024]{1,0:T(8,128)(2,1)S(1)}, bf16[72,1024]{1,0:T(8,128)(2,1)S(1)}, u32[]{:S(2)}, u32[]{:S(2)}) collective-permute-start(bf16[72,1024]{1,0:T(8,128)(2,1)S(1)} %attend_send.2), channel_id=1, source_target_pairs={{0,2},{1,3},{2,0},{3,1},{4,6},{5,7},{6,4},{7,5},{8,10},{9,11},{10,... | collective-permute-start | bytes 442376 | tf_op jit(solution)/shard_map/ppermute | solution.py:590
  77.8 5.4 %collective-permute-start.18 = (bf16[72,1024]{1,0:T(8,128)(2,1)S(1)}, bf16[72,1024]{1,0:T(8,128)(2,1)S(1)}, u32[]{:S(2)}, u32[]{:S(2)}) collective-permute-start(bf16[72,1024]{1,0:T(8,128)(2,1)S(1)} %shard_map.114), channel_id=1, source_target_pairs={{0,4},{1,5},{2,6},{3,7},{4,0},{5,1},{6,2},{7,3},{8,12},{9,13},{10,... | collective-permute-start | bytes 442376 | tf_op jit(solution)/shard_map/ppermute | solution.py:590
  83.3 8.9 %collective-permute-start.19 = (bf16[72,1024]{1,0:T(8,128)(2,1)S(1)}, bf16[72,1024]{1,0:T(8,128)(2,1)S(1)}, u32[]{:S(2)}, u32[]{:S(2)}) collective-permute-start(bf16[72,1024]{1,0:T(8,128)(2,1)S(1)} %shard_map.115.mine), channel_id=1, source_target_pairs={{0,8},{1,9},{2,10},{3,11},{4,12},{5,13},{6,14},{7,15},{8,0},{9,1},... | collective-permute-start | bytes 442376 | tf_op jit(solution)/shard_map/ppermute | solution.py:590
  92.4 6.4 %collective-permute-start.20 = (bf16[64,1024]{1,0:T(8,128)(2,1)S(1)}, bf16[64,1024]{1,0:T(8,128)(2,1)S(1)}, u32[]{:S(2)}, u32[]{:S(2)}) collective-permute-start(bf16[64,1024]{1,0:T(8,128)(2,1)S(1)} %shard_map.116.refs_0_), channel_id=1, source_target_pairs={{0,4},{1,5},{2,6},{3,7},{4,0},{5,1},{6,2},{7,3},{8,12},{9,13},{10,... | collective-permute-start | bytes 393224 | tf_op jit(solution)/shard_map/ppermute | solution.py:590
  92.9 6.6 %collective-permute-start.21 = (bf16[64,1024]{1,0:T(8,128)(2,1)S(1)}, bf16[64,1024]{1,0:T(8,128)(2,1)S(1)}, u32[]{:S(2)}, u32[]{:S(2)}) collective-permute-start(bf16[64,1024]{1,0:T(8,128)(2,1)S(1)} %shard_map.116.refs_0_), channel_id=1, source_target_pairs={{0,2},{1,3},{2,0},{3,1},{4,6},{5,7},{6,4},{7,5},{8,10},{9,11},{10,... | collective-permute-start | bytes 393224 | tf_op jit(solution)/shard_map/ppermute | solution.py:590
  94.4 6.7 %collective-permute-start.22 = (bf16[64,1024]{1,0:T(8,128)(2,1)S(1)}, bf16[64,1024]{1,0:T(8,128)(2,1)S(1)}, u32[]{:S(2)}, u32[]{:S(2)}) collective-permute-start(bf16[64,1024]{1,0:T(8,128)(2,1)S(1)} %shard_map.116.refs_0_), channel_id=1, source_target_pairs={{0,6},{1,7},{2,4},{3,5},{4,2},{5,3},{6,0},{7,1},{8,14},{9,15},{10,... | collective-permute-start | bytes 393224 | tf_op jit(solution)/shard_map/ppermute | solution.py:590
  95.9 5.2 %collective-permute-start.23 = (bf16[64,1024]{1,0:T(8,128)(2,1)S(1)}, bf16[64,1024]{1,0:T(8,128)(2,1)S(1)}, u32[]{:S(2)}, u32[]{:S(2)}) collective-permute-start(bf16[64,1024]{1,0:T(8,128)(2,1)S(1)} %shard_map.116.refs_0_), channel_id=1, source_target_pairs={{0,1},{1,0},{2,3},{3,2},{4,5},{5,4},{6,7},{7,6},{8,9},{9,8},{10,11... | collective-permute-start | bytes 393224 | tf_op jit(solution)/shard_map/ppermute | solution.py:590
  98.8 2.4 %collective-permute-start.24 = (bf16[64,1024]{1,0:T(8,128)(2,1)S(1)}, bf16[64,1024]{1,0:T(8,128)(2,1)S(1)}, u32[]{:S(2)}, u32[]{:S(2)}) collective-permute-start(bf16[64,1024]{1,0:T(8,128)(2,1)S(1)} %collective-permute-done.20.refs_1_), channel_id=1, source_target_pairs={{0,1},{1,0},{2,3},{3,2},{4,5},{5,4},{6,7},{7,6},{8,9},{9,8},{10,11... | collective-permute-start | bytes 393224 | tf_op jit(solution)/shard_map/ppermute | solution.py:590
  99.5 1.7 %collective-permute-start.25 = (bf16[64,1024]{1,0:T(8,128)(2,1)S(1)}, bf16[64,1024]{1,0:T(8,128)(2,1)S(1)}, u32[]{:S(2)}, u32[]{:S(2)}) collective-permute-start(bf16[64,1024]{1,0:T(8,128)(2,1)S(1)} %collective-permute-done.21.refs_2_), channel_id=1, source_target_pairs={{0,1},{1,0},{2,3},{3,2},{4,5},{5,4},{6,7},{7,6},{8,9},{9,8},{10,11... | collective-permute-start | bytes 393224 | tf_op jit(solution)/shard_map/ppermute | solution.py:590
  (12 other events, 165.3 us)

commit v8 on v5

--- a/solution.py
+++ b/solution.py
@@ -136,21 +136,30 @@
     return jnp.dot(left, right, preferred_element_type=jnp.float32)
 
 
-def first_kernel(side, *refs):
-    sources, (mine, theirs), held, done = refs[:6], refs[6:8], refs[8:14], refs[14]
+def rows_of(part, count):
+    return pl.ds(pl.multiple_of(part * count, count), count)
+
+
+def first_kernel(side, core, *refs):
+    sources, (mine, theirs), held, done = refs[:7], refs[7:9], refs[9:15], refs[15]
+    slab = sources[0].shape[0]
+    own_w, own, own_edge, other_w, other, other_edge = held
+    targets = (
+        other_w.at[rows_of(core[0], slab), :], other_w.at[rows_of(1 - core[0], slab), :],
+        own_w, own, own_edge, other, other_edge,
+    )
     copies = [
         pltpu.make_async_copy(source, target, done.at[n])
-        for n, (source, target) in enumerate(zip(sources, held))
+        for n, (source, target) in enumerate(zip(sources, targets))
     ]
     for copy in copies:
         copy.start()
     for copy in copies:
         copy.wait()
-    own_w, other_w, own, other, own_edge, other_edge = held
     frames = own.shape[1]
     rows = mine.shape[0]
     for out, part in ((mine, side[0]), (theirs, 1 - side[0])):
-        here = pl.ds(pl.multiple_of(part * rows, rows), rows)
+        here = rows_of(part, rows)
         left, right = own_w[here, :], other_w[here, :]
         out[:, :frames] = (dot(left, own[...]) + dot(right, other[...])).astype(out.dtype)
         out[:, frames:] = (dot(left, own_edge[...]) + dot(right, other_edge[...])).astype(out.dtype)
@@ -473,16 +482,22 @@
     twins = [(i, i ^ 1) for i in range(blocks)]
 
     other_rec = lax.ppermute(recording, "sensor", across)
-    other_w = lax.ppermute(spatial_w, "sensor", across)
-    tail = lax.ppermute(
-        recording[:, frames - EDGE :], "tm", [(i, i + 1) for i in range(blocks - 1)]
-    )
-    head = lax.ppermute(recording[:, :EDGE], "tm", [(i + 1, i) for i in range(blocks - 1)])
+    even = core[0] == 0
+    slab = ch // 2
+    near_sp = lax.ppermute(jnp.where(even, spatial_w[:slab], spatial_w[slab:]), "sensor", across)
+    far_sp = lax.ppermute(near_sp, "tm", twins)
+    last_part, first_part = recording[:, frames - EDGE :], recording[:, :EDGE]
+    links = [(i, i + 1) for i in range(1, blocks - 1, 2)]
+    outer = lax.ppermute(
+        jnp.where(even, first_part, last_part), "tm",
+        links + [(j, i) for i, j in links],
+    )
+    inner = lax.ppermute(jnp.where(even, last_part, first_part), "tm", twins)
     lane = jnp.arange(EDGE, dtype=jnp.int32)[None, :]
-    edge = jnp.where(lane < HALF, head, tail)
+    edge = jnp.where((lane < HALF) == even, inner, outer)
     other_edge = lax.ppermute(edge, "sensor", across)
     other_b = lax.ppermute(conv_b, "sensor", across)
-    later_w = lax.optimization_barrier((conv_w, head))[0]
+    later_w = lax.optimization_barrier((conv_w, edge))[0]
     mine = [
         lax.dynamic_slice(
             later_w if layer else conv_w, (layer, 0, core[0] * half, 0), (1, 3, half, ch)
@@ -493,11 +508,13 @@
     far = [lax.ppermute(near[n], "tm", twins) for n in range(LAYERS)]
     asked = simple(ask_kernel, jax.ShapeDtypeStruct((latents, half), bf16), (core,), (queries,))
     half_shape = jax.ShapeDtypeStruct((ch_loc, span), bf16)
-    parts = (spatial_w, other_w, recording, other_rec, edge, other_edge)
+    fixed = [pltpu.with_memory_space_constraint(v, pltpu.HBM) for v in (spatial_w, recording)]
     own_h, other_h = simple(
-        first_kernel, [half_shape, half_shape], (side,), parts,
-        [VMEM(part.shape, bf16) for part in parts] + [pltpu.SemaphoreType.DMA((len(parts),))],
-        specs=[pl.BlockSpec(memory_space=pltpu.HBM)] * len(parts),
+        first_kernel, [half_shape, half_shape], (side, core),
+        (near_sp, far_sp, *fixed, edge, other_rec, other_edge),
+        [VMEM(part.shape, bf16) for part in (spatial_w, recording, edge) * 2]
+        + [pltpu.SemaphoreType.DMA((7,))],
+        specs=[pl.BlockSpec(memory_space=pltpu.HBM)] * 7,
     )
     taps_shape = jax.ShapeDtypeStruct((3, ch, span), bf16)
     col = [VMEM((ch_loc, EDGE), jnp.float32)]
@@ -564,7 +581,7 @@
         bit *= 2
     above = flip(done, 4)
     beside = flip(done, 2)
-    corner = flip(above, 2)
+    corner = flip(done, 6)
     pieces = [done, above, beside, corner]
     pieces += [flip(piece, 1) for piece in pieces]
     attended = simple(

time: 116 us -> 116 us (level)
  starting transfers between devices: 30 us -> 36.7 us
  local copies, waits for them, and re-layouts: 11.3 us -> 7.32 us
  waiting for transfers between devices: 38 us -> 34.2 us
    ppermute x3, starting transfers between devices: 2.96 us -> 11.9 us  [pair_device(): far = [lax.ppermute(near[n], 'tm', twins) for n in range(LAYERS)]]
    ppermute x3, waiting for transfers between devices: 17.4 us -> 11.4 us  [pair_device(): near = [lax.ppermute(mine[n], 'sensor', across) for n in range(LAYERS)]]
    ppermute x1, waiting for transfers between devices: 2.1 us -> 6.47 us  [pair_device(): other_edge = lax.ppermute(edge, 'sensor', across)]
    ppermute x3 -> x4, starting transfers between devices: 6.64 us -> 2.95 us  [the longest x1 1.74 us: pair_device(): lax.ppermute(jnp.where(even, spatial_w[:slab], spatial_w[slab:]), 'sensor...]
    unnamed x34 -> x28, local copies, waits for them, and re-layouts: 7.52 us -> 5.09 us
    ppermute x11, starting transfers between devices: 10.4 us -> 12.7 us  [flip(): return lax.ppermute(value, 'tm', [(i, i ^ bit) for i in range(blocks)])]
    ppermute x1, starting transfers between devices: 1.74 us -> 0.02 us  [pair_device(): other_edge = lax.ppermute(edge, 'sensor', across)]
    slice x1 -> x0, local copies, waits for them, and re-layouts: 1.55 us -> none  [pair_device(): recording[:, frames - EDGE:]]
  transfers between devices with their start and end apart: 26 -> 27, of which waited for: 11 -> 13; matrix products, arithmetic and copies ran while one was open for 3% -> 3% of each run, Pallas kernels for 23% -> 23%
where the time goes in v8:
time: 116 us; the launch traced here: 115 us
  starting transfers between devices  36.7 us (32%)
  waiting for transfers between devices  34.2 us (29%)
  Pallas kernels  33.7 us (29%)
  local copies, waits for them, and re-layouts  7.32 us (6%)
  other arithmetic  1.83 us (2%)
  between operations  1.61 us (1%)
    pallas_call x12, Pallas kernels, simple(): pl.pallas_call(kernel, grid=(1,), out_shape=out_shape, in_specs=smem(len(...  19.6 us
    pallas_call x4, Pallas kernels, attend(): pl.pallas_call(functools.partial(attend_kernel, packed), out_shape=out_sh...  14.1 us
    ppermute x11, starting transfers between devices, flip(): return lax.ppermute(value, 'tm', [(i, i ^ bit) for i in range(blocks)])  12.7 us
    ppermute x11, waiting for transfers between devices, flip(): return lax.ppermute(value, 'tm', [(i, i ^ bit) for i in range(blocks)])  12.6 us
    ppermute x3, starting transfers between devices, pair_device(): far = [lax.ppermute(near[n], 'tm', twins) for n in range(LAYERS)]  11.9 us
    ppermute x3, waiting for transfers between devices, pair_device(): near = [lax.ppermute(mine[n], 'sensor', across) for n in range(LAYERS)]  11.4 us
    ppermute x1, waiting for transfers between devices, pair_device(): other_edge = lax.ppermute(edge, 'sensor', across)  6.47 us
    unnamed x28, local copies, waits for them, and re-layouts  5.09 us
  transfers between devices with their start and end apart: 27, of which 13 were waited for; matrix products, arithmetic and copies ran while one was open for 3% of the time, Pallas kernels for 23%

profile of v8, /device:TPU:0, one launch (start us, length us, event | category | flops | bytes accessed | tf_op | source)
XLA Modules:
  0.0 115.4 jit_solution(12533709680577841820)
XLA Ops:
  3.9 2.6 %collective-permute-start.6 = (bf16[3,128,512]{2,1,0:T(8,128)(2,1)S(1)}, bf16[3,128,512]{2,1,0:T(8,128)(2,1)S(1)}, u32[]{:S(2)}, u32[]{:S(2)}) collective-permute-start(bf16[3,128,512]{2,1,0:T(8,128)(2,1)S(1)} %dynamic-slice_bitcast_fusion.2), channel_id=1, source_target_pairs={{0,16},{16,0},{1,17},{17,1},{2,18},{18,2},{3,19},{19,3},{4,20},{20... | collective-permute-start | bytes 1179656 | tf_op jit(solution)/shard_map/ppermute | solution.py:507
  9.8 4.3 %collective-permute-done.6.near_w = bf16[3,128,512]{2,1,0:T(8,128)(2,1)S(1)} collective-permute-done((bf16[3,128,512]{2,1,0:T(8,128)(2,1)S(1)}, bf16[3,128,512]{2,1,0:T(8,128)(2,1)S(1)}, u32[]{:S(2)}, u32[]{:S(2)}) %collective-permute-start.6) | collective-permute-done | bytes 393248 | tf_op jit(solution)/shard_map/ppermute | solution.py:507
  14.1 4.9 %collective-permute-start.7 = (bf16[3,128,512]{2,1,0:T(8,128)(2,1)S(1)}, bf16[3,128,512]{2,1,0:T(8,128)(2,1)}, u32[]{:S(2)}, u32[]{:S(2)}) collective-permute-start(bf16[3,128,512]{2,1,0:T(8,128)(2,1)S(1)} %collective-permute-done.6.near_w), channel_id=1, source_target_pairs={{0,1},{1,0},{2,3},{3,2},{4,5},{5,4},{6,7},{7,6},{8,9},{9,8},{10,11... | collective-permute-start | bytes 1179656 | tf_op jit(solution)/shard_map/ppermute | solution.py:508
  19.0 3.5 %collective-permute-done.9.near_w = bf16[3,128,512]{2,1,0:T(8,128)(2,1)} collective-permute-done((bf16[3,128,512]{2,1,0:T(8,128)(2,1)S(1)}, bf16[3,128,512]{2,1,0:T(8,128)(2,1)}, u32[]{:S(2)}, u32[]{:S(2)}) %collective-permute-start.9) | collective-permute-done | bytes 393248 | tf_op jit(solution)/shard_map/ppermute | solution.py:507
  22.6 4.8 %collective-permute-start.10 = (bf16[3,128,512]{2,1,0:T(8,128)(2,1)}, bf16[3,128,512]{2,1,0:T(8,128)(2,1)}, u32[]{:S(2)}, u32[]{:S(2)}) collective-permute-start(bf16[3,128,512]{2,1,0:T(8,128)(2,1)} %collective-permute-done.9.near_w), channel_id=1, source_target_pairs={{0,1},{1,0},{2,3},{3,2},{4,5},{5,4},{6,7},{7,6},{8,9},{9,8},{10,11... | collective-permute-start | bytes 1179656 | tf_op jit(solution)/shard_map/ppermute | solution.py:508
  27.3 3.6 %collective-permute-done.12.near_w = bf16[3,128,512]{2,1,0:T(8,128)(2,1)S(1)} collective-permute-done((bf16[3,128,512]{2,1,0:T(8,128)(2,1)S(1)}, bf16[3,128,512]{2,1,0:T(8,128)(2,1)S(1)}, u32[]{:S(2)}, u32[]{:S(2)}) %collective-permute-start.12) | collective-permute-done | bytes 393248 | tf_op jit(solution)/shard_map/ppermute | solution.py:507
  30.9 2.2 %collective-permute-start.13 = (bf16[3,128,512]{2,1,0:T(8,128)(2,1)S(1)}, bf16[3,128,512]{2,1,0:T(8,128)(2,1)S(1)}, u32[]{:S(2)}, u32[]{:S(2)}) collective-permute-start(bf16[3,128,512]{2,1,0:T(8,128)(2,1)S(1)} %collective-permute-done.12.near_w), channel_id=1, source_target_pairs={{0,1},{1,0},{2,3},{3,2},{4,5},{5,4},{6,7},{7,6},{8,9},{9,8},{10,11... | collective-permute-start | bytes 1179656 | tf_op jit(solution)/shard_map/ppermute | solution.py:508
  36.0 6.5 %collective-permute-done.5.refs_6_ = bf16[128,128]{1,0:T(8,128)(2,1)S(1)} collective-permute-done((bf16[128,128]{1,0:T(8,128)(2,1)S(1)}, bf16[128,128]{1,0:T(8,128)(2,1)S(1)}, u32[]{:S(2)}, u32[]{:S(2)}) %collective-permute-start.5) | collective-permute-done | bytes 32800 | tf_op jit(solution)/shard_map/ppermute | solution.py:498
  44.8 2.5 %collective-permute-done.refs_0_ = bf16[256,128]{1,0:T(8,128)(2,1)S(1)} collective-permute-done((bf16[256,128]{1,0:T(8,128)(2,1)S(1)}, bf16[256,128]{1,0:T(8,128)(2,1)S(1)}, u32[]{:S(2)}, u32[]{:S(2)}) %collective-permute-start) | collective-permute-done | bytes 65568 | tf_op jit(solution)/shard_map/ppermute | solution.py:487
  54.2 2.1 %shard_map.104 = (bf16[256,1152]{1,0:T(8,128)(2,1)S(1)}, bf16[256,1152]{1,0:T(8,128)(2,1)S(1)}) custom-call(s32[1]{0:T(128)} %bitcast.side, s32[1]{0:T(128)S(6)} %and.14.core, bf16[256,128]{1,0:T(8,128)(2,1)S(1)} %copy-done.7, bf16[256,128]{1,0:T(8,128)(2,1)S(1)} %copy-done.9, bf16[512,128]{1,0:T(8,128)(2,1)} %refs_2_.1, bf16[128,1024]{1,0:T(8,128)(2,1)} %refs_3_.1, ...), custom_call_target="tpu_custom_call" | custom-call | tf_op jit(solution)/shard_map/pallas_call | solution.py:455
  56.3 2.9 %shard_map.105 = (bf16[256,1152]{1,0:T(8,128)(2,1)S(1)}, bf16[3,512,1152]{2,1,0:T(8,128)(2,1)S(1)}) custom-call(s32[3]{0:T(128)S(1)} %copy-done.13, s32[1]{0:T(128)} %bitcast.side, s32[1]{0:T(128)} %bitcast.1.place, bf16[256,1152]{1,0:T(8,128)(2,1)S(1)} %get-tuple-element.22.mine, bf16[256,1152]{1,0:T(8,128)(2,1)S(1)} %get-tuple-element.23.theirs, ...), custom_call_target="tpu_custom_call" | custom-call | tf_op jit(solution)/shard_map/pallas_call | solution.py:455
  59.2 2.4 %shard_map.106.theirs = bf16[256,1152]{1,0:T(8,128)(2,1)S(1)} custom-call(s32[1]{0:T(128)S(6)} %and.14.core, s32[1]{0:T(128)} %bitcast.1.place, bf16[256,1152]{1,0:T(8,128)(2,1)S(1)} %get-tuple-element.23.theirs, bf16[3,512,1152]{2,1,0:T(8,128)(2,1)S(1)} %get-tuple-element.25.taps, bf16[3,128,512]{2,1,0:T(8,128)(2,1)S(1)} %collective-permute-done.6.near_w, ...), custom_call_target="tpu_custom_call" | custom-call | tf_op jit(solution)/shard_map/pallas_call | solution.py:455
  61.6 2.9 %shard_map.107 = (bf16[256,1152]{1,0:T(8,128)(2,1)S(1)}, bf16[3,512,1152]{2,1,0:T(8,128)(2,1)S(1)}) custom-call(s32[3]{0:T(128)S(1)} %copy-done.13, s32[1]{0:T(128)} %bitcast.side, s32[1]{0:T(128)} %bitcast.1.place, bf16[256,1152]{1,0:T(8,128)(2,1)S(1)} %get-tuple-element.24.mine, bf16[256,1152]{1,0:T(8,128)(2,1)S(1)} %shard_map.106.theirs, ...), custom_call_target="tpu_custom_call" | custom-call | tf_op jit(solution)/shard_map/pallas_call | solution.py:455
  64.5 2.6 %shard_map.108.theirs = bf16[256,1152]{1,0:T(8,128)(2,1)S(1)} custom-call(s32[1]{0:T(128)S(6)} %and.14.core, s32[1]{0:T(128)} %bitcast.1.place, bf16[256,1152]{1,0:T(8,128)(2,1)S(1)} %shard_map.106.theirs, bf16[3,512,1152]{2,1,0:T(8,128)(2,1)S(1)} %get-tuple-element.27.taps, bf16[3,128,512]{2,1,0:T(8,128)(2,1)} %collective-permute-done.9.near_w, ...), custom_call_target="tpu_custom_call" | custom-call | tf_op jit(solution)/shard_map/pallas_call | solution.py:455
  67.1 3.3 %shard_map.109 = (bf16[256,1024]{1,0:T(8,128)(2,1)}, bf16[256,1024]{1,0:T(8,128)(2,1)S(1)}, bf16[3,512,1152]{2,1,0:T(8,128)(2,1)S(1)}) custom-call(s32[3]{0:T(128)S(1)} %copy-done.13, s32[1]{0:T(128)} %bitcast.side, s32[1]{0:T(128)} %bitcast.1.place, bf16[256,1152]{1,0:T(8,128)(2,1)S(1)} %get-tuple-element.26.mine, bf16[256,1152]{1,0:T(8,128)(2,1)S(1)} %shard_map.108.theirs, ...), custom_call_target="tpu_custom_call" | custom-call | tf_op jit(solution)/shard_map/pallas_call | solution.py:455
  74.5 3.7 %attend_send.3 = bf16[72,1024]{1,0:T(8,128)(2,1)S(1)} custom-call(s32[1]{0:T(128)S(6)} %sub.8.which, s32[1]{0:T(128)S(6)} %sub.9.half, s32[1]{0:T(128)S(6)} %copy.11.valid_own, s32[1]{0:T(128)} %collective-permute-done.11.valid_rec, bf16[128,1024]{1,0:T(8,128)(2,1)S(1)} %get-tuple-element.32.key_own, bf16[128,1024]{1,0:T(8,128)(2,1)S(1)} %collective-permute-done.14.key_rec, ...), custom_call_target="tpu_custom_call" | custom-call | tf_op jit(solution)/shard_map/attend_send/pallas_call | solution.py:422
  78.2 4.0 %collective-permute-start.17 = (bf16[72,1024]{1,0:T(8,128)(2,1)S(1)}, bf16[72,1024]{1,0:T(8,128)(2,1)S(1)}, u32[]{:S(2)}, u32[]{:S(2)}) collective-permute-start(bf16[72,1024]{1,0:T(8,128)(2,1)S(1)} %attend_send.3), channel_id=1, source_target_pairs={{0,2},{1,3},{2,0},{3,1},{4,6},{5,7},{6,4},{7,5},{8,10},{9,11},{10,... | collective-permute-start | bytes 442376 | tf_op jit(solution)/shard_map/ppermute | solution.py:556
  82.2 3.5 %attend_send.2 = bf16[72,1024]{1,0:T(8,128)(2,1)S(1)} custom-call(s32[1]{0:T(128)S(6)} %sub.8.which, s32[1]{0:T(128)S(6)} %and.16.half.lower, s32[1]{0:T(128)S(6)} %copy.11.valid_own, s32[1]{0:T(128)} %collective-permute-done.11.valid_rec, bf16[128,1024]{1,0:T(8,128)(2,1)S(1)} %get-tuple-element.32.key_own, ...), custom_call_target="tpu_custom_call" | custom-call | tf_op jit(solution)/shard_map/attend_send/pallas_call | solution.py:422
  85.8 3.5 %attend_keep.3 = (f32[1,1024]{1,0:T(1,128)S(1)}, f32[1,1024]{1,0:T(1,128)S(1)}, f32[64,1024]{1,0:T(8,128)S(1)}) custom-call(s32[1]{0:T(128)S(6)} %and.15.which.cross, s32[1]{0:T(128)S(6)} %sub.9.half, s32[1]{0:T(128)S(6)} %copy.11.valid_own, s32[1]{0:T(128)} %collective-permute-done.11.valid_rec, bf16[128,1024]{1,0:T(8,128)(2,1)S(1)} %get-tuple-element.32.key_own, ...), custom_call_target="tpu_custom_call" | custom-call | tf_op jit(solution)/shard_map/attend_keep/pallas_call | solution.py:422
  89.4 2.2 %collective-permute-start.18 = (bf16[72,1024]{1,0:T(8,128)(2,1)S(1)}, bf16[72,1024]{1,0:T(8,128)(2,1)S(1)}, u32[]{:S(2)}, u32[]{:S(2)}) collective-permute-start(bf16[72,1024]{1,0:T(8,128)(2,1)S(1)} %shard_map.112), channel_id=1, source_target_pairs={{0,4},{1,5},{2,6},{3,7},{4,0},{5,1},{6,2},{7,3},{8,12},{9,13},{10,... | collective-permute-start | bytes 442376 | tf_op jit(solution)/shard_map/ppermute | solution.py:556
  91.6 3.5 %attend_keep.2 = (f32[1,1024]{1,0:T(1,128)S(1)}, f32[1,1024]{1,0:T(1,128)S(1)}, f32[64,1024]{1,0:T(8,128)S(1)}) custom-call(s32[1]{0:T(128)S(6)} %and.15.which.cross, s32[1]{0:T(128)S(6)} %and.16.half.lower, s32[1]{0:T(128)S(6)} %copy.11.valid_own, s32[1]{0:T(128)} %collective-permute-done.11.valid_rec, bf16[128,1024]{1,0:T(8,128)(2,1)S(1)} %get-tuple-element.32.key_own, ...), custom_call_target="tpu_custom_call" | custom-call | tf_op jit(solution)/shard_map/attend_keep/pallas_call | solution.py:422
  95.4 2.8 %collective-permute-start.19 = (bf16[72,1024]{1,0:T(8,128)(2,1)S(1)}, bf16[72,1024]{1,0:T(8,128)(2,1)S(1)}, u32[]{:S(2)}, u32[]{:S(2)}) collective-permute-start(bf16[72,1024]{1,0:T(8,128)(2,1)S(1)} %shard_map.113.mine), channel_id=1, source_target_pairs={{0,8},{1,9},{2,10},{3,11},{4,12},{5,13},{6,14},{7,15},{8,0},{9,1},... | collective-permute-start | bytes 442376 | tf_op jit(solution)/shard_map/ppermute | solution.py:556
  98.2 6.3 %collective-permute-done.19.theirs = bf16[72,1024]{1,0:T(8,128)(2,1)S(1)} collective-permute-done((bf16[72,1024]{1,0:T(8,128)(2,1)S(1)}, bf16[72,1024]{1,0:T(8,128)(2,1)S(1)}, u32[]{:S(2)}, u32[]{:S(2)}) %collective-permute-start.19) | collective-permute-done | bytes 147488 | tf_op jit(solution)/shard_map/ppermute | solution.py:556
  108.1 2.8 %collective-permute-done.20.refs_1_ = bf16[64,1024]{1,0:T(8,128)(2,1)S(1)} collective-permute-done((bf16[64,1024]{1,0:T(8,128)(2,1)S(1)}, bf16[64,1024]{1,0:T(8,128)(2,1)S(1)}, u32[]{:S(2)}, u32[]{:S(2)}) %collective-permute-start.20) | collective-permute-done | bytes 131104 | tf_op jit(solution)/shard_map/ppermute | solution.py:556
  (80 shorter events, 30.5 us)
Async XLA Ops:
  1.6 4.8 %collective-permute-start.2 = (bf16[128,128]{1,0:T(8,128)(2,1)S(1)}, bf16[128,128]{1,0:T(8,128)(2,1)S(1)}, u32[]{:S(2)}, u32[]{:S(2)}) collective-permute-start(bf16[128,128]{1,0:T(8,128)(2,1)S(1)} %get-tuple-element.45), channel_id=1, source_target_pairs={{0,1},{1,0},{2,3},{3,2},{4,5},{5,4},{6,7},{7,6},{8,9},{9,8},{10,11... | collective-permute-start | bytes 98312 | tf_op jit(solution)/shard_map/ppermute | solution.py:495
  2.2 4.3 %collective-permute-start.3 = (bf16[128,128]{1,0:T(8,128)(2,1)S(1)}, bf16[128,128]{1,0:T(8,128)(2,1)S(1)}, u32[]{:S(2)}, u32[]{:S(2)}) collective-permute-start(bf16[128,128]{1,0:T(8,128)(2,1)S(1)} %get-tuple-element.44), channel_id=1, source_target_pairs={{1,2},{3,4},{5,6},{7,8},{9,10},{11,12},{13,14},{2,1},{4,3},{6,5},{... | collective-permute-start | bytes 98312 | tf_op jit(solution)/shard_map/ppermute | solution.py:491
  3.9 10.2 %collective-permute-start.6 = (bf16[3,128,512]{2,1,0:T(8,128)(2,1)S(1)}, bf16[3,128,512]{2,1,0:T(8,128)(2,1)S(1)}, u32[]{:S(2)}, u32[]{:S(2)}) collective-permute-start(bf16[3,128,512]{2,1,0:T(8,128)(2,1)S(1)} %dynamic-slice_bitcast_fusion.2), channel_id=1, source_target_pairs={{0,16},{16,0},{1,17},{17,1},{2,18},{18,2},{3,19},{19,3},{4,20},{20... | collective-permute-start | bytes 1179656 | tf_op jit(solution)/shard_map/ppermute | solution.py:507
  7.7 14.9 %collective-permute-start.9 = (bf16[3,128,512]{2,1,0:T(8,128)(2,1)S(1)}, bf16[3,128,512]{2,1,0:T(8,128)(2,1)}, u32[]{:S(2)}, u32[]{:S(2)}) collective-permute-start(bf16[3,128,512]{2,1,0:T(8,128)(2,1)S(1)} %get-tuple-element.43), channel_id=1, source_target_pairs={{0,16},{16,0},{1,17},{17,1},{2,18},{18,2},{3,19},{19,3},{4,20},{20... | collective-permute-start | bytes 1179656 | tf_op jit(solution)/shard_map/ppermute | solution.py:507
  7.8 23.1 %collective-permute-start.12 = (bf16[3,128,512]{2,1,0:T(8,128)(2,1)S(1)}, bf16[3,128,512]{2,1,0:T(8,128)(2,1)S(1)}, u32[]{:S(2)}, u32[]{:S(2)}) collective-permute-start(bf16[3,128,512]{2,1,0:T(8,128)(2,1)S(1)} %get-tuple-element.42), channel_id=1, source_target_pairs={{0,16},{16,0},{1,17},{17,1},{2,18},{18,2},{3,19},{19,3},{4,20},{20... | collective-permute-start | bytes 1179656 | tf_op jit(solution)/shard_map/ppermute | solution.py:507
  14.1 45.1 %collective-permute-start.7 = (bf16[3,128,512]{2,1,0:T(8,128)(2,1)S(1)}, bf16[3,128,512]{2,1,0:T(8,128)(2,1)}, u32[]{:S(2)}, u32[]{:S(2)}) collective-permute-start(bf16[3,128,512]{2,1,0:T(8,128)(2,1)S(1)} %collective-permute-done.6.near_w), channel_id=1, source_target_pairs={{0,1},{1,0},{2,3},{3,2},{4,5},{5,4},{6,7},{7,6},{8,9},{9,8},{10,11... | collective-permute-start | bytes 1179656 | tf_op jit(solution)/shard_map/ppermute | solution.py:508
  22.6 41.9 %collective-permute-start.10 = (bf16[3,128,512]{2,1,0:T(8,128)(2,1)}, bf16[3,128,512]{2,1,0:T(8,128)(2,1)}, u32[]{:S(2)}, u32[]{:S(2)}) collective-permute-start(bf16[3,128,512]{2,1,0:T(8,128)(2,1)} %collective-permute-done.9.near_w), channel_id=1, source_target_pairs={{0,1},{1,0},{2,3},{3,2},{4,5},{5,4},{6,7},{7,6},{8,9},{9,8},{10,11... | collective-permute-start | bytes 1179656 | tf_op jit(solution)/shard_map/ppermute | solution.py:508
  30.9 39.5 %collective-permute-start.13 = (bf16[3,128,512]{2,1,0:T(8,128)(2,1)S(1)}, bf16[3,128,512]{2,1,0:T(8,128)(2,1)S(1)}, u32[]{:S(2)}, u32[]{:S(2)}) collective-permute-start(bf16[3,128,512]{2,1,0:T(8,128)(2,1)S(1)} %collective-permute-done.12.near_w), channel_id=1, source_target_pairs={{0,1},{1,0},{2,3},{3,2},{4,5},{5,4},{6,7},{7,6},{8,9},{9,8},{10,11... | collective-permute-start | bytes 1179656 | tf_op jit(solution)/shard_map/ppermute | solution.py:508
  33.1 17.9 %collective-permute-start.4 = (bf16[128,1024]{1,0:T(8,128)(2,1)}, bf16[128,1024]{1,0:T(8,128)(2,1)}, u32[]{:S(2)}, u32[]{:S(2)}) collective-permute-start(bf16[128,1024]{1,0:T(8,128)(2,1)} %refs_3_.1), channel_id=1, source_target_pairs={{0,16},{16,0},{1,17},{17,1},{2,18},{18,2},{3,19},{19,3},{4,20},{20... | collective-permute-start | bytes 786440 | tf_op jit(solution)/shard_map/ppermute | solution.py:484
  35.1 7.4 %collective-permute-start.5 = (bf16[128,128]{1,0:T(8,128)(2,1)S(1)}, bf16[128,128]{1,0:T(8,128)(2,1)S(1)}, u32[]{:S(2)}, u32[]{:S(2)}) collective-permute-start(bf16[128,128]{1,0:T(8,128)(2,1)S(1)} %broadcast_select_fusion.2.refs_4_), channel_id=1, source_target_pairs={{0,16},{16,0},{1,17},{17,1},{2,18},{18,2},{3,19},{19,3},{4,20},{20... | collective-permute-start | bytes 98312 | tf_op jit(solution)/shard_map/ppermute | solution.py:498
  43.1 4.3 %collective-permute-start = (bf16[256,128]{1,0:T(8,128)(2,1)S(1)}, bf16[256,128]{1,0:T(8,128)(2,1)S(1)}, u32[]{:S(2)}, u32[]{:S(2)}) collective-permute-start(bf16[256,128]{1,0:T(8,128)(2,1)S(1)} %slice_select_fusion), channel_id=1, source_target_pairs={{0,16},{16,0},{1,17},{17,1},{2,18},{18,2},{3,19},{19,3},{4,20},{20... | collective-permute-start | bytes 196616 | tf_op jit(solution)/shard_map/ppermute | solution.py:487
  49.2 9.9 %collective-permute-start.8 = (f32[3,256]{1,0:T(4,128)}, f32[3,256]{1,0:T(4,128)S(1)}, u32[]{:S(2)}, u32[]{:S(2)}) collective-permute-start(f32[3,256]{1,0:T(4,128)} %biases.5), channel_id=1, source_target_pairs={{0,16},{16,0},{1,17},{17,1},{2,18},{18,2},{3,19},{19,3},{4,20},{20... | collective-permute-start | bytes 9224 | tf_op jit(solution)/shard_map/ppermute | solution.py:499
  72.4 2.1 %collective-permute-start.14 = (bf16[128,1024]{1,0:T(8,128)(2,1)S(1)}, bf16[128,1024]{1,0:T(8,128)(2,1)S(1)}, u32[]{:S(2)}, u32[]{:S(2)}) collective-permute-start(bf16[128,1024]{1,0:T(8,128)(2,1)S(1)} %get-tuple-element.33), channel_id=1, source_target_pairs={{0,1},{1,0},{2,3},{3,2},{4,5},{5,4},{6,7},{7,6},{8,9},{9,8},{10,11... | collective-permute-start | bytes 786440 | tf_op jit(solution)/shard_map/ppermute | solution.py:551
  72.4 2.0 %collective-permute-start.15 = (bf16[1024,128]{1,0:T(8,128)(2,1)S(1)}, bf16[1024,128]{1,0:T(8,128)(2,1)S(1)}, u32[]{:S(2)}, u32[]{:S(2)}) collective-permute-start(bf16[1024,128]{1,0:T(8,128)(2,1)S(1)} %get-tuple-element.35), channel_id=1, source_target_pairs={{0,1},{1,0},{2,3},{3,2},{4,5},{5,4},{6,7},{7,6},{8,9},{9,8},{10,11... | collective-permute-start | bytes 786440 | tf_op jit(solution)/shard_map/ppermute | solution.py:552
  78.2 11.1 %collective-permute-start.17 = (bf16[72,1024]{1,0:T(8,128)(2,1)S(1)}, bf16[72,1024]{1,0:T(8,128)(2,1)S(1)}, u32[]{:S(2)}, u32[]{:S(2)}) collective-permute-start(bf16[72,1024]{1,0:T(8,128)(2,1)S(1)} %attend_send.3), channel_id=1, source_target_pairs={{0,2},{1,3},{2,0},{3,1},{4,6},{5,7},{6,4},{7,5},{8,10},{9,11},{10,... | collective-permute-start | bytes 442376 | tf_op jit(solution)/shard_map/ppermute | solution.py:556
  85.7 9.4 %collective-permute-start.16 = (bf16[72,1024]{1,0:T(8,128)(2,1)S(1)}, bf16[72,1024]{1,0:T(8,128)(2,1)S(1)}, u32[]{:S(2)}, u32[]{:S(2)}) collective-permute-start(bf16[72,1024]{1,0:T(8,128)(2,1)S(1)} %attend_send.2), channel_id=1, source_target_pairs={{0,2},{1,3},{2,0},{3,1},{4,6},{5,7},{6,4},{7,5},{8,10},{9,11},{10,... | collective-permute-start | bytes 442376 | tf_op jit(solution)/shard_map/ppermute | solution.py:556
  89.4 5.8 %collective-permute-start.18 = (bf16[72,1024]{1,0:T(8,128)(2,1)S(1)}, bf16[72,1024]{1,0:T(8,128)(2,1)S(1)}, u32[]{:S(2)}, u32[]{:S(2)}) collective-permute-start(bf16[72,1024]{1,0:T(8,128)(2,1)S(1)} %shard_map.112), channel_id=1, source_target_pairs={{0,4},{1,5},{2,6},{3,7},{4,0},{5,1},{6,2},{7,3},{8,12},{9,13},{10,... | collective-permute-start | bytes 442376 | tf_op jit(solution)/shard_map/ppermute | solution.py:556
  95.4 9.1 %collective-permute-start.19 = (bf16[72,1024]{1,0:T(8,128)(2,1)S(1)}, bf16[72,1024]{1,0:T(8,128)(2,1)S(1)}, u32[]{:S(2)}, u32[]{:S(2)}) collective-permute-start(bf16[72,1024]{1,0:T(8,128)(2,1)S(1)} %shard_map.113.mine), channel_id=1, source_target_pairs={{0,8},{1,9},{2,10},{3,11},{4,12},{5,13},{6,14},{7,15},{8,0},{9,1},... | collective-permute-start | bytes 442376 | tf_op jit(solution)/shard_map/ppermute | solution.py:556
  104.6 6.4 %collective-permute-start.20 = (bf16[64,1024]{1,0:T(8,128)(2,1)S(1)}, bf16[64,1024]{1,0:T(8,128)(2,1)S(1)}, u32[]{:S(2)}, u32[]{:S(2)}) collective-permute-start(bf16[64,1024]{1,0:T(8,128)(2,1)S(1)} %shard_map.114.refs_0_), channel_id=1, source_target_pairs={{0,4},{1,5},{2,6},{3,7},{4,0},{5,1},{6,2},{7,3},{8,12},{9,13},{10,... | collective-permute-start | bytes 393224 | tf_op jit(solution)/shard_map/ppermute | solution.py:556
  105.1 6.4 %collective-permute-start.21 = (bf16[64,1024]{1,0:T(8,128)(2,1)S(1)}, bf16[64,1024]{1,0:T(8,128)(2,1)S(1)}, u32[]{:S(2)}, u32[]{:S(2)}) collective-permute-start(bf16[64,1024]{1,0:T(8,128)(2,1)S(1)} %shard_map.114.refs_0_), channel_id=1, source_target_pairs={{0,2},{1,3},{2,0},{3,1},{4,6},{5,7},{6,4},{7,5},{8,10},{9,11},{10,... | collective-permute-start | bytes 393224 | tf_op jit(solution)/shard_map/ppermute | solution.py:556
  106.1 6.9 %collective-permute-start.22 = (bf16[64,1024]{1,0:T(8,128)(2,1)S(1)}, bf16[64,1024]{1,0:T(8,128)(2,1)S(1)}, u32[]{:S(2)}, u32[]{:S(2)}) collective-permute-start(bf16[64,1024]{1,0:T(8,128)(2,1)S(1)} %shard_map.114.refs_0_), channel_id=1, source_target_pairs={{0,6},{1,7},{2,4},{3,5},{4,2},{5,3},{6,0},{7,1},{8,14},{9,15},{10,... | collective-permute-start | bytes 393224 | tf_op jit(solution)/shard_map/ppermute | solution.py:556
  108.1 4.9 %collective-permute-start.23 = (bf16[64,1024]{1,0:T(8,128)(2,1)S(1)}, bf16[64,1024]{1,0:T(8,128)(2,1)S(1)}, u32[]{:S(2)}, u32[]{:S(2)}) collective-permute-start(bf16[64,1024]{1,0:T(8,128)(2,1)S(1)} %shard_map.114.refs_0_), channel_id=1, source_target_pairs={{0,1},{1,0},{2,3},{3,2},{4,5},{5,4},{6,7},{7,6},{8,9},{9,8},{10,11... | collective-permute-start | bytes 393224 | tf_op jit(solution)/shard_map/ppermute | solution.py:556
  111.0 2.1 %collective-permute-start.24 = (bf16[64,1024]{1,0:T(8,128)(2,1)S(1)}, bf16[64,1024]{1,0:T(8,128)(2,1)S(1)}, u32[]{:S(2)}, u32[]{:S(2)}) collective-permute-start(bf16[64,1024]{1,0:T(8,128)(2,1)S(1)} %collective-permute-done.20.refs_1_), channel_id=1, source_target_pairs={{0,1},{1,0},{2,3},{3,2},{4,5},{5,4},{6,7},{7,6},{8,9},{9,8},{10,11... | collective-permute-start | bytes 393224 | tf_op jit(solution)/shard_map/ppermute | solution.py:556
  111.5 1.6 %collective-permute-start.25 = (bf16[64,1024]{1,0:T(8,128)(2,1)S(1)}, bf16[64,1024]{1,0:T(8,128)(2,1)S(1)}, u32[]{:S(2)}, u32[]{:S(2)}) collective-permute-start(bf16[64,1024]{1,0:T(8,128)(2,1)S(1)} %collective-permute-done.21.refs_2_), channel_id=1, source_target_pairs={{0,1},{1,0},{2,3},{3,2},{4,5},{5,4},{6,7},{7,6},{8,9},{9,8},{10,11... | collective-permute-start | bytes 393224 | tf_op jit(solution)/shard_map/ppermute | solution.py:556
  (17 other events, 219.8 us)

commit v9 on v5

--- a/solution.py
+++ b/solution.py
@@ -474,15 +474,19 @@
 
     other_rec = lax.ppermute(recording, "sensor", across)
     other_w = lax.ppermute(spatial_w, "sensor", across)
-    tail = lax.ppermute(
-        recording[:, frames - EDGE :], "tm", [(i, i + 1) for i in range(blocks - 1)]
-    )
-    head = lax.ppermute(recording[:, :EDGE], "tm", [(i + 1, i) for i in range(blocks - 1)])
+    even = core[0] == 0
+    last_part, first_part = recording[:, frames - EDGE :], recording[:, :EDGE]
+    links = [(i, i + 1) for i in range(1, blocks - 1, 2)]
+    outer = lax.ppermute(
+        jnp.where(even, first_part, last_part), "tm",
+        links + [(j, i) for i, j in links],
+    )
+    inner = lax.ppermute(jnp.where(even, last_part, first_part), "tm", twins)
     lane = jnp.arange(EDGE, dtype=jnp.int32)[None, :]
-    edge = jnp.where(lane < HALF, head, tail)
+    edge = jnp.where((lane < HALF) == even, inner, outer)
     other_edge = lax.ppermute(edge, "sensor", across)
     other_b = lax.ppermute(conv_b, "sensor", across)
-    later_w = lax.optimization_barrier((conv_w, head))[0]
+    later_w = lax.optimization_barrier((conv_w, edge))[0]
     mine = [
         lax.dynamic_slice(
             later_w if layer else conv_w, (layer, 0, core[0] * half, 0), (1, 3, half, ch)
@@ -493,7 +497,8 @@
     far = [lax.ppermute(near[n], "tm", twins) for n in range(LAYERS)]
     asked = simple(ask_kernel, jax.ShapeDtypeStruct((latents, half), bf16), (core,), (queries,))
     half_shape = jax.ShapeDtypeStruct((ch_loc, span), bf16)
-    parts = (spatial_w, other_w, recording, other_rec, edge, other_edge)
+    fixed = [pltpu.with_memory_space_constraint(v, pltpu.HBM) for v in (spatial_w, recording)]
+    parts = (fixed[0], other_w, fixed[1], other_rec, edge, other_edge)
     own_h, other_h = simple(
         first_kernel, [half_shape, half_shape], (side,), parts,
         [VMEM(part.shape, bf16) for part in parts] + [pltpu.SemaphoreType.DMA((len(parts),))],
@@ -564,7 +569,7 @@
         bit *= 2
     above = flip(done, 4)
     beside = flip(done, 2)
-    corner = flip(above, 2)
+    corner = flip(done, 6)
     pieces = [done, above, beside, corner]
     pieces += [flip(piece, 1) for piece in pieces]
     attended = simple(

time: 116 us -> 116 us (level)
  starting transfers between devices: 30 us -> 36.9 us
  local copies, waits for them, and re-layouts: 11.3 us -> 7.29 us
  waiting for transfers between devices: 38 us -> 35.1 us
    ppermute x3, starting transfers between devices: 2.96 us -> 11.9 us  [pair_device(): far = [lax.ppermute(near[n], 'tm', twins) for n in range(LAYERS)]]
    ppermute x3, waiting for transfers between devices: 17.4 us -> 11.4 us  [pair_device(): near = [lax.ppermute(mine[n], 'sensor', across) for n in range(LAYERS)]]
    ppermute x1, waiting for transfers between devices: 2.1 us -> 7.36 us  [pair_device(): other_edge = lax.ppermute(edge, 'sensor', across)]
    ppermute x2, starting transfers between devices: 4.34 us -> 1.2 us  [the longest x1 0.65 us: pair_device(): lax.ppermute(jnp.where(even, first_part, last_part), 'tm', links + [(j, i...]
    ppermute x11, starting transfers between devices: 10.4 us -> 13 us  [flip(): return lax.ppermute(value, 'tm', [(i, i ^ bit) for i in range(blocks)])]
    unnamed x34 -> x24, local copies, waits for them, and re-layouts: 7.52 us -> 5.05 us
    ppermute x1, starting transfers between devices: 1.74 us -> 0.02 us  [pair_device(): other_edge = lax.ppermute(edge, 'sensor', across)]
    slice x1 -> x0, local copies, waits for them, and re-layouts: 1.55 us -> none  [pair_device(): recording[:, frames - EDGE:]]
  transfers between devices with their start and end apart: 26 -> 26, of which waited for: 11 -> 12; matrix products, arithmetic and copies ran while one was open for 3% -> 2% of each run, Pallas kernels for 23% -> 23%
where the time goes in v9:
time: 116 us; the launch traced here: 115 us
  starting transfers between devices  36.9 us (32%)
  waiting for transfers between devices  35.1 us (30%)
  Pallas kernels  33.4 us (29%)
  local copies, waits for them, and re-layouts  7.29 us (6%)
  between operations  1.58 us (1%)
    pallas_call x12, Pallas kernels, simple(): pl.pallas_call(kernel, grid=(1,), out_shape=out_shape, in_specs=smem(len(...  19.7 us
    pallas_call x4, Pallas kernels, attend(): pl.pallas_call(functools.partial(attend_kernel, packed), out_shape=out_sh...  13.8 us
    ppermute x11, starting transfers between devices, flip(): return lax.ppermute(value, 'tm', [(i, i ^ bit) for i in range(blocks)])  13 us
    ppermute x11, waiting for transfers between devices, flip(): return lax.ppermute(value, 'tm', [(i, i ^ bit) for i in range(blocks)])  12.3 us
    ppermute x3, starting transfers between devices, pair_device(): far = [lax.ppermute(near[n], 'tm', twins) for n in range(LAYERS)]  11.9 us
    ppermute x3, waiting for transfers between devices, pair_device(): near = [lax.ppermute(mine[n], 'sensor', across) for n in range(LAYERS)]  11.4 us
    ppermute x1, waiting for transfers between devices, pair_device(): other_edge = lax.ppermute(edge, 'sensor', across)  7.36 us
    unnamed x24, local copies, waits for them, and re-layouts  5.05 us
  transfers between devices with their start and end apart: 26, of which 12 were waited for; matrix products, arithmetic and copies ran while one was open for 2% of the time, Pallas kernels for 23%

profile of v9, /device:TPU:0, one launch (start us, length us, event | category | flops | bytes accessed | tf_op | source)
XLA Modules:
  0.0 115.3 jit_solution(7595186133499255592)
XLA Ops:
  3.8 2.6 %collective-permute-start.5 = (bf16[3,128,512]{2,1,0:T(8,128)(2,1)S(1)}, bf16[3,128,512]{2,1,0:T(8,128)(2,1)S(1)}, u32[]{:S(2)}, u32[]{:S(2)}) collective-permute-start(bf16[3,128,512]{2,1,0:T(8,128)(2,1)S(1)} %dynamic-slice_bitcast_fusion.2), channel_id=1, source_target_pairs={{0,16},{16,0},{1,17},{17,1},{2,18},{18,2},{3,19},{19,3},{4,20},{20... | collective-permute-start | bytes 1179656 | tf_op jit(solution)/shard_map/ppermute | solution.py:496
  9.8 4.3 %collective-permute-done.5.near_w = bf16[3,128,512]{2,1,0:T(8,128)(2,1)S(1)} collective-permute-done((bf16[3,128,512]{2,1,0:T(8,128)(2,1)S(1)}, bf16[3,128,512]{2,1,0:T(8,128)(2,1)S(1)}, u32[]{:S(2)}, u32[]{:S(2)}) %collective-permute-start.5) | collective-permute-done | bytes 393248 | tf_op jit(solution)/shard_map/ppermute | solution.py:496
  14.1 4.9 %collective-permute-start.6 = (bf16[3,128,512]{2,1,0:T(8,128)(2,1)S(1)}, bf16[3,128,512]{2,1,0:T(8,128)(2,1)}, u32[]{:S(2)}, u32[]{:S(2)}) collective-permute-start(bf16[3,128,512]{2,1,0:T(8,128)(2,1)S(1)} %collective-permute-done.5.near_w), channel_id=1, source_target_pairs={{0,1},{1,0},{2,3},{3,2},{4,5},{5,4},{6,7},{7,6},{8,9},{9,8},{10,11... | collective-permute-start | bytes 1179656 | tf_op jit(solution)/shard_map/ppermute | solution.py:497
  19.0 3.5 %collective-permute-done.8.near_w = bf16[3,128,512]{2,1,0:T(8,128)(2,1)} collective-permute-done((bf16[3,128,512]{2,1,0:T(8,128)(2,1)S(1)}, bf16[3,128,512]{2,1,0:T(8,128)(2,1)}, u32[]{:S(2)}, u32[]{:S(2)}) %collective-permute-start.8) | collective-permute-done | bytes 393248 | tf_op jit(solution)/shard_map/ppermute | solution.py:496
  22.5 4.8 %collective-permute-start.9 = (bf16[3,128,512]{2,1,0:T(8,128)(2,1)}, bf16[3,128,512]{2,1,0:T(8,128)(2,1)}, u32[]{:S(2)}, u32[]{:S(2)}) collective-permute-start(bf16[3,128,512]{2,1,0:T(8,128)(2,1)} %collective-permute-done.8.near_w), channel_id=1, source_target_pairs={{0,1},{1,0},{2,3},{3,2},{4,5},{5,4},{6,7},{7,6},{8,9},{9,8},{10,11... | collective-permute-start | bytes 1179656 | tf_op jit(solution)/shard_map/ppermute | solution.py:497
  27.3 3.6 %collective-permute-done.11.near_w = bf16[3,128,512]{2,1,0:T(8,128)(2,1)S(1)} collective-permute-done((bf16[3,128,512]{2,1,0:T(8,128)(2,1)S(1)}, bf16[3,128,512]{2,1,0:T(8,128)(2,1)S(1)}, u32[]{:S(2)}, u32[]{:S(2)}) %collective-permute-start.11) | collective-permute-done | bytes 393248 | tf_op jit(solution)/shard_map/ppermute | solution.py:496
  30.9 2.2 %collective-permute-start.12 = (bf16[3,128,512]{2,1,0:T(8,128)(2,1)S(1)}, bf16[3,128,512]{2,1,0:T(8,128)(2,1)S(1)}, u32[]{:S(2)}, u32[]{:S(2)}) collective-permute-start(bf16[3,128,512]{2,1,0:T(8,128)(2,1)S(1)} %collective-permute-done.11.near_w), channel_id=1, source_target_pairs={{0,1},{1,0},{2,3},{3,2},{4,5},{5,4},{6,7},{7,6},{8,9},{9,8},{10,11... | collective-permute-start | bytes 1179656 | tf_op jit(solution)/shard_map/ppermute | solution.py:497
  35.1 7.4 %collective-permute-done.4.refs_5_ = bf16[128,128]{1,0:T(8,128)(2,1)S(1)} collective-permute-done((bf16[128,128]{1,0:T(8,128)(2,1)S(1)}, bf16[128,128]{1,0:T(8,128)(2,1)S(1)}, u32[]{:S(2)}, u32[]{:S(2)}) %collective-permute-start.4) | collective-permute-done | bytes 32800 | tf_op jit(solution)/shard_map/ppermute | solution.py:487
  44.8 3.4 %collective-permute-done.refs_1_ = bf16[512,128]{1,0:T(8,128)(2,1)S(1)} collective-permute-done((bf16[512,128]{1,0:T(8,128)(2,1)}, bf16[512,128]{1,0:T(8,128)(2,1)S(1)}, u32[]{:S(2)}, u32[]{:S(2)}) %collective-permute-start) | collective-permute-done | bytes 131104 | tf_op jit(solution)/shard_map/ppermute | solution.py:476
  56.5 2.9 %shard_map.105 = (bf16[256,1152]{1,0:T(8,128)(2,1)S(1)}, bf16[3,512,1152]{2,1,0:T(8,128)(2,1)S(1)}) custom-call(s32[3]{0:T(128)S(1)} %copy-done.11, s32[1]{0:T(128)} %bitcast.side, s32[1]{0:T(128)} %bitcast.1.place, bf16[256,1152]{1,0:T(8,128)(2,1)S(1)} %get-tuple-element.22.mine, bf16[256,1152]{1,0:T(8,128)(2,1)S(1)} %get-tuple-element.23.theirs, ...), custom_call_target="tpu_custom_call" | custom-call | tf_op jit(solution)/shard_map/pallas_call | solution.py:446
  59.4 2.5 %shard_map.106.theirs = bf16[256,1152]{1,0:T(8,128)(2,1)S(1)} custom-call(s32[1]{0:T(128)S(6)} %and.14.core, s32[1]{0:T(128)} %bitcast.1.place, bf16[256,1152]{1,0:T(8,128)(2,1)S(1)} %get-tuple-element.23.theirs, bf16[3,512,1152]{2,1,0:T(8,128)(2,1)S(1)} %get-tuple-element.25.taps, bf16[3,128,512]{2,1,0:T(8,128)(2,1)S(1)} %collective-permute-done.5.near_w, ...), custom_call_target="tpu_custom_call" | custom-call | tf_op jit(solution)/shard_map/pallas_call | solution.py:446
  61.9 2.9 %shard_map.107 = (bf16[256,1152]{1,0:T(8,128)(2,1)S(1)}, bf16[3,512,1152]{2,1,0:T(8,128)(2,1)S(1)}) custom-call(s32[3]{0:T(128)S(1)} %copy-done.11, s32[1]{0:T(128)} %bitcast.side, s32[1]{0:T(128)} %bitcast.1.place, bf16[256,1152]{1,0:T(8,128)(2,1)S(1)} %get-tuple-element.24.mine, bf16[256,1152]{1,0:T(8,128)(2,1)S(1)} %shard_map.106.theirs, ...), custom_call_target="tpu_custom_call" | custom-call | tf_op jit(solution)/shard_map/pallas_call | solution.py:446
  64.8 2.6 %shard_map.108.theirs = bf16[256,1152]{1,0:T(8,128)(2,1)S(1)} custom-call(s32[1]{0:T(128)S(6)} %and.14.core, s32[1]{0:T(128)} %bitcast.1.place, bf16[256,1152]{1,0:T(8,128)(2,1)S(1)} %shard_map.106.theirs, bf16[3,512,1152]{2,1,0:T(8,128)(2,1)S(1)} %get-tuple-element.27.taps, bf16[3,128,512]{2,1,0:T(8,128)(2,1)} %collective-permute-done.8.near_w, ...), custom_call_target="tpu_custom_call" | custom-call | tf_op jit(solution)/shard_map/pallas_call | solution.py:446
  67.4 3.3 %shard_map.109 = (bf16[256,1024]{1,0:T(8,128)(2,1)}, bf16[256,1024]{1,0:T(8,128)(2,1)S(1)}, bf16[3,512,1152]{2,1,0:T(8,128)(2,1)S(1)}) custom-call(s32[3]{0:T(128)S(1)} %copy-done.11, s32[1]{0:T(128)} %bitcast.side, s32[1]{0:T(128)} %bitcast.1.place, bf16[256,1152]{1,0:T(8,128)(2,1)S(1)} %get-tuple-element.26.mine, bf16[256,1152]{1,0:T(8,128)(2,1)S(1)} %shard_map.108.theirs, ...), custom_call_target="tpu_custom_call" | custom-call | tf_op jit(solution)/shard_map/pallas_call | solution.py:446
  74.7 3.6 %attend_send.3 = bf16[72,1024]{1,0:T(8,128)(2,1)S(1)} custom-call(s32[1]{0:T(128)S(6)} %sub.8.which, s32[1]{0:T(128)S(6)} %sub.9.half, s32[1]{0:T(128)S(6)} %copy.11.valid_own, s32[1]{0:T(128)} %collective-permute-done.10.valid_rec, bf16[128,1024]{1,0:T(8,128)(2,1)S(1)} %get-tuple-element.32.key_own, bf16[128,1024]{1,0:T(8,128)(2,1)S(1)} %collective-permute-done.13.key_rec, ...), custom_call_target="tpu_custom_call" | custom-call | tf_op jit(solution)/shard_map/attend_send/pallas_call | solution.py:413
  78.3 4.1 %collective-permute-start.16 = (bf16[72,1024]{1,0:T(8,128)(2,1)S(1)}, bf16[72,1024]{1,0:T(8,128)(2,1)S(1)}, u32[]{:S(2)}, u32[]{:S(2)}) collective-permute-start(bf16[72,1024]{1,0:T(8,128)(2,1)S(1)} %attend_send.3), channel_id=1, source_target_pairs={{0,2},{1,3},{2,0},{3,1},{4,6},{5,7},{6,4},{7,5},{8,10},{9,11},{10,... | collective-permute-start | bytes 442376 | tf_op jit(solution)/shard_map/ppermute | solution.py:544
  82.4 3.4 %attend_send.2 = bf16[72,1024]{1,0:T(8,128)(2,1)S(1)} custom-call(s32[1]{0:T(128)S(6)} %sub.8.which, s32[1]{0:T(128)S(6)} %and.16.half.lower, s32[1]{0:T(128)S(6)} %copy.11.valid_own, s32[1]{0:T(128)} %collective-permute-done.10.valid_rec, bf16[128,1024]{1,0:T(8,128)(2,1)S(1)} %get-tuple-element.32.key_own, ...), custom_call_target="tpu_custom_call" | custom-call | tf_op jit(solution)/shard_map/attend_send/pallas_call | solution.py:413
  85.9 3.4 %attend_keep.3 = (f32[1,1024]{1,0:T(1,128)S(1)}, f32[1,1024]{1,0:T(1,128)S(1)}, f32[64,1024]{1,0:T(8,128)S(1)}) custom-call(s32[1]{0:T(128)S(6)} %and.15.which.cross, s32[1]{0:T(128)S(6)} %sub.9.half, s32[1]{0:T(128)S(6)} %copy.11.valid_own, s32[1]{0:T(128)} %collective-permute-done.10.valid_rec, bf16[128,1024]{1,0:T(8,128)(2,1)S(1)} %get-tuple-element.32.key_own, ...), custom_call_target="tpu_custom_call" | custom-call | tf_op jit(solution)/shard_map/attend_keep/pallas_call | solution.py:413
  89.5 2.3 %collective-permute-start.17 = (bf16[72,1024]{1,0:T(8,128)(2,1)S(1)}, bf16[72,1024]{1,0:T(8,128)(2,1)S(1)}, u32[]{:S(2)}, u32[]{:S(2)}) collective-permute-start(bf16[72,1024]{1,0:T(8,128)(2,1)S(1)} %shard_map.112), channel_id=1, source_target_pairs={{0,4},{1,5},{2,6},{3,7},{4,0},{5,1},{6,2},{7,3},{8,12},{9,13},{10,... | collective-permute-start | bytes 442376 | tf_op jit(solution)/shard_map/ppermute | solution.py:544
  91.8 3.4 %attend_keep.2 = (f32[1,1024]{1,0:T(1,128)S(1)}, f32[1,1024]{1,0:T(1,128)S(1)}, f32[64,1024]{1,0:T(8,128)S(1)}) custom-call(s32[1]{0:T(128)S(6)} %and.15.which.cross, s32[1]{0:T(128)S(6)} %and.16.half.lower, s32[1]{0:T(128)S(6)} %copy.11.valid_own, s32[1]{0:T(128)} %collective-permute-done.10.valid_rec, bf16[128,1024]{1,0:T(8,128)(2,1)S(1)} %get-tuple-element.32.key_own, ...), custom_call_target="tpu_custom_call" | custom-call | tf_op jit(solution)/shard_map/attend_keep/pallas_call | solution.py:413
  95.5 2.8 %collective-permute-start.18 = (bf16[72,1024]{1,0:T(8,128)(2,1)S(1)}, bf16[72,1024]{1,0:T(8,128)(2,1)S(1)}, u32[]{:S(2)}, u32[]{:S(2)}) collective-permute-start(bf16[72,1024]{1,0:T(8,128)(2,1)S(1)} %shard_map.113.mine), channel_id=1, source_target_pairs={{0,8},{1,9},{2,10},{3,11},{4,12},{5,13},{6,14},{7,15},{8,0},{9,1},... | collective-permute-start | bytes 442376 | tf_op jit(solution)/shard_map/ppermute | solution.py:544
  98.4 6.2 %collective-permute-done.18.theirs = bf16[72,1024]{1,0:T(8,128)(2,1)S(1)} collective-permute-done((bf16[72,1024]{1,0:T(8,128)(2,1)S(1)}, bf16[72,1024]{1,0:T(8,128)(2,1)S(1)}, u32[]{:S(2)}, u32[]{:S(2)}) %collective-permute-start.18) | collective-permute-done | bytes 147488 | tf_op jit(solution)/shard_map/ppermute | solution.py:544
  106.1 2.1 %collective-permute-start.21 = (bf16[64,1024]{1,0:T(8,128)(2,1)S(1)}, bf16[64,1024]{1,0:T(8,128)(2,1)S(1)}, u32[]{:S(2)}, u32[]{:S(2)}) collective-permute-start(bf16[64,1024]{1,0:T(8,128)(2,1)S(1)} %shard_map.114.refs_0_), channel_id=1, source_target_pairs={{0,6},{1,7},{2,4},{3,5},{4,2},{5,3},{6,0},{7,1},{8,14},{9,15},{10,... | collective-permute-start | bytes 393224 | tf_op jit(solution)/shard_map/ppermute | solution.py:544
  108.2 2.8 %collective-permute-done.19.refs_1_ = bf16[64,1024]{1,0:T(8,128)(2,1)S(1)} collective-permute-done((bf16[64,1024]{1,0:T(8,128)(2,1)S(1)}, bf16[64,1024]{1,0:T(8,128)(2,1)S(1)}, u32[]{:S(2)}, u32[]{:S(2)}) %collective-permute-start.19) | collective-permute-done | bytes 131104 | tf_op jit(solution)/shard_map/ppermute | solution.py:544
  (73 shorter events, 28.7 us)
Async XLA Ops:
  1.6 4.8 %collective-permute-start.2 = (bf16[128,128]{1,0:T(8,128)(2,1)S(1)}, bf16[128,128]{1,0:T(8,128)(2,1)S(1)}, u32[]{:S(2)}, u32[]{:S(2)}) collective-permute-start(bf16[128,128]{1,0:T(8,128)(2,1)S(1)} %get-tuple-element.45), channel_id=1, source_target_pairs={{0,1},{1,0},{2,3},{3,2},{4,5},{5,4},{6,7},{7,6},{8,9},{9,8},{10,11... | collective-permute-start | bytes 98312 | tf_op jit(solution)/shard_map/ppermute | solution.py:484
  2.1 4.3 %collective-permute-start.3 = (bf16[128,128]{1,0:T(8,128)(2,1)S(1)}, bf16[128,128]{1,0:T(8,128)(2,1)S(1)}, u32[]{:S(2)}, u32[]{:S(2)}) collective-permute-start(bf16[128,128]{1,0:T(8,128)(2,1)S(1)} %get-tuple-element.44), channel_id=1, source_target_pairs={{1,2},{3,4},{5,6},{7,8},{9,10},{11,12},{13,14},{2,1},{4,3},{6,5},{... | collective-permute-start | bytes 98312 | tf_op jit(solution)/shard_map/ppermute | solution.py:480
  3.8 10.2 %collective-permute-start.5 = (bf16[3,128,512]{2,1,0:T(8,128)(2,1)S(1)}, bf16[3,128,512]{2,1,0:T(8,128)(2,1)S(1)}, u32[]{:S(2)}, u32[]{:S(2)}) collective-permute-start(bf16[3,128,512]{2,1,0:T(8,128)(2,1)S(1)} %dynamic-slice_bitcast_fusion.2), channel_id=1, source_target_pairs={{0,16},{16,0},{1,17},{17,1},{2,18},{18,2},{3,19},{19,3},{4,20},{20... | collective-permute-start | bytes 1179656 | tf_op jit(solution)/shard_map/ppermute | solution.py:496
  7.7 14.9 %collective-permute-start.8 = (bf16[3,128,512]{2,1,0:T(8,128)(2,1)S(1)}, bf16[3,128,512]{2,1,0:T(8,128)(2,1)}, u32[]{:S(2)}, u32[]{:S(2)}) collective-permute-start(bf16[3,128,512]{2,1,0:T(8,128)(2,1)S(1)} %get-tuple-element.43), channel_id=1, source_target_pairs={{0,16},{16,0},{1,17},{17,1},{2,18},{18,2},{3,19},{19,3},{4,20},{20... | collective-permute-start | bytes 1179656 | tf_op jit(solution)/shard_map/ppermute | solution.py:496
  7.8 23.1 %collective-permute-start.11 = (bf16[3,128,512]{2,1,0:T(8,128)(2,1)S(1)}, bf16[3,128,512]{2,1,0:T(8,128)(2,1)S(1)}, u32[]{:S(2)}, u32[]{:S(2)}) collective-permute-start(bf16[3,128,512]{2,1,0:T(8,128)(2,1)S(1)} %get-tuple-element.42), channel_id=1, source_target_pairs={{0,16},{16,0},{1,17},{17,1},{2,18},{18,2},{3,19},{19,3},{4,20},{20... | collective-permute-start | bytes 1179656 | tf_op jit(solution)/shard_map/ppermute | solution.py:496
  14.1 45.3 %collective-permute-start.6 = (bf16[3,128,512]{2,1,0:T(8,128)(2,1)S(1)}, bf16[3,128,512]{2,1,0:T(8,128)(2,1)}, u32[]{:S(2)}, u32[]{:S(2)}) collective-permute-start(bf16[3,128,512]{2,1,0:T(8,128)(2,1)S(1)} %collective-permute-done.5.near_w), channel_id=1, source_target_pairs={{0,1},{1,0},{2,3},{3,2},{4,5},{5,4},{6,7},{7,6},{8,9},{9,8},{10,11... | collective-permute-start | bytes 1179656 | tf_op jit(solution)/shard_map/ppermute | solution.py:497
  22.5 42.2 %collective-permute-start.9 = (bf16[3,128,512]{2,1,0:T(8,128)(2,1)}, bf16[3,128,512]{2,1,0:T(8,128)(2,1)}, u32[]{:S(2)}, u32[]{:S(2)}) collective-permute-start(bf16[3,128,512]{2,1,0:T(8,128)(2,1)} %collective-permute-done.8.near_w), channel_id=1, source_target_pairs={{0,1},{1,0},{2,3},{3,2},{4,5},{5,4},{6,7},{7,6},{8,9},{9,8},{10,11... | collective-permute-start | bytes 1179656 | tf_op jit(solution)/shard_map/ppermute | solution.py:497
  30.9 39.8 %collective-permute-start.12 = (bf16[3,128,512]{2,1,0:T(8,128)(2,1)S(1)}, bf16[3,128,512]{2,1,0:T(8,128)(2,1)S(1)}, u32[]{:S(2)}, u32[]{:S(2)}) collective-permute-start(bf16[3,128,512]{2,1,0:T(8,128)(2,1)S(1)} %collective-permute-done.11.near_w), channel_id=1, source_target_pairs={{0,1},{1,0},{2,3},{3,2},{4,5},{5,4},{6,7},{7,6},{8,9},{9,8},{10,11... | collective-permute-start | bytes 1179656 | tf_op jit(solution)/shard_map/ppermute | solution.py:497
  33.1 17.6 %collective-permute-start.1 = (bf16[128,1024]{1,0:T(8,128)(2,1)}, bf16[128,1024]{1,0:T(8,128)(2,1)}, u32[]{:S(2)}, u32[]{:S(2)}) collective-permute-start(bf16[128,1024]{1,0:T(8,128)(2,1)} %refs_2_.1), channel_id=1, source_target_pairs={{0,16},{16,0},{1,17},{17,1},{2,18},{18,2},{3,19},{19,3},{4,20},{20... | collective-permute-start | bytes 786440 | tf_op jit(solution)/shard_map/ppermute | solution.py:475
  35.1 7.4 %collective-permute-start.4 = (bf16[128,128]{1,0:T(8,128)(2,1)S(1)}, bf16[128,128]{1,0:T(8,128)(2,1)S(1)}, u32[]{:S(2)}, u32[]{:S(2)}) collective-permute-start(bf16[128,128]{1,0:T(8,128)(2,1)S(1)} %broadcast_select_fusion.2.refs_4_), channel_id=1, source_target_pairs={{0,16},{16,0},{1,17},{17,1},{2,18},{18,2},{3,19},{19,3},{4,20},{20... | collective-permute-start | bytes 98312 | tf_op jit(solution)/shard_map/ppermute | solution.py:487
  43.1 5.2 %collective-permute-start = (bf16[512,128]{1,0:T(8,128)(2,1)}, bf16[512,128]{1,0:T(8,128)(2,1)S(1)}, u32[]{:S(2)}, u32[]{:S(2)}) collective-permute-start(bf16[512,128]{1,0:T(8,128)(2,1)} %refs_0_.1), channel_id=1, source_target_pairs={{0,16},{16,0},{1,17},{17,1},{2,18},{18,2},{3,19},{19,3},{4,20},{20... | collective-permute-start | bytes 393224 | tf_op jit(solution)/shard_map/ppermute | solution.py:476
  48.9 10.4 %collective-permute-start.7 = (f32[3,256]{1,0:T(4,128)}, f32[3,256]{1,0:T(4,128)S(1)}, u32[]{:S(2)}, u32[]{:S(2)}) collective-permute-start(f32[3,256]{1,0:T(4,128)} %biases.5), channel_id=1, source_target_pairs={{0,16},{16,0},{1,17},{17,1},{2,18},{18,2},{3,19},{19,3},{4,20},{20... | collective-permute-start | bytes 9224 | tf_op jit(solution)/shard_map/ppermute | solution.py:488
  72.6 2.1 %collective-permute-start.13 = (bf16[128,1024]{1,0:T(8,128)(2,1)S(1)}, bf16[128,1024]{1,0:T(8,128)(2,1)S(1)}, u32[]{:S(2)}, u32[]{:S(2)}) collective-permute-start(bf16[128,1024]{1,0:T(8,128)(2,1)S(1)} %get-tuple-element.33), channel_id=1, source_target_pairs={{0,1},{1,0},{2,3},{3,2},{4,5},{5,4},{6,7},{7,6},{8,9},{9,8},{10,11... | collective-permute-start | bytes 786440 | tf_op jit(solution)/shard_map/ppermute | solution.py:539
  72.7 2.0 %collective-permute-start.14 = (bf16[1024,128]{1,0:T(8,128)(2,1)S(1)}, bf16[1024,128]{1,0:T(8,128)(2,1)S(1)}, u32[]{:S(2)}, u32[]{:S(2)}) collective-permute-start(bf16[1024,128]{1,0:T(8,128)(2,1)S(1)} %get-tuple-element.35), channel_id=1, source_target_pairs={{0,1},{1,0},{2,3},{3,2},{4,5},{5,4},{6,7},{7,6},{8,9},{9,8},{10,11... | collective-permute-start | bytes 786440 | tf_op jit(solution)/shard_map/ppermute | solution.py:540
  73.2 1.5 %collective-permute-start.10 = (s32[1]{0:T(128)}, s32[1]{0:T(128)}, u32[]{:S(2)}, u32[]{:S(2)}) collective-permute-start(s32[1]{0:T(128)} %param.14), channel_id=1, source_target_pairs={{0,1},{1,0},{2,3},{3,2},{4,5},{5,4},{6,7},{7,6},{8,9},{9,8},{10,11... | collective-permute-start | bytes 20 | tf_op jit(solution)/shard_map/ppermute | solution.py:541
  78.3 11.0 %collective-permute-start.16 = (bf16[72,1024]{1,0:T(8,128)(2,1)S(1)}, bf16[72,1024]{1,0:T(8,128)(2,1)S(1)}, u32[]{:S(2)}, u32[]{:S(2)}) collective-permute-start(bf16[72,1024]{1,0:T(8,128)(2,1)S(1)} %attend_send.3), channel_id=1, source_target_pairs={{0,2},{1,3},{2,0},{3,1},{4,6},{5,7},{6,4},{7,5},{8,10},{9,11},{10,... | collective-permute-start | bytes 442376 | tf_op jit(solution)/shard_map/ppermute | solution.py:544
  85.9 9.3 %collective-permute-start.15 = (bf16[72,1024]{1,0:T(8,128)(2,1)S(1)}, bf16[72,1024]{1,0:T(8,128)(2,1)S(1)}, u32[]{:S(2)}, u32[]{:S(2)}) collective-permute-start(bf16[72,1024]{1,0:T(8,128)(2,1)S(1)} %attend_send.2), channel_id=1, source_target_pairs={{0,2},{1,3},{2,0},{3,1},{4,6},{5,7},{6,4},{7,5},{8,10},{9,11},{10,... | collective-permute-start | bytes 442376 | tf_op jit(solution)/shard_map/ppermute | solution.py:544
  89.5 5.9 %collective-permute-start.17 = (bf16[72,1024]{1,0:T(8,128)(2,1)S(1)}, bf16[72,1024]{1,0:T(8,128)(2,1)S(1)}, u32[]{:S(2)}, u32[]{:S(2)}) collective-permute-start(bf16[72,1024]{1,0:T(8,128)(2,1)S(1)} %shard_map.112), channel_id=1, source_target_pairs={{0,4},{1,5},{2,6},{3,7},{4,0},{5,1},{6,2},{7,3},{8,12},{9,13},{10,... | collective-permute-start | bytes 442376 | tf_op jit(solution)/shard_map/ppermute | solution.py:544
  95.5 9.0 %collective-permute-start.18 = (bf16[72,1024]{1,0:T(8,128)(2,1)S(1)}, bf16[72,1024]{1,0:T(8,128)(2,1)S(1)}, u32[]{:S(2)}, u32[]{:S(2)}) collective-permute-start(bf16[72,1024]{1,0:T(8,128)(2,1)S(1)} %shard_map.113.mine), channel_id=1, source_target_pairs={{0,8},{1,9},{2,10},{3,11},{4,12},{5,13},{6,14},{7,15},{8,0},{9,1},... | collective-permute-start | bytes 442376 | tf_op jit(solution)/shard_map/ppermute | solution.py:544
  104.7 6.4 %collective-permute-start.19 = (bf16[64,1024]{1,0:T(8,128)(2,1)S(1)}, bf16[64,1024]{1,0:T(8,128)(2,1)S(1)}, u32[]{:S(2)}, u32[]{:S(2)}) collective-permute-start(bf16[64,1024]{1,0:T(8,128)(2,1)S(1)} %shard_map.114.refs_0_), channel_id=1, source_target_pairs={{0,4},{1,5},{2,6},{3,7},{4,0},{5,1},{6,2},{7,3},{8,12},{9,13},{10,... | collective-permute-start | bytes 393224 | tf_op jit(solution)/shard_map/ppermute | solution.py:544
  105.3 6.2 %collective-permute-start.20 = (bf16[64,1024]{1,0:T(8,128)(2,1)S(1)}, bf16[64,1024]{1,0:T(8,128)(2,1)S(1)}, u32[]{:S(2)}, u32[]{:S(2)}) collective-permute-start(bf16[64,1024]{1,0:T(8,128)(2,1)S(1)} %shard_map.114.refs_0_), channel_id=1, source_target_pairs={{0,2},{1,3},{2,0},{3,1},{4,6},{5,7},{6,4},{7,5},{8,10},{9,11},{10,... | collective-permute-start | bytes 393224 | tf_op jit(solution)/shard_map/ppermute | solution.py:544
  106.1 6.8 %collective-permute-start.21 = (bf16[64,1024]{1,0:T(8,128)(2,1)S(1)}, bf16[64,1024]{1,0:T(8,128)(2,1)S(1)}, u32[]{:S(2)}, u32[]{:S(2)}) collective-permute-start(bf16[64,1024]{1,0:T(8,128)(2,1)S(1)} %shard_map.114.refs_0_), channel_id=1, source_target_pairs={{0,6},{1,7},{2,4},{3,5},{4,2},{5,3},{6,0},{7,1},{8,14},{9,15},{10,... | collective-permute-start | bytes 393224 | tf_op jit(solution)/shard_map/ppermute | solution.py:544
  108.2 4.7 %collective-permute-start.22 = (bf16[64,1024]{1,0:T(8,128)(2,1)S(1)}, bf16[64,1024]{1,0:T(8,128)(2,1)S(1)}, u32[]{:S(2)}, u32[]{:S(2)}) collective-permute-start(bf16[64,1024]{1,0:T(8,128)(2,1)S(1)} %shard_map.114.refs_0_), channel_id=1, source_target_pairs={{0,1},{1,0},{2,3},{3,2},{4,5},{5,4},{6,7},{7,6},{8,9},{9,8},{10,11... | collective-permute-start | bytes 393224 | tf_op jit(solution)/shard_map/ppermute | solution.py:544
  111.1 1.9 %collective-permute-start.23 = (bf16[64,1024]{1,0:T(8,128)(2,1)S(1)}, bf16[64,1024]{1,0:T(8,128)(2,1)S(1)}, u32[]{:S(2)}, u32[]{:S(2)}) collective-permute-start(bf16[64,1024]{1,0:T(8,128)(2,1)S(1)} %collective-permute-done.19.refs_1_), channel_id=1, source_target_pairs={{0,1},{1,0},{2,3},{3,2},{4,5},{5,4},{6,7},{7,6},{8,9},{9,8},{10,11... | collective-permute-start | bytes 393224 | tf_op jit(solution)/shard_map/ppermute | solution.py:544
  (14 other events, 106.0 us)

commit v10 on v9

--- a/solution.py
+++ b/solution.py
@@ -248,20 +248,37 @@
     )
 
 
+def near_kernel(layer, core, theirs, taps, weights, biases, out, col):
+    rows, frames = out.shape
+    column(biases[layer : layer + 1, :], col)
+    here = pl.ds(pl.multiple_of(core[0] * rows, rows), rows)
+
+    def store(cols, value):
+        out[:, cols] = value
+
+    conv_rows(
+        taps, lambda cols: theirs[here, cols], weights, col[here, 0:1], None, store, frames, 256
+    )
+
+
 def last_kernel(
-    layer, side, core, features, theirs, taps, near_w, far_w, biases, key_w, value_w,
+    layer, side, core, features, near_rows, theirs, taps, weights, biases, key_w, value_w,
     key_keep, key_send, value_keep, value_send, col, full,
 ):
     rows, frames = features.shape
+    half = rows // 2
     base = (1 - side[0]) * rows
     full[pl.ds(pl.multiple_of(side[0] * rows, rows), rows), :] = features[...]
-    half = rows // 2
-
-    def target(part, here, value):
-        full[pl.ds(pl.multiple_of(base + part.start, half), half), here] = value
-
-    other_rows(
-        layer, core, theirs, taps, near_w, far_w, biases, col, None, target, frames, 256
+    full[pl.ds(pl.multiple_of(base + core[0] * half, half), half), :] = near_rows[...]
+    column(biases[layer : layer + 1, :], col)
+    here = pl.ds(pl.multiple_of((1 - core[0]) * half, half), half)
+    there = pl.ds(pl.multiple_of(base + (1 - core[0]) * half, half), half)
+
+    def store(cols, value):
+        full[there, cols] = value
+
+    conv_rows(
+        taps, lambda cols: theirs[here, cols], weights, col[here, 0:1], None, store, frames, 256
     )
     for key_out, value_out, part in (
         (key_send, value_send, 1 - core[0]), (key_keep, value_keep, core[0])
@@ -428,17 +445,39 @@
     )(*scalars, *keys, *values, queries)
 
 
-def assemble_kernel(core, cross, lower, *refs):
-    out = refs[-1]
-    latents = refs[0].shape[1]
+def assemble_kernel(spots, core, cross, lower, *refs):
+    pieces, out, done = refs[: len(spots)], refs[-2], refs[-1]
+    latents = pieces[0].shape[1]
     mine, theirs = 2 * core[0], 2 - 2 * core[0]
     heads = (mine + cross[0], mine + 1 - cross[0], theirs + cross[0], theirs + 1 - cross[0])
-    for index, piece in enumerate(refs[:-1]):
-        part = lower[0] if index % 2 == 0 else 1 - lower[0]
-        out[
-            pl.ds(pl.multiple_of(heads[index // 2] * HD, HD), HD),
+    copies = []
+    for n, (spot, piece) in enumerate(zip(spots, pieces)):
+        part = lower[0] if spot % 2 == 0 else 1 - lower[0]
+        target = out.at[
+            pl.ds(pl.multiple_of(heads[spot // 2] * HD, HD), HD),
             pl.ds(pl.multiple_of(part * latents, latents), latents),
-        ] = piece[...]
+        ]
+        copies.append(pltpu.make_async_copy(piece, target, done.at[n]))
+    for copy in copies:
+        copy.start()
+    for copy in copies:
+        copy.wait()
+
+
+def assemble(spots, out_shape, scalars, pieces, into=None):
+    extra = [] if into is None else [into]
+    call = pl.pallas_call(
+        functools.partial(assemble_kernel, spots),
+        out_shape=out_shape,
+        in_specs=smem(len(scalars)) + whole(len(pieces))
+        + [pl.BlockSpec(memory_space=pltpu.HBM)] * len(extra),
+        out_specs=pl.BlockSpec(memory_space=pltpu.HBM),
+        scratch_shapes=[pltpu.SemaphoreType.DMA((len(spots),))],
+        input_output_aliases={len(scalars) + len(pieces): 0} if extra else {},
+        compiler_params=params(16),
+        name="assemble_rest" if extra else "assemble",
+    )
+    return call(*scalars, *pieces, *extra)
 
 
 def simple(kernel, out_shape, scalars, arrays, scratch=(), mib=16, specs=None):
@@ -525,9 +564,14 @@
                 jax.ShapeDtypeStruct((frames, half), bf16),
                 jax.ShapeDtypeStruct((frames, half), bf16),
             ]
+            near_rows = simple(
+                functools.partial(near_kernel, layer), jax.ShapeDtypeStruct((half, frames), bf16),
+                (core,), (other_h, taps, near[layer], other_b), col, mib=24,
+            )
             key_keep, key_send, value_keep, value_send = simple(
                 functools.partial(last_kernel, layer), shapes, (side, core),
-                (kept_features,) + arrays + (key_w, value_w), col + [VMEM((ch, frames), bf16)],
+                (kept_features, near_rows, other_h, taps, far[layer], other_b, key_w, value_w),
+                col + [VMEM((ch, frames), bf16)],
                 mib=24,
             )
         else:
@@ -572,10 +616,10 @@
     corner = flip(done, 6)
     pieces = [done, above, beside, corner]
     pieces += [flip(piece, 1) for piece in pieces]
-    attended = simple(
-        assemble_kernel, jax.ShapeDtypeStruct((ch_loc, latents), bf16), (core, cross, lower),
-        pieces,
-    )
+    shape = jax.ShapeDtypeStruct((ch_loc, latents), bf16)
+    scalars = (core, cross, lower)
+    attended = assemble((0, 1, 3, 4, 5, 7), shape, scalars, pieces[:2] + pieces[3:6] + pieces[7:])
+    attended = assemble((2, 6), shape, scalars, [pieces[2], pieces[6]], attended)
     return (features, attended)
 
 

time: 116 us -> 118 us (1.017)
  Pallas kernels: 33.4 us -> 35.1 us
    pallas_call x0 -> x2, Pallas kernels: none -> 1.65 us  [assemble(): return call(*scalars, *pieces, *extra)]
  transfers between devices with their start and end apart: 26 -> 26, of which waited for: 12 -> 12; matrix products, arithmetic and copies ran while one was open for 2% -> 2% of each run, Pallas kernels for 23% -> 24%
where the time goes in v10:
time: 118 us
  starting transfers between devices  36.8 us (31%)
  waiting for transfers between devices  35.7 us (30%)
  Pallas kernels  35.1 us (30%)
  local copies, waits for them, and re-layouts  7.29 us (6%)
  between operations  1.78 us (2%)
    pallas_call x12, Pallas kernels, simple(): pl.pallas_call(kernel, grid=(1,), out_shape=out_shape, in_specs=smem(len(...  19.7 us
    pallas_call x4, Pallas kernels, attend(): pl.pallas_call(functools.partial(attend_kernel, packed), out_shape=out_sh...  13.8 us
    ppermute x11, starting transfers between devices, flip(): return lax.ppermute(value, 'tm', [(i, i ^ bit) for i in range(blocks)])  12.9 us
    ppermute x11, waiting for transfers between devices, flip(): return lax.ppermute(value, 'tm', [(i, i ^ bit) for i in range(blocks)])  12.9 us
    ppermute x3, starting transfers between devices, pair_device(): far = [lax.ppermute(near[n], 'tm', twins) for n in range(LAYERS)]  11.8 us
    ppermute x3, waiting for transfers between devices, pair_device(): near = [lax.ppermute(mine[n], 'sensor', across) for n in range(LAYERS)]  11.4 us
    ppermute x1, waiting for transfers between devices, pair_device(): other_edge = lax.ppermute(edge, 'sensor', across)  7.36 us
    unnamed x24, local copies, waits for them, and re-layouts  5.06 us
  transfers between devices with their start and end apart: 26, of which 12 were waited for; matrix products, arithmetic and copies ran while one was open for 2% of the time, Pallas kernels for 24%

profile of v10, /device:TPU:0, one launch (start us, length us, event | category | flops | bytes accessed | tf_op | source)
XLA Modules:
  0.0 117.7 jit_solution(14489491873030844837)
XLA Ops:
  3.8 2.6 %collective-permute-start.5 = (bf16[3,128,512]{2,1,0:T(8,128)(2,1)S(1)}, bf16[3,128,512]{2,1,0:T(8,128)(2,1)S(1)}, u32[]{:S(2)}, u32[]{:S(2)}) collective-permute-start(bf16[3,128,512]{2,1,0:T(8,128)(2,1)S(1)} %dynamic-slice_bitcast_fusion.2), channel_id=1, source_target_pairs={{0,16},{16,0},{1,17},{17,1},{2,18},{18,2},{3,19},{19,3},{4,20},{20... | collective-permute-start | bytes 1179656 | tf_op jit(solution)/shard_map/ppermute | solution.py:535
  9.8 4.3 %collective-permute-done.5.near_w = bf16[3,128,512]{2,1,0:T(8,128)(2,1)S(1)} collective-permute-done((bf16[3,128,512]{2,1,0:T(8,128)(2,1)S(1)}, bf16[3,128,512]{2,1,0:T(8,128)(2,1)S(1)}, u32[]{:S(2)}, u32[]{:S(2)}) %collective-permute-start.5) | collective-permute-done | bytes 393248 | tf_op jit(solution)/shard_map/ppermute | solution.py:535
  14.1 4.8 %collective-permute-start.6 = (bf16[3,128,512]{2,1,0:T(8,128)(2,1)S(1)}, bf16[3,128,512]{2,1,0:T(8,128)(2,1)}, u32[]{:S(2)}, u32[]{:S(2)}) collective-permute-start(bf16[3,128,512]{2,1,0:T(8,128)(2,1)S(1)} %collective-permute-done.5.near_w), channel_id=1, source_target_pairs={{0,1},{1,0},{2,3},{3,2},{4,5},{5,4},{6,7},{7,6},{8,9},{9,8},{10,11... | collective-permute-start | bytes 1179656 | tf_op jit(solution)/shard_map/ppermute | solution.py:536
  18.9 3.6 %collective-permute-done.8.near_w = bf16[3,128,512]{2,1,0:T(8,128)(2,1)S(1)} collective-permute-done((bf16[3,128,512]{2,1,0:T(8,128)(2,1)S(1)}, bf16[3,128,512]{2,1,0:T(8,128)(2,1)S(1)}, u32[]{:S(2)}, u32[]{:S(2)}) %collective-permute-start.8) | collective-permute-done | bytes 393248 | tf_op jit(solution)/shard_map/ppermute | solution.py:535
  22.5 4.8 %collective-permute-start.9 = (bf16[3,128,512]{2,1,0:T(8,128)(2,1)S(1)}, bf16[3,128,512]{2,1,0:T(8,128)(2,1)}, u32[]{:S(2)}, u32[]{:S(2)}) collective-permute-start(bf16[3,128,512]{2,1,0:T(8,128)(2,1)S(1)} %collective-permute-done.8.near_w), channel_id=1, source_target_pairs={{0,1},{1,0},{2,3},{3,2},{4,5},{5,4},{6,7},{7,6},{8,9},{9,8},{10,11... | collective-permute-start | bytes 1179656 | tf_op jit(solution)/shard_map/ppermute | solution.py:536
  27.3 3.6 %collective-permute-done.11.weights = bf16[3,128,512]{2,1,0:T(8,128)(2,1)S(1)} collective-permute-done((bf16[3,128,512]{2,1,0:T(8,128)(2,1)S(1)}, bf16[3,128,512]{2,1,0:T(8,128)(2,1)S(1)}, u32[]{:S(2)}, u32[]{:S(2)}) %collective-permute-start.11) | collective-permute-done | bytes 393248 | tf_op jit(solution)/shard_map/ppermute | solution.py:535
  35.1 7.4 %collective-permute-done.4.refs_5_ = bf16[128,128]{1,0:T(8,128)(2,1)S(1)} collective-permute-done((bf16[128,128]{1,0:T(8,128)(2,1)S(1)}, bf16[128,128]{1,0:T(8,128)(2,1)S(1)}, u32[]{:S(2)}, u32[]{:S(2)}) %collective-permute-start.4) | collective-permute-done | bytes 32800 | tf_op jit(solution)/shard_map/ppermute | solution.py:526
  44.8 3.4 %collective-permute-done.refs_1_ = bf16[512,128]{1,0:T(8,128)(2,1)S(1)} collective-permute-done((bf16[512,128]{1,0:T(8,128)(2,1)}, bf16[512,128]{1,0:T(8,128)(2,1)S(1)}, u32[]{:S(2)}, u32[]{:S(2)}) %collective-permute-start) | collective-permute-done | bytes 131104 | tf_op jit(solution)/shard_map/ppermute | solution.py:515
  56.5 2.9 %shard_map.105 = (bf16[256,1152]{1,0:T(8,128)(2,1)S(1)}, bf16[3,512,1152]{2,1,0:T(8,128)(2,1)S(1)}) custom-call(s32[3]{0:T(128)S(1)} %copy-done.11, s32[1]{0:T(128)} %bitcast.side, s32[1]{0:T(128)} %bitcast.1.place, bf16[256,1152]{1,0:T(8,128)(2,1)S(1)} %get-tuple-element.22.mine, bf16[256,1152]{1,0:T(8,128)(2,1)S(1)} %get-tuple-element.23.theirs, ...), custom_call_target="tpu_custom_call" | custom-call | tf_op jit(solution)/shard_map/pallas_call | solution.py:485
  59.4 2.5 %shard_map.106.theirs = bf16[256,1152]{1,0:T(8,128)(2,1)S(1)} custom-call(s32[1]{0:T(128)S(6)} %and.14.core, s32[1]{0:T(128)} %bitcast.1.place, bf16[256,1152]{1,0:T(8,128)(2,1)S(1)} %get-tuple-element.23.theirs, bf16[3,512,1152]{2,1,0:T(8,128)(2,1)S(1)} %get-tuple-element.25.taps, bf16[3,128,512]{2,1,0:T(8,128)(2,1)S(1)} %collective-permute-done.5.near_w, ...), custom_call_target="tpu_custom_call" | custom-call | tf_op jit(solution)/shard_map/pallas_call | solution.py:485
  61.9 2.9 %shard_map.107 = (bf16[256,1152]{1,0:T(8,128)(2,1)S(1)}, bf16[3,512,1152]{2,1,0:T(8,128)(2,1)S(1)}) custom-call(s32[3]{0:T(128)S(1)} %copy-done.11, s32[1]{0:T(128)} %bitcast.side, s32[1]{0:T(128)} %bitcast.1.place, bf16[256,1152]{1,0:T(8,128)(2,1)S(1)} %get-tuple-element.24.mine, bf16[256,1152]{1,0:T(8,128)(2,1)S(1)} %shard_map.106.theirs, ...), custom_call_target="tpu_custom_call" | custom-call | tf_op jit(solution)/shard_map/pallas_call | solution.py:485
  64.7 2.4 %shard_map.108.theirs = bf16[256,1152]{1,0:T(8,128)(2,1)S(1)} custom-call(s32[1]{0:T(128)S(6)} %and.14.core, s32[1]{0:T(128)} %bitcast.1.place, bf16[256,1152]{1,0:T(8,128)(2,1)S(1)} %shard_map.106.theirs, bf16[3,512,1152]{2,1,0:T(8,128)(2,1)S(1)} %get-tuple-element.27.taps, bf16[3,128,512]{2,1,0:T(8,128)(2,1)S(1)} %collective-permute-done.8.near_w, ...), custom_call_target="tpu_custom_call" | custom-call | tf_op jit(solution)/shard_map/pallas_call | solution.py:485
  67.2 3.3 %shard_map.109 = (bf16[256,1024]{1,0:T(8,128)(2,1)}, bf16[256,1024]{1,0:T(8,128)(2,1)S(1)}, bf16[3,512,1152]{2,1,0:T(8,128)(2,1)S(1)}) custom-call(s32[3]{0:T(128)S(1)} %copy-done.11, s32[1]{0:T(128)} %bitcast.side, s32[1]{0:T(128)} %bitcast.1.place, bf16[256,1152]{1,0:T(8,128)(2,1)S(1)} %get-tuple-element.26.mine, bf16[256,1152]{1,0:T(8,128)(2,1)S(1)} %shard_map.108.theirs, ...), custom_call_target="tpu_custom_call" | custom-call | tf_op jit(solution)/shard_map/pallas_call | solution.py:485
  71.2 2.6 %shard_map.111 = (bf16[128,1024]{1,0:T(8,128)(2,1)S(1)}, bf16[128,1024]{1,0:T(8,128)(2,1)S(1)}, bf16[1024,128]{1,0:T(8,128)(2,1)S(1)}, bf16[1024,128]{1,0:T(8,128)(2,1)S(1)}) custom-call(s32[1]{0:T(128)} %bitcast.side, s32[1]{0:T(128)S(6)} %and.14.core, bf16[256,1024]{1,0:T(8,128)(2,1)S(1)} %get-tuple-element.30.features, ...), custom_call_target="tpu_custom_call" | custom-call | tf_op jit(solution)/shard_map/pallas_call | solution.py:485
  75.8 3.6 %attend_send.3 = bf16[72,1024]{1,0:T(8,128)(2,1)S(1)} custom-call(s32[1]{0:T(128)S(6)} %sub.8.which, s32[1]{0:T(128)S(6)} %sub.9.half, s32[1]{0:T(128)S(6)} %copy.13.valid_own, s32[1]{0:T(128)} %collective-permute-done.10.valid_rec, bf16[128,1024]{1,0:T(8,128)(2,1)S(1)} %get-tuple-element.32.key_own, bf16[128,1024]{1,0:T(8,128)(2,1)S(1)} %collective-permute-done.13.key_rec, ...), custom_call_target="tpu_custom_call" | custom-call | tf_op jit(solution)/shard_map/attend_send/pallas_call | solution.py:430
  79.5 4.1 %collective-permute-start.16 = (bf16[72,1024]{1,0:T(8,128)(2,1)S(1)}, bf16[72,1024]{1,0:T(8,128)(2,1)S(1)}, u32[]{:S(2)}, u32[]{:S(2)}) collective-permute-start(bf16[72,1024]{1,0:T(8,128)(2,1)S(1)} %attend_send.3), channel_id=1, source_target_pairs={{0,2},{1,3},{2,0},{3,1},{4,6},{5,7},{6,4},{7,5},{8,10},{9,11},{10,... | collective-permute-start | bytes 442376 | tf_op jit(solution)/shard_map/ppermute | solution.py:588
  83.6 3.4 %attend_send.2 = bf16[72,1024]{1,0:T(8,128)(2,1)S(1)} custom-call(s32[1]{0:T(128)S(6)} %sub.8.which, s32[1]{0:T(128)S(6)} %and.16.half.lower, s32[1]{0:T(128)S(6)} %copy.13.valid_own, s32[1]{0:T(128)} %collective-permute-done.10.valid_rec, bf16[128,1024]{1,0:T(8,128)(2,1)S(1)} %get-tuple-element.32.key_own, ...), custom_call_target="tpu_custom_call" | custom-call | tf_op jit(solution)/shard_map/attend_send/pallas_call | solution.py:430
  87.1 3.4 %attend_keep.3 = (f32[1,1024]{1,0:T(1,128)S(1)}, f32[1,1024]{1,0:T(1,128)S(1)}, f32[64,1024]{1,0:T(8,128)S(1)}) custom-call(s32[1]{0:T(128)S(6)} %and.15.which.cross, s32[1]{0:T(128)S(6)} %sub.9.half, s32[1]{0:T(128)S(6)} %copy.13.valid_own, s32[1]{0:T(128)} %collective-permute-done.10.valid_rec, bf16[128,1024]{1,0:T(8,128)(2,1)S(1)} %get-tuple-element.32.key_own, ...), custom_call_target="tpu_custom_call" | custom-call | tf_op jit(solution)/shard_map/attend_keep/pallas_call | solution.py:430
  90.6 2.3 %collective-permute-start.17 = (bf16[72,1024]{1,0:T(8,128)(2,1)S(1)}, bf16[72,1024]{1,0:T(8,128)(2,1)S(1)}, u32[]{:S(2)}, u32[]{:S(2)}) collective-permute-start(bf16[72,1024]{1,0:T(8,128)(2,1)S(1)} %shard_map.113), channel_id=1, source_target_pairs={{0,4},{1,5},{2,6},{3,7},{4,0},{5,1},{6,2},{7,3},{8,12},{9,13},{10,... | collective-permute-start | bytes 442376 | tf_op jit(solution)/shard_map/ppermute | solution.py:588
  92.9 3.4 %attend_keep.2 = (f32[1,1024]{1,0:T(1,128)S(1)}, f32[1,1024]{1,0:T(1,128)S(1)}, f32[64,1024]{1,0:T(8,128)S(1)}) custom-call(s32[1]{0:T(128)S(6)} %and.15.which.cross, s32[1]{0:T(128)S(6)} %and.16.half.lower, s32[1]{0:T(128)S(6)} %copy.13.valid_own, s32[1]{0:T(128)} %collective-permute-done.10.valid_rec, bf16[128,1024]{1,0:T(8,128)(2,1)S(1)} %get-tuple-element.32.key_own, ...), custom_call_target="tpu_custom_call" | custom-call | tf_op jit(solution)/shard_map/attend_keep/pallas_call | solution.py:430
  96.7 2.8 %collective-permute-start.18 = (bf16[72,1024]{1,0:T(8,128)(2,1)S(1)}, bf16[72,1024]{1,0:T(8,128)(2,1)S(1)}, u32[]{:S(2)}, u32[]{:S(2)}) collective-permute-start(bf16[72,1024]{1,0:T(8,128)(2,1)S(1)} %shard_map.114.mine), channel_id=1, source_target_pairs={{0,8},{1,9},{2,10},{3,11},{4,12},{5,13},{6,14},{7,15},{8,0},{9,1},... | collective-permute-start | bytes 442376 | tf_op jit(solution)/shard_map/ppermute | solution.py:588
  99.5 6.2 %collective-permute-done.18.theirs = bf16[72,1024]{1,0:T(8,128)(2,1)S(1)} collective-permute-done((bf16[72,1024]{1,0:T(8,128)(2,1)S(1)}, bf16[72,1024]{1,0:T(8,128)(2,1)S(1)}, u32[]{:S(2)}, u32[]{:S(2)}) %collective-permute-start.18) | collective-permute-done | bytes 147488 | tf_op jit(solution)/shard_map/ppermute | solution.py:588
  106.4 2.2 %collective-permute-start.22 = (bf16[64,1024]{1,0:T(8,128)(2,1)S(1)}, bf16[64,1024]{1,0:T(8,128)(2,1)S(1)}, u32[]{:S(2)}, u32[]{:S(2)}) collective-permute-start(bf16[64,1024]{1,0:T(8,128)(2,1)S(1)} %shard_map.115.refs_0_), channel_id=1, source_target_pairs={{0,6},{1,7},{2,4},{3,5},{4,2},{5,3},{6,0},{7,1},{8,14},{9,15},{10,... | collective-permute-start | bytes 393224 | tf_op jit(solution)/shard_map/ppermute | solution.py:588
  109.4 2.5 %collective-permute-done.21.refs_1_ = bf16[64,1024]{1,0:T(8,128)(2,1)S(1)} collective-permute-done((bf16[64,1024]{1,0:T(8,128)(2,1)S(1)}, bf16[64,1024]{1,0:T(8,128)(2,1)S(1)}, u32[]{:S(2)}, u32[]{:S(2)}) %collective-permute-start.21) | collective-permute-done | bytes 131104 | tf_op jit(solution)/shard_map/ppermute | solution.py:588
  (75 shorter events, 30.9 us)
Async XLA Ops:
  1.6 4.8 %collective-permute-start.2 = (bf16[128,128]{1,0:T(8,128)(2,1)S(1)}, bf16[128,128]{1,0:T(8,128)(2,1)S(1)}, u32[]{:S(2)}, u32[]{:S(2)}) collective-permute-start(bf16[128,128]{1,0:T(8,128)(2,1)S(1)} %get-tuple-element.45), channel_id=1, source_target_pairs={{0,1},{1,0},{2,3},{3,2},{4,5},{5,4},{6,7},{7,6},{8,9},{9,8},{10,11... | collective-permute-start | bytes 98312 | tf_op jit(solution)/shard_map/ppermute | solution.py:523
  2.1 4.3 %collective-permute-start.3 = (bf16[128,128]{1,0:T(8,128)(2,1)S(1)}, bf16[128,128]{1,0:T(8,128)(2,1)S(1)}, u32[]{:S(2)}, u32[]{:S(2)}) collective-permute-start(bf16[128,128]{1,0:T(8,128)(2,1)S(1)} %get-tuple-element.44), channel_id=1, source_target_pairs={{1,2},{3,4},{5,6},{7,8},{9,10},{11,12},{13,14},{2,1},{4,3},{6,5},{... | collective-permute-start | bytes 98312 | tf_op jit(solution)/shard_map/ppermute | solution.py:519
  3.8 10.2 %collective-permute-start.5 = (bf16[3,128,512]{2,1,0:T(8,128)(2,1)S(1)}, bf16[3,128,512]{2,1,0:T(8,128)(2,1)S(1)}, u32[]{:S(2)}, u32[]{:S(2)}) collective-permute-start(bf16[3,128,512]{2,1,0:T(8,128)(2,1)S(1)} %dynamic-slice_bitcast_fusion.2), channel_id=1, source_target_pairs={{0,16},{16,0},{1,17},{17,1},{2,18},{18,2},{3,19},{19,3},{4,20},{20... | collective-permute-start | bytes 1179656 | tf_op jit(solution)/shard_map/ppermute | solution.py:535
  7.7 14.8 %collective-permute-start.8 = (bf16[3,128,512]{2,1,0:T(8,128)(2,1)S(1)}, bf16[3,128,512]{2,1,0:T(8,128)(2,1)S(1)}, u32[]{:S(2)}, u32[]{:S(2)}) collective-permute-start(bf16[3,128,512]{2,1,0:T(8,128)(2,1)S(1)} %get-tuple-element.43), channel_id=1, source_target_pairs={{0,16},{16,0},{1,17},{17,1},{2,18},{18,2},{3,19},{19,3},{4,20},{20... | collective-permute-start | bytes 1179656 | tf_op jit(solution)/shard_map/ppermute | solution.py:535
  7.8 23.1 %collective-permute-start.11 = (bf16[3,128,512]{2,1,0:T(8,128)(2,1)S(1)}, bf16[3,128,512]{2,1,0:T(8,128)(2,1)S(1)}, u32[]{:S(2)}, u32[]{:S(2)}) collective-permute-start(bf16[3,128,512]{2,1,0:T(8,128)(2,1)S(1)} %get-tuple-element.42), channel_id=1, source_target_pairs={{0,16},{16,0},{1,17},{17,1},{2,18},{18,2},{3,19},{19,3},{4,20},{20... | collective-permute-start | bytes 1179656 | tf_op jit(solution)/shard_map/ppermute | solution.py:535
  14.1 45.3 %collective-permute-start.6 = (bf16[3,128,512]{2,1,0:T(8,128)(2,1)S(1)}, bf16[3,128,512]{2,1,0:T(8,128)(2,1)}, u32[]{:S(2)}, u32[]{:S(2)}) collective-permute-start(bf16[3,128,512]{2,1,0:T(8,128)(2,1)S(1)} %collective-permute-done.5.near_w), channel_id=1, source_target_pairs={{0,1},{1,0},{2,3},{3,2},{4,5},{5,4},{6,7},{7,6},{8,9},{9,8},{10,11... | collective-permute-start | bytes 1179656 | tf_op jit(solution)/shard_map/ppermute | solution.py:536
  22.5 42.2 %collective-permute-start.9 = (bf16[3,128,512]{2,1,0:T(8,128)(2,1)S(1)}, bf16[3,128,512]{2,1,0:T(8,128)(2,1)}, u32[]{:S(2)}, u32[]{:S(2)}) collective-permute-start(bf16[3,128,512]{2,1,0:T(8,128)(2,1)S(1)} %collective-permute-done.8.near_w), channel_id=1, source_target_pairs={{0,1},{1,0},{2,3},{3,2},{4,5},{5,4},{6,7},{7,6},{8,9},{9,8},{10,11... | collective-permute-start | bytes 1179656 | tf_op jit(solution)/shard_map/ppermute | solution.py:536
  30.9 40.2 %collective-permute-start.12 = (bf16[3,128,512]{2,1,0:T(8,128)(2,1)S(1)}, bf16[3,128,512]{2,1,0:T(8,128)(2,1)}, u32[]{:S(2)}, u32[]{:S(2)}) collective-permute-start(bf16[3,128,512]{2,1,0:T(8,128)(2,1)S(1)} %collective-permute-done.11.weights), channel_id=1, source_target_pairs={{0,1},{1,0},{2,3},{3,2},{4,5},{5,4},{6,7},{7,6},{8,9},{9,8},{10,11... | collective-permute-start | bytes 1179656 | tf_op jit(solution)/shard_map/ppermute | solution.py:536
  33.1 17.6 %collective-permute-start.1 = (bf16[128,1024]{1,0:T(8,128)(2,1)}, bf16[128,1024]{1,0:T(8,128)(2,1)}, u32[]{:S(2)}, u32[]{:S(2)}) collective-permute-start(bf16[128,1024]{1,0:T(8,128)(2,1)} %refs_2_.1), channel_id=1, source_target_pairs={{0,16},{16,0},{1,17},{17,1},{2,18},{18,2},{3,19},{19,3},{4,20},{20... | collective-permute-start | bytes 786440 | tf_op jit(solution)/shard_map/ppermute | solution.py:514
  35.1 7.4 %collective-permute-start.4 = (bf16[128,128]{1,0:T(8,128)(2,1)S(1)}, bf16[128,128]{1,0:T(8,128)(2,1)S(1)}, u32[]{:S(2)}, u32[]{:S(2)}) collective-permute-start(bf16[128,128]{1,0:T(8,128)(2,1)S(1)} %broadcast_select_fusion.2.refs_4_), channel_id=1, source_target_pairs={{0,16},{16,0},{1,17},{17,1},{2,18},{18,2},{3,19},{19,3},{4,20},{20... | collective-permute-start | bytes 98312 | tf_op jit(solution)/shard_map/ppermute | solution.py:526
  43.1 5.2 %collective-permute-start = (bf16[512,128]{1,0:T(8,128)(2,1)}, bf16[512,128]{1,0:T(8,128)(2,1)S(1)}, u32[]{:S(2)}, u32[]{:S(2)}) collective-permute-start(bf16[512,128]{1,0:T(8,128)(2,1)} %refs_0_.1), channel_id=1, source_target_pairs={{0,16},{16,0},{1,17},{17,1},{2,18},{18,2},{3,19},{19,3},{4,20},{20... | collective-permute-start | bytes 393224 | tf_op jit(solution)/shard_map/ppermute | solution.py:515
  48.9 10.4 %collective-permute-start.7 = (f32[3,256]{1,0:T(4,128)}, f32[3,256]{1,0:T(4,128)S(1)}, u32[]{:S(2)}, u32[]{:S(2)}) collective-permute-start(f32[3,256]{1,0:T(4,128)} %biases.5), channel_id=1, source_target_pairs={{0,16},{16,0},{1,17},{17,1},{2,18},{18,2},{3,19},{19,3},{4,20},{20... | collective-permute-start | bytes 9224 | tf_op jit(solution)/shard_map/ppermute | solution.py:527
  73.7 2.1 %collective-permute-start.13 = (bf16[128,1024]{1,0:T(8,128)(2,1)S(1)}, bf16[128,1024]{1,0:T(8,128)(2,1)S(1)}, u32[]{:S(2)}, u32[]{:S(2)}) collective-permute-start(bf16[128,1024]{1,0:T(8,128)(2,1)S(1)} %get-tuple-element.33), channel_id=1, source_target_pairs={{0,1},{1,0},{2,3},{3,2},{4,5},{5,4},{6,7},{7,6},{8,9},{9,8},{10,11... | collective-permute-start | bytes 786440 | tf_op jit(solution)/shard_map/ppermute | solution.py:583
  73.8 2.0 %collective-permute-start.14 = (bf16[1024,128]{1,0:T(8,128)(2,1)S(1)}, bf16[1024,128]{1,0:T(8,128)(2,1)S(1)}, u32[]{:S(2)}, u32[]{:S(2)}) collective-permute-start(bf16[1024,128]{1,0:T(8,128)(2,1)S(1)} %get-tuple-element.35), channel_id=1, source_target_pairs={{0,1},{1,0},{2,3},{3,2},{4,5},{5,4},{6,7},{7,6},{8,9},{9,8},{10,11... | collective-permute-start | bytes 786440 | tf_op jit(solution)/shard_map/ppermute | solution.py:584
  74.3 1.5 %collective-permute-start.10 = (s32[1]{0:T(128)}, s32[1]{0:T(128)}, u32[]{:S(2)}, u32[]{:S(2)}) collective-permute-start(s32[1]{0:T(128)} %param.14), channel_id=1, source_target_pairs={{0,1},{1,0},{2,3},{3,2},{4,5},{5,4},{6,7},{7,6},{8,9},{9,8},{10,11... | collective-permute-start | bytes 20 | tf_op jit(solution)/shard_map/ppermute | solution.py:585
  79.5 11.0 %collective-permute-start.16 = (bf16[72,1024]{1,0:T(8,128)(2,1)S(1)}, bf16[72,1024]{1,0:T(8,128)(2,1)S(1)}, u32[]{:S(2)}, u32[]{:S(2)}) collective-permute-start(bf16[72,1024]{1,0:T(8,128)(2,1)S(1)} %attend_send.3), channel_id=1, source_target_pairs={{0,2},{1,3},{2,0},{3,1},{4,6},{5,7},{6,4},{7,5},{8,10},{9,11},{10,... | collective-permute-start | bytes 442376 | tf_op jit(solution)/shard_map/ppermute | solution.py:588
  87.0 9.3 %collective-permute-start.15 = (bf16[72,1024]{1,0:T(8,128)(2,1)S(1)}, bf16[72,1024]{1,0:T(8,128)(2,1)S(1)}, u32[]{:S(2)}, u32[]{:S(2)}) collective-permute-start(bf16[72,1024]{1,0:T(8,128)(2,1)S(1)} %attend_send.2), channel_id=1, source_target_pairs={{0,2},{1,3},{2,0},{3,1},{4,6},{5,7},{6,4},{7,5},{8,10},{9,11},{10,... | collective-permute-start | bytes 442376 | tf_op jit(solution)/shard_map/ppermute | solution.py:588
  90.6 6.0 %collective-permute-start.17 = (bf16[72,1024]{1,0:T(8,128)(2,1)S(1)}, bf16[72,1024]{1,0:T(8,128)(2,1)S(1)}, u32[]{:S(2)}, u32[]{:S(2)}) collective-permute-start(bf16[72,1024]{1,0:T(8,128)(2,1)S(1)} %shard_map.113), channel_id=1, source_target_pairs={{0,4},{1,5},{2,6},{3,7},{4,0},{5,1},{6,2},{7,3},{8,12},{9,13},{10,... | collective-permute-start | bytes 442376 | tf_op jit(solution)/shard_map/ppermute | solution.py:588
  96.7 9.0 %collective-permute-start.18 = (bf16[72,1024]{1,0:T(8,128)(2,1)S(1)}, bf16[72,1024]{1,0:T(8,128)(2,1)S(1)}, u32[]{:S(2)}, u32[]{:S(2)}) collective-permute-start(bf16[72,1024]{1,0:T(8,128)(2,1)S(1)} %shard_map.114.mine), channel_id=1, source_target_pairs={{0,8},{1,9},{2,10},{3,11},{4,12},{5,13},{6,14},{7,15},{8,0},{9,1},... | collective-permute-start | bytes 442376 | tf_op jit(solution)/shard_map/ppermute | solution.py:588
  105.8 6.1 %collective-permute-start.21 = (bf16[64,1024]{1,0:T(8,128)(2,1)S(1)}, bf16[64,1024]{1,0:T(8,128)(2,1)S(1)}, u32[]{:S(2)}, u32[]{:S(2)}) collective-permute-start(bf16[64,1024]{1,0:T(8,128)(2,1)S(1)} %shard_map.115.refs_0_), channel_id=1, source_target_pairs={{0,4},{1,5},{2,6},{3,7},{4,0},{5,1},{6,2},{7,3},{8,12},{9,13},{10,... | collective-permute-start | bytes 393224 | tf_op jit(solution)/shard_map/ppermute | solution.py:588
  106.4 7.6 %collective-permute-start.22 = (bf16[64,1024]{1,0:T(8,128)(2,1)S(1)}, bf16[64,1024]{1,0:T(8,128)(2,1)S(1)}, u32[]{:S(2)}, u32[]{:S(2)}) collective-permute-start(bf16[64,1024]{1,0:T(8,128)(2,1)S(1)} %shard_map.115.refs_0_), channel_id=1, source_target_pairs={{0,6},{1,7},{2,4},{3,5},{4,2},{5,3},{6,0},{7,1},{8,14},{9,15},{10,... | collective-permute-start | bytes 393224 | tf_op jit(solution)/shard_map/ppermute | solution.py:588
  108.6 6.8 %collective-permute-start.19 = (bf16[64,1024]{1,0:T(8,128)(2,1)S(1)}, bf16[64,1024]{1,0:T(8,128)(2,1)S(1)}, u32[]{:S(2)}, u32[]{:S(2)}) collective-permute-start(bf16[64,1024]{1,0:T(8,128)(2,1)S(1)} %shard_map.115.refs_0_), channel_id=1, source_target_pairs={{0,2},{1,3},{2,0},{3,1},{4,6},{5,7},{6,4},{7,5},{8,10},{9,11},{10,... | collective-permute-start | bytes 393224 | tf_op jit(solution)/shard_map/ppermute | solution.py:588
  109.4 6.1 %collective-permute-start.23 = (bf16[64,1024]{1,0:T(8,128)(2,1)S(1)}, bf16[64,1024]{1,0:T(8,128)(2,1)S(1)}, u32[]{:S(2)}, u32[]{:S(2)}) collective-permute-start(bf16[64,1024]{1,0:T(8,128)(2,1)S(1)} %shard_map.115.refs_0_), channel_id=1, source_target_pairs={{0,1},{1,0},{2,3},{3,2},{4,5},{5,4},{6,7},{7,6},{8,9},{9,8},{10,11... | collective-permute-start | bytes 393224 | tf_op jit(solution)/shard_map/ppermute | solution.py:588
  111.9 3.5 %collective-permute-start.24 = (bf16[64,1024]{1,0:T(8,128)(2,1)S(1)}, bf16[64,1024]{1,0:T(8,128)(2,1)S(1)}, u32[]{:S(2)}, u32[]{:S(2)}) collective-permute-start(bf16[64,1024]{1,0:T(8,128)(2,1)S(1)} %collective-permute-done.21.refs_1_), channel_id=1, source_target_pairs={{0,1},{1,0},{2,3},{3,2},{4,5},{5,4},{6,7},{7,6},{8,9},{9,8},{10,11... | collective-permute-start | bytes 393224 | tf_op jit(solution)/shard_map/ppermute | solution.py:588
  (14 other events, 102.8 us)

commit v11 on v10

--- a/solution.py
+++ b/solution.py
@@ -359,7 +359,7 @@
     frames = key_own.shape[1]
     latents = asked.shape[0]
     rows = score_a.shape[0]
-    chunk = frames // 2
+    chunk = frames
     slot = which[0]
     spare = (1 - slot) * HD
     row = lax.broadcasted_iota(jnp.int32, (2 * HD, frames), 0)
@@ -618,8 +618,8 @@
     pieces += [flip(piece, 1) for piece in pieces]
     shape = jax.ShapeDtypeStruct((ch_loc, latents), bf16)
     scalars = (core, cross, lower)
-    attended = assemble((0, 1, 3, 4, 5, 7), shape, scalars, pieces[:2] + pieces[3:6] + pieces[7:])
-    attended = assemble((2, 6), shape, scalars, [pieces[2], pieces[6]], attended)
+    attended = assemble((0, 1, 2, 4, 5, 6), shape, scalars, pieces[:3] + pieces[4:7])
+    attended = assemble((3, 7), shape, scalars, [pieces[3], pieces[7]], attended)
     return (features, attended)
 
 

time: 118 us -> 117 us (level)
  waiting for transfers between devices: 35.7 us -> 34.2 us
    ppermute x11, waiting for transfers between devices: 12.9 us -> 11.4 us  [flip(): return lax.ppermute(value, 'tm', [(i, i ^ bit) for i in range(blocks)])]
where the time goes in v11:
time: 117 us; the launch traced here: 116 us
  starting transfers between devices  36.9 us (32%)
  Pallas kernels  35.1 us (30%)
  waiting for transfers between devices  34.2 us (29%)
  local copies, waits for them, and re-layouts  7.29 us (6%)
  between operations  1.78 us (2%)
    pallas_call x12, Pallas kernels, simple(): pl.pallas_call(kernel, grid=(1,), out_shape=out_shape, in_specs=smem(len(...  19.7 us
    pallas_call x4, Pallas kernels, attend(): pl.pallas_call(functools.partial(attend_kernel, packed), out_shape=out_sh...  13.8 us
    ppermute x11, starting transfers between devices, flip(): return lax.ppermute(value, 'tm', [(i, i ^ bit) for i in range(blocks)])  13 us
    ppermute x3, starting transfers between devices, pair_device(): far = [lax.ppermute(near[n], 'tm', twins) for n in range(LAYERS)]  11.8 us
    ppermute x3, waiting for transfers between devices, pair_device(): near = [lax.ppermute(mine[n], 'sensor', across) for n in range(LAYERS)]  11.4 us
    ppermute x11, waiting for transfers between devices, flip(): return lax.ppermute(value, 'tm', [(i, i ^ bit) for i in range(blocks)])  11.4 us
    ppermute x1, waiting for transfers between devices, pair_device(): other_edge = lax.ppermute(edge, 'sensor', across)  7.36 us
    unnamed x24, local copies, waits for them, and re-layouts  5.06 us
  transfers between devices with their start and end apart: 26, of which 12 were waited for; matrix products, arithmetic and copies ran while one was open for 2% of the time, Pallas kernels for 24%

profile of v11, /device:TPU:0, one launch (start us, length us, event | category | flops | bytes accessed | tf_op | source)
XLA Modules:
  0.0 116.2 jit_solution(5098150956797628816)
XLA Ops:
  3.8 2.6 %collective-permute-start.5 = (bf16[3,128,512]{2,1,0:T(8,128)(2,1)S(1)}, bf16[3,128,512]{2,1,0:T(8,128)(2,1)S(1)}, u32[]{:S(2)}, u32[]{:S(2)}) collective-permute-start(bf16[3,128,512]{2,1,0:T(8,128)(2,1)S(1)} %dynamic-slice_bitcast_fusion.2), channel_id=1, source_target_pairs={{0,16},{16,0},{1,17},{17,1},{2,18},{18,2},{3,19},{19,3},{4,20},{20... | collective-permute-start | bytes 1179656 | tf_op jit(solution)/shard_map/ppermute | solution.py:535
  9.8 4.3 %collective-permute-done.5.near_w = bf16[3,128,512]{2,1,0:T(8,128)(2,1)S(1)} collective-permute-done((bf16[3,128,512]{2,1,0:T(8,128)(2,1)S(1)}, bf16[3,128,512]{2,1,0:T(8,128)(2,1)S(1)}, u32[]{:S(2)}, u32[]{:S(2)}) %collective-permute-start.5) | collective-permute-done | bytes 393248 | tf_op jit(solution)/shard_map/ppermute | solution.py:535
  14.1 4.8 %collective-permute-start.6 = (bf16[3,128,512]{2,1,0:T(8,128)(2,1)S(1)}, bf16[3,128,512]{2,1,0:T(8,128)(2,1)}, u32[]{:S(2)}, u32[]{:S(2)}) collective-permute-start(bf16[3,128,512]{2,1,0:T(8,128)(2,1)S(1)} %collective-permute-done.5.near_w), channel_id=1, source_target_pairs={{0,1},{1,0},{2,3},{3,2},{4,5},{5,4},{6,7},{7,6},{8,9},{9,8},{10,11... | collective-permute-start | bytes 1179656 | tf_op jit(solution)/shard_map/ppermute | solution.py:536
  18.9 3.6 %collective-permute-done.8.near_w = bf16[3,128,512]{2,1,0:T(8,128)(2,1)S(1)} collective-permute-done((bf16[3,128,512]{2,1,0:T(8,128)(2,1)S(1)}, bf16[3,128,512]{2,1,0:T(8,128)(2,1)S(1)}, u32[]{:S(2)}, u32[]{:S(2)}) %collective-permute-start.8) | collective-permute-done | bytes 393248 | tf_op jit(solution)/shard_map/ppermute | solution.py:535
  22.5 4.8 %collective-permute-start.9 = (bf16[3,128,512]{2,1,0:T(8,128)(2,1)S(1)}, bf16[3,128,512]{2,1,0:T(8,128)(2,1)}, u32[]{:S(2)}, u32[]{:S(2)}) collective-permute-start(bf16[3,128,512]{2,1,0:T(8,128)(2,1)S(1)} %collective-permute-done.8.near_w), channel_id=1, source_target_pairs={{0,1},{1,0},{2,3},{3,2},{4,5},{5,4},{6,7},{7,6},{8,9},{9,8},{10,11... | collective-permute-start | bytes 1179656 | tf_op jit(solution)/shard_map/ppermute | solution.py:536
  27.3 3.6 %collective-permute-done.11.weights = bf16[3,128,512]{2,1,0:T(8,128)(2,1)S(1)} collective-permute-done((bf16[3,128,512]{2,1,0:T(8,128)(2,1)S(1)}, bf16[3,128,512]{2,1,0:T(8,128)(2,1)S(1)}, u32[]{:S(2)}, u32[]{:S(2)}) %collective-permute-start.11) | collective-permute-done | bytes 393248 | tf_op jit(solution)/shard_map/ppermute | solution.py:535
  30.9 2.2 %collective-permute-start.12 = (bf16[3,128,512]{2,1,0:T(8,128)(2,1)S(1)}, bf16[3,128,512]{2,1,0:T(8,128)(2,1)}, u32[]{:S(2)}, u32[]{:S(2)}) collective-permute-start(bf16[3,128,512]{2,1,0:T(8,128)(2,1)S(1)} %collective-permute-done.11.weights), channel_id=1, source_target_pairs={{0,1},{1,0},{2,3},{3,2},{4,5},{5,4},{6,7},{7,6},{8,9},{9,8},{10,11... | collective-permute-start | bytes 1179656 | tf_op jit(solution)/shard_map/ppermute | solution.py:536
  35.1 7.4 %collective-permute-done.4.refs_5_ = bf16[128,128]{1,0:T(8,128)(2,1)S(1)} collective-permute-done((bf16[128,128]{1,0:T(8,128)(2,1)S(1)}, bf16[128,128]{1,0:T(8,128)(2,1)S(1)}, u32[]{:S(2)}, u32[]{:S(2)}) %collective-permute-start.4) | collective-permute-done | bytes 32800 | tf_op jit(solution)/shard_map/ppermute | solution.py:526
  44.8 3.4 %collective-permute-done.refs_1_ = bf16[512,128]{1,0:T(8,128)(2,1)S(1)} collective-permute-done((bf16[512,128]{1,0:T(8,128)(2,1)}, bf16[512,128]{1,0:T(8,128)(2,1)S(1)}, u32[]{:S(2)}, u32[]{:S(2)}) %collective-permute-start) | collective-permute-done | bytes 131104 | tf_op jit(solution)/shard_map/ppermute | solution.py:515
  56.5 2.9 %shard_map.105 = (bf16[256,1152]{1,0:T(8,128)(2,1)S(1)}, bf16[3,512,1152]{2,1,0:T(8,128)(2,1)S(1)}) custom-call(s32[3]{0:T(128)S(1)} %copy-done.11, s32[1]{0:T(128)} %bitcast.side, s32[1]{0:T(128)} %bitcast.1.place, bf16[256,1152]{1,0:T(8,128)(2,1)S(1)} %get-tuple-element.22.mine, bf16[256,1152]{1,0:T(8,128)(2,1)S(1)} %get-tuple-element.23.theirs, ...), custom_call_target="tpu_custom_call" | custom-call | tf_op jit(solution)/shard_map/pallas_call | solution.py:485
  59.4 2.5 %shard_map.106.theirs = bf16[256,1152]{1,0:T(8,128)(2,1)S(1)} custom-call(s32[1]{0:T(128)S(6)} %and.14.core, s32[1]{0:T(128)} %bitcast.1.place, bf16[256,1152]{1,0:T(8,128)(2,1)S(1)} %get-tuple-element.23.theirs, bf16[3,512,1152]{2,1,0:T(8,128)(2,1)S(1)} %get-tuple-element.25.taps, bf16[3,128,512]{2,1,0:T(8,128)(2,1)S(1)} %collective-permute-done.5.near_w, ...), custom_call_target="tpu_custom_call" | custom-call | tf_op jit(solution)/shard_map/pallas_call | solution.py:485
  61.9 2.9 %shard_map.107 = (bf16[256,1152]{1,0:T(8,128)(2,1)S(1)}, bf16[3,512,1152]{2,1,0:T(8,128)(2,1)S(1)}) custom-call(s32[3]{0:T(128)S(1)} %copy-done.11, s32[1]{0:T(128)} %bitcast.side, s32[1]{0:T(128)} %bitcast.1.place, bf16[256,1152]{1,0:T(8,128)(2,1)S(1)} %get-tuple-element.24.mine, bf16[256,1152]{1,0:T(8,128)(2,1)S(1)} %shard_map.106.theirs, ...), custom_call_target="tpu_custom_call" | custom-call | tf_op jit(solution)/shard_map/pallas_call | solution.py:485
  64.7 2.4 %shard_map.108.theirs = bf16[256,1152]{1,0:T(8,128)(2,1)S(1)} custom-call(s32[1]{0:T(128)S(6)} %and.14.core, s32[1]{0:T(128)} %bitcast.1.place, bf16[256,1152]{1,0:T(8,128)(2,1)S(1)} %shard_map.106.theirs, bf16[3,512,1152]{2,1,0:T(8,128)(2,1)S(1)} %get-tuple-element.27.taps, bf16[3,128,512]{2,1,0:T(8,128)(2,1)S(1)} %collective-permute-done.8.near_w, ...), custom_call_target="tpu_custom_call" | custom-call | tf_op jit(solution)/shard_map/pallas_call | solution.py:485
  67.2 3.3 %shard_map.109 = (bf16[256,1024]{1,0:T(8,128)(2,1)}, bf16[256,1024]{1,0:T(8,128)(2,1)S(1)}, bf16[3,512,1152]{2,1,0:T(8,128)(2,1)S(1)}) custom-call(s32[3]{0:T(128)S(1)} %copy-done.11, s32[1]{0:T(128)} %bitcast.side, s32[1]{0:T(128)} %bitcast.1.place, bf16[256,1152]{1,0:T(8,128)(2,1)S(1)} %get-tuple-element.26.mine, bf16[256,1152]{1,0:T(8,128)(2,1)S(1)} %shard_map.108.theirs, ...), custom_call_target="tpu_custom_call" | custom-call | tf_op jit(solution)/shard_map/pallas_call | solution.py:485
  71.2 2.6 %shard_map.111 = (bf16[128,1024]{1,0:T(8,128)(2,1)S(1)}, bf16[128,1024]{1,0:T(8,128)(2,1)S(1)}, bf16[1024,128]{1,0:T(8,128)(2,1)S(1)}, bf16[1024,128]{1,0:T(8,128)(2,1)S(1)}) custom-call(s32[1]{0:T(128)} %bitcast.side, s32[1]{0:T(128)S(6)} %and.14.core, bf16[256,1024]{1,0:T(8,128)(2,1)S(1)} %get-tuple-element.30.features, ...), custom_call_target="tpu_custom_call" | custom-call | tf_op jit(solution)/shard_map/pallas_call | solution.py:485
  75.8 3.6 %attend_send.3 = bf16[72,1024]{1,0:T(8,128)(2,1)S(1)} custom-call(s32[1]{0:T(128)S(6)} %sub.8.which, s32[1]{0:T(128)S(6)} %sub.9.half, s32[1]{0:T(128)S(6)} %copy.13.valid_own, s32[1]{0:T(128)} %collective-permute-done.10.valid_rec, bf16[128,1024]{1,0:T(8,128)(2,1)S(1)} %get-tuple-element.32.key_own, bf16[128,1024]{1,0:T(8,128)(2,1)S(1)} %collective-permute-done.13.key_rec, ...), custom_call_target="tpu_custom_call" | custom-call | tf_op jit(solution)/shard_map/attend_send/pallas_call | solution.py:430
  79.4 4.1 %collective-permute-start.16 = (bf16[72,1024]{1,0:T(8,128)(2,1)S(1)}, bf16[72,1024]{1,0:T(8,128)(2,1)S(1)}, u32[]{:S(2)}, u32[]{:S(2)}) collective-permute-start(bf16[72,1024]{1,0:T(8,128)(2,1)S(1)} %attend_send.3), channel_id=1, source_target_pairs={{0,2},{1,3},{2,0},{3,1},{4,6},{5,7},{6,4},{7,5},{8,10},{9,11},{10,... | collective-permute-start | bytes 442376 | tf_op jit(solution)/shard_map/ppermute | solution.py:588
  83.6 3.4 %attend_send.2 = bf16[72,1024]{1,0:T(8,128)(2,1)S(1)} custom-call(s32[1]{0:T(128)S(6)} %sub.8.which, s32[1]{0:T(128)S(6)} %and.16.half.lower, s32[1]{0:T(128)S(6)} %copy.13.valid_own, s32[1]{0:T(128)} %collective-permute-done.10.valid_rec, bf16[128,1024]{1,0:T(8,128)(2,1)S(1)} %get-tuple-element.32.key_own, ...), custom_call_target="tpu_custom_call" | custom-call | tf_op jit(solution)/shard_map/attend_send/pallas_call | solution.py:430
  87.1 3.4 %attend_keep.3 = (f32[1,1024]{1,0:T(1,128)S(1)}, f32[1,1024]{1,0:T(1,128)S(1)}, f32[64,1024]{1,0:T(8,128)S(1)}) custom-call(s32[1]{0:T(128)S(6)} %and.15.which.cross, s32[1]{0:T(128)S(6)} %sub.9.half, s32[1]{0:T(128)S(6)} %copy.13.valid_own, s32[1]{0:T(128)} %collective-permute-done.10.valid_rec, bf16[128,1024]{1,0:T(8,128)(2,1)S(1)} %get-tuple-element.32.key_own, ...), custom_call_target="tpu_custom_call" | custom-call | tf_op jit(solution)/shard_map/attend_keep/pallas_call | solution.py:430
  90.6 2.3 %collective-permute-start.17 = (bf16[72,1024]{1,0:T(8,128)(2,1)S(1)}, bf16[72,1024]{1,0:T(8,128)(2,1)S(1)}, u32[]{:S(2)}, u32[]{:S(2)}) collective-permute-start(bf16[72,1024]{1,0:T(8,128)(2,1)S(1)} %shard_map.113), channel_id=1, source_target_pairs={{0,4},{1,5},{2,6},{3,7},{4,0},{5,1},{6,2},{7,3},{8,12},{9,13},{10,... | collective-permute-start | bytes 442376 | tf_op jit(solution)/shard_map/ppermute | solution.py:588
  92.9 3.4 %attend_keep.2 = (f32[1,1024]{1,0:T(1,128)S(1)}, f32[1,1024]{1,0:T(1,128)S(1)}, f32[64,1024]{1,0:T(8,128)S(1)}) custom-call(s32[1]{0:T(128)S(6)} %and.15.which.cross, s32[1]{0:T(128)S(6)} %and.16.half.lower, s32[1]{0:T(128)S(6)} %copy.13.valid_own, s32[1]{0:T(128)} %collective-permute-done.10.valid_rec, bf16[128,1024]{1,0:T(8,128)(2,1)S(1)} %get-tuple-element.32.key_own, ...), custom_call_target="tpu_custom_call" | custom-call | tf_op jit(solution)/shard_map/attend_keep/pallas_call | solution.py:430
  96.7 2.8 %collective-permute-start.18 = (bf16[72,1024]{1,0:T(8,128)(2,1)S(1)}, bf16[72,1024]{1,0:T(8,128)(2,1)S(1)}, u32[]{:S(2)}, u32[]{:S(2)}) collective-permute-start(bf16[72,1024]{1,0:T(8,128)(2,1)S(1)} %shard_map.114.mine), channel_id=1, source_target_pairs={{0,8},{1,9},{2,10},{3,11},{4,12},{5,13},{6,14},{7,15},{8,0},{9,1},... | collective-permute-start | bytes 442376 | tf_op jit(solution)/shard_map/ppermute | solution.py:588
  99.5 6.2 %collective-permute-done.18.theirs = bf16[72,1024]{1,0:T(8,128)(2,1)S(1)} collective-permute-done((bf16[72,1024]{1,0:T(8,128)(2,1)S(1)}, bf16[72,1024]{1,0:T(8,128)(2,1)S(1)}, u32[]{:S(2)}, u32[]{:S(2)}) %collective-permute-start.18) | collective-permute-done | bytes 147488 | tf_op jit(solution)/shard_map/ppermute | solution.py:588
  109.3 2.8 %collective-permute-done.21.refs_1_ = bf16[64,1024]{1,0:T(8,128)(2,1)S(1)} collective-permute-done((bf16[64,1024]{1,0:T(8,128)(2,1)S(1)}, bf16[64,1024]{1,0:T(8,128)(2,1)S(1)}, u32[]{:S(2)}, u32[]{:S(2)}) %collective-permute-start.21) | collective-permute-done | bytes 131104 | tf_op jit(solution)/shard_map/ppermute | solution.py:588
  (75 shorter events, 29.3 us)
Async XLA Ops:
  1.6 4.8 %collective-permute-start.2 = (bf16[128,128]{1,0:T(8,128)(2,1)S(1)}, bf16[128,128]{1,0:T(8,128)(2,1)S(1)}, u32[]{:S(2)}, u32[]{:S(2)}) collective-permute-start(bf16[128,128]{1,0:T(8,128)(2,1)S(1)} %get-tuple-element.45), channel_id=1, source_target_pairs={{0,1},{1,0},{2,3},{3,2},{4,5},{5,4},{6,7},{7,6},{8,9},{9,8},{10,11... | collective-permute-start | bytes 98312 | tf_op jit(solution)/shard_map/ppermute | solution.py:523
  2.1 4.3 %collective-permute-start.3 = (bf16[128,128]{1,0:T(8,128)(2,1)S(1)}, bf16[128,128]{1,0:T(8,128)(2,1)S(1)}, u32[]{:S(2)}, u32[]{:S(2)}) collective-permute-start(bf16[128,128]{1,0:T(8,128)(2,1)S(1)} %get-tuple-element.44), channel_id=1, source_target_pairs={{1,2},{3,4},{5,6},{7,8},{9,10},{11,12},{13,14},{2,1},{4,3},{6,5},{... | collective-permute-start | bytes 98312 | tf_op jit(solution)/shard_map/ppermute | solution.py:519
  3.8 10.2 %collective-permute-start.5 = (bf16[3,128,512]{2,1,0:T(8,128)(2,1)S(1)}, bf16[3,128,512]{2,1,0:T(8,128)(2,1)S(1)}, u32[]{:S(2)}, u32[]{:S(2)}) collective-permute-start(bf16[3,128,512]{2,1,0:T(8,128)(2,1)S(1)} %dynamic-slice_bitcast_fusion.2), channel_id=1, source_target_pairs={{0,16},{16,0},{1,17},{17,1},{2,18},{18,2},{3,19},{19,3},{4,20},{20... | collective-permute-start | bytes 1179656 | tf_op jit(solution)/shard_map/ppermute | solution.py:535
  7.7 14.8 %collective-permute-start.8 = (bf16[3,128,512]{2,1,0:T(8,128)(2,1)S(1)}, bf16[3,128,512]{2,1,0:T(8,128)(2,1)S(1)}, u32[]{:S(2)}, u32[]{:S(2)}) collective-permute-start(bf16[3,128,512]{2,1,0:T(8,128)(2,1)S(1)} %get-tuple-element.43), channel_id=1, source_target_pairs={{0,16},{16,0},{1,17},{17,1},{2,18},{18,2},{3,19},{19,3},{4,20},{20... | collective-permute-start | bytes 1179656 | tf_op jit(solution)/shard_map/ppermute | solution.py:535
  7.8 23.1 %collective-permute-start.11 = (bf16[3,128,512]{2,1,0:T(8,128)(2,1)S(1)}, bf16[3,128,512]{2,1,0:T(8,128)(2,1)S(1)}, u32[]{:S(2)}, u32[]{:S(2)}) collective-permute-start(bf16[3,128,512]{2,1,0:T(8,128)(2,1)S(1)} %get-tuple-element.42), channel_id=1, source_target_pairs={{0,16},{16,0},{1,17},{17,1},{2,18},{18,2},{3,19},{19,3},{4,20},{20... | collective-permute-start | bytes 1179656 | tf_op jit(solution)/shard_map/ppermute | solution.py:535
  14.1 45.3 %collective-permute-start.6 = (bf16[3,128,512]{2,1,0:T(8,128)(2,1)S(1)}, bf16[3,128,512]{2,1,0:T(8,128)(2,1)}, u32[]{:S(2)}, u32[]{:S(2)}) collective-permute-start(bf16[3,128,512]{2,1,0:T(8,128)(2,1)S(1)} %collective-permute-done.5.near_w), channel_id=1, source_target_pairs={{0,1},{1,0},{2,3},{3,2},{4,5},{5,4},{6,7},{7,6},{8,9},{9,8},{10,11... | collective-permute-start | bytes 1179656 | tf_op jit(solution)/shard_map/ppermute | solution.py:536
  22.5 42.2 %collective-permute-start.9 = (bf16[3,128,512]{2,1,0:T(8,128)(2,1)S(1)}, bf16[3,128,512]{2,1,0:T(8,128)(2,1)}, u32[]{:S(2)}, u32[]{:S(2)}) collective-permute-start(bf16[3,128,512]{2,1,0:T(8,128)(2,1)S(1)} %collective-permute-done.8.near_w), channel_id=1, source_target_pairs={{0,1},{1,0},{2,3},{3,2},{4,5},{5,4},{6,7},{7,6},{8,9},{9,8},{10,11... | collective-permute-start | bytes 1179656 | tf_op jit(solution)/shard_map/ppermute | solution.py:536
  30.9 40.2 %collective-permute-start.12 = (bf16[3,128,512]{2,1,0:T(8,128)(2,1)S(1)}, bf16[3,128,512]{2,1,0:T(8,128)(2,1)}, u32[]{:S(2)}, u32[]{:S(2)}) collective-permute-start(bf16[3,128,512]{2,1,0:T(8,128)(2,1)S(1)} %collective-permute-done.11.weights), channel_id=1, source_target_pairs={{0,1},{1,0},{2,3},{3,2},{4,5},{5,4},{6,7},{7,6},{8,9},{9,8},{10,11... | collective-permute-start | bytes 1179656 | tf_op jit(solution)/shard_map/ppermute | solution.py:536
  33.1 17.6 %collective-permute-start.1 = (bf16[128,1024]{1,0:T(8,128)(2,1)}, bf16[128,1024]{1,0:T(8,128)(2,1)}, u32[]{:S(2)}, u32[]{:S(2)}) collective-permute-start(bf16[128,1024]{1,0:T(8,128)(2,1)} %refs_2_.1), channel_id=1, source_target_pairs={{0,16},{16,0},{1,17},{17,1},{2,18},{18,2},{3,19},{19,3},{4,20},{20... | collective-permute-start | bytes 786440 | tf_op jit(solution)/shard_map/ppermute | solution.py:514
  35.1 7.4 %collective-permute-start.4 = (bf16[128,128]{1,0:T(8,128)(2,1)S(1)}, bf16[128,128]{1,0:T(8,128)(2,1)S(1)}, u32[]{:S(2)}, u32[]{:S(2)}) collective-permute-start(bf16[128,128]{1,0:T(8,128)(2,1)S(1)} %broadcast_select_fusion.2.refs_4_), channel_id=1, source_target_pairs={{0,16},{16,0},{1,17},{17,1},{2,18},{18,2},{3,19},{19,3},{4,20},{20... | collective-permute-start | bytes 98312 | tf_op jit(solution)/shard_map/ppermute | solution.py:526
  43.1 5.2 %collective-permute-start = (bf16[512,128]{1,0:T(8,128)(2,1)}, bf16[512,128]{1,0:T(8,128)(2,1)S(1)}, u32[]{:S(2)}, u32[]{:S(2)}) collective-permute-start(bf16[512,128]{1,0:T(8,128)(2,1)} %refs_0_.1), channel_id=1, source_target_pairs={{0,16},{16,0},{1,17},{17,1},{2,18},{18,2},{3,19},{19,3},{4,20},{20... | collective-permute-start | bytes 393224 | tf_op jit(solution)/shard_map/ppermute | solution.py:515
  48.9 10.4 %collective-permute-start.7 = (f32[3,256]{1,0:T(4,128)}, f32[3,256]{1,0:T(4,128)S(1)}, u32[]{:S(2)}, u32[]{:S(2)}) collective-permute-start(f32[3,256]{1,0:T(4,128)} %biases.5), channel_id=1, source_target_pairs={{0,16},{16,0},{1,17},{17,1},{2,18},{18,2},{3,19},{19,3},{4,20},{20... | collective-permute-start | bytes 9224 | tf_op jit(solution)/shard_map/ppermute | solution.py:527
  73.7 2.1 %collective-permute-start.13 = (bf16[128,1024]{1,0:T(8,128)(2,1)S(1)}, bf16[128,1024]{1,0:T(8,128)(2,1)S(1)}, u32[]{:S(2)}, u32[]{:S(2)}) collective-permute-start(bf16[128,1024]{1,0:T(8,128)(2,1)S(1)} %get-tuple-element.33), channel_id=1, source_target_pairs={{0,1},{1,0},{2,3},{3,2},{4,5},{5,4},{6,7},{7,6},{8,9},{9,8},{10,11... | collective-permute-start | bytes 786440 | tf_op jit(solution)/shard_map/ppermute | solution.py:583
  73.8 2.0 %collective-permute-start.14 = (bf16[1024,128]{1,0:T(8,128)(2,1)S(1)}, bf16[1024,128]{1,0:T(8,128)(2,1)S(1)}, u32[]{:S(2)}, u32[]{:S(2)}) collective-permute-start(bf16[1024,128]{1,0:T(8,128)(2,1)S(1)} %get-tuple-element.35), channel_id=1, source_target_pairs={{0,1},{1,0},{2,3},{3,2},{4,5},{5,4},{6,7},{7,6},{8,9},{9,8},{10,11... | collective-permute-start | bytes 786440 | tf_op jit(solution)/shard_map/ppermute | solution.py:584
  74.3 1.5 %collective-permute-start.10 = (s32[1]{0:T(128)}, s32[1]{0:T(128)}, u32[]{:S(2)}, u32[]{:S(2)}) collective-permute-start(s32[1]{0:T(128)} %param.14), channel_id=1, source_target_pairs={{0,1},{1,0},{2,3},{3,2},{4,5},{5,4},{6,7},{7,6},{8,9},{9,8},{10,11... | collective-permute-start | bytes 20 | tf_op jit(solution)/shard_map/ppermute | solution.py:585
  79.4 11.0 %collective-permute-start.16 = (bf16[72,1024]{1,0:T(8,128)(2,1)S(1)}, bf16[72,1024]{1,0:T(8,128)(2,1)S(1)}, u32[]{:S(2)}, u32[]{:S(2)}) collective-permute-start(bf16[72,1024]{1,0:T(8,128)(2,1)S(1)} %attend_send.3), channel_id=1, source_target_pairs={{0,2},{1,3},{2,0},{3,1},{4,6},{5,7},{6,4},{7,5},{8,10},{9,11},{10,... | collective-permute-start | bytes 442376 | tf_op jit(solution)/shard_map/ppermute | solution.py:588
  87.0 9.3 %collective-permute-start.15 = (bf16[72,1024]{1,0:T(8,128)(2,1)S(1)}, bf16[72,1024]{1,0:T(8,128)(2,1)S(1)}, u32[]{:S(2)}, u32[]{:S(2)}) collective-permute-start(bf16[72,1024]{1,0:T(8,128)(2,1)S(1)} %attend_send.2), channel_id=1, source_target_pairs={{0,2},{1,3},{2,0},{3,1},{4,6},{5,7},{6,4},{7,5},{8,10},{9,11},{10,... | collective-permute-start | bytes 442376 | tf_op jit(solution)/shard_map/ppermute | solution.py:588
  90.6 5.9 %collective-permute-start.17 = (bf16[72,1024]{1,0:T(8,128)(2,1)S(1)}, bf16[72,1024]{1,0:T(8,128)(2,1)S(1)}, u32[]{:S(2)}, u32[]{:S(2)}) collective-permute-start(bf16[72,1024]{1,0:T(8,128)(2,1)S(1)} %shard_map.113), channel_id=1, source_target_pairs={{0,4},{1,5},{2,6},{3,7},{4,0},{5,1},{6,2},{7,3},{8,12},{9,13},{10,... | collective-permute-start | bytes 442376 | tf_op jit(solution)/shard_map/ppermute | solution.py:588
  96.7 9.0 %collective-permute-start.18 = (bf16[72,1024]{1,0:T(8,128)(2,1)S(1)}, bf16[72,1024]{1,0:T(8,128)(2,1)S(1)}, u32[]{:S(2)}, u32[]{:S(2)}) collective-permute-start(bf16[72,1024]{1,0:T(8,128)(2,1)S(1)} %shard_map.114.mine), channel_id=1, source_target_pairs={{0,8},{1,9},{2,10},{3,11},{4,12},{5,13},{6,14},{7,15},{8,0},{9,1},... | collective-permute-start | bytes 442376 | tf_op jit(solution)/shard_map/ppermute | solution.py:588
  105.8 6.4 %collective-permute-start.21 = (bf16[64,1024]{1,0:T(8,128)(2,1)S(1)}, bf16[64,1024]{1,0:T(8,128)(2,1)S(1)}, u32[]{:S(2)}, u32[]{:S(2)}) collective-permute-start(bf16[64,1024]{1,0:T(8,128)(2,1)S(1)} %shard_map.115.refs_0_), channel_id=1, source_target_pairs={{0,4},{1,5},{2,6},{3,7},{4,0},{5,1},{6,2},{7,3},{8,12},{9,13},{10,... | collective-permute-start | bytes 393224 | tf_op jit(solution)/shard_map/ppermute | solution.py:588
  106.4 6.2 %collective-permute-start.22 = (bf16[64,1024]{1,0:T(8,128)(2,1)S(1)}, bf16[64,1024]{1,0:T(8,128)(2,1)S(1)}, u32[]{:S(2)}, u32[]{:S(2)}) collective-permute-start(bf16[64,1024]{1,0:T(8,128)(2,1)S(1)} %shard_map.115.refs_0_), channel_id=1, source_target_pairs={{0,2},{1,3},{2,0},{3,1},{4,6},{5,7},{6,4},{7,5},{8,10},{9,11},{10,... | collective-permute-start | bytes 393224 | tf_op jit(solution)/shard_map/ppermute | solution.py:588
  107.2 6.8 %collective-permute-start.19 = (bf16[64,1024]{1,0:T(8,128)(2,1)S(1)}, bf16[64,1024]{1,0:T(8,128)(2,1)S(1)}, u32[]{:S(2)}, u32[]{:S(2)}) collective-permute-start(bf16[64,1024]{1,0:T(8,128)(2,1)S(1)} %shard_map.115.refs_0_), channel_id=1, source_target_pairs={{0,6},{1,7},{2,4},{3,5},{4,2},{5,3},{6,0},{7,1},{8,14},{9,15},{10,... | collective-permute-start | bytes 393224 | tf_op jit(solution)/shard_map/ppermute | solution.py:588
  109.3 4.7 %collective-permute-start.23 = (bf16[64,1024]{1,0:T(8,128)(2,1)S(1)}, bf16[64,1024]{1,0:T(8,128)(2,1)S(1)}, u32[]{:S(2)}, u32[]{:S(2)}) collective-permute-start(bf16[64,1024]{1,0:T(8,128)(2,1)S(1)} %shard_map.115.refs_0_), channel_id=1, source_target_pairs={{0,1},{1,0},{2,3},{3,2},{4,5},{5,4},{6,7},{7,6},{8,9},{9,8},{10,11... | collective-permute-start | bytes 393224 | tf_op jit(solution)/shard_map/ppermute | solution.py:588
  112.1 1.9 %collective-permute-start.24 = (bf16[64,1024]{1,0:T(8,128)(2,1)S(1)}, bf16[64,1024]{1,0:T(8,128)(2,1)S(1)}, u32[]{:S(2)}, u32[]{:S(2)}) collective-permute-start(bf16[64,1024]{1,0:T(8,128)(2,1)S(1)} %collective-permute-done.21.refs_1_), channel_id=1, source_target_pairs={{0,1},{1,0},{2,3},{3,2},{4,5},{5,4},{6,7},{7,6},{8,9},{9,8},{10,11... | collective-permute-start | bytes 393224 | tf_op jit(solution)/shard_map/ppermute | solution.py:588
  (14 other events, 102.8 us)
